TPU v7x, 32 devices: a whole 2x2x4 slice. The times are simulated.
32 devices in a mesh: groups: 2 (over x), ctx: 16 (over z, y, core).
Axes of the slice: x: 2, y: 2, z: 4, core: 2. Of those that a mesh axis runs over, the one named last changes fastest.
Arguments:
- hidden: bfloat16 [4096, 2048], P(('groups', 'ctx')), parts along dimension 0, may hold values from -6 to 6
- w_query: bfloat16 [2048, 2048], P('ctx')
- w_keyval: bfloat16 [2048, 1024], P('ctx')
- w_out: bfloat16 [2048, 2048], P('ctx'), may hold values from -1.796875 to 1.796875
- global_blocks: int32 [4], P('groups'), parts along dimension 0, may hold values from 0 to 15, as said below
- cotangent: bfloat16 [4096, 2048], P(('groups', 'ctx')), parts along dimension 0, may hold values from -6 to 6
Outputs:
- combined: bfloat16 [4096, 2048], P(('groups', 'ctx')), parts along dimension 0
- input_grad: bfloat16 [4096, 2048], P(('groups', 'ctx')), parts along dimension 0
There are 2 independent parts, one for each index of `groups`. A program takes and returns all parts, laid end to end along the dimension named above; an argument that names none is the same for every part. Nothing has to cross between parts.
Inputs may be any that keep to these rules, and one draw needn't show every extreme that they name: `global_blocks`: 2 distinct block indices; the last block, 15, is always one of them, at a position drawn from the seed.
All inputs are finite; a program needn't handle non-finite values.
Results may differ from a plain program's by a relative error of at most 0.0098.
Values may be sent and summed in bfloat16 or wider, within the bound.
No kernel may reach another device: no remote copies, remote signals or barrier semaphores. Data moves between devices by JAX's collectives and lax.ppermute only.
A program may use at most 128 MiB of HBM per device.

v0:
```python
import jax
import jax.numpy as jnp
from jax import lax
from jax.sharding import PartitionSpec as P

HEADS = 16
KVH = 4
HDIM = 128
BLK = 128


epsilon = 1e-05


def with_halo(cells, sides, width):
    for axis, dim in sides:
        count = lax.axis_size(axis)
        ends = count - 1
        head = lax.slice_in_dim(cells, 0, width, axis=dim)
        tail = lax.slice_in_dim(cells, cells.shape[dim] - width, cells.shape[dim], axis=dim)
        cells = jnp.concatenate(
            [
                lax.ppermute(tail, axis, [(i, (i + 1) % count) for i in range(ends)]),
                cells,
                lax.ppermute(head, axis, [((i + 1) % count, i) for i in range(ends)]),
            ],
            axis=dim,
        )
    return cells


def spread_2(value, axis, source):
    kept = jnp.where(lax.axis_index(axis) == source, value, 0).astype(value.dtype)
    return lax.psum(kept, axis)


def normalize(values):
    widened = values.astype(jnp.float32)
    inv_rms = lax.rsqrt(jnp.mean(widened * widened, axis=1, keepdims=True) + epsilon)
    return (widened * inv_rms, inv_rms)


def split_heads(row_values, block_count):
    return row_values.reshape(block_count, BLK, KVH, HEADS // KVH, HDIM)


def body(hidden, w_query, w_keyval, w_out, global_blocks, cotangent):
    row_count = hidden.shape[0]
    per_device = row_count // BLK
    block_count = 2 * per_device
    kv_width = w_keyval.shape[1]
    half_width = kv_width // 2
    global_count = global_blocks.shape[0]
    devices = lax.axis_size("ctx")
    my_index = lax.axis_index("ctx")
    full_query, full_keyval, full_output = (
        lax.all_gather(w_query, "ctx", axis=0, tiled=True),
        lax.all_gather(w_keyval, "ctx", axis=0, tiled=True),
        lax.all_gather(w_out, "ctx", axis=0, tiled=True),
    )
    stacked = jnp.concatenate([hidden, hidden[::-1, ::-1]], axis=0)
    scaled, inv_rms = normalize(stacked)
    normed = scaled.astype(jnp.bfloat16)
    queries = jnp.dot(normed, full_query, preferred_element_type=jnp.float32).astype(jnp.bfloat16)
    keyvals = jnp.dot(normed, full_keyval, preferred_element_type=jnp.float32).astype(jnp.bfloat16)
    kv_blocks = keyvals.reshape(2, per_device, BLK, kv_width)
    border = jnp.concatenate([kv_blocks[1, -1], kv_blocks[0, -1]], axis=0)
    padded = with_halo(border, (("ctx", 0),), BLK)
    neighbors = jnp.stack([padded[:BLK], padded[3 * BLK :]])
    extended = jnp.concatenate([neighbors[:, None], kv_blocks], axis=1)
    slot_index = global_blocks % per_device
    plain_owner = global_blocks // per_device
    owners = jnp.stack([plain_owner, devices - 1 - plain_owner])
    pieces = jnp.take(kv_blocks, slot_index, axis=1)
    collected = []
    for branch in range(2):
        for position in range(global_count):
            collected.append(spread_2(pieces[branch, position], "ctx", owners[branch, position]))
    global_keys = jnp.stack(collected).reshape(2, global_count, BLK, kv_width)
    paired = jnp.concatenate([extended[:, :-1], extended[:, 1:]], axis=2)
    spread = global_keys.reshape(2, 1, global_count * BLK, kv_width)
    key_sets = jnp.concatenate([paired, spread], axis=2).reshape(block_count, -1, kv_width)
    key_count = key_sets.shape[1]
    keys_only = key_sets[:, :, :half_width].reshape(block_count, key_count, KVH, HDIM)
    values_only = key_sets[:, :, half_width:].reshape(block_count, key_count, KVH, HDIM)
    first_ids = jnp.stack([my_index * per_device, (devices - 1 - my_index) * per_device])
    block_ids = (first_ids[:, None] + jnp.arange(per_device)[None, :]).reshape(block_count)
    global_flags = (global_blocks[None, :] != block_ids[:, None]) & (
        global_blocks[None, :] != block_ids[:, None] - 1
    )
    key_flags = jnp.concatenate(
        [(block_ids >= 1)[:, None], (block_ids >= 0)[:, None], global_flags], axis=1
    )
    validity = jnp.repeat(key_flags, BLK, axis=1)[:, None, None, None, :]
    query_heads = split_heads(queries, block_count)
    scores = jnp.einsum(
        "bqgrd,bkgd->bgrqk", query_heads, keys_only, preferred_element_type=jnp.float32
    ) * HDIM ** (-0.5)
    scores = jnp.where(validity, scores, -jnp.inf)
    exponent = jnp.exp(scores - jnp.max(scores, axis=-1, keepdims=True))
    prob_full = exponent / jnp.sum(exponent, axis=-1, keepdims=True)
    prob_half = prob_full.astype(jnp.bfloat16)
    attended = jnp.einsum(
        "bgrqk,bkgd->bqgrd", prob_half, values_only, preferred_element_type=jnp.float32
    )
    attended = attended.astype(jnp.bfloat16).reshape(2 * row_count, -1)
    outputs = jnp.dot(attended, full_output, preferred_element_type=jnp.float32)
    combined = (outputs[:row_count] + outputs[row_count:][::-1]).astype(jnp.bfloat16)
    grad_rows = jnp.concatenate([cotangent, cotangent[::-1]], axis=0)
    grad_att = jnp.dot(grad_rows, full_output.T, preferred_element_type=jnp.float32).astype(
        jnp.bfloat16
    )
    upstream = split_heads(grad_att, block_count)
    grad_prob = jnp.einsum(
        "bqgrd,bkgd->bgrqk", upstream, values_only, preferred_element_type=jnp.float32
    )
    center = jnp.sum(prob_full * grad_prob, axis=-1, keepdims=True)
    grad_score = (prob_full * (grad_prob - center) * HDIM ** (-0.5)).astype(jnp.bfloat16)
    grad_query = jnp.einsum(
        "bgrqk,bkgd->bqgrd", grad_score, keys_only, preferred_element_type=jnp.float32
    )
    grad_query = grad_query.astype(jnp.bfloat16).reshape(2 * row_count, -1)
    grad_keys = jnp.einsum(
        "bgrqk,bqgrd->bkgd", grad_score, query_heads, preferred_element_type=jnp.float32
    ).reshape(block_count, key_count, half_width)
    grad_values = jnp.einsum(
        "bgrqk,bqgrd->bkgd", prob_half, upstream, preferred_element_type=jnp.float32
    ).reshape(block_count, key_count, half_width)
    key_terms = jnp.concatenate([grad_keys, grad_values], axis=-1).reshape(
        2, per_device, 2 + global_count, BLK, kv_width
    )
    ext_grad = jnp.pad(key_terms[:, :, 0], ((0, 0), (0, 1), (0, 0), (0, 0))) + jnp.pad(
        key_terms[:, :, 1], ((0, 0), (1, 0), (0, 0), (0, 0))
    )
    outgoing = jnp.concatenate([ext_grad[0, 0], ext_grad[1, 0]], axis=0)
    returned = with_halo(outgoing.astype(jnp.bfloat16), (("ctx", 0),), BLK).astype(outgoing.dtype)
    own_grads = ext_grad[:, 1:]
    own_grads = own_grads.at[0, -1].add(returned[3 * BLK :])
    own_grads = own_grads.at[1, -1].add(returned[:BLK])
    totals = lax.psum(jnp.sum(key_terms[:, :, 2:], axis=1), "ctx")
    hot_table = (
        (jnp.arange(per_device)[None, None, :] == slot_index[None, :, None])
        & (owners[:, :, None] == my_index)
    ).astype(jnp.float32)
    own_grads = own_grads + jnp.sum(hot_table[:, :, :, None, None] * totals[:, :, None], axis=1)
    key_grads = own_grads.reshape(2 * row_count, kv_width).astype(jnp.bfloat16)
    grad_norm = jnp.dot(grad_query, full_query.T, preferred_element_type=jnp.float32)
    grad_norm = grad_norm + jnp.dot(key_grads, full_keyval.T, preferred_element_type=jnp.float32)
    grad_in = inv_rms * (grad_norm - scaled * jnp.mean(grad_norm * scaled, axis=1, keepdims=True))
    input_grad = (grad_in[:row_count] + grad_in[row_count:][::-1, ::-1]).astype(jnp.bfloat16)
    return (combined, input_grad)


def solution(mesh):
    return jax.shard_map(
        body,
        mesh=mesh,
        in_specs=(
            P(("groups", "ctx"), None),
            P("ctx", None),
            P("ctx", None),
            P("ctx", None),
            P("groups"),
            P(("groups", "ctx"), None),
        ),
        out_specs=(P(("groups", "ctx"), None), P(("groups", "ctx"), None)),
        check_vma=False,
    )
```

profile of v0, /device:TPU:0, one launch (start us, length us, event | category | flops | bytes accessed | tf_op | source)
XLA Modules:
  0.0 514.8 jit_solution(2713949893909427027)
XLA Ops:
  7.2 0.7 all-gather.4.cloned.1.call-update
  7.9 7.0 %rev.12 = bf16[128,2048]{1,0:T(8,128)(2,1)S(1)} reverse(bf16[128,2048]{1,0:T(8,128)(2,1)} %param.10), dimensions={0,1} | reverse | bytes 1048576 | tf_op jit(solution)/shard_map/rev | solution.py:61
  14.9 1.4 fusion.65
  17.7 0.7 subtract_bitcast_fusion
  18.4 0.7 fusion.66
  20.4 1.3 fusion.21
  21.7 41.7 %all-gather.4.cloned.1.call-done = bf16[2048,1024]{1,0:T(8,128)(2,1)} async-done(((bf16[128,1024]{1,0:T(8,128)(2,1)}), bf16[2048,1024]{1,0:T(8,128)(2,1)}) %all-gather.4.cloned.1.call-update) | async-done | bytes 4194320 | tf_op jit(solution)/shard_map/all_gather | solution.py:58
  63.5 3.6 convolution_convert_fusion.2
  67.1 1.0 fusion.64
  68.2 0.7 all-gather.6.cloned.1.call-update
  69.0 0.5 all-gather.8.cloned.1.call-update
  69.8 1.3 collective-permute-start.1
  71.1 3.0 collective-permute-start
  74.2 5.2 %rev.14 = bf16[128,2048]{1,0:T(8,128)(2,1)} reverse(bf16[128,2048]{1,0:T(8,128)(2,1)S(1)} %copy-done.12), dimensions={0} | reverse | bytes 1048576 | tf_op jit(solution)/shard_map/rev | solution.py:109
  79.5 1.0 copy.24
  80.5 1.0 copy.23
  81.5 79.1 %all-reduce.8.cloned.1.call-done = (bf16[1,128,1024]{2,1,0:T(8,128)(2,1)}, bf16[1,128,1024]{2,1,0:T(8,128)(2,1)}, bf16[1,128,1024]{2,1,0:T(8,128)(2,1)}, bf16[1,128,1024]{2,1,0:T(8,128)(2,1)}) async-done(((bf16[1,128,1024]{2,1,0:T(8,128)(2,1)}, bf16[1,128,1024]{2,1,0:T(8,128)(2,1)}, bf16[1,128,1024]{2,1,0:T(8,128)(2,1)}, bf16[1,128,1024]{2,1,0:T(8,128)(2,1)}), (bf16[1,128,1024]{2,1,0:T(8,128)(2,1)}, ...) | async-done | bytes 1048592 | tf_op jit(solution)/shard_map/psum | solution.py:34
  160.7 1.3 pad_maximum_fusion.2
  162.0 0.5 copy.25
  162.5 1.4 maximum_bitcast_fusion
  164.0 1.1 fusion.63
  165.1 72.0 %all-gather.6.cloned.1.call-done = bf16[2048,2048]{1,0:T(8,128)(2,1)} async-done(((bf16[128,2048]{1,0:T(8,128)(2,1)}), bf16[2048,2048]{1,0:T(8,128)(2,1)}) %all-gather.6.cloned.1.call-update) | async-done | bytes 8388624 | tf_op jit(solution)/shard_map/all_gather | solution.py:57
  237.2 5.8 %convolution_convert_fusion.1 = bf16[256,2048]{1,0:T(8,128)(2,1)S(1)} fusion(bf16[2048,2048]{1,0:T(8,128)(2,1)} %all-gather.6.cloned.1.call-done, f32[256]{0:T(256)S(1)} %add_rsqrt_fusion, bf16[128,2048]{1,0:T(8,128)(2,1)S(1)} %rev.12, bf16[128,2048]{1,0:T(8,128)(2,1)S(1)} %copy-done.2), kind=kOutput, calls=%fused_computation.31 | convolution fusion | flops 2151153664 | bytes 10486784 | tf_op jit(solution)/shard_map/dot_general | solution.py:64
  242.9 0.8 reshape.284
  243.7 1.7 copy.34
  245.4 67.0 %all-gather.8.cloned.1.call-done = bf16[2048,2048]{1,0:T(8,128)(2,1)} async-done(((bf16[128,2048]{1,0:T(8,128)(2,1)}), bf16[2048,2048]{1,0:T(8,128)(2,1)}) %all-gather.8.cloned.1.call-update) | async-done | bytes 8388624 | tf_op jit(solution)/shard_map/all_gather | solution.py:59
  312.3 6.1 %convolution_convert_fusion = bf16[256,2048]{1,0:T(8,128)(2,1)S(1)} fusion(bf16[2048,2048]{1,0:T(8,128)(2,1)} %all-gather.8.cloned.1.call-done, bf16[128,2048]{1,0:T(8,128)(2,1)} %rev.14, bf16[128,2048]{1,0:T(8,128)(2,1)} %param.15), kind=kOutput, calls=%fused_computation.30 | convolution fusion | flops 2150105088 | bytes 10485760 | tf_op jit(solution)/shard_map/dot_general | solution.py:110
  318.4 0.8 reshape.286
  319.2 1.2 copy.36
  320.4 4.5 fusion.69
  324.9 7.5 %fusion.67 = (f32[2,4,4,128]{3,2,1,0:T(4,128)S(1)}, f32[2,4,4,128,512]{3,4,2,1,0:T(8,128)}) fusion(pred[2,512]{1,0:T(4,128)(4,1)S(1)} %bitcast.176, bf16[2,512,4,128,1]{1,3,4,2,0:T(8,128)(2,1)} %bitcast.170, bf16[2,128,4,4,128]{1,4,3,2,0:T(8,128)(2,1)S(1)} %copy-done.10), kind=kOutput, calls=%fused_computation.108 | convolution fusion | flops 545260032 | bytes 10503168 | tf_op jit(solution)/shard_map/sub | solution.py:100
  332.4 5.3 %fusion.37 = bf16[2,128,4,4,128]{1,4,3,2,0:T(8,128)(2,1)} fusion(bf16[2,512,4,128,1]{1,3,4,2,0:T(8,128)(2,1)S(1)} %bitcast.166, f32[2,4,4,128,512]{3,4,2,1,0:T(8,128)} %get-tuple-element.49, f32[2,4,4,128]{3,2,1,0:T(4,128)S(1)} %get-tuple-element.48), kind=kOutput, calls=%fused_computation.50 | convolution fusion | flops 541589504 | bytes 10502144 | tf_op jit(solution)/shard_map/bgrqk,bkgd->bqgrd/dot_general | solution.py:103
  337.8 0.8 copy-done.14
  338.6 1.5 fusion.28
  340.1 14.6 %fusion.36 = bf16[2,128,4,4,128]{1,4,3,2,0:T(8,128)(2,1)} fusion(bf16[2,512,4,128,1]{1,3,4,2,0:T(8,128)(2,1)} %bitcast.171, f32[2,4,512,128,4]{3,2,4,1,0:T(8,128)} %fusion.69, f32[2,4,4,128,512]{3,4,2,1,0:T(8,128)} %get-tuple-element.49, f32[2,4,4,128]{3,2,1,0:T(4,128)S(1)} %get-tuple-element.48), kind=kOutput, calls=%fused_computation.49 | convolution fusion | flops 552079872 | bytes 18890752 | tf_op jit(solution)/shard_map/bgrqk,bkgd->bqgrd/dot_general | solution.py:119
  354.6 13.4 %fusion.31 = f32[2,512,4,128]{1,3,2,0:T(8,128)} fusion(bf16[2,128,4,4,128]{1,4,3,2,0:T(8,128)(2,1)S(1)} %copy-done.11, f32[2,4,512,128,4]{3,2,4,1,0:T(8,128)} %fusion.69, f32[2,4,4,128,512]{3,4,2,1,0:T(8,128)} %get-tuple-element.49, f32[2,4,4,128]{3,2,1,0:T(4,128)S(1)} %get-tuple-element.48), kind=kOutput, calls=%fused_computation.46 | convolution fusion | flops 551555584 | bytes 19939328 | tf_op jit(solution)/shard_map/bgrqk,bqgrd->bkgd/dot_general | solution.py:123
  368.1 1.7 concatenate.59
  369.8 1.9 copy.39
  371.7 2.9 concatenate.58
  374.6 2.9 copy.38
  377.5 2.5 maximum_bitcast_fusion.2
  380.0 1.5 fusion.23
  381.5 2.0 copy.29
  383.5 1.9 reshape.285
  385.4 1.9 copy.33
  387.3 1.6 reshape.287
  389.1 0.7 slice_bitcast_fusion.2
  389.8 1.3 collective-permute-start.3
  391.1 3.7 collective-permute-start.2
  394.9 5.8 %fusion.68 = f32[256,2048]{1,0:T(8,128)S(1)} fusion(bf16[256,2048]{1,0:T(8,128)(2,1)S(1)} %copy-done.8, bf16[2048,2048]{1,0:T(8,128)(2,1)} %all-gather.8.cloned.1.call-done), kind=kOutput, calls=%fused_computation.109 | convolution fusion | flops 2147483648 | bytes 11534336 | tf_op jit(solution)/shard_map/dot_general | solution.py:107
  400.7 7.9 %fusion.70 = f32[256,2048]{1,0:T(8,128)} fusion(bf16[256,2048]{1,0:T(8,128)(2,1)S(1)} %copy-done.9, bf16[2048,2048]{1,0:T(8,128)(2,1)} %all-gather.6.cloned.1.call-done), kind=kOutput, calls=%fused_computation.111 | convolution fusion | flops 2147483648 | bytes 11534336 | tf_op jit(solution)/shard_map/dot_general | solution.py:147
  408.6 1.1 slice.178
  409.7 6.8 %rev.13 = f32[128,2048]{1,0:T(8,128)S(1)} reverse(f32[128,2048]{1,0:T(8,128)} %slice.178), dimensions={0} | reverse | bytes 2097152 | tf_op jit(solution)/shard_map/rev | solution.py:108
  416.6 2.1 fusion.42
  418.8 1.0 fusion.51
  420.0 1.1 fusion.53
  421.1 71.3 %all-reduce.6.cloned.1.call-done = f32[2,2,128,1024]{3,2,0,1:T(8,128)} async-done(((f32[2,2,128,1024]{3,2,0,1:T(8,128)}), f32[2,2,128,1024]{3,2,0,1:T(8,128)}) %all-reduce.6.cloned.1.call-update) | async-done | bytes 2097168 | tf_op jit(solution)/shard_map/psum | solution.py:140
  492.4 2.2 multiply_reduce_fusion
  494.7 0.5 copy-done.6
  495.2 3.1 fusion.18
  498.4 0.4 fusion.20
  498.8 1.1 slice.187
  499.8 7.5 %rev.15 = f32[128,2048]{1,0:T(8,128)S(1)} reverse(f32[128,2048]{1,0:T(8,128)} %slice.187), dimensions={0,1} | reverse | bytes 2097152 | tf_op jit(solution)/shard_map/rev | solution.py:150
  507.3 0.9 fusion.41
  (54 shorter events, 1.3 us)
Async XLA Ops:
  7.2 56.3 %all-gather.4.cloned.1.call-start = ((), (), s32[]{:S(2)}) async-start(), calls=%async_computation | async-start | bytes 4456448 | tf_op jit(solution)/shard_map/all_gather | solution.py:58
  7.9 152.8 %all-reduce.8.cloned.1.call-start = ((), (), s32[]{:S(2)}) async-start(), calls=%async_computation.4 | async-start | bytes 2097152 | tf_op jit(solution)/shard_map/psum | solution.py:34
  14.9 222.2 %copy-start.4 = (bf16[128,2048]{1,0:T(8,128)(2,1)}, bf16[128,2048]{1,0:T(8,128)(2,1)S(1)}, u32[]{:S(2)}) copy-start(bf16[128,2048]{1,0:T(8,128)(2,1)S(1)} %rev.12) | copy-start | bytes 1572868
  21.7 47.9 %copy-start.13 = (s32[2]{0:T(128)S(1)}, s32[2]{0:T(128)}, u32[]{:S(2)}) copy-start(s32[2]{0:T(128)} %param.14) | copy-start | bytes 28
  21.7 52.5 %copy-start.12 = (bf16[128,2048]{1,0:T(8,128)(2,1)S(1)}, bf16[128,2048]{1,0:T(8,128)(2,1)}, u32[]{:S(2)}) copy-start(bf16[128,2048]{1,0:T(8,128)(2,1)} %param.15) | copy-start | bytes 1572868
  68.2 169.0 %all-gather.6.cloned.1.call-start = ((), (), s32[]{:S(2)}) async-start(), calls=%async_computation.1 | async-start | bytes 8912896 | tf_op jit(solution)/shard_map/all_gather | solution.py:57
  68.9 243.4 %all-gather.8.cloned.1.call-start = ((), (), s32[]{:S(2)}) async-start(), calls=%async_computation.2 | async-start | bytes 8912896 | tf_op jit(solution)/shard_map/all_gather | solution.py:59
  69.5 422.9 %all-reduce.6.cloned.1.call-start = ((), (), s32[]{:S(2)}) async-start(), calls=%async_computation.3 | async-start | bytes 4194304 | tf_op jit(solution)/shard_map/psum | solution.py:140
  69.8 10.7 %collective-permute-start.1 = (bf16[128,1024]{1,0:T(8,128)(2,1)S(1)}, bf16[128,1024]{1,0:T(8,128)(2,1)S(1)}, u32[]{:S(2)}, u32[]{:S(2)}) collective-permute-start(bf16[128,1024]{1,0:T(8,128)(2,1)S(1)} %get-tuple-element.43), channel_id=1, source_target_pairs={{1,0},{2,1},{3,2},{4,3},{5,4},{6,5},{7,6},{8,7},{9,8},{10,9},{11,1... | collective-permute-start | bytes 786440 | tf_op jit(solution)/shard_map/ppermute | solution.py:25
  71.1 9.4 %collective-permute-start = (bf16[128,1024]{1,0:T(8,128)(2,1)S(1)}, bf16[128,1024]{1,0:T(8,128)(2,1)S(1)}, u32[]{:S(2)}, u32[]{:S(2)}) collective-permute-start(bf16[128,1024]{1,0:T(8,128)(2,1)S(1)} %get-tuple-element.38), channel_id=1, source_target_pairs={{0,1},{1,2},{2,3},{3,4},{4,5},{5,6},{6,7},{7,8},{8,9},{9,10},{10,1... | collective-permute-start | bytes 786440 | tf_op jit(solution)/shard_map/ppermute | solution.py:23
  162.5 74.6 %copy-start.2 = (bf16[128,2048]{1,0:T(8,128)(2,1)S(1)}, bf16[128,2048]{1,0:T(8,128)(2,1)}, u32[]{:S(2)}) copy-start(bf16[128,2048]{1,0:T(8,128)(2,1)} %param.10) | copy-start | bytes 1572868
  320.4 4.5 copy-start.10
  332.4 6.1 %copy-start.14 = (f32[2,4,4,128,512]{3,4,2,1,0:T(8,128)S(1)}, f32[2,4,4,128,512]{3,4,2,1,0:T(8,128)}, u32[]{:S(2)}) copy-start(f32[2,4,4,128,512]{3,4,2,1,0:T(8,128)} %get-tuple-element.49) | copy-start | bytes 25165828
  340.1 14.6 %copy-start.11 = (bf16[2,128,4,4,128]{1,4,3,2,0:T(8,128)(2,1)S(1)}, bf16[2,128,4,4,128]{1,4,3,2,0:T(8,128)(2,1)}, u32[]{:S(2)}) copy-start(bf16[2,128,4,4,128]{1,4,3,2,0:T(8,128)(2,1)} %copy.34) | copy-start | bytes 3145732
  377.5 2.5 copy-start
  381.5 7.4 %copy-start.1 = (f32[2,1,128,1024]{3,2,1,0:T(8,128)S(1)}, f32[2,1,128,1024]{3,2,1,0:T(8,128)}, u32[]{:S(2)}) copy-start(f32[2,1,128,1024]{3,2,1,0:T(8,128)} %get-tuple-element.33) | copy-start | bytes 3145732
  388.9 5.9 %copy-start.8 = (bf16[256,2048]{1,0:T(8,128)(2,1)S(1)}, bf16[256,2048]{1,0:T(8,128)(2,1)}, u32[]{:S(2)}) copy-start(bf16[256,2048]{1,0:T(8,128)(2,1)} %reshape.285) | copy-start | bytes 3145732
  389.8 29.0 %collective-permute-start.3 = (bf16[128,1024]{1,0:T(8,128)(2,1)}, bf16[128,1024]{1,0:T(8,128)(2,1)}, u32[]{:S(2)}, u32[]{:S(2)}) collective-permute-start(bf16[128,1024]{1,0:T(8,128)(2,1)} %get-tuple-element.37), channel_id=1, source_target_pairs={{1,0},{2,1},{3,2},{4,3},{5,4},{6,5},{7,6},{8,7},{9,8},{10,9},{11,1... | collective-permute-start | bytes 786440 | tf_op jit(solution)/shard_map/ppermute | solution.py:25
  391.1 27.7 %collective-permute-start.2 = (bf16[128,1024]{1,0:T(8,128)(2,1)S(1)}, bf16[128,1024]{1,0:T(8,128)(2,1)}, u32[]{:S(2)}, u32[]{:S(2)}) collective-permute-start(bf16[128,1024]{1,0:T(8,128)(2,1)S(1)} %get-tuple-element.36), channel_id=1, source_target_pairs={{0,1},{1,2},{2,3},{3,4},{4,5},{5,6},{6,7},{7,8},{8,9},{9,10},{10,1... | collective-permute-start | bytes 786440 | tf_op jit(solution)/shard_map/ppermute | solution.py:23
  394.9 5.8 %copy-start.9 = (bf16[256,2048]{1,0:T(8,128)(2,1)S(1)}, bf16[256,2048]{1,0:T(8,128)(2,1)}, u32[]{:S(2)}) copy-start(bf16[256,2048]{1,0:T(8,128)(2,1)} %reshape.287) | copy-start | bytes 3145732
  400.7 7.9 %copy-start.7 = (f32[256,2048]{1,0:T(8,128)}, f32[256,2048]{1,0:T(8,128)S(1)}, u32[]{:S(2)}) copy-start(f32[256,2048]{1,0:T(8,128)S(1)} %fusion.68) | copy-start | bytes 6291460
  420.0 74.8 %copy-start.3 = (bf16[128,2048]{1,0:T(8,128)(2,1)S(1)}, bf16[128,2048]{1,0:T(8,128)(2,1)}, u32[]{:S(2)}) copy-start(bf16[128,2048]{1,0:T(8,128)(2,1)} %param.10) | copy-start | bytes 1572868
  420.0 74.8 %copy-start.5 = (bf16[128,2048]{1,0:T(8,128)(2,1)S(1)}, bf16[128,2048]{1,0:T(8,128)(2,1)}, u32[]{:S(2)}) copy-start(bf16[128,2048]{1,0:T(8,128)(2,1)} %copy-done.4) | copy-start | bytes 1572868
  492.4 2.8 copy-start.6
Sparse Core Ops, SparseCore 0:
  10.2 53.2 all-gather.3
  68.3 92.3 all-reduce.7
  162.8 74.2 all-gather.5
  239.2 73.1 all-gather.7
  395.0 97.3 all-reduce.5
where the time goes:
time: 517 us; the launch traced here: 515 us
  waiting for transfers between devices  333 us (64%)
  matrix products  79.2 us (15%)
  local copies, waits for them, and re-layouts  57.9 us (11%)
  other arithmetic  18.3 us (4%)
  between operations  16.8 us (3%)
  starting transfers between devices  9.53 us (2%)
    psum x1, waiting for transfers between devices, spread_2(): return lax.psum(kept, axis)  79.1 us
    all_gather x1, waiting for transfers between devices, body(): lax.all_gather(w_query, 'ctx', axis=0, tiled=True)  72 us
    psum x1, waiting for transfers between devices, body(): totals = lax.psum(jnp.sum(key_terms[:, :, 2:], axis=1), 'ctx')  71.3 us
    all_gather x1, waiting for transfers between devices, body(): lax.all_gather(w_out, 'ctx', axis=0, tiled=True)  67 us
    all_gather x1, waiting for transfers between devices, body(): lax.all_gather(w_keyval, 'ctx', axis=0, tiled=True)  41.7 us
    dot_general x1, matrix products, body(): jnp.einsum('bgrqk,bkgd->bqgrd', grad_score, keys_only, preferred_element_...  14.6 us
    dot_general x1, matrix products, body(): jnp.einsum('bgrqk,bqgrd->bkgd', grad_score, query_heads, preferred_elemen...  13.4 us
  transfers between devices with their start and end apart: 9, of which 5 were waited for; matrix products, arithmetic and copies ran while one was open for 11% of the time, Pallas kernels for 0%

commit v1 on v0

v1 whole, which is shorter than its diff:
```python
import jax
import jax.numpy as jnp
from jax import lax
from jax.experimental import pallas as pl
from jax.experimental.pallas import tpu as pltpu
from jax.sharding import Mesh, PartitionSpec as P

HEADS = 16
KVH = 4
HDIM = 128
BLK = 128
REP = HEADS // KVH
EPS = 1e-05
SCALE = HDIM ** (-0.5)
F32 = jnp.float32
BF16 = jnp.bfloat16
VMEM = 56 * 1024 * 1024


def dot(a, b, ca, cb):
    return lax.dot_general(a, b, (((ca,), (cb,)), ((), ())), preferred_element_type=F32)


def flip_matrix(n):
    i = lax.broadcasted_iota(jnp.int32, (n, n), 0)
    j = lax.broadcasted_iota(jnp.int32, (n, n), 1)
    return jnp.where(i + j == n - 1, 1.0, 0.0).astype(BF16)


def params():
    return pltpu.CompilerParams(vmem_limit_bytes=VMEM)


def whole():
    return pl.BlockSpec(memory_space=pltpu.VMEM)


def smem():
    return pl.BlockSpec(memory_space=pltpu.SMEM)


def norm_kernel(info, h00, h01, h10, h11, out):
    core = info[0]
    flip = flip_matrix(128)
    for side, refs in enumerate(((h00, h01), (h10, h11))):
        place = core if side == 0 else 1 - core
        for grp in range(2):
            u = refs[grp][...].astype(F32)
            inv = lax.rsqrt(jnp.mean(u * u, axis=1, keepdims=True) + EPS)
            n = (u * inv).astype(BF16)
            row = pl.multiple_of(place * (2 * BLK) + grp * BLK, BLK)
            out[0, pl.ds(row, BLK), :] = n
            count = n.shape[1] // 128
            for k in range(count):
                m = count - 1 - k
                out[1, pl.ds(row, BLK), m * 128 : m * 128 + 128] = dot(
                    n[:, k * 128 : k * 128 + 128], flip, 1, 0
                ).astype(BF16)


def grad_att_kernel(info, c00, c01, c10, c11, w, out):
    core = info[0]
    for side, refs in enumerate(((c00, c01), (c10, c11))):
        place = core if side == 0 else 1 - core
        rows = jnp.concatenate([refs[0][...], refs[1][...]], axis=0)
        row = pl.multiple_of(place * (2 * BLK), 2 * BLK)
        out[pl.ds(row, 2 * BLK), :] = dot(rows, w[...], 1, 1).astype(BF16)


def attention_kernel(info, q, ga, kv, halo, static, dyn, att, gq, dkv, dhalo, dstatic, ddyn):
    last = info[2] - 1
    t = info[1]
    g_dyn = info[3 + pl.program_id(0)]
    for strand in range(2):
        sets = [kv[strand, 0, 0], kv[strand, 1, 0], halo[strand, 0], static[strand, 0], dyn[strand, 0]]
        stat_block = last if strand == 0 else 0
        dyn_block = g_dyn if strand == 0 else last - g_dyn
        sums = [None] * 5
        for side in range(2):
            block = 2 * t + side
            near = block - 1 if strand == 0 else block + 1
            if strand == 0:
                near_set = 2 if side == 0 else 0
            else:
                near_set = 1 if side == 0 else 2
            order = (near_set, side, 3, 4)
            flags = (
                (near >= 0) & (near <= last),
                None,
                (stat_block != block) & (stat_block != near),
                (dyn_block != block) & (dyn_block != near),
            )
            keys = jnp.concatenate([sets[i][:, :HDIM] for i in order], axis=0)
            values = jnp.concatenate([sets[i][:, HDIM:] for i in order], axis=0)
            qs = q[strand, side, 0]
            gs = ga[side, 0]
            rows = jnp.concatenate([qs[:, i * HDIM : (i + 1) * HDIM] for i in range(REP)], axis=0)
            ups = jnp.concatenate([gs[:, i * HDIM : (i + 1) * HDIM] for i in range(REP)], axis=0)
            s = dot(rows, keys, 1, 1) * SCALE
            parts = []
            for i in range(4):
                part = s[:, i * BLK : (i + 1) * BLK]
                if flags[i] is not None:
                    part = jnp.where(flags[i], part, -jnp.inf)
                parts.append(part)
            s = jnp.concatenate(parts, axis=1)
            e = jnp.exp(s - jnp.max(s, axis=1, keepdims=True))
            p = e * (1.0 / jnp.sum(e, axis=1, keepdims=True))
            ph = p.astype(BF16)
            o = dot(ph, values, 1, 0)
            dp = dot(ups, values, 1, 1)
            center = jnp.sum(p * dp, axis=1, keepdims=True)
            ds = (p * (dp - center) * SCALE).astype(BF16)
            dq = dot(ds, keys, 1, 0)
            dk = dot(ds, rows, 0, 0)
            dv = dot(ph, ups, 0, 0)
            for i in range(REP):
                att[strand, side, 0, :, i * HDIM : (i + 1) * HDIM] = o[i * BLK : (i + 1) * BLK].astype(BF16)
                gq[strand, side, 0, :, i * HDIM : (i + 1) * HDIM] = dq[i * BLK : (i + 1) * BLK].astype(BF16)
            for i in range(4):
                term = (dk[i * BLK : (i + 1) * BLK], dv[i * BLK : (i + 1) * BLK])
                old = sums[order[i]]
                sums[order[i]] = term if old is None else (old[0] + term[0], old[1] + term[1])
        targets = (dkv.at[strand, 0, 0], dkv.at[strand, 1, 0], dhalo.at[strand, 0], dstatic.at[strand, 0], ddyn.at[strand, 0])
        for target, (dk, dv) in zip(targets, sums):
            target[:, :HDIM] = dk.astype(target.dtype)
            target[:, HDIM:] = dv.astype(target.dtype)


def output_kernel(info, att, w, keep, send):
    core = info[0]
    for target, place in ((keep, core), (send, 1 - core)):
        total = dot(att[0, place], w[...], 1, 0) + dot(att[1, place], w[...], 1, 0)
        target[...] = total.astype(target.dtype)


def grad_norm_kernel(info, gq, dkv, halo, static, dyn, wq, wkv, wqm, wkvm, keep, send, kg):
    core = info[0]
    t = info[1]
    blocks = info[2]
    last = blocks - 1

    @pl.when(pl.program_id(0) == 0)
    def _():
        for strand in range(2):
            stat_block = last if strand == 0 else 0
            for side in range(2):
                for grp in range(2):
                    total = dkv[strand, side, grp]
                    if side != strand:
                        total = total + halo[strand, grp].astype(F32)
                        total = total + jnp.where(2 * t + side == stat_block, static[strand, grp].astype(F32), 0.0)
                    dyn_block = info[3 + grp] if strand == 0 else last - info[3 + grp]
                    total = total + jnp.where(2 * t + side == dyn_block, dyn[strand, grp].astype(F32), 0.0)
                    kg[strand, side, grp * BLK : (grp + 1) * BLK, :] = total.astype(BF16)

    width = wq.shape[0]
    flip = flip_matrix(width)
    wqf = dot(flip, wqm[...], 1, 0).astype(BF16)
    wkvf = dot(flip, wkvm[...], 1, 0).astype(BF16)
    for target, place in ((keep, core), (send, 1 - core)):
        total = dot(gq[0, place], wq[...], 1, 1) + dot(kg[0, place], wkv[...], 1, 1)
        total = total + dot(gq[1, place], wqf, 1, 1) + dot(kg[1, place], wkvf, 1, 1)
        target[...] = total.astype(target.dtype)


def swap(value, axis):
    return lax.ppermute(value, axis, [(0, 1), (1, 0)])


def pair(own, other, index):
    return jnp.where(index == 0, jnp.concatenate([own, other], 0), jnp.concatenate([other, own], 0))


def ring(value, axis):
    count = lax.axis_size(axis)
    return lax.ppermute(value, axis, [(i, (i + 1) % count) for i in range(count)])


def gather_rows(chunk):
    na, nb = lax.axis_size("a"), lax.axis_size("b")
    a, b = lax.axis_index("a"), lax.axis_index("b")
    size = chunk.shape[0]
    pieces = []
    for step in range(na):
        inner = chunk
        for turn in range(nb):
            pos = ((a - step) % na) * nb + (b - turn) % nb
            pieces.append((pos, inner))
            if turn + 1 < nb:
                inner = ring(inner, "b")
        if step + 1 < na:
            chunk = ring(chunk, "a")
    full = jnp.zeros((na * nb * size, chunk.shape[1]), chunk.dtype)
    for pos, piece in pieces:
        full = lax.dynamic_update_slice(full, piece, (pos * size, 0))
    return full


def output_rows(w_out, x, a, b, c):
    na, nb = lax.axis_size("a"), lax.axis_size("b")
    mine = 2 * x + c
    if (na, nb) != (4, 2):
        full = lax.all_gather(w_out, ("a", "b", "c"), axis=0, tiled=True)
        return lax.dynamic_slice(full, (mine * REP * HDIM, 0), (REP * HDIM, full.shape[1]))
    source = pair(w_out, swap(w_out, "c"), c)
    current = jnp.where(a == mine, source, 0).astype(source.dtype)

    def spot(x, a, c):
        return (x * na + a) * 2 + c

    def send(value, moves):
        pairs = []
        for (sx, sc), links in moves.items():
            pairs += [(spot(sx, i, sc), spot(sx, j, sc)) for i, j in links]
        return lax.ppermute(value, ("x", "a", "c"), pairs)

    def across(value, holders):
        pairs = []
        for (sx, sc), levels in holders.items():
            for i in levels:
                at = (sx * na + i) * 4 + sc
                pairs += [(at, at + 2), (at + 2, at)]
        return lax.ppermute(value, ("x", "a", "b", "c"), pairs)

    first = {(0, 0): [(0, 1)], (0, 1): [(1, 2)], (1, 0): [(2, 1)], (1, 1): [(3, 2)]}
    second = {(0, 0): [(0, 2), (1, 3)], (0, 1): [(1, 0), (2, 3)], (1, 0): [(2, 3), (1, 0)], (1, 1): [(3, 1), (2, 0)]}
    other = across(current, {(0, 0): [0], (0, 1): [1], (1, 0): [2], (1, 1): [3]})
    got = send(current, first)
    other = other + across(got, {k: [j for _, j in v] for k, v in first.items()})
    current = current + got
    got = send(current, second)
    other = other + across(got, {k: [j for _, j in v] for k, v in second.items()})
    current = current + got
    return pair(current, other, b)


def exchange_bits(index, axis):
    count = lax.axis_size(axis)
    bit = 1
    while bit < count:
        yield (index // bit) % 2, [(i, i ^ bit) for i in range(count)]
        bit *= 2


def body(hidden, w_query, w_keyval, w_out, global_blocks, cotangent):
    x, a, b, c = (lax.axis_index(n) for n in ("x", "a", "b", "c"))
    na, nb = lax.axis_size("a"), lax.axis_size("b")
    n = na * nb
    t = a * nb + b
    blocks = 2 * n
    width = hidden.shape[1]
    mine = 2 * x + c
    theirs = 2 * x + 1 - c
    line_up = [(i, i + 1) for i in range(n - 1)]
    line_down = [(i + 1, i) for i in range(n - 1)]

    g_own = jnp.sum(global_blocks) - (blocks - 1)
    g_own = jnp.reshape(g_own, (1,)).astype(jnp.int32)
    g_both = jnp.concatenate([g_own, swap(g_own, "x")])
    info = jnp.concatenate([jnp.stack([c, t, jnp.int32(blocks)]).astype(jnp.int32), g_both])

    h10 = swap(hidden, "c")
    h01 = swap(hidden, "x")
    h11 = swap(h01, "c")

    half = KVH * HDIM

    def kv_columns(j):
        return jnp.concatenate(
            [
                lax.dynamic_slice_in_dim(w_keyval, j * HDIM, HDIM, 1),
                lax.dynamic_slice_in_dim(w_keyval, half + j * HDIM, HDIM, 1),
            ],
            axis=1,
        )

    def q_columns(j):
        return lax.dynamic_slice_in_dim(w_query, j * REP * HDIM, REP * HDIM, 1)

    kv_weight = gather_rows(pair(kv_columns(mine), swap(kv_columns(theirs), "c"), c))
    normed = pl.pallas_call(
        norm_kernel,
        out_shape=jax.ShapeDtypeStruct((2, 4 * BLK, width), BF16),
        in_specs=[smem()] + [whole()] * 4,
        out_specs=whole(),
        compiler_params=params(),
        name="norm",
    )(info, hidden, h01, h10, h11)
    normed = normed.reshape(8 * BLK, width)
    kv = dot(normed, kv_weight, 1, 0).astype(BF16).reshape(2, 2, 2, BLK, 2 * HDIM)

    ctx = ("a", "b")
    up = kv[0, 1]
    down = kv[1, 0]
    halo = jnp.stack([lax.ppermute(up, ctx, line_up), lax.ppermute(down, ctx, line_down)])
    dyn_plain = g_both
    dyn_blocks = jnp.stack([dyn_plain, blocks - 1 - dyn_plain])
    dyn_side = (dyn_blocks % 2)[:, :, None, None]
    dyn_own = (dyn_blocks // 2 == t)[:, :, None, None]
    dyn = jnp.where(dyn_own, jnp.where(dyn_side == 0, kv[:, 0], kv[:, 1]), 0).astype(BF16)
    upper = jnp.where(t == n - 1, up, 0).astype(BF16)
    lower = jnp.where(t == 0, down, 0).astype(BF16)
    for index, axis in ((b, "b"), (a, "a")):
        for bit, pairs in exchange_bits(index, axis):
            packed = jnp.concatenate([dyn, jnp.where(bit == 1, upper, lower)[None]], axis=0)
            got = lax.ppermute(packed, axis, pairs)
            dyn = dyn + got[:2]
            upper = jnp.where(bit == 0, upper + got[2], upper)
            lower = jnp.where(bit == 1, lower + got[2], lower)
    static = jnp.stack([upper, lower])

    q_weight = gather_rows(pair(q_columns(mine), swap(q_columns(theirs), "c"), c))
    queries = dot(normed, q_weight, 1, 0).astype(BF16).reshape(2, 2, 2, BLK, REP * HDIM)

    c10 = swap(cotangent, "c")
    c01 = swap(cotangent, "x")
    c11 = swap(c01, "c")
    o_weight = output_rows(w_out, x, a, b, c)
    grad_att = pl.pallas_call(
        grad_att_kernel,
        out_shape=jax.ShapeDtypeStruct((4 * BLK, REP * HDIM), BF16),
        in_specs=[smem()] + [whole()] * 5,
        out_specs=whole(),
        compiler_params=params(),
        name="grad_att",
    )(info, cotangent, c01, c10, c11, o_weight)
    grad_att = grad_att.reshape(2, 2, BLK, REP * HDIM)

    wide = pl.BlockSpec((2, 2, 1, BLK, REP * HDIM), lambda g: (0, 0, g, 0, 0))
    pairs_spec = pl.BlockSpec((2, 2, 1, BLK, 2 * HDIM), lambda g: (0, 0, g, 0, 0))
    strand_spec = pl.BlockSpec((2, 1, BLK, 2 * HDIM), lambda g: (0, g, 0, 0))
    small = jax.ShapeDtypeStruct((2, 2, BLK, 2 * HDIM), BF16)
    att, gq, dkv, dhalo, dstatic, ddyn = pl.pallas_call(
        attention_kernel,
        grid=(2,),
        out_shape=(
            jax.ShapeDtypeStruct(queries.shape, BF16),
            jax.ShapeDtypeStruct(queries.shape, BF16),
            jax.ShapeDtypeStruct(kv.shape, F32),
            small,
            small,
            small,
        ),
        in_specs=[
            smem(),
            wide,
            pl.BlockSpec((2, 1, BLK, REP * HDIM), lambda g: (0, g, 0, 0)),
            pairs_spec,
            strand_spec,
            strand_spec,
            strand_spec,
        ],
        out_specs=(wide, wide, pairs_spec, strand_spec, strand_spec, strand_spec),
        compiler_params=params(),
        name="attention",
    )(info, queries, grad_att, kv, halo, static, dyn)

    halo_back = jnp.stack([lax.ppermute(dhalo[0], ctx, line_down), lax.ppermute(dhalo[1], ctx, line_up)])
    upper, lower = dstatic[0], dstatic[1]
    for index, axis in ((b, "b"), (a, "a")):
        for bit, pairs in exchange_bits(index, axis):
            packed = jnp.concatenate([ddyn, jnp.where(bit == 0, upper, lower)[None]], axis=0)
            got = lax.ppermute(packed, axis, pairs)
            ddyn = ddyn + got[:2]
            upper = jnp.where(bit == 1, upper + got[2], upper)
            lower = jnp.where(bit == 0, lower + got[2], lower)
    static_back = jnp.stack([upper, lower])

    rows = 2 * BLK

    def finish(keep, send):
        total = keep + swap(send, "c").astype(F32)
        return total[:BLK] + swap(total[BLK:].astype(BF16), "x").astype(F32)

    chunk = width // 4
    partial = (jax.ShapeDtypeStruct((rows, width), F32), jax.ShapeDtypeStruct((rows, width), BF16))
    combined = finish(
        *pl.pallas_call(
            output_kernel,
            grid=(width // chunk,),
            out_shape=partial,
            in_specs=[
                smem(),
                pl.BlockSpec((2, 2, rows, REP * HDIM), lambda k: (0, 0, 0, 0)),
                pl.BlockSpec((REP * HDIM, chunk), lambda k: (0, k)),
            ],
            out_specs=[pl.BlockSpec((rows, chunk), lambda k: (0, k))] * 2,
            compiler_params=params(),
            name="output",
        )(info, att.reshape(2, 2, rows, REP * HDIM), o_weight)
    ).astype(BF16)

    chunk = 256
    steps = width // chunk

    def fixed(shape):
        return pl.BlockSpec(shape, lambda k: (0,) * len(shape))

    keep, send = pl.pallas_call(
        grad_norm_kernel,
        grid=(steps,),
        out_shape=partial,
        in_specs=[
            smem(),
            fixed((2, 2, rows, REP * HDIM)),
            fixed(dkv.shape),
            fixed(small.shape),
            fixed(small.shape),
            fixed(small.shape),
            pl.BlockSpec((chunk, REP * HDIM), lambda k: (k, 0)),
            pl.BlockSpec((chunk, 2 * HDIM), lambda k: (k, 0)),
            pl.BlockSpec((chunk, REP * HDIM), lambda k: (steps - 1 - k, 0)),
            pl.BlockSpec((chunk, 2 * HDIM), lambda k: (steps - 1 - k, 0)),
        ],
        out_specs=[pl.BlockSpec((rows, chunk), lambda k: (0, k))] * 2,
        scratch_shapes=[pltpu.VMEM((2, 2, rows, 2 * HDIM), BF16)],
        compiler_params=params(),
        name="grad_norm",
    )(info, gq.reshape(2, 2, rows, REP * HDIM), dkv, halo_back, static_back, ddyn, q_weight, kv_weight, q_weight, kv_weight)
    grad_norm = finish(keep, send)

    u = hidden.astype(F32)
    inv_rms = lax.rsqrt(jnp.mean(u * u, axis=1, keepdims=True) + EPS)
    scaled = u * inv_rms
    grad_in = inv_rms * (grad_norm - scaled * jnp.mean(grad_norm * scaled, axis=1, keepdims=True))
    return (combined, grad_in.astype(BF16))


def split(count):
    inner = 1
    while (2 * inner) ** 2 <= count:
        inner *= 2
    return count // inner, inner


def solution(mesh):
    na, nb = split(mesh.shape["ctx"] // 2)
    grid = Mesh(mesh.devices.reshape(mesh.shape["groups"], na, nb, 2), ("x", "a", "b", "c"))
    return jax.shard_map(
        body,
        mesh=grid,
        in_specs=(
            P(("x", "a", "b", "c"), None),
            P(("a", "b", "c"), None),
            P(("a", "b", "c"), None),
            P(("a", "b", "c"), None),
            P("x"),
            P(("x", "a", "b", "c"), None),
        ),
        out_specs=(P(("x", "a", "b", "c"), None), P(("x", "a", "b", "c"), None)),
        check_vma=False,
    )
```

time: 517 us -> 241 us (0.47)
  waiting for transfers between devices: 333 us -> 88.4 us
  matrix products: 79.2 us -> 6.74 us
  starting transfers between devices: 9.53 us -> 81 us
  local copies, waits for them, and re-layouts: 57.9 us -> 6.92 us
  Pallas kernels: 0 us -> 37.9 us
  between operations: 16.8 us -> 2.19 us
    all_gather x3 -> x0, waiting for transfers between devices: 181 us -> none  [the longest x1 72 us: body(): lax.all_gather(w_query, 'ctx', axis=0, tiled=True)]
    psum x2 -> x0, waiting for transfers between devices: 150 us -> none  [the longest x1 79.1 us: spread_2(): return lax.psum(kept, axis)]
    ppermute x4 -> x43, waiting for transfers between devices: 0.01 us -> 88.4 us  [the longest x14 30.3 us: ring(): lax.ppermute(value, axis, [(i, (i + 1) % count) for i in range(count)])]
    ppermute x4 -> x43, starting transfers between devices: 9.34 us -> 81 us  [the longest x6 35.2 us: body(): got = lax.ppermute(packed, axis, pairs)]
    dot_general x11 -> x2, matrix products: 71.7 us -> 6.74 us  [dot(): lax.dot_general(a, b, (((ca,), (cb,)), ((), ())), preferred_element_type=...]
    pallas_call x0 -> x5, Pallas kernels: none -> 37.9 us  [the longest x1 12.5 us: body(): pl.pallas_call(attention_kernel, grid=(2,), out_shape=(jax.ShapeDtypeStru...]
    rev x4 -> x0, local copies, waits for them, and re-layouts: 26.5 us -> none  [the longest x1 7.5 us: body(): grad_in[row_count:][::-1, ::-1]]
    reshape x7 -> x0, local copies, waits for them, and re-layouts: 8.85 us -> none  [the longest x4 4.39 us: split_heads(): return row_values.reshape(block_count, BLK, KVH, HEADS // KVH, HDIM)]
  transfers between devices with their start and end apart: 9 -> 43, of which waited for: 5 -> 15; matrix products, arithmetic and copies ran while one was open for 11% -> 10% of each run, Pallas kernels for 0% -> 9%
where the time goes in v1:
time: 241 us; the launch traced here: 240 us
  waiting for transfers between devices  88.4 us (37%)
  starting transfers between devices  81 us (34%)
  Pallas kernels  37.9 us (16%)
  other arithmetic  17.2 us (7%)
  local copies, waits for them, and re-layouts  6.92 us (3%)
  matrix products  6.74 us (3%)
    ppermute x6, starting transfers between devices, body(): got = lax.ppermute(packed, axis, pairs)  35.2 us
    ppermute x14, waiting for transfers between devices, ring(): lax.ppermute(value, axis, [(i, (i + 1) % count) for i in range(count)])  30.3 us
    ppermute x6, waiting for transfers between devices, body(): got = lax.ppermute(packed, axis, pairs)  26.2 us
    ppermute x14, waiting for transfers between devices, swap(): return lax.ppermute(value, axis, [(0, 1), (1, 0)])  23.5 us
    ppermute x14, starting transfers between devices, swap(): return lax.ppermute(value, axis, [(0, 1), (1, 0)])  14.8 us
    pallas_call x1, Pallas kernels, body(): pl.pallas_call(attention_kernel, grid=(2,), out_shape=(jax.ShapeDtypeStru...  12.5 us
    pallas_call x1, Pallas kernels, body(): pl.pallas_call(grad_norm_kernel, grid=(steps,), out_shape=partial, in_spe...  10.7 us
    ppermute x14, starting transfers between devices, ring(): lax.ppermute(value, axis, [(i, (i + 1) % count) for i in range(count)])  10 us
  transfers between devices with their start and end apart: 43, of which 15 were waited for; matrix products, arithmetic and copies ran while one was open for 10% of the time, Pallas kernels for 9%

profile of v1, /device:TPU:0, one launch (start us, length us, event | category | flops | bytes accessed | tf_op | source)
XLA Modules:
  0.0 240.4 jit_solution(16841454289796854049)
XLA Ops:
  0.6 3.0 %collective-permute-start.1 = (bf16[128,2048]{1,0:T(8,128)(2,1)}, bf16[128,2048]{1,0:T(8,128)(2,1)S(1)}, u32[]{:S(2)}, u32[]{:S(2)}) collective-permute-start(bf16[128,2048]{1,0:T(8,128)(2,1)} %h00.1), channel_id=1, source_target_pairs={{0,16},{16,0},{1,17},{17,1},{2,18},{18,2},{3,19},{19,3},{4,20},{20... | collective-permute-start | bytes 1572872 | tf_op jit(solution)/shard_map/ppermute | solution.py:168
  3.6 0.8 constant_dynamic-slice_fusion.1
  5.0 1.3 reduce_sum.27
  7.0 8.1 %collective-permute-start = (s32[1]{0:T(128)}, s32[1]{0:T(128)}, u32[]{:S(2)}, u32[]{:S(2)}) collective-permute-start(s32[1]{0:T(128)} %bitcast.2), channel_id=1, source_target_pairs={{0,16},{16,0},{1,17},{17,1},{2,18},{18,2},{3,19},{19,3},{4,20},{20... | collective-permute-start | bytes 20 | tf_op jit(solution)/shard_map/ppermute | solution.py:168
  15.1 1.0 constant_dynamic-slice_fusion.4
  16.4 0.6 add_subtract_fusion
  17.0 0.6 add_bitcast_fusion
  17.8 1.6 collective-permute-start.22
  19.4 1.6 collective-permute-start.23
  21.0 1.2 concatenate.99.info
  23.0 3.7 %collective-permute-done.23 = bf16[256,256]{1,0:T(8,128)(2,1)S(1)} collective-permute-done((bf16[256,256]{1,0:T(8,128)(2,1)S(1)}, bf16[256,256]{1,0:T(8,128)(2,1)S(1)}, u32[]{:S(2)}, u32[]{:S(2)}) %collective-permute-start.23) | collective-permute-done | bytes 131104 | tf_op jit(solution)/shard_map/ppermute | solution.py:177
  27.2 6.0 %collective-permute-done.24 = bf16[256,256]{1,0:T(8,128)(2,1)S(1)} collective-permute-done((bf16[256,256]{1,0:T(8,128)(2,1)S(1)}, bf16[256,256]{1,0:T(8,128)(2,1)S(1)}, u32[]{:S(2)}, u32[]{:S(2)}) %collective-permute-start.24) | collective-permute-done | bytes 131104 | tf_op jit(solution)/shard_map/ppermute | solution.py:177
  33.3 1.6 collective-permute-start.6
  35.6 6.5 %collective-permute-done.6 = bf16[256,512]{1,0:T(8,128)(2,1)S(1)} collective-permute-done((bf16[256,512]{1,0:T(8,128)(2,1)S(1)}, bf16[256,512]{1,0:T(8,128)(2,1)S(1)}, u32[]{:S(2)}, u32[]{:S(2)}) %collective-permute-start.6) | collective-permute-done | bytes 262176 | tf_op jit(solution)/shard_map/ppermute | solution.py:177
  42.2 1.0 collective-permute-start.7
  43.2 5.7 %collective-permute-done.27 = bf16[256,256]{1,0:T(8,128)(2,1)S(1)} collective-permute-done((bf16[256,256]{1,0:T(8,128)(2,1)S(1)}, bf16[256,256]{1,0:T(8,128)(2,1)S(1)}, u32[]{:S(2)}, u32[]{:S(2)}) %collective-permute-start.27) | collective-permute-done | bytes 131104 | tf_op jit(solution)/shard_map/ppermute | solution.py:177
  48.9 1.0 collective-permute-start.28
  50.3 3.6 %collective-permute-done.28 = bf16[256,256]{1,0:T(8,128)(2,1)S(1)} collective-permute-done((bf16[256,256]{1,0:T(8,128)(2,1)S(1)}, bf16[256,256]{1,0:T(8,128)(2,1)S(1)}, u32[]{:S(2)}, u32[]{:S(2)}) %collective-permute-start.28) | collective-permute-done | bytes 131104 | tf_op jit(solution)/shard_map/ppermute | solution.py:177
  54.0 1.5 collective-permute-start.16
  55.5 1.6 collective-permute-done.8
  57.1 1.0 collective-permute-start.9
  58.1 0.8 copy-done.10
  58.8 0.8 copy-done.12
  59.7 4.9 %norm.1 = bf16[2,512,2048]{2,1,0:T(8,128)(2,1)} custom-call(s32[5]{0:T(128)} %concatenate.99.info, bf16[128,2048]{1,0:T(8,128)(2,1)} %h00.1, bf16[128,2048]{1,0:T(8,128)(2,1)} %copy-done.9, bf16[128,2048]{1,0:T(8,128)(2,1)} %copy-done.10, bf16[128,2048]{1,0:T(8,128)(2,1)} %copy-done.12), custom_call_target="tpu_custom_call" | custom-call | tf_op jit(solution)/shard_map/norm/pallas_call | solution.py:282
  64.6 3.4 %convolution_convert_fusion.1 = bf16[1024,256]{1,0:T(8,128)(2,1)S(1)} fusion(bf16[1024,2048]{1,0:T(8,128)(2,1)} %bitcast.59, bf16[2048,256]{1,0:T(8,128)(2,1)S(1)} %constant_dynamic-update-slice_fusion.wkv.wkvm), kind=kOutput, calls=%fused_computation.6 | convolution fusion | flops 1074003968 | bytes 5767168 | tf_op jit(solution)/shard_map/dot_general | solution.py:21
  68.2 1.1 collective-permute-start.31
  69.4 3.2 %collective-permute-done.10 = bf16[256,512]{1,0:T(8,128)(2,1)S(1)} collective-permute-done((bf16[256,512]{1,0:T(8,128)(2,1)S(1)}, bf16[256,512]{1,0:T(8,128)(2,1)S(1)}, u32[]{:S(2)}, u32[]{:S(2)}) %collective-permute-start.10) | collective-permute-done | bytes 262176 | tf_op jit(solution)/shard_map/ppermute | solution.py:177
  73.2 1.3 collective-permute-start.30
  74.5 6.0 %collective-permute-done.31 = bf16[3,2,128,256]{3,2,1,0:T(8,128)(2,1)S(1)} collective-permute-done((bf16[3,2,128,256]{3,2,1,0:T(8,128)(2,1)S(1)}, bf16[3,2,128,256]{3,2,1,0:T(8,128)(2,1)S(1)}, u32[]{:S(2)}, u32[]{:S(2)}) %collective-permute-start.31) | collective-permute-done | bytes 393248 | tf_op jit(solution)/shard_map/ppermute | solution.py:307
  80.5 4.5 %collective-permute-start.29 = (bf16[2,128,256]{2,1,0:T(8,128)(2,1)S(1)}, bf16[2,128,256]{2,1,0:T(8,128)(2,1)S(1)}, u32[]{:S(2)}, u32[]{:S(2)}) collective-permute-start(bf16[2,128,256]{2,1,0:T(8,128)(2,1)S(1)} %get-tuple-element.36), channel_id=1, source_target_pairs={{0,2},{2,4},{4,6},{6,8},{8,10},{10,12},{12,14},{1,3},{3,5},{5,7},{... | collective-permute-start | bytes 393224 | tf_op jit(solution)/shard_map/ppermute | solution.py:296
  85.7 2.0 collective-permute-start.17
  88.0 3.9 %collective-permute-start.18 = (bf16[256,2048]{1,0:T(8,128)(2,1)S(1)}, bf16[256,2048]{1,0:T(8,128)(2,1)S(1)}, u32[]{:S(2)}, u32[]{:S(2)}) collective-permute-start(bf16[256,2048]{1,0:T(8,128)(2,1)S(1)} %fusion.8), channel_id=1, source_target_pairs={{0,2},{2,0},{5,7},{7,5},{24,26},{26,24},{29,31},{31,29}} | collective-permute-start | bytes 3145736 | tf_op jit(solution)/shard_map/ppermute | solution.py:224
  91.9 0.7 pad_maximum_fusion.6.halo
  92.6 0.7 collective-permute-start.19
  93.4 4.3 %collective-permute-done.32 = bf16[3,2,128,256]{3,2,1,0:T(8,128)(2,1)S(1)} collective-permute-done((bf16[3,2,128,256]{3,2,1,0:T(8,128)(2,1)S(1)}, bf16[3,2,128,256]{3,2,1,0:T(8,128)(2,1)S(1)}, u32[]{:S(2)}, u32[]{:S(2)}) %collective-permute-start.32) | collective-permute-done | bytes 393248 | tf_op jit(solution)/shard_map/ppermute | solution.py:307
  97.8 8.3 %collective-permute-done.17 = bf16[256,2048]{1,0:T(8,128)(2,1)S(1)} collective-permute-done((bf16[256,2048]{1,0:T(8,128)(2,1)S(1)}, bf16[256,2048]{1,0:T(8,128)(2,1)S(1)}, u32[]{:S(2)}, u32[]{:S(2)}) %collective-permute-start.17) | collective-permute-done | bytes 1048608 | tf_op jit(solution)/shard_map/ppermute | solution.py:216
  106.1 0.9 collective-permute-start.20
  107.0 3.3 %convolution_convert_fusion = bf16[1024,512]{1,0:T(8,128)(2,1)} fusion(bf16[1024,2048]{1,0:T(8,128)(2,1)S(1)} %bitcast.60, bf16[2048,512]{1,0:T(8,128)(2,1)S(1)} %constant_dynamic-update-slice_fusion.8.wq.wqm), kind=kOutput, calls=%fused_computation.3 | convolution fusion | flops 2148007936 | bytes 7340032 | tf_op jit(solution)/shard_map/dot_general | solution.py:21
  110.4 1.9 collective-permute-start.13
  112.4 0.9 slice_add_fusion.5
  114.0 2.4 %maximum_select_fusion.w = bf16[512,2048]{1,0:T(8,128)(2,1)} fusion(bf16[256,2048]{1,0:T(8,128)(2,1)S(1)} %add_add_fusion, bf16[256,2048]{1,0:T(8,128)(2,1)S(1)} %add.321, pred[]{:T(512)S(6)} %eq.107), kind=kLoop, calls=%fused_computation | loop fusion | flops 9437184 | bytes 4194305 | tf_op jit(solution)/shard_map/jit(_where)/select_n | solution.py:172
  116.4 0.8 copy-done.13
  117.2 0.8 copy-done.14
  118.0 4.3 %grad_att.1 = bf16[512,512]{1,0:T(8,128)(2,1)} custom-call(s32[5]{0:T(128)} %concatenate.99.info, bf16[128,2048]{1,0:T(8,128)(2,1)} %c00.1, bf16[128,2048]{1,0:T(8,128)(2,1)} %copy-done.11, bf16[128,2048]{1,0:T(8,128)(2,1)} %copy-done.13, bf16[128,2048]{1,0:T(8,128)(2,1)} %copy-done.14, bf16[512,2048]{1,0:T(8,128)(2,1)} %maximum_select_fusion.w), custom_call_target="tpu_custom_call" | custom-call | tf_op jit(solution)/shard_map/grad_att/pallas_call | solution.py:320
  122.3 12.5 %attention.1 = (bf16[2,2,2,128,512]{4,3,2,1,0:T(8,128)(2,1)}, bf16[2,2,2,128,512]{4,3,2,1,0:T(8,128)(2,1)}, f32[2,2,2,128,256]{4,3,2,1,0:T(8,128)}, bf16[2,2,128...) custom-call(s32[5]{0:T(128)} %concatenate.99.info, ...), custom_call_target="tpu_custom_call" | custom-call | tf_op jit(solution)/shard_map/attention/pallas_call | solution.py:334
  134.9 1.0 broadcast_select_fusion.4
  135.9 1.0 pad_maximum_fusion.3
  137.2 7.5 %collective-permute-done.38 = bf16[3,2,128,256]{3,2,1,0:T(8,128)(2,1)S(1)} collective-permute-done((bf16[3,2,128,256]{3,2,1,0:T(8,128)(2,1)S(1)}, bf16[3,2,128,256]{3,2,1,0:T(8,128)(2,1)S(1)}, u32[]{:S(2)}, u32[]{:S(2)}) %collective-permute-start.38) | collective-permute-done | bytes 393248 | tf_op jit(solution)/shard_map/ppermute | solution.py:364
  144.7 1.0 slice_add_fusion.4
  145.8 21.8 %collective-permute-start.39 = (bf16[3,2,128,256]{3,2,1,0:T(8,128)(2,1)S(1)}, bf16[3,2,128,256]{3,2,1,0:T(8,128)(2,1)S(1)}, u32[]{:S(2)}, u32[]{:S(2)}) collective-permute-start(bf16[3,2,128,256]{3,2,1,0:T(8,128)(2,1)S(1)} %pad_maximum_fusion.4), channel_id=1, source_target_pairs={{0,4},{4,0},{8,12},{12,8},{1,5},{5,1},{9,13},{13,9},{2,6},{6,2},{1... | collective-permute-start | bytes 1179656 | tf_op jit(solution)/shard_map/ppermute | solution.py:364
  167.6 8.5 %collective-permute-done.39 = bf16[3,2,128,256]{3,2,1,0:T(8,128)(2,1)S(1)} collective-permute-done((bf16[3,2,128,256]{3,2,1,0:T(8,128)(2,1)S(1)}, bf16[3,2,128,256]{3,2,1,0:T(8,128)(2,1)S(1)}, u32[]{:S(2)}, u32[]{:S(2)}) %collective-permute-start.39) | collective-permute-done | bytes 393248 | tf_op jit(solution)/shard_map/ppermute | solution.py:364
  176.2 11.8 %collective-permute-start.40 = (bf16[3,2,128,256]{3,2,1,0:T(8,128)(2,1)S(1)}, bf16[3,2,128,256]{3,2,1,0:T(8,128)(2,1)S(1)}, u32[]{:S(2)}, u32[]{:S(2)}) collective-permute-start(bf16[3,2,128,256]{3,2,1,0:T(8,128)(2,1)S(1)} %pad_maximum_fusion.5), channel_id=1, source_target_pairs={{0,8},{4,12},{8,0},{12,4},{1,9},{5,13},{9,1},{13,5},{2,10},{6,14},... | collective-permute-start | bytes 1179656 | tf_op jit(solution)/shard_map/ppermute | solution.py:364
  188.1 1.3 collective-permute-start.36
  189.4 4.8 %collective-permute-start.37 = (bf16[2,128,256]{2,1,0:T(8,128)(2,1)S(1)}, bf16[2,128,256]{2,1,0:T(8,128)(2,1)S(1)}, u32[]{:S(2)}, u32[]{:S(2)}) collective-permute-start(bf16[2,128,256]{2,1,0:T(8,128)(2,1)S(1)} %get-tuple-element.41), channel_id=1, source_target_pairs={{0,2},{2,4},{4,6},{6,8},{8,10},{10,12},{12,14},{1,3},{3,5},{5,7},{... | collective-permute-start | bytes 393224 | tf_op jit(solution)/shard_map/ppermute | solution.py:359
  194.2 5.5 %output.1 = (f32[256,2048]{1,0:T(8,128)}, bf16[256,2048]{1,0:T(8,128)(2,1)}) custom-call(s32[5]{0:T(128)} %concatenate.99.info, bf16[2,2,256,512]{3,2,1,0:T(8,128)(2,1)} %bitcast.64, bf16[512,2048]{1,0:T(8,128)(2,1)} %maximum_select_fusion.w), custom_call_target="tpu_custom_call" | custom-call | tf_op jit(solution)/shard_map/output/pallas_call | solution.py:379
  199.7 0.7 pad_maximum_fusion.8.halo
  200.4 0.7 pad_maximum_fusion.9.static
  201.2 0.7 slice_add_fusion.2.dyn
  201.9 10.7 %grad_norm.1 = (f32[256,2048]{1,0:T(8,128)}, bf16[256,2048]{1,0:T(8,128)(2,1)}) custom-call(s32[5]{0:T(128)} %concatenate.99.info, bf16[2,2,256,512]{3,2,1,0:T(8,128)(2,1)} %bitcast.62, f32[2,2,2,128,256]{4,3,2,1,0:T(8,128)} %get-tuple-element.16.dkv, bf16[2,2,128,256]{3,2,1,0:T(8,128)(2,1)} %pad_maximum_fusion.8.halo, ...), custom_call_target="tpu_custom_call" | custom-call | tf_op jit(solution)/shard_map/grad_norm/pallas_call | solution.py:400
  213.8 1.9 collective-permute-done.41
  216.3 12.2 %collective-permute-done.35 = bf16[128,2048]{1,0:T(8,128)(2,1)S(1)} collective-permute-done((bf16[128,2048]{1,0:T(8,128)(2,1)S(1)}, bf16[128,2048]{1,0:T(8,128)(2,1)S(1)}, u32[]{:S(2)}, u32[]{:S(2)}) %collective-permute-start.35) | collective-permute-done | bytes 524320 | tf_op jit(solution)/shard_map/ppermute | solution.py:168
  228.5 0.9 fusion.7
  229.4 9.4 %collective-permute-done.42 = bf16[128,2048]{1,0:T(8,128)(2,1)S(1)} collective-permute-done((bf16[128,2048]{1,0:T(8,128)(2,1)S(1)}, bf16[128,2048]{1,0:T(8,128)(2,1)S(1)}, u32[]{:S(2)}, u32[]{:S(2)}) %collective-permute-start.42) | collective-permute-done | bytes 524320 | tf_op jit(solution)/shard_map/ppermute | solution.py:168
  239.2 1.2 fusion.5
  (130 shorter events, 8.6 us)
Async XLA Ops:
  0.6 42.6 %collective-permute-start.1 = (bf16[128,2048]{1,0:T(8,128)(2,1)}, bf16[128,2048]{1,0:T(8,128)(2,1)S(1)}, u32[]{:S(2)}, u32[]{:S(2)}) collective-permute-start(bf16[128,2048]{1,0:T(8,128)(2,1)} %h00.1), channel_id=1, source_target_pairs={{0,16},{16,0},{1,17},{17,1},{2,18},{18,2},{3,19},{19,3},{4,20},{20... | collective-permute-start | bytes 1572872 | tf_op jit(solution)/shard_map/ppermute | solution.py:168
  3.6 54.4 %collective-permute-start.2 = (bf16[128,2048]{1,0:T(8,128)(2,1)}, bf16[128,2048]{1,0:T(8,128)(2,1)S(1)}, u32[]{:S(2)}, u32[]{:S(2)}) collective-permute-start(bf16[128,2048]{1,0:T(8,128)(2,1)} %h00.1), channel_id=1, source_target_pairs={{0,1},{1,0},{2,3},{3,2},{4,5},{5,4},{6,7},{7,6},{8,9},{9,8},{10,11... | collective-permute-start | bytes 1572872 | tf_op jit(solution)/shard_map/ppermute | solution.py:168
  4.5 13.2 %collective-permute-start.21 = (bf16[128,256]{1,0:T(8,128)(2,1)S(1)}, bf16[128,256]{1,0:T(8,128)(2,1)S(1)}, u32[]{:S(2)}, u32[]{:S(2)}) collective-permute-start(bf16[128,256]{1,0:T(8,128)(2,1)S(1)} %pad_maximum_fusion.10), channel_id=1, source_target_pairs={{0,1},{1,0},{2,3},{3,2},{4,5},{5,4},{6,7},{7,6},{8,9},{9,8},{10,11... | collective-permute-start | bytes 196616 | tf_op jit(solution)/shard_map/ppermute | solution.py:168
  7.0 9.4 %collective-permute-start = (s32[1]{0:T(128)}, s32[1]{0:T(128)}, u32[]{:S(2)}, u32[]{:S(2)}) collective-permute-start(s32[1]{0:T(128)} %bitcast.2), channel_id=1, source_target_pairs={{0,16},{16,0},{1,17},{17,1},{2,18},{18,2},{3,19},{19,3},{4,20},{20... | collective-permute-start | bytes 20 | tf_op jit(solution)/shard_map/ppermute | solution.py:168
  16.1 6.1 %collective-permute-start.4 = (bf16[128,512]{1,0:T(8,128)(2,1)S(1)}, bf16[128,512]{1,0:T(8,128)(2,1)S(1)}, u32[]{:S(2)}, u32[]{:S(2)}) collective-permute-start(bf16[128,512]{1,0:T(8,128)(2,1)S(1)} %get-tuple-element.38), channel_id=1, source_target_pairs={{0,1},{1,0},{2,3},{3,2},{4,5},{5,4},{6,7},{7,6},{8,9},{9,8},{10,11... | collective-permute-start | bytes 393224 | tf_op jit(solution)/shard_map/ppermute | solution.py:168
  17.8 17.1 %copy-start.15 = (bf16[128,2048]{1,0:T(8,128)(2,1)S(1)}, bf16[128,2048]{1,0:T(8,128)(2,1)}, u32[]{:S(2)}) copy-start(bf16[128,2048]{1,0:T(8,128)(2,1)} %param.9) | copy-start | bytes 1572868
  17.8 9.4 %collective-permute-start.22 = (bf16[256,256]{1,0:T(8,128)(2,1)S(1)}, bf16[256,256]{1,0:T(8,128)(2,1)S(1)}, u32[]{:S(2)}, u32[]{:S(2)}) collective-permute-start(bf16[256,256]{1,0:T(8,128)(2,1)S(1)} %get-tuple-element.29), channel_id=1, source_target_pairs={{0,2},{2,0},{1,3},{3,1},{4,6},{6,4},{5,7},{7,5},{8,10},{10,8},{9,1... | collective-permute-start | bytes 393224 | tf_op jit(solution)/shard_map/ppermute | solution.py:177
  19.4 7.3 %collective-permute-start.23 = (bf16[256,256]{1,0:T(8,128)(2,1)S(1)}, bf16[256,256]{1,0:T(8,128)(2,1)S(1)}, u32[]{:S(2)}, u32[]{:S(2)}) collective-permute-start(bf16[256,256]{1,0:T(8,128)(2,1)S(1)} %get-tuple-element.29), channel_id=1, source_target_pairs={{0,4},{4,8},{8,12},{12,0},{1,5},{5,9},{9,13},{13,1},{2,6},{6,10},{... | collective-permute-start | bytes 393224 | tf_op jit(solution)/shard_map/ppermute | solution.py:177
  22.4 12.6 %collective-permute-start.5 = (bf16[256,512]{1,0:T(8,128)(2,1)S(1)}, bf16[256,512]{1,0:T(8,128)(2,1)S(1)}, u32[]{:S(2)}, u32[]{:S(2)}) collective-permute-start(bf16[256,512]{1,0:T(8,128)(2,1)S(1)} %get-tuple-element.31), channel_id=1, source_target_pairs={{0,2},{2,0},{1,3},{3,1},{4,6},{6,4},{5,7},{7,5},{8,10},{10,8},{9,1... | collective-permute-start | bytes 786440 | tf_op jit(solution)/shard_map/ppermute | solution.py:177
  26.7 6.6 %collective-permute-start.24 = (bf16[256,256]{1,0:T(8,128)(2,1)S(1)}, bf16[256,256]{1,0:T(8,128)(2,1)S(1)}, u32[]{:S(2)}, u32[]{:S(2)}) collective-permute-start(bf16[256,256]{1,0:T(8,128)(2,1)S(1)} %collective-permute-done.23), channel_id=1, source_target_pairs={{0,2},{2,0},{1,3},{3,1},{4,6},{6,4},{5,7},{7,5},{8,10},{10,8},{9,1... | collective-permute-start | bytes 393224 | tf_op jit(solution)/shard_map/ppermute | solution.py:177
  27.2 7.7 %collective-permute-start.25 = (bf16[256,256]{1,0:T(8,128)(2,1)S(1)}, bf16[256,256]{1,0:T(8,128)(2,1)S(1)}, u32[]{:S(2)}, u32[]{:S(2)}) collective-permute-start(bf16[256,256]{1,0:T(8,128)(2,1)S(1)} %collective-permute-done.23), channel_id=1, source_target_pairs={{0,4},{4,8},{8,12},{12,0},{1,5},{5,9},{9,13},{13,1},{2,6},{6,10},{... | collective-permute-start | bytes 393224 | tf_op jit(solution)/shard_map/ppermute | solution.py:177
  33.3 8.9 %collective-permute-start.6 = (bf16[256,512]{1,0:T(8,128)(2,1)S(1)}, bf16[256,512]{1,0:T(8,128)(2,1)S(1)}, u32[]{:S(2)}, u32[]{:S(2)}) collective-permute-start(bf16[256,512]{1,0:T(8,128)(2,1)S(1)} %get-tuple-element.31), channel_id=1, source_target_pairs={{0,4},{4,8},{8,12},{12,0},{1,5},{5,9},{9,13},{13,1},{2,6},{6,10},{... | collective-permute-start | bytes 786440 | tf_op jit(solution)/shard_map/ppermute | solution.py:177
  34.9 14.0 %collective-permute-start.15 = (bf16[128,2048]{1,0:T(8,128)(2,1)S(1)}, bf16[128,2048]{1,0:T(8,128)(2,1)S(1)}, u32[]{:S(2)}, u32[]{:S(2)}) collective-permute-start(bf16[128,2048]{1,0:T(8,128)(2,1)S(1)} %copy-done.15), channel_id=1, source_target_pairs={{0,1},{1,0},{2,3},{3,2},{4,5},{5,4},{6,7},{7,6},{8,9},{9,8},{10,11... | collective-permute-start | bytes 1572872 | tf_op jit(solution)/shard_map/ppermute | solution.py:168
  35.0 7.2 %collective-permute-start.26 = (bf16[256,256]{1,0:T(8,128)(2,1)S(1)}, bf16[256,256]{1,0:T(8,128)(2,1)S(1)}, u32[]{:S(2)}, u32[]{:S(2)}) collective-permute-start(bf16[256,256]{1,0:T(8,128)(2,1)S(1)} %collective-permute-done.25), channel_id=1, source_target_pairs={{0,2},{2,0},{1,3},{3,1},{4,6},{6,4},{5,7},{7,5},{8,10},{10,8},{9,1... | collective-permute-start | bytes 393224 | tf_op jit(solution)/shard_map/ppermute | solution.py:177
  42.1 6.8 %collective-permute-start.27 = (bf16[256,256]{1,0:T(8,128)(2,1)S(1)}, bf16[256,256]{1,0:T(8,128)(2,1)S(1)}, u32[]{:S(2)}, u32[]{:S(2)}) collective-permute-start(bf16[256,256]{1,0:T(8,128)(2,1)S(1)} %collective-permute-done.25), channel_id=1, source_target_pairs={{0,4},{4,8},{8,12},{12,0},{1,5},{5,9},{9,13},{13,1},{2,6},{6,10},{... | collective-permute-start | bytes 393224 | tf_op jit(solution)/shard_map/ppermute | solution.py:177
  42.2 27.2 %collective-permute-start.7 = (bf16[256,512]{1,0:T(8,128)(2,1)S(1)}, bf16[256,512]{1,0:T(8,128)(2,1)S(1)}, u32[]{:S(2)}, u32[]{:S(2)}) collective-permute-start(bf16[256,512]{1,0:T(8,128)(2,1)S(1)} %collective-permute-done.6), channel_id=1, source_target_pairs={{0,2},{2,0},{1,3},{3,1},{4,6},{6,4},{5,7},{7,5},{8,10},{10,8},{9,1... | collective-permute-start | bytes 786440 | tf_op jit(solution)/shard_map/ppermute | solution.py:177
  43.2 14.9 %copy-start.9 = (bf16[128,2048]{1,0:T(8,128)(2,1)}, bf16[128,2048]{1,0:T(8,128)(2,1)S(1)}, u32[]{:S(2)}) copy-start(bf16[128,2048]{1,0:T(8,128)(2,1)S(1)} %collective-permute-done.1.h01) | copy-start | bytes 1572868
  43.2 14.8 %collective-permute-start.3 = (bf16[128,2048]{1,0:T(8,128)(2,1)S(1)}, bf16[128,2048]{1,0:T(8,128)(2,1)S(1)}, u32[]{:S(2)}, u32[]{:S(2)}) collective-permute-start(bf16[128,2048]{1,0:T(8,128)(2,1)S(1)} %collective-permute-done.1.h01), channel_id=1, source_target_pairs={{0,1},{1,0},{2,3},{3,2},{4,5},{5,4},{6,7},{7,6},{8,9},{9,8},{10,11... | collective-permute-start | bytes 1572872 | tf_op jit(solution)/shard_map/ppermute | solution.py:168
  48.9 8.2 %collective-permute-start.8 = (bf16[256,512]{1,0:T(8,128)(2,1)S(1)}, bf16[256,512]{1,0:T(8,128)(2,1)S(1)}, u32[]{:S(2)}, u32[]{:S(2)}) collective-permute-start(bf16[256,512]{1,0:T(8,128)(2,1)S(1)} %collective-permute-done.6), channel_id=1, source_target_pairs={{0,4},{4,8},{8,12},{12,0},{1,5},{5,9},{9,13},{13,1},{2,6},{6,10},{... | collective-permute-start | bytes 786440 | tf_op jit(solution)/shard_map/ppermute | solution.py:177
  48.9 5.0 %collective-permute-start.28 = (bf16[256,256]{1,0:T(8,128)(2,1)S(1)}, bf16[256,256]{1,0:T(8,128)(2,1)S(1)}, u32[]{:S(2)}, u32[]{:S(2)}) collective-permute-start(bf16[256,256]{1,0:T(8,128)(2,1)S(1)} %collective-permute-done.27), channel_id=1, source_target_pairs={{0,2},{2,0},{1,3},{3,1},{4,6},{6,4},{5,7},{7,5},{8,10},{10,8},{9,1... | collective-permute-start | bytes 393224 | tf_op jit(solution)/shard_map/ppermute | solution.py:177
  54.0 31.3 %collective-permute-start.16 = (bf16[256,2048]{1,0:T(8,128)(2,1)S(1)}, bf16[256,2048]{1,0:T(8,128)(2,1)S(1)}, u32[]{:S(2)}, u32[]{:S(2)}) collective-permute-start(bf16[256,2048]{1,0:T(8,128)(2,1)S(1)} %fusion.8), channel_id=1, source_target_pairs={{0,4},{5,9},{24,20},{29,25},{2,6},{7,11},{26,22},{31,27}} | collective-permute-start | bytes 3145736 | tf_op jit(solution)/shard_map/ppermute | solution.py:216
  55.5 9.1 %copy-start.2 = (bf16[2048,256]{1,0:T(8,128)(2,1)}, bf16[2048,256]{1,0:T(8,128)(2,1)S(1)}, u32[]{:S(2)}) copy-start(bf16[2048,256]{1,0:T(8,128)(2,1)S(1)} %constant_dynamic-update-slice_fusion.wkv.wkvm) | copy-start | bytes 3145732
  57.1 28.7 %collective-permute-start.9 = (bf16[256,512]{1,0:T(8,128)(2,1)S(1)}, bf16[256,512]{1,0:T(8,128)(2,1)S(1)}, u32[]{:S(2)}, u32[]{:S(2)}) collective-permute-start(bf16[256,512]{1,0:T(8,128)(2,1)S(1)} %collective-permute-done.8), channel_id=1, source_target_pairs={{0,2},{2,0},{1,3},{3,1},{4,6},{6,4},{5,7},{7,5},{8,10},{10,8},{9,1... | collective-permute-start | bytes 786440 | tf_op jit(solution)/shard_map/ppermute | solution.py:177
  58.0 0.8 copy-start.10
  58.0 14.5 %collective-permute-start.10 = (bf16[256,512]{1,0:T(8,128)(2,1)S(1)}, bf16[256,512]{1,0:T(8,128)(2,1)S(1)}, u32[]{:S(2)}, u32[]{:S(2)}) collective-permute-start(bf16[256,512]{1,0:T(8,128)(2,1)S(1)} %collective-permute-done.8), channel_id=1, source_target_pairs={{0,4},{4,8},{8,12},{12,0},{1,5},{5,9},{9,13},{13,1},{2,6},{6,10},{... | collective-permute-start | bytes 786440 | tf_op jit(solution)/shard_map/ppermute | solution.py:177
  58.8 0.8 copy-start.12
  68.0 17.1 %copy-start.1 = (bf16[1024,256]{1,0:T(8,128)(2,1)}, bf16[1024,256]{1,0:T(8,128)(2,1)S(1)}, u32[]{:S(2)}) copy-start(bf16[1024,256]{1,0:T(8,128)(2,1)S(1)} %convolution_convert_fusion.1) | copy-start | bytes 1572868
  68.2 12.3 %collective-permute-start.31 = (bf16[3,2,128,256]{3,2,1,0:T(8,128)(2,1)S(1)}, bf16[3,2,128,256]{3,2,1,0:T(8,128)(2,1)S(1)}, u32[]{:S(2)}, u32[]{:S(2)}) collective-permute-start(bf16[3,2,128,256]{3,2,1,0:T(8,128)(2,1)S(1)} %pad_maximum_fusion), channel_id=1, source_target_pairs={{0,2},{2,0},{1,3},{3,1},{4,6},{6,4},{5,7},{7,5},{8,10},{10,8},{9,1... | collective-permute-start | bytes 1179656 | tf_op jit(solution)/shard_map/ppermute | solution.py:307
  72.6 20.0 %collective-permute-start.11 = (bf16[256,512]{1,0:T(8,128)(2,1)S(1)}, bf16[256,512]{1,0:T(8,128)(2,1)S(1)}, u32[]{:S(2)}, u32[]{:S(2)}) collective-permute-start(bf16[256,512]{1,0:T(8,128)(2,1)S(1)} %collective-permute-done.10), channel_id=1, source_target_pairs={{0,2},{2,0},{1,3},{3,1},{4,6},{6,4},{5,7},{7,5},{8,10},{10,8},{9,1... | collective-permute-start | bytes 786440 | tf_op jit(solution)/shard_map/ppermute | solution.py:177
  73.2 14.6 %collective-permute-start.30 = (bf16[2,128,256]{2,1,0:T(8,128)(2,1)S(1)}, bf16[2,128,256]{2,1,0:T(8,128)(2,1)S(1)}, u32[]{:S(2)}, u32[]{:S(2)}) collective-permute-start(bf16[2,128,256]{2,1,0:T(8,128)(2,1)S(1)} %get-tuple-element.37), channel_id=1, source_target_pairs={{2,0},{4,2},{6,4},{8,6},{10,8},{12,10},{14,12},{3,1},{5,3},{7,5},{... | collective-permute-start | bytes 393224 | tf_op jit(solution)/shard_map/ppermute | solution.py:296
  80.5 7.5 %collective-permute-start.29 = (bf16[2,128,256]{2,1,0:T(8,128)(2,1)S(1)}, bf16[2,128,256]{2,1,0:T(8,128)(2,1)S(1)}, u32[]{:S(2)}, u32[]{:S(2)}) collective-permute-start(bf16[2,128,256]{2,1,0:T(8,128)(2,1)S(1)} %get-tuple-element.36), channel_id=1, source_target_pairs={{0,2},{2,4},{4,6},{6,8},{8,10},{10,12},{12,14},{1,3},{3,5},{5,7},{... | collective-permute-start | bytes 393224 | tf_op jit(solution)/shard_map/ppermute | solution.py:296
  85.2 2.6 %copy-start.8 = (bf16[128,2048]{1,0:T(8,128)(2,1)S(1)}, bf16[128,2048]{1,0:T(8,128)(2,1)}, u32[]{:S(2)}) copy-start(bf16[128,2048]{1,0:T(8,128)(2,1)} %c00.1) | copy-start | bytes 1572868
  85.3 12.4 %collective-permute-start.32 = (bf16[3,2,128,256]{3,2,1,0:T(8,128)(2,1)S(1)}, bf16[3,2,128,256]{3,2,1,0:T(8,128)(2,1)S(1)}, u32[]{:S(2)}, u32[]{:S(2)}) collective-permute-start(bf16[3,2,128,256]{3,2,1,0:T(8,128)(2,1)S(1)} %pad_maximum_fusion.1), channel_id=1, source_target_pairs={{0,4},{4,0},{8,12},{12,8},{1,5},{5,1},{9,13},{13,9},{2,6},{6,2},{1... | collective-permute-start | bytes 1179656 | tf_op jit(solution)/shard_map/ppermute | solution.py:307
  85.7 21.3 %copy-start.4 = (bf16[2,512,2048]{2,1,0:T(8,128)(2,1)S(1)}, bf16[2,512,2048]{2,1,0:T(8,128)(2,1)}, u32[]{:S(2)}) copy-start(bf16[2,512,2048]{2,1,0:T(8,128)(2,1)} %norm.1) | copy-start | bytes 12582916
  85.7 20.4 %collective-permute-start.17 = (bf16[256,2048]{1,0:T(8,128)(2,1)S(1)}, bf16[256,2048]{1,0:T(8,128)(2,1)S(1)}, u32[]{:S(2)}, u32[]{:S(2)}) collective-permute-start(bf16[256,2048]{1,0:T(8,128)(2,1)S(1)} %add.320), channel_id=1, source_target_pairs={{0,8},{4,12},{5,1},{9,13},{24,28},{20,16},{29,21},{25,17},{2,10},{... | collective-permute-start | bytes 3145736 | tf_op jit(solution)/shard_map/ppermute | solution.py:216
  87.9 22.5 %collective-permute-start.12 = (bf16[128,2048]{1,0:T(8,128)(2,1)S(1)}, bf16[128,2048]{1,0:T(8,128)(2,1)S(1)}, u32[]{:S(2)}, u32[]{:S(2)}) collective-permute-start(bf16[128,2048]{1,0:T(8,128)(2,1)S(1)} %copy-done.8), channel_id=1, source_target_pairs={{0,16},{16,0},{1,17},{17,1},{2,18},{18,2},{3,19},{19,3},{4,20},{20... | collective-permute-start | bytes 1572872 | tf_op jit(solution)/shard_map/ppermute | solution.py:168
  88.0 25.8 %collective-permute-start.18 = (bf16[256,2048]{1,0:T(8,128)(2,1)S(1)}, bf16[256,2048]{1,0:T(8,128)(2,1)S(1)}, u32[]{:S(2)}, u32[]{:S(2)}) collective-permute-start(bf16[256,2048]{1,0:T(8,128)(2,1)S(1)} %fusion.8), channel_id=1, source_target_pairs={{0,2},{2,0},{5,7},{7,5},{24,26},{26,24},{29,31},{31,29}} | collective-permute-start | bytes 3145736 | tf_op jit(solution)/shard_map/ppermute | solution.py:224
  92.6 17.7 %copy-start = (bf16[2048,512]{1,0:T(8,128)(2,1)}, bf16[2048,512]{1,0:T(8,128)(2,1)S(1)}, u32[]{:S(2)}) copy-start(bf16[2048,512]{1,0:T(8,128)(2,1)S(1)} %constant_dynamic-update-slice_fusion.8.wq.wqm) | copy-start | bytes 6291460
  92.6 21.2 %collective-permute-start.19 = (bf16[256,2048]{1,0:T(8,128)(2,1)S(1)}, bf16[256,2048]{1,0:T(8,128)(2,1)S(1)}, u32[]{:S(2)}, u32[]{:S(2)}) collective-permute-start(bf16[256,2048]{1,0:T(8,128)(2,1)S(1)} %collective-permute-done.16), channel_id=1, source_target_pairs={{4,6},{6,4},{9,11},{11,9},{20,22},{22,20},{25,27},{27,25}} | collective-permute-start | bytes 3145736 | tf_op jit(solution)/shard_map/ppermute | solution.py:224
  97.7 14.6 %collective-permute-start.33 = (bf16[3,2,128,256]{3,2,1,0:T(8,128)(2,1)S(1)}, bf16[3,2,128,256]{3,2,1,0:T(8,128)(2,1)S(1)}, u32[]{:S(2)}, u32[]{:S(2)}) collective-permute-start(bf16[3,2,128,256]{3,2,1,0:T(8,128)(2,1)S(1)} %pad_maximum_fusion.2), channel_id=1, source_target_pairs={{0,8},{4,12},{8,0},{12,4},{1,9},{5,13},{9,1},{13,5},{2,10},{6,14},... | collective-permute-start | bytes 1179656 | tf_op jit(solution)/shard_map/ppermute | solution.py:307
  106.1 7.7 %collective-permute-start.20 = (bf16[256,2048]{1,0:T(8,128)(2,1)S(1)}, bf16[256,2048]{1,0:T(8,128)(2,1)S(1)}, u32[]{:S(2)}, u32[]{:S(2)}) collective-permute-start(bf16[256,2048]{1,0:T(8,128)(2,1)S(1)} %collective-permute-done.17), channel_id=1, source_target_pairs={{8,10},{10,8},{12,14},{14,12},{1,3},{3,1},{13,15},{15,13},{28,30},... | collective-permute-start | bytes 3145736 | tf_op jit(solution)/shard_map/ppermute | solution.py:224
  110.4 3.4 %copy-start.11 = (bf16[128,2048]{1,0:T(8,128)(2,1)}, bf16[128,2048]{1,0:T(8,128)(2,1)S(1)}, u32[]{:S(2)}) copy-start(bf16[128,2048]{1,0:T(8,128)(2,1)S(1)} %collective-permute-done.12.c01) | copy-start | bytes 1572868
  110.4 6.0 %collective-permute-start.13 = (bf16[128,2048]{1,0:T(8,128)(2,1)S(1)}, bf16[128,2048]{1,0:T(8,128)(2,1)S(1)}, u32[]{:S(2)}, u32[]{:S(2)}) collective-permute-start(bf16[128,2048]{1,0:T(8,128)(2,1)S(1)} %copy-done.8), channel_id=1, source_target_pairs={{0,1},{1,0},{2,3},{3,2},{4,5},{5,4},{6,7},{7,6},{8,9},{9,8},{10,11... | collective-permute-start | bytes 1572872 | tf_op jit(solution)/shard_map/ppermute | solution.py:168
  112.3 4.1 %collective-permute-start.14 = (bf16[128,2048]{1,0:T(8,128)(2,1)S(1)}, bf16[128,2048]{1,0:T(8,128)(2,1)S(1)}, u32[]{:S(2)}, u32[]{:S(2)}) collective-permute-start(bf16[128,2048]{1,0:T(8,128)(2,1)S(1)} %collective-permute-done.12.c01), channel_id=1, source_target_pairs={{0,1},{1,0},{2,3},{3,2},{4,5},{5,4},{6,7},{7,6},{8,9},{9,8},{10,11... | collective-permute-start | bytes 1572872 | tf_op jit(solution)/shard_map/ppermute | solution.py:168
  116.4 0.8 copy-start.13
  117.2 0.8 copy-start.14
  134.8 10.9 %copy-start.7 = (bf16[2,2,128,256]{3,2,1,0:T(8,128)(2,1)S(1)}, bf16[2,2,128,256]{3,2,1,0:T(8,128)(2,1)}, u32[]{:S(2)}) copy-start(bf16[2,2,128,256]{3,2,1,0:T(8,128)(2,1)} %get-tuple-element.18) | copy-start | bytes 786436
  136.9 51.2 %copy-start.16 = (bf16[2,2,128,256]{3,2,1,0:T(8,128)(2,1)S(1)}, bf16[2,2,128,256]{3,2,1,0:T(8,128)(2,1)}, u32[]{:S(2)}) copy-start(bf16[2,2,128,256]{3,2,1,0:T(8,128)(2,1)} %get-tuple-element.17) | copy-start | bytes 786436
  136.9 7.8 %collective-permute-start.38 = (bf16[3,2,128,256]{3,2,1,0:T(8,128)(2,1)S(1)}, bf16[3,2,128,256]{3,2,1,0:T(8,128)(2,1)S(1)}, u32[]{:S(2)}, u32[]{:S(2)}) collective-permute-start(bf16[3,2,128,256]{3,2,1,0:T(8,128)(2,1)S(1)} %pad_maximum_fusion.3), channel_id=1, source_target_pairs={{0,2},{2,0},{1,3},{3,1},{4,6},{6,4},{5,7},{7,5},{8,10},{10,8},{9,1... | collective-permute-start | bytes 1179656 | tf_op jit(solution)/shard_map/ppermute | solution.py:364
  145.8 30.3 %collective-permute-start.39 = (bf16[3,2,128,256]{3,2,1,0:T(8,128)(2,1)S(1)}, bf16[3,2,128,256]{3,2,1,0:T(8,128)(2,1)S(1)}, u32[]{:S(2)}, u32[]{:S(2)}) collective-permute-start(bf16[3,2,128,256]{3,2,1,0:T(8,128)(2,1)S(1)} %pad_maximum_fusion.4), channel_id=1, source_target_pairs={{0,4},{4,0},{8,12},{12,8},{1,5},{5,1},{9,13},{13,9},{2,6},{6,2},{1... | collective-permute-start | bytes 1179656 | tf_op jit(solution)/shard_map/ppermute | solution.py:364
  176.2 24.2 %collective-permute-start.40 = (bf16[3,2,128,256]{3,2,1,0:T(8,128)(2,1)S(1)}, bf16[3,2,128,256]{3,2,1,0:T(8,128)(2,1)S(1)}, u32[]{:S(2)}, u32[]{:S(2)}) collective-permute-start(bf16[3,2,128,256]{3,2,1,0:T(8,128)(2,1)S(1)} %pad_maximum_fusion.5), channel_id=1, source_target_pairs={{0,8},{4,12},{8,0},{12,4},{1,9},{5,13},{9,1},{13,5},{2,10},{6,14},... | collective-permute-start | bytes 1179656 | tf_op jit(solution)/shard_map/ppermute | solution.py:364
  188.1 11.6 %collective-permute-start.36 = (bf16[2,128,256]{2,1,0:T(8,128)(2,1)S(1)}, bf16[2,128,256]{2,1,0:T(8,128)(2,1)S(1)}, u32[]{:S(2)}, u32[]{:S(2)}) collective-permute-start(bf16[2,128,256]{2,1,0:T(8,128)(2,1)S(1)} %get-tuple-element.40), channel_id=1, source_target_pairs={{2,0},{4,2},{6,4},{8,6},{10,8},{12,10},{14,12},{3,1},{5,3},{7,5},{... | collective-permute-start | bytes 393224 | tf_op jit(solution)/shard_map/ppermute | solution.py:359
  189.4 10.3 %collective-permute-start.37 = (bf16[2,128,256]{2,1,0:T(8,128)(2,1)S(1)}, bf16[2,128,256]{2,1,0:T(8,128)(2,1)S(1)}, u32[]{:S(2)}, u32[]{:S(2)}) collective-permute-start(bf16[2,128,256]{2,1,0:T(8,128)(2,1)S(1)} %get-tuple-element.41), channel_id=1, source_target_pairs={{0,2},{2,4},{4,6},{6,8},{8,10},{10,12},{12,14},{1,3},{3,5},{5,7},{... | collective-permute-start | bytes 393224 | tf_op jit(solution)/shard_map/ppermute | solution.py:359
  199.6 13.7 %collective-permute-start.34 = (bf16[256,2048]{1,0:T(8,128)(2,1)}, bf16[256,2048]{1,0:T(8,128)(2,1)S(1)}, u32[]{:S(2)}, u32[]{:S(2)}) collective-permute-start(bf16[256,2048]{1,0:T(8,128)(2,1)} %get-tuple-element.14), channel_id=1, source_target_pairs={{0,1},{1,0},{2,3},{3,2},{4,5},{5,4},{6,7},{7,6},{8,9},{9,8},{10,11... | collective-permute-start | bytes 3145736 | tf_op jit(solution)/shard_map/ppermute | solution.py:168
  201.9 11.2 %copy-start.3 = (bf16[128,2048]{1,0:T(8,128)(2,1)S(1)}, bf16[128,2048]{1,0:T(8,128)(2,1)}, u32[]{:S(2)}) copy-start(bf16[128,2048]{1,0:T(8,128)(2,1)} %h00.1) | copy-start | bytes 1572868
  201.9 11.4 %copy-start.5 = (f32[256,2048]{1,0:T(8,128)S(1)}, f32[256,2048]{1,0:T(8,128)}, u32[]{:S(2)}) copy-start(f32[256,2048]{1,0:T(8,128)} %get-tuple-element.13) | copy-start | bytes 6291460
  212.6 3.0 %collective-permute-start.41 = (bf16[256,2048]{1,0:T(8,128)(2,1)}, bf16[256,2048]{1,0:T(8,128)(2,1)S(1)}, u32[]{:S(2)}, u32[]{:S(2)}) collective-permute-start(bf16[256,2048]{1,0:T(8,128)(2,1)} %get-tuple-element.21), channel_id=1, source_target_pairs={{0,1},{1,0},{2,3},{3,2},{4,5},{5,4},{6,7},{7,6},{8,9},{9,8},{10,11... | collective-permute-start | bytes 3145736 | tf_op jit(solution)/shard_map/ppermute | solution.py:168
  213.3 2.3 copy-start.6
  213.7 14.8 %collective-permute-start.35 = (bf16[128,2048]{1,0:T(8,128)(2,1)S(1)}, bf16[128,2048]{1,0:T(8,128)(2,1)S(1)}, u32[]{:S(2)}, u32[]{:S(2)}) collective-permute-start(bf16[128,2048]{1,0:T(8,128)(2,1)S(1)} %slice.195), channel_id=1, source_target_pairs={{0,16},{16,0},{1,17},{17,1},{2,18},{18,2},{3,19},{19,3},{4,20},{20... | collective-permute-start | bytes 1572872 | tf_op jit(solution)/shard_map/ppermute | solution.py:168
  216.1 22.8 %collective-permute-start.42 = (bf16[128,2048]{1,0:T(8,128)(2,1)S(1)}, bf16[128,2048]{1,0:T(8,128)(2,1)S(1)}, u32[]{:S(2)}, u32[]{:S(2)}) collective-permute-start(bf16[128,2048]{1,0:T(8,128)(2,1)S(1)} %slice.194), channel_id=1, source_target_pairs={{0,16},{16,0},{1,17},{17,1},{2,18},{18,2},{3,19},{19,3},{4,20},{20... | collective-permute-start | bytes 1572872 | tf_op jit(solution)/shard_map/ppermute | solution.py:168

commit v2 on v1

v2 whole, which is shorter than its diff:
```python
import jax
import jax.numpy as jnp
from jax import lax
from jax.experimental import pallas as pl
from jax.experimental.pallas import tpu as pltpu
from jax.sharding import Mesh, PartitionSpec as P

HEADS = 16
KVH = 4
HDIM = 128
BLK = 128
REP = HEADS // KVH
EPS = 1e-05
SCALE = HDIM ** (-0.5)
F32 = jnp.float32
BF16 = jnp.bfloat16
VMEM = 56 * 1024 * 1024


def dot(a, b, ca, cb):
    return lax.dot_general(a, b, (((ca,), (cb,)), ((), ())), preferred_element_type=F32)


def flip_matrix(n):
    i = lax.broadcasted_iota(jnp.int32, (n, n), 0)
    j = lax.broadcasted_iota(jnp.int32, (n, n), 1)
    return jnp.where(i + j == n - 1, 1.0, 0.0).astype(BF16)


def params():
    return pltpu.CompilerParams(vmem_limit_bytes=VMEM)


def whole():
    return pl.BlockSpec(memory_space=pltpu.VMEM)


def smem():
    return pl.BlockSpec(memory_space=pltpu.SMEM)


def norm_kernel(h00, h01, h10, h11, out):
    core = lax.axis_index("c")
    flip = flip_matrix(128)
    for side, refs in enumerate(((h00, h01), (h10, h11))):
        place = core if side == 0 else 1 - core
        for grp in range(2):
            u = refs[grp][...].astype(F32)
            inv = lax.rsqrt(jnp.mean(u * u, axis=1, keepdims=True) + EPS)
            n = (u * inv).astype(BF16)
            row = pl.multiple_of(place * (2 * BLK) + grp * BLK, BLK)
            out[0, pl.ds(row, BLK), :] = n
            count = n.shape[1] // 128
            for k in range(count):
                m = count - 1 - k
                out[1, pl.ds(row, BLK), m * 128 : m * 128 + 128] = dot(
                    n[:, k * 128 : k * 128 + 128], flip, 1, 0
                ).astype(BF16)


def grad_att_kernel(c00, c01, c10, c11, *refs):
    pieces, (out, w) = refs[:8], refs[8:]
    core = lax.axis_index("c")
    own = lax.axis_index("b") % 2
    half = pieces[0].shape[1]
    rows = pieces[0].shape[0]
    for i in range(4):
        row = pl.multiple_of((own if i < 2 else 1 - own) * rows, rows)
        column = (i % 2) * half
        w[pl.ds(row, rows), column : column + half] = pieces[2 * i][...] + pieces[2 * i + 1][...]
    for side, refs in enumerate(((c00, c01), (c10, c11))):
        place = core if side == 0 else 1 - core
        rows = jnp.concatenate([refs[0][...], refs[1][...]], axis=0)
        row = pl.multiple_of(place * (2 * BLK), 2 * BLK)
        out[pl.ds(row, 2 * BLK), :] = dot(rows, w[...], 1, 1).astype(BF16)


def position():
    return lax.axis_index("a") * lax.axis_size("b") + lax.axis_index("b")


def last_block():
    return 2 * lax.axis_size("a") * lax.axis_size("b") - 1


def attention_kernel(chosen, q, ga, kv, near_p, near_m, far_p, far_m, att, gq, dkv, dnear_p, dnear_m, dfar_p, dfar_m):
    last = last_block()
    t = position()
    g_dyn = chosen[pl.program_id(0)]
    for strand in range(2):
        near, far, dnear, dfar = ((near_p, far_p, dnear_p, dfar_p), (near_m, far_m, dnear_m, dfar_m))[strand]
        sets = [kv[strand, 0, 0], kv[strand, 1, 0], near[0], far[0, 0], far[1, 0]]
        stat_block = last if strand == 0 else 0
        dyn_block = g_dyn if strand == 0 else last - g_dyn
        sums = [None] * 5
        for side in range(2):
            block = 2 * t + side
            next_to = block - 1 if strand == 0 else block + 1
            if strand == 0:
                near_set = 2 if side == 0 else 0
            else:
                near_set = 1 if side == 0 else 2
            order = (near_set, side, 3, 4)
            flags = (
                (next_to >= 0) & (next_to <= last),
                None,
                (stat_block != block) & (stat_block != next_to),
                (dyn_block != block) & (dyn_block != next_to),
            )
            keys = jnp.concatenate([sets[i][:, :HDIM] for i in order], axis=0)
            values = jnp.concatenate([sets[i][:, HDIM:] for i in order], axis=0)
            qs = q[strand, side, 0]
            gs = ga[side, 0]
            rows = jnp.concatenate([qs[:, i * HDIM : (i + 1) * HDIM] for i in range(REP)], axis=0)
            ups = jnp.concatenate([gs[:, i * HDIM : (i + 1) * HDIM] for i in range(REP)], axis=0)
            s = dot(rows, keys, 1, 1) * SCALE
            parts = []
            for i in range(4):
                part = s[:, i * BLK : (i + 1) * BLK]
                if flags[i] is not None:
                    part = jnp.where(flags[i], part, -jnp.inf)
                parts.append(part)
            s = jnp.concatenate(parts, axis=1)
            e = jnp.exp(s - jnp.max(s, axis=1, keepdims=True))
            p = e * (1.0 / jnp.sum(e, axis=1, keepdims=True))
            ph = p.astype(BF16)
            o = dot(ph, values, 1, 0)
            dp = dot(ups, values, 1, 1)
            center = jnp.sum(p * dp, axis=1, keepdims=True)
            ds = (p * (dp - center) * SCALE).astype(BF16)
            dq = dot(ds, keys, 1, 0)
            dk = dot(ds, rows, 0, 0)
            dv = dot(ph, ups, 0, 0)
            for i in range(REP):
                att[strand, side, 0, :, i * HDIM : (i + 1) * HDIM] = o[i * BLK : (i + 1) * BLK].astype(BF16)
                gq[strand, side, 0, :, i * HDIM : (i + 1) * HDIM] = dq[i * BLK : (i + 1) * BLK].astype(BF16)
            for i in range(4):
                term = (dk[i * BLK : (i + 1) * BLK], dv[i * BLK : (i + 1) * BLK])
                old = sums[order[i]]
                sums[order[i]] = term if old is None else (old[0] + term[0], old[1] + term[1])
        targets = (dkv.at[strand, 0, 0], dkv.at[strand, 1, 0], dnear.at[0], dfar.at[0, 0], dfar.at[1, 0])
        for target, (dk, dv) in zip(targets, sums):
            target[:, :HDIM] = dk.astype(target.dtype)
            target[:, HDIM:] = dv.astype(target.dtype)


def output_kernel(att, w, keep, send):
    core = lax.axis_index("c")
    for target, place in ((keep, core), (send, 1 - core)):
        total = dot(att[0, place], w[...], 1, 0) + dot(att[1, place], w[...], 1, 0)
        target[...] = total.astype(target.dtype)


def query_part_kernel(gq, w, wm, part, wkv, wkvf):
    core = lax.axis_index("c")
    flipped = dot(flip_matrix(w.shape[0]), wm[...], 1, 0).astype(BF16)
    wkv[...] = w[:, : 2 * HDIM]
    wkvf[...] = flipped[:, : 2 * HDIM]
    for i, place in enumerate((core, 1 - core)):
        part[i] = dot(gq[0, place], w[:, 2 * HDIM :], 1, 1) + dot(gq[1, place], flipped[:, 2 * HDIM :], 1, 1)


def key_part_kernel(chosen, dkv, near_p, near_m, far_p, far_m, part, wkv, wkvf, keep, send, kg):
    core = lax.axis_index("c")
    t = position()
    last = last_block()

    @pl.when(pl.program_id(0) == 0)
    def _():
        for strand in range(2):
            stat_block = last if strand == 0 else 0
            near, far = ((near_p, far_p), (near_m, far_m))[strand]
            for side in range(2):
                for grp in range(2):
                    total = dkv[strand, side, grp]
                    if side != strand:
                        total = total + near[grp].astype(F32)
                        total = total + jnp.where(2 * t + side == stat_block, far[0, grp].astype(F32), 0.0)
                    dyn_block = chosen[grp] if strand == 0 else last - chosen[grp]
                    total = total + jnp.where(2 * t + side == dyn_block, far[1, grp].astype(F32), 0.0)
                    kg[strand, side, grp * BLK : (grp + 1) * BLK, :] = total.astype(BF16)

    for i, (target, place) in enumerate(((keep, core), (send, 1 - core))):
        total = part[i] + dot(kg[0, place], wkv[...], 1, 1) + dot(kg[1, place], wkvf[...], 1, 1)
        target[...] = total.astype(target.dtype)


def head_group(x, c):
    return x + c * (3 - 2 * x)


def cost(flops, moved):
    return pl.CostEstimate(flops=flops, transcendentals=0, bytes_accessed=moved)


def swap(value, axis):
    return lax.ppermute(value, axis, [(0, 1), (1, 0)])


def after(value, *others):
    return lax.optimization_barrier((value,) + others)[0]


def pair(own, other, index):
    return jnp.where(index == 0, jnp.concatenate([own, other], 0), jnp.concatenate([other, own], 0))


def ring(value, axis):
    count = lax.axis_size(axis)
    return lax.ppermute(value, axis, [(i, (i + 1) % count) for i in range(count)])


def gather_rows(chunk, held):
    na, nb = lax.axis_size("a"), lax.axis_size("b")
    a, b = lax.axis_index("a"), lax.axis_index("b")
    size = chunk.shape[0]
    full = jnp.zeros((na * nb * size, chunk.shape[1]), chunk.dtype)
    across = []
    for step in range(na):
        if 0 < step:
            chunk = ring(after(chunk, *held.get(step, ()), *across[: step - 1][-1:]), "a")
        inner = chunk
        for turn in range(nb):
            pos = ((a - step) % na) * nb + (b - turn) % nb
            full = lax.dynamic_update_slice(full, inner, (pos * size, 0))
            if turn + 1 < nb:
                if step + 1 == na and turn == 0:
                    inner = after(inner, *held.get(-1, ()), *across[-1:])
                inner = ring(inner, "b")
        across.append(inner)
    return full, chunk


def output_rows(w_out, x, a, b, c, held, arrived):
    na, nb = lax.axis_size("a"), lax.axis_size("b")
    mine = head_group(x, c)
    half = w_out.shape[1] // 2
    if (na, nb) != (4, 2):
        full = lax.all_gather(w_out, ("a", "b", "c"), axis=0, tiled=True)
        rows = REP * HDIM // 2
        place = b % 2
        pieces = []
        for where in (place, 1 - place):
            piece = lax.dynamic_slice(full, (mine * 2 * rows + where * rows, 0), (rows, full.shape[1]))
            pieces += [piece[:, :half], piece[:, half:]]
        return [(piece, jnp.zeros_like(piece)) for piece in pieces]
    source = pair(w_out, swap(w_out, "c"), c)
    current = jnp.where(a == mine, source, 0).astype(source.dtype)

    def spot(x, a, c):
        return (x * na + a) * 2 + c

    def send(value, moves):
        pairs = []
        for (sx, sc), (i, j) in moves.items():
            pairs.append((spot(sx, i, sc), spot(sx, j, sc)))
        return lax.ppermute(value, ("x", "a", "c"), pairs)

    def across(value, holders):
        pairs = []
        for (sx, sc), spots in holders.items():
            for i in spots:
                at = (sx * na + i) * 4 + sc
                pairs += [(at, at + 2), (at + 2, at)]
        return lax.ppermute(value, ("x", "a", "b", "c"), pairs)

    start = after(current, held)
    parts = [start[:, :half], start[:, half:]]
    first = [send(v, {(0, 0): (0, 1), (0, 1): (3, 2), (1, 0): (1, 0), (1, 1): (2, 3)}) for v in parts]
    parts = [after(v + w, z) for v, w, z in zip(parts, first, arrived)]
    second = [send(v, {(0, 0): (1, 2), (0, 1): (2, 1), (1, 0): (1, 2), (1, 1): (2, 1)}) for v in parts]
    early = [across(v, {(0, 0): (0, 1), (0, 1): (3, 2), (1, 0): (1, 0), (1, 1): (2, 3)}) for v in parts]
    third = [
        send(after(v, w), {(0, 0): (2, 3), (0, 1): (1, 0), (1, 0): (2, 3), (1, 1): (1, 0)})
        for v, w in zip(second, early)
    ]
    late = [v + w for v, w in zip(second, third)]
    beyond = [across(v, {(0, 0): (2, 3), (0, 1): (1, 0), (1, 0): (2, 3), (1, 1): (1, 0)}) for v in late]
    return list(zip(parts, late)) + list(zip(early, beyond))


def rounds():
    for axis, low in (("b", 1), ("a", lax.axis_size("b"))):
        count = lax.axis_size(axis)
        bit = 1
        while bit < count:
            yield axis, bit * low, [(i, i ^ bit) for i in range(count)]
            bit *= 2


def trade(first, second, t, owner, inward, states, held=()):
    for number, (axis, weight, pairs) in enumerate(rounds()):
        if number == 2:
            first = after(first, *held)
        same = (t // weight) % 2 == (owner // weight) % 2
        give = same != inward
        got = lax.ppermute(jnp.where(give, first, second), axis, pairs)
        states.append(got)
        first, second = jnp.where(give, first, first + got), jnp.where(give, second + got, second)
    return first, second


def body(hidden, w_query, w_keyval, w_out, global_blocks, cotangent):
    x, a, b, c = (lax.axis_index(n) for n in ("x", "a", "b", "c"))
    na, nb = lax.axis_size("a"), lax.axis_size("b")
    n = na * nb
    t = a * nb + b
    blocks = 2 * n
    width = hidden.shape[1]
    mine = head_group(x, c)
    theirs = head_group(x, 1 - c)
    line_up = [(i, i + 1) for i in range(n - 1)]
    line_down = [(i + 1, i) for i in range(n - 1)]

    h10 = swap(hidden, "c")
    h01 = swap(hidden, "x")
    h11 = swap(h01, "c")
    g_own = jnp.sum(global_blocks) - (blocks - 1)
    g_other = swap(after(jnp.full((8, 128), g_own, F32), h01), "x")
    chosen = jnp.stack([g_own, g_other[0, 0].astype(jnp.int32)])
    c10 = swap(cotangent, "c")
    c01 = swap(after(cotangent, g_other), "x")
    c11 = swap(c01, "c")

    half = KVH * HDIM

    def kv_columns(j):
        return jnp.concatenate(
            [
                lax.dynamic_slice_in_dim(w_keyval, j * HDIM, HDIM, 1),
                lax.dynamic_slice_in_dim(w_keyval, half + j * HDIM, HDIM, 1),
            ],
            axis=1,
        )

    def q_columns(j):
        return lax.dynamic_slice_in_dim(w_query, j * REP * HDIM, REP * HDIM, 1)

    normed = pl.pallas_call(
        norm_kernel,
        out_shape=jax.ShapeDtypeStruct((2, 4 * BLK, width), BF16),
        in_specs=[whole()] * 4,
        out_specs=whole(),
        cost_estimate=cost(10**9, 6 * 2**20),
        compiler_params=params(),
        name="norm",
    )(hidden, h01, h10, h11)
    def columns(j):
        return jnp.concatenate([kv_columns(j), q_columns(j)], axis=1)

    held = {3: (h01,), -1: (normed, c01)}
    weight, far_chunk = gather_rows(pair(columns(mine), swap(columns(theirs), "c"), c), held)
    q_weight = weight[:, 2 * HDIM :]
    kv_weight = weight[:, : 2 * HDIM]
    normed = normed.reshape(8 * BLK, width)
    kv = dot(normed, kv_weight, 1, 0).astype(BF16).reshape(2, 2, 2, BLK, 2 * HDIM)

    ctx = ("a", "b")
    up = kv[0, 1]
    down = kv[1, 0]
    near_p, near_m = lax.ppermute(up, ctx, line_up), lax.ppermute(down, ctx, line_down)
    owner = jnp.stack([jnp.full((2,), n - 1, jnp.int32), chosen // 2])
    side = jnp.stack([jnp.ones((2,), jnp.int32), chosen % 2])[:, :, None, None]
    owner = owner[:, :, None, None]
    first = jnp.where(owner == t, jnp.where(side == 0, kv[0, 0], kv[0, 1]), 0).astype(BF16)
    second = jnp.where(n - 1 - owner == t, jnp.where(side == 1, kv[1, 0], kv[1, 1]), 0).astype(BF16)
    first = after(first, c01)
    arrived = []
    first, second = trade(first, second, t, owner, False, arrived)
    wo_parts = output_rows(w_out, x, a, b, c, far_chunk, arrived)

    queries = dot(normed, q_weight, 1, 0).astype(BF16).reshape(2, 2, 2, BLK, REP * HDIM)

    grad_att, o_weight = pl.pallas_call(
        grad_att_kernel,
        out_shape=(
            jax.ShapeDtypeStruct((4 * BLK, REP * HDIM), BF16),
            jax.ShapeDtypeStruct((REP * HDIM, width), BF16),
        ),
        in_specs=[whole()] * 12,
        out_specs=[whole()] * 2,
        cost_estimate=cost(10**9, 9 * 2**20),
        compiler_params=params(),
        name="grad_att",
    )(cotangent, c01, c10, c11, *[v for piece in wo_parts for v in piece])
    grad_att = grad_att.reshape(2, 2, BLK, REP * HDIM)

    wide = pl.BlockSpec((2, 2, 1, BLK, REP * HDIM), lambda g: (0, 0, g, 0, 0))
    pairs_spec = pl.BlockSpec((2, 2, 1, BLK, 2 * HDIM), lambda g: (0, 0, g, 0, 0))
    near_spec = pl.BlockSpec((1, BLK, 2 * HDIM), lambda g: (g, 0, 0))
    far_spec = pl.BlockSpec((2, 1, BLK, 2 * HDIM), lambda g: (0, g, 0, 0))
    near_shape = jax.ShapeDtypeStruct((2, BLK, 2 * HDIM), BF16)
    far_shape = jax.ShapeDtypeStruct((2, 2, BLK, 2 * HDIM), BF16)
    extras = [near_spec, near_spec, far_spec, far_spec]
    att, gq, dkv, dnear_p, dnear_m, dfar_p, dfar_m = pl.pallas_call(
        attention_kernel,
        grid=(2,),
        out_shape=(
            jax.ShapeDtypeStruct(queries.shape, BF16),
            jax.ShapeDtypeStruct(queries.shape, BF16),
            jax.ShapeDtypeStruct(kv.shape, F32),
            near_shape,
            near_shape,
            far_shape,
            far_shape,
        ),
        in_specs=[smem(), wide, pl.BlockSpec((2, 1, BLK, REP * HDIM), lambda g: (0, g, 0, 0)), pairs_spec] + extras,
        out_specs=[wide, wide, pairs_spec] + extras,
        cost_estimate=cost(8 * 10**9, 10 * 2**20),
        compiler_params=params(),
        name="attention",
    )(chosen, queries, grad_att, kv, near_p, near_m, first, second)

    near_p, near_m = lax.ppermute(dnear_p, ctx, line_down), lax.ppermute(dnear_m, ctx, line_up)
    rows = 2 * BLK

    def finish(keep, send):
        got = swap(send, "c")
        total = keep + got.astype(F32)
        return total[:BLK] + swap(total[BLK:].astype(BF16), "x").astype(F32), total

    chunk = width // 4
    partial = (jax.ShapeDtypeStruct((rows, width), F32), jax.ShapeDtypeStruct((rows, width), BF16))
    out_parts = pl.pallas_call(
            output_kernel,
            grid=(width // chunk,),
            out_shape=partial,
            in_specs=[
                pl.BlockSpec((2, 2, rows, REP * HDIM), lambda k: (0, 0, 0, 0)),
                pl.BlockSpec((REP * HDIM, chunk), lambda k: (0, k)),
            ],
            out_specs=[pl.BlockSpec((rows, chunk), lambda k: (0, k))] * 2,
            cost_estimate=cost(2 * 10**9, 7 * 2**20),
            compiler_params=params(),
            name="output",
        )(att.reshape(2, 2, rows, REP * HDIM), o_weight)
    arrived = []
    far_p, far_m = trade(dfar_p, dfar_m, t, owner, True, arrived, (out_parts[1],))
    combined, _ = finish(*out_parts)
    combined = combined.astype(BF16)

    chunk = 256
    steps = width // chunk

    def fixed(shape):
        return pl.BlockSpec(shape, lambda k: (0,) * len(shape))

    part, kv_plain, kv_flipped = pl.pallas_call(
        query_part_kernel,
        grid=(steps,),
        out_shape=(
            jax.ShapeDtypeStruct((2, rows, width), F32),
            jax.ShapeDtypeStruct((width, 2 * HDIM), BF16),
            jax.ShapeDtypeStruct((width, 2 * HDIM), BF16),
        ),
        in_specs=[
            fixed((2, 2, rows, REP * HDIM)),
            pl.BlockSpec((chunk, (2 + REP) * HDIM), lambda k: (k, 0)),
            pl.BlockSpec((chunk, (2 + REP) * HDIM), lambda k: (steps - 1 - k, 0)),
        ],
        out_specs=(
            pl.BlockSpec((2, rows, chunk), lambda k: (0, 0, k)),
            pl.BlockSpec((chunk, 2 * HDIM), lambda k: (k, 0)),
            pl.BlockSpec((chunk, 2 * HDIM), lambda k: (k, 0)),
        ),
        cost_estimate=cost(3 * 10**9, 13 * 2**20),
        compiler_params=params(),
        name="query_part",
    )(after(gq, arrived[1]).reshape(2, 2, rows, REP * HDIM), weight, weight)

    far_p = after(far_p, combined)
    chunk = width // 4
    halves = []
    for start in (0, 2):
        half, total = finish(
                *pl.pallas_call(
                    key_part_kernel,
                    grid=(2,),
                    out_shape=(
                        jax.ShapeDtypeStruct((rows, 2 * chunk), F32),
                        jax.ShapeDtypeStruct((rows, 2 * chunk), BF16),
                    ),
                    in_specs=[
                        smem(),
                        fixed(dkv.shape),
                        fixed(near_shape.shape),
                        fixed(near_shape.shape),
                        fixed(far_shape.shape),
                        fixed(far_shape.shape),
                        pl.BlockSpec((2, rows, chunk), lambda k, start=start: (0, 0, k + start)),
                        pl.BlockSpec((chunk, 2 * HDIM), lambda k, start=start: (k + start, 0)),
                        pl.BlockSpec((chunk, 2 * HDIM), lambda k, start=start: (k + start, 0)),
                    ],
                    out_specs=[pl.BlockSpec((rows, chunk), lambda k: (0, k))] * 2,
                    scratch_shapes=[pltpu.VMEM((2, 2, rows, 2 * HDIM), BF16)],
                    cost_estimate=cost(5 * 10**8, 8 * 2**20),
                    compiler_params=params(),
                    name="key_part",
                )(chosen, dkv, near_p, near_m, far_p, far_m, part, kv_plain, kv_flipped)
        )
        halves.append(half)
        far_p = after(far_p, total)
    grad_norm = jnp.concatenate(halves, axis=1)

    u = hidden.astype(F32)
    inv_rms = lax.rsqrt(jnp.mean(u * u, axis=1, keepdims=True) + EPS)
    scaled = u * inv_rms
    grad_in = inv_rms * (grad_norm - scaled * jnp.mean(grad_norm * scaled, axis=1, keepdims=True))
    return (combined, grad_in.astype(BF16))


def split(count):
    inner = 1
    while (2 * inner) ** 2 <= count:
        inner *= 2
    return count // inner, inner


def solution(mesh):
    na, nb = split(mesh.shape["ctx"] // 2)
    grid = Mesh(mesh.devices.reshape(mesh.shape["groups"], na, nb, 2), ("x", "a", "b", "c"))
    return jax.shard_map(
        body,
        mesh=grid,
        in_specs=(
            P(("x", "a", "b", "c"), None),
            P(("a", "b", "c"), None),
            P(("a", "b", "c"), None),
            P(("a", "b", "c"), None),
            P("x"),
            P(("x", "a", "b", "c"), None),
        ),
        out_specs=(P(("x", "a", "b", "c"), None), P(("x", "a", "b", "c"), None)),
        check_vma=False,
    )
```

time: 241 us -> 191 us (0.79)
  waiting for transfers between devices: 88.4 us -> 55.5 us
  starting transfers between devices: 81 us -> 54.4 us
  Pallas kernels: 37.9 us -> 46 us
  local copies, waits for them, and re-layouts: 6.92 us -> 12.7 us
  other arithmetic: 17.2 us -> 14.2 us
    ppermute x8, starting transfers between devices: 41.3 us -> 14.4 us  [the longest x6 8.52 us: trade(): got = lax.ppermute(jnp.where(give, first, second), axis, pairs)]
    ppermute x14 -> x7, waiting for transfers between devices: 30.3 us -> 14.7 us  [ring(): lax.ppermute(value, axis, [(i, (i + 1) % count) for i in range(count)])]
    ppermute x8, waiting for transfers between devices: 26.2 us -> 15.6 us  [the longest x6 15.6 us: trade(): got = lax.ppermute(jnp.where(give, first, second), axis, pairs)]
    ppermute x2 -> x6, waiting for transfers between devices: 8.3 us -> 0.02 us  [send(): return lax.ppermute(value, ('x', 'a', 'c'), pairs)]
    pallas_call x2 -> x4, Pallas kernels: 15 us -> 23 us  [the longest x1 9.87 us: body(): pl.pallas_call(query_part_kernel, grid=(steps,), out_shape=(jax.ShapeDtyp...]
    ppermute x3 -> x4, waiting for transfers between devices: 0.01 us -> 6.85 us  [across(): return lax.ppermute(value, ('x', 'a', 'b', 'c'), pairs)]
    ppermute x14 -> x15, waiting for transfers between devices: 23.5 us -> 18.4 us  [swap(): return lax.ppermute(value, axis, [(0, 1), (1, 0)])]
    dynamic_update_slice x14 -> x7, local copies, waits for them, and re-layouts: 0.26 us -> 4.23 us  [gather_rows(): full = lax.dynamic_update_slice(full, inner, (pos * size, 0))]
  transfers between devices with their start and end apart: 43 -> 42, of which waited for: 15 -> 19; matrix products, arithmetic and copies ran while one was open for 10% -> 12% of each run, Pallas kernels for 9% -> 13%
where the time goes in v2:
time: 191 us; the launch traced here: 190 us
  waiting for transfers between devices  55.5 us (29%)
  starting transfers between devices  54.4 us (28%)
  Pallas kernels  46 us (24%)
  other arithmetic  14.2 us (7%)
  local copies, waits for them, and re-layouts  12.7 us (7%)
  matrix products  4.59 us (2%)
  between operations  2.63 us (1%)
    ppermute x15, waiting for transfers between devices, swap(): return lax.ppermute(value, axis, [(0, 1), (1, 0)])  18.4 us
    ppermute x6, waiting for transfers between devices, trade(): got = lax.ppermute(jnp.where(give, first, second), axis, pairs)  15.6 us
    ppermute x7, waiting for transfers between devices, ring(): lax.ppermute(value, axis, [(i, (i + 1) % count) for i in range(count)])  14.7 us
    ppermute x15, starting transfers between devices, swap(): return lax.ppermute(value, axis, [(0, 1), (1, 0)])  13.3 us
    pallas_call x1, Pallas kernels, body(): pl.pallas_call(attention_kernel, grid=(2,), out_shape=(jax.ShapeDtypeStru...  12.5 us
    pallas_call x1, Pallas kernels, body(): pl.pallas_call(query_part_kernel, grid=(steps,), out_shape=(jax.ShapeDtyp...  9.87 us
    ppermute x4, starting transfers between devices, across(): return lax.ppermute(value, ('x', 'a', 'b', 'c'), pairs)  9.01 us
    ppermute x6, starting transfers between devices, trade(): got = lax.ppermute(jnp.where(give, first, second), axis, pairs)  8.52 us
  transfers between devices with their start and end apart: 42, of which 19 were waited for; matrix products, arithmetic and copies ran while one was open for 12% of the time, Pallas kernels for 13%

profile of v2, /device:TPU:0, one launch (start us, length us, event | category | flops | bytes accessed | tf_op | source)
XLA Modules:
  0.0 190.0 jit_solution(12155076848364599887)
XLA Ops:
  0.7 3.0 %collective-permute-start = (bf16[128,2048]{1,0:T(8,128)(2,1)}, bf16[128,2048]{1,0:T(8,128)(2,1)S(1)}, u32[]{:S(2)}, u32[]{:S(2)}) collective-permute-start(bf16[128,2048]{1,0:T(8,128)(2,1)} %h00.1), channel_id=1, source_target_pairs={{0,16},{16,0},{1,17},{17,1},{2,18},{18,2},{3,19},{19,3},{4,20},{20... | collective-permute-start | bytes 1572872 | tf_op jit(solution)/shard_map/ppermute | solution.py:197
  3.7 1.0 constant_dynamic-slice_fusion
  4.7 0.8 constant_dynamic-slice_fusion.2
  6.1 1.1 collective-permute-done.4
  7.4 0.8 constant_dynamic-update-slice_fusion.7
  8.2 1.5 collective-permute-start.5
  9.9 1.6 collective-permute-start.6
  12.9 2.9 %collective-permute-done.h01 = bf16[128,2048]{1,0:T(8,128)(2,1)S(1)} collective-permute-done((bf16[128,2048]{1,0:T(8,128)(2,1)}, bf16[128,2048]{1,0:T(8,128)(2,1)S(1)}, u32[]{:S(2)}, u32[]{:S(2)}) %collective-permute-start) | collective-permute-done | bytes 524320 | tf_op jit(solution)/shard_map/ppermute | solution.py:197
  15.8 1.7 collective-permute-start.1
  17.6 1.6 fusion.14
  20.6 1.8 collective-permute-start.11
  22.5 0.8 collective-permute-done.6
  23.4 0.8 collective-permute-start.8
  24.2 1.5 collective-permute-start.7
  26.5 7.5 %collective-permute-done.7 = bf16[256,768]{1,0:T(8,128)(2,1)S(1)} collective-permute-done((bf16[256,768]{1,0:T(8,128)(2,1)S(1)}, bf16[256,768]{1,0:T(8,128)(2,1)S(1)}, u32[]{:S(2)}, u32[]{:S(2)}) %collective-permute-start.7) | collective-permute-done | bytes 393248 | tf_op jit(solution)/shard_map/ppermute | solution.py:210
  34.0 1.8 collective-permute-done.8
  35.8 1.5 collective-permute-start.9
  40.5 0.9 copy-done.22
  41.3 4.9 %norm.1 = bf16[2,512,2048]{2,1,0:T(8,128)(2,1)} custom-call(bf16[128,2048]{1,0:T(8,128)(2,1)} %h00.1, bf16[128,2048]{1,0:T(8,128)(2,1)} %copy-done.16, bf16[128,2048]{1,0:T(8,128)(2,1)} %copy-done.17, bf16[128,2048]{1,0:T(8,128)(2,1)} %copy-done.22), custom_call_target="tpu_custom_call" | custom-call | flops 1000000000 | bytes 6291456 | tf_op jit(solution)/shard_map/norm/pallas_call | solution.py:339
  46.3 1.1 collective-permute-done.10
  47.3 1.5 collective-permute-start.12
  49.0 1.3 collective-permute-start.21
  50.3 1.3 collective-permute-start.16
  51.6 1.0 constant_dynamic-update-slice_fusion.2
  52.7 3.5 %collective-permute-done.12 = bf16[256,768]{1,0:T(8,128)(2,1)S(1)} collective-permute-done((bf16[256,768]{1,0:T(8,128)(2,1)S(1)}, bf16[256,768]{1,0:T(8,128)(2,1)S(1)}, u32[]{:S(2)}, u32[]{:S(2)}) %collective-permute-start.12) | collective-permute-done | bytes 393248 | tf_op jit(solution)/shard_map/ppermute | solution.py:210
  56.2 1.3 convolution_convert_fusion
  58.5 1.6 collective-permute-start.17
  60.1 4.9 %collective-permute-done.17 = bf16[2,2,128,256]{3,2,1,0:T(8,128)(2,1)S(1)} collective-permute-done((bf16[2,2,128,256]{3,2,1,0:T(8,128)(2,1)S(1)}, bf16[2,2,128,256]{3,2,1,0:T(8,128)(2,1)S(1)}, u32[]{:S(2)}, u32[]{:S(2)}) %collective-permute-start.17) | collective-permute-done | bytes 262176 | tf_op jit(solution)/shard_map/ppermute | solution.py:297
  66.1 3.4 %collective-permute-start.19 = (bf16[256,1024]{1,0:T(8,128)(2,1)S(1)}, bf16[256,1024]{1,0:T(8,128)(2,1)S(1)}, u32[]{:S(2)}, u32[]{:S(2)}) collective-permute-start(bf16[256,1024]{1,0:T(8,128)(2,1)S(1)} %get-tuple-element.42.refs_0_), channel_id=1, source_target_pairs={{0,2},{2,0},{4,6},{6,4},{13,15},{15,13},{9,11},{11,9},{20,22},{22,... | collective-permute-start | bytes 1572872 | tf_op jit(solution)/shard_map/ppermute | solution.py:265
  69.5 2.1 %collective-permute-done.22 = bf16[2,2,128,256]{3,2,1,0:T(8,128)(2,1)S(1)} collective-permute-done((bf16[2,2,128,256]{3,2,1,0:T(8,128)(2,1)S(1)}, bf16[2,2,128,256]{3,2,1,0:T(8,128)(2,1)S(1)}, u32[]{:S(2)}, u32[]{:S(2)}) %collective-permute-start.22) | collective-permute-done | bytes 262176 | tf_op jit(solution)/shard_map/ppermute | solution.py:297
  72.3 3.4 %collective-permute-start.24 = (bf16[256,1024]{1,0:T(8,128)(2,1)S(1)}, bf16[256,1024]{1,0:T(8,128)(2,1)S(1)}, u32[]{:S(2)}, u32[]{:S(2)}) collective-permute-start(bf16[256,1024]{1,0:T(8,128)(2,1)S(1)} %get-tuple-element.44.refs_2_), channel_id=1, source_target_pairs={{0,2},{2,0},{4,6},{6,4},{13,15},{15,13},{9,11},{11,9},{20,22},{22,... | collective-permute-start | bytes 1572872 | tf_op jit(solution)/shard_map/ppermute | solution.py:265
  75.8 1.4 collective-permute-done.19.refs_4_
  77.9 5.5 %collective-permute-done.24.refs_6_ = bf16[256,1024]{1,0:T(8,128)(2,1)S(1)} collective-permute-done((bf16[256,1024]{1,0:T(8,128)(2,1)S(1)}, bf16[256,1024]{1,0:T(8,128)(2,1)S(1)}, u32[]{:S(2)}, u32[]{:S(2)}) %collective-permute-start.24) | collective-permute-done | bytes 524320 | tf_op jit(solution)/shard_map/ppermute | solution.py:265
  85.1 3.1 %collective-permute-start.30 = (bf16[2,2,128,256]{3,2,1,0:T(8,128)(2,1)S(1)}, bf16[2,2,128,256]{3,2,1,0:T(8,128)(2,1)S(1)}, u32[]{:S(2)}, u32[]{:S(2)}) collective-permute-start(bf16[2,2,128,256]{3,2,1,0:T(8,128)(2,1)S(1)} %get-tuple-element.76), channel_id=1, source_target_pairs={{0,8},{4,12},{8,0},{12,4},{1,9},{5,13},{9,1},{13,5},{2,10},{6,14},... | collective-permute-start | bytes 786440 | tf_op jit(solution)/shard_map/ppermute | solution.py:297
  89.3 1.5 collective-permute-start.27
  90.8 3.3 %fusion.2 = bf16[1024,512]{1,0:T(8,128)(2,1)} fusion(bf16[1024,2048]{1,0:T(8,128)(2,1)S(1)} %bitcast.20, bf16[2048,768]{1,0:T(8,128)(2,1)S(1)} %constant_dynamic-update-slice_fusion.w.wm), kind=kOutput, calls=%fused_computation.3 | convolution fusion | flops 2148007936 | bytes 7340032 | tf_op jit(solution)/shard_map/dot_general | solution.py:21
  94.2 2.4 %collective-permute-start.28 = (bf16[2,128,256]{2,1,0:T(8,128)(2,1)S(1)}, bf16[2,128,256]{2,1,0:T(8,128)(2,1)S(1)}, u32[]{:S(2)}, u32[]{:S(2)}) collective-permute-start(bf16[2,128,256]{2,1,0:T(8,128)(2,1)S(1)} %get-tuple-element.88), channel_id=1, source_target_pairs={{0,2},{2,4},{4,6},{6,8},{8,10},{10,12},{12,14},{1,3},{3,5},{5,7},{... | collective-permute-start | bytes 393224 | tf_op jit(solution)/shard_map/ppermute | solution.py:361
  96.6 4.2 %collective-permute-done.30 = bf16[2,2,128,256]{3,2,1,0:T(8,128)(2,1)S(1)} collective-permute-done((bf16[2,2,128,256]{3,2,1,0:T(8,128)(2,1)S(1)}, bf16[2,2,128,256]{3,2,1,0:T(8,128)(2,1)S(1)}, u32[]{:S(2)}, u32[]{:S(2)}) %collective-permute-start.30) | collective-permute-done | bytes 262176 | tf_op jit(solution)/shard_map/ppermute | solution.py:297
  100.8 1.5 collective-permute-start.29
  102.3 0.9 add_select_fusion.6
  104.0 0.8 copy-done.24
  104.9 5.1 %grad_att.1 = (bf16[512,512]{1,0:T(8,128)(2,1)}, bf16[512,2048]{1,0:T(8,128)(2,1)}) custom-call(bf16[128,2048]{1,0:T(8,128)(2,1)} %c00.1, bf16[128,2048]{1,0:T(8,128)(2,1)} %copy-done.18, bf16[128,2048]{1,0:T(8,128)(2,1)} %copy-done.21, bf16[128,2048]{1,0:T(8,128)(2,1)} %copy-done.23, bf16[256,1024]{1,0:T(8,128)(2,1)} %copy-done.12, ...), custom_call_target="tpu_custom_call" | custom-call | flops 1000000000 | bytes 9437184 | tf_op jit(solution)/shard_map/grad_att/pallas_call | solution.py:374
  110.8 12.5 %attention.1 = (bf16[2,2,2,128,512]{4,3,2,1,0:T(8,128)(2,1)}, bf16[2,2,2,128,512]{4,3,2,1,0:T(8,128)(2,1)}, f32[2,2,2,128,256]{4,3,2,1,0:T(8,128)}, bf16[2,128,2...) custom-call(s32[2]{0:T(128)} %pad_add_fusion.chosen, ...), custom_call_target="tpu_custom_call" | custom-call | flops 8000000000 | bytes 10485760 | tf_op jit(solution)/shard_map/attention/pallas_call | solution.py:395
  123.3 1.1 broadcast_select_fusion
  124.4 2.7 %collective-permute-start.35 = (bf16[2,2,128,256]{3,2,1,0:T(8,128)(2,1)S(1)}, bf16[2,2,128,256]{3,2,1,0:T(8,128)(2,1)S(1)}, u32[]{:S(2)}, u32[]{:S(2)}) collective-permute-start(bf16[2,2,128,256]{3,2,1,0:T(8,128)(2,1)S(1)} %broadcast_select_fusion), channel_id=1, source_target_pairs={{0,2},{2,0},{1,3},{3,1},{4,6},{6,4},{5,7},{7,5},{8,10},{10,8},{9,1... | collective-permute-start | bytes 786440 | tf_op jit(solution)/shard_map/ppermute | solution.py:297
  127.1 5.5 %output.1 = (f32[256,2048]{1,0:T(8,128)}, bf16[256,2048]{1,0:T(8,128)(2,1)}) custom-call(bf16[2,2,256,512]{3,2,1,0:T(8,128)(2,1)} %bitcast.26, bf16[512,2048]{1,0:T(8,128)(2,1)} %get-tuple-element.48.w), custom_call_target="tpu_custom_call" | custom-call | flops 2000000000 | bytes 7340032 | tf_op jit(solution)/shard_map/output/pallas_call | solution.py:424
  132.7 4.4 %collective-permute-start.31 = (bf16[256,2048]{1,0:T(8,128)(2,1)}, bf16[256,2048]{1,0:T(8,128)(2,1)S(1)}, u32[]{:S(2)}, u32[]{:S(2)}) collective-permute-start(bf16[256,2048]{1,0:T(8,128)(2,1)} %get-tuple-element.50), channel_id=1, source_target_pairs={{0,1},{1,0},{2,3},{3,2},{4,5},{5,4},{6,7},{7,6},{8,9},{9,8},{10,11... | collective-permute-start | bytes 3145736 | tf_op jit(solution)/shard_map/ppermute | solution.py:197
  137.3 1.3 collective-permute-start.33
  138.6 4.6 %collective-permute-start.34 = (bf16[2,128,256]{2,1,0:T(8,128)(2,1)S(1)}, bf16[2,128,256]{2,1,0:T(8,128)(2,1)S(1)}, u32[]{:S(2)}, u32[]{:S(2)}) collective-permute-start(bf16[2,128,256]{2,1,0:T(8,128)(2,1)S(1)} %copy-done.27), channel_id=1, source_target_pairs={{0,2},{2,4},{4,6},{6,8},{8,10},{10,12},{12,14},{1,3},{3,5},{5,7},{... | collective-permute-start | bytes 393224 | tf_op jit(solution)/shard_map/ppermute | solution.py:414
  143.2 3.3 %collective-permute-done.36 = bf16[2,2,128,256]{3,2,1,0:T(8,128)(2,1)S(1)} collective-permute-done((bf16[2,2,128,256]{3,2,1,0:T(8,128)(2,1)S(1)}, bf16[2,2,128,256]{3,2,1,0:T(8,128)(2,1)S(1)}, u32[]{:S(2)}, u32[]{:S(2)}) %collective-permute-start.36) | collective-permute-done | bytes 262176 | tf_op jit(solution)/shard_map/ppermute | solution.py:297
  146.7 0.9 collective-permute-start.37
  148.7 9.9 %query_part.1 = (f32[2,256,2048]{2,1,0:T(8,128)}, bf16[2048,256]{1,0:T(8,128)(2,1)}, bf16[2048,256]{1,0:T(8,128)(2,1)}) custom-call(bf16[2,2,256,512]{3,2,1,0:T(8,128)(2,1)} %bitcast.24, bf16[2048,768]{1,0:T(8,128)(2,1)} %copy-done.5, bf16[2048,768]{1,0:T(8,128)(2,1)} %copy-done.5), custom_call_target="tpu_custom_call" | custom-call | flops 3000000000 | bytes 13631488 | tf_op jit(solution)/shard_map/query_part/pallas_call | solution.py:448
  158.6 1.2 collective-permute-done.37
  159.8 0.9 add_select_fusion
  160.7 0.9 fusion.12
  162.3 4.0 %key_part.2 = (f32[256,1024]{1,0:T(8,128)}, bf16[256,1024]{1,0:T(8,128)(2,1)}) custom-call(s32[2]{0:T(128)} %pad_add_fusion.chosen, f32[2,2,2,128,256]{4,3,2,1,0:T(8,128)} %get-tuple-element.51.dkv, bf16[2,128,256]{2,1,0:T(8,128)(2,1)} %copy-done.13, bf16[2,128,256]{2,1,0:T(8,128)(2,1)} %copy-done.14, bf16[2,2,128,256]{3,2,1,0:T(8,128)(2,1)} %get-tuple-element.65.far_p, ...), custom_call_target="tpu_custom_call" | custom-call | flops 500000000 | bytes 8388608 | tf_op jit(solution)/shard_map/key_part/pallas_call | solution.py:476
  166.3 2.1 %collective-permute-done.38 = bf16[256,1024]{1,0:T(8,128)(2,1)S(1)} collective-permute-done((bf16[256,1024]{1,0:T(8,128)(2,1)}, bf16[256,1024]{1,0:T(8,128)(2,1)S(1)}, u32[]{:S(2)}, u32[]{:S(2)}) %collective-permute-start.38) | collective-permute-done | bytes 524320 | tf_op jit(solution)/shard_map/ppermute | solution.py:197
  168.4 1.4 convert_add_fusion.2
  169.8 4.0 %key_part.3 = (f32[256,1024]{1,0:T(8,128)}, bf16[256,1024]{1,0:T(8,128)(2,1)}) custom-call(s32[2]{0:T(128)} %pad_add_fusion.chosen, f32[2,2,2,128,256]{4,3,2,1,0:T(8,128)} %get-tuple-element.51.dkv, bf16[2,128,256]{2,1,0:T(8,128)(2,1)} %copy-done.13, bf16[2,128,256]{2,1,0:T(8,128)(2,1)} %copy-done.14, bf16[2,2,128,256]{3,2,1,0:T(8,128)(2,1)} %get-tuple-element.65.far_p, ...), custom_call_target="tpu_custom_call" | custom-call | flops 500000000 | bytes 8388608 | tf_op jit(solution)/shard_map/key_part/pallas_call | solution.py:476
  174.5 1.4 collective-permute-done.40
  176.0 1.4 convert_add_fusion.1
  177.8 5.6 %collective-permute-done.39 = bf16[128,1024]{1,0:T(8,128)(2,1)S(1)} collective-permute-done((bf16[128,1024]{1,0:T(8,128)(2,1)S(1)}, bf16[128,1024]{1,0:T(8,128)(2,1)S(1)}, u32[]{:S(2)}, u32[]{:S(2)}) %collective-permute-start.39) | collective-permute-done | bytes 262176 | tf_op jit(solution)/shard_map/ppermute | solution.py:197
  183.5 5.0 %collective-permute-done.41 = bf16[128,1024]{1,0:T(8,128)(2,1)S(1)} collective-permute-done((bf16[128,1024]{1,0:T(8,128)(2,1)S(1)}, bf16[128,1024]{1,0:T(8,128)(2,1)S(1)}, u32[]{:S(2)}, u32[]{:S(2)}) %collective-permute-start.41) | collective-permute-done | bytes 262176 | tf_op jit(solution)/shard_map/ppermute | solution.py:197
  188.9 1.1 fusion.10
  (144 shorter events, 18.3 us)
Async XLA Ops:
  0.6 10.9 %copy-start = (bf16[128,2048]{1,0:T(8,128)(2,1)S(1)}, bf16[128,2048]{1,0:T(8,128)(2,1)}, u32[]{:S(2)}) copy-start(bf16[128,2048]{1,0:T(8,128)(2,1)} %h00.1) | copy-start | bytes 1572868
  0.6 16.9 %copy-start.26 = (bf16[128,2048]{1,0:T(8,128)(2,1)S(1)}, bf16[128,2048]{1,0:T(8,128)(2,1)}, u32[]{:S(2)}) copy-start(bf16[128,2048]{1,0:T(8,128)(2,1)} %param.9) | copy-start | bytes 1572868
  0.7 10.9 %copy-start.31 = (s32[2]{0:T(128)S(1)}, s32[2]{0:T(128)}, u32[]{:S(2)}) copy-start(s32[2]{0:T(128)} %param.10) | copy-start | bytes 28
  0.7 15.1 %collective-permute-start = (bf16[128,2048]{1,0:T(8,128)(2,1)}, bf16[128,2048]{1,0:T(8,128)(2,1)S(1)}, u32[]{:S(2)}, u32[]{:S(2)}) collective-permute-start(bf16[128,2048]{1,0:T(8,128)(2,1)} %h00.1), channel_id=1, source_target_pairs={{0,16},{16,0},{1,17},{17,1},{2,18},{18,2},{3,19},{19,3},{4,20},{20... | collective-permute-start | bytes 1572872 | tf_op jit(solution)/shard_map/ppermute | solution.py:197
  3.7 13.9 %collective-permute-start.15 = (bf16[128,2048]{1,0:T(8,128)(2,1)}, bf16[128,2048]{1,0:T(8,128)(2,1)}, u32[]{:S(2)}, u32[]{:S(2)}) collective-permute-start(bf16[128,2048]{1,0:T(8,128)(2,1)} %param.9), channel_id=1, source_target_pairs={{0,1},{1,0},{2,3},{3,2},{4,5},{5,4},{6,7},{7,6},{8,9},{9,8},{10,11... | collective-permute-start | bytes 1572872 | tf_op jit(solution)/shard_map/ppermute | solution.py:197
  5.5 1.6 collective-permute-start.4
  7.2 13.4 %copy-start.15 = (bf16[128,2048]{1,0:T(8,128)(2,1)S(1)}, bf16[128,2048]{1,0:T(8,128)(2,1)}, u32[]{:S(2)}) copy-start(bf16[128,2048]{1,0:T(8,128)(2,1)} %c00.1) | copy-start | bytes 1572868
  8.2 14.3 %collective-permute-start.5 = (bf16[256,768]{1,0:T(8,128)(2,1)}, bf16[256,768]{1,0:T(8,128)(2,1)S(1)}, u32[]{:S(2)}, u32[]{:S(2)}) collective-permute-start(bf16[256,768]{1,0:T(8,128)(2,1)} %get-tuple-element.81), channel_id=1, source_target_pairs={{0,2},{2,0},{1,3},{3,1},{4,6},{6,4},{5,7},{7,5},{8,10},{10,8},{9,1... | collective-permute-start | bytes 1179656 | tf_op jit(solution)/shard_map/ppermute | solution.py:210
  9.9 13.5 %collective-permute-start.6 = (bf16[256,768]{1,0:T(8,128)(2,1)}, bf16[256,768]{1,0:T(8,128)(2,1)S(1)}, u32[]{:S(2)}, u32[]{:S(2)}) collective-permute-start(bf16[256,768]{1,0:T(8,128)(2,1)} %get-tuple-element.81), channel_id=1, source_target_pairs={{0,4},{4,8},{8,12},{12,0},{1,5},{5,9},{9,13},{13,1},{2,6},{6,10},{... | collective-permute-start | bytes 1179656 | tf_op jit(solution)/shard_map/ppermute | solution.py:210
  11.5 28.2 %collective-permute-start.2 = (bf16[128,2048]{1,0:T(8,128)(2,1)S(1)}, bf16[128,2048]{1,0:T(8,128)(2,1)S(1)}, u32[]{:S(2)}, u32[]{:S(2)}) collective-permute-start(bf16[128,2048]{1,0:T(8,128)(2,1)S(1)} %copy-done), channel_id=1, source_target_pairs={{0,1},{1,0},{2,3},{3,2},{4,5},{5,4},{6,7},{7,6},{8,9},{9,8},{10,11... | collective-permute-start | bytes 1572872 | tf_op jit(solution)/shard_map/ppermute | solution.py:197
  15.8 23.9 %copy-start.16 = (bf16[128,2048]{1,0:T(8,128)(2,1)}, bf16[128,2048]{1,0:T(8,128)(2,1)S(1)}, u32[]{:S(2)}) copy-start(bf16[128,2048]{1,0:T(8,128)(2,1)S(1)} %collective-permute-done.h01) | copy-start | bytes 1572868
  15.8 3.6 %collective-permute-start.1 = (f32[8,128]{1,0:T(8,128)S(1)}, f32[8,128]{1,0:T(8,128)S(1)}, u32[]{:S(2)}, u32[]{:S(2)}) collective-permute-start(f32[8,128]{1,0:T(8,128)S(1)} %broadcast_in_dim.128), channel_id=1, source_target_pairs={{0,16},{16,0},{1,17},{17,1},{2,18},{18,2},{3,19},{19,3},{4,20},{20... | collective-permute-start | bytes 12296 | tf_op jit(solution)/shard_map/ppermute | solution.py:197
  17.5 22.1 %collective-permute-start.3 = (bf16[128,2048]{1,0:T(8,128)(2,1)S(1)}, bf16[128,2048]{1,0:T(8,128)(2,1)S(1)}, u32[]{:S(2)}, u32[]{:S(2)}) collective-permute-start(bf16[128,2048]{1,0:T(8,128)(2,1)S(1)} %collective-permute-done.h01), channel_id=1, source_target_pairs={{0,1},{1,0},{2,3},{3,2},{4,5},{5,4},{6,7},{7,6},{8,9},{9,8},{10,11... | collective-permute-start | bytes 1572872 | tf_op jit(solution)/shard_map/ppermute | solution.py:197
  20.6 25.6 %collective-permute-start.11 = (bf16[128,2048]{1,0:T(8,128)(2,1)S(1)}, bf16[128,2048]{1,0:T(8,128)(2,1)S(1)}, u32[]{:S(2)}, u32[]{:S(2)}) collective-permute-start(bf16[128,2048]{1,0:T(8,128)(2,1)S(1)} %copy-done.15), channel_id=1, source_target_pairs={{0,16},{16,0},{1,17},{17,1},{2,18},{18,2},{3,19},{19,3},{4,20},{20... | collective-permute-start | bytes 1572872 | tf_op jit(solution)/shard_map/ppermute | solution.py:197
  23.4 12.4 %collective-permute-start.8 = (bf16[256,768]{1,0:T(8,128)(2,1)S(1)}, bf16[256,768]{1,0:T(8,128)(2,1)S(1)}, u32[]{:S(2)}, u32[]{:S(2)}) collective-permute-start(bf16[256,768]{1,0:T(8,128)(2,1)S(1)} %collective-permute-done.6), channel_id=1, source_target_pairs={{0,4},{4,8},{8,12},{12,0},{1,5},{5,9},{9,13},{13,1},{2,6},{6,10},{... | collective-permute-start | bytes 1179656 | tf_op jit(solution)/shard_map/ppermute | solution.py:210
  24.2 9.8 %collective-permute-start.7 = (bf16[256,768]{1,0:T(8,128)(2,1)S(1)}, bf16[256,768]{1,0:T(8,128)(2,1)S(1)}, u32[]{:S(2)}, u32[]{:S(2)}) collective-permute-start(bf16[256,768]{1,0:T(8,128)(2,1)S(1)} %collective-permute-done.6), channel_id=1, source_target_pairs={{0,2},{2,0},{1,3},{3,1},{4,6},{6,4},{5,7},{7,5},{8,10},{10,8},{9,1... | collective-permute-start | bytes 1179656 | tf_op jit(solution)/shard_map/ppermute | solution.py:210
  35.8 11.5 %collective-permute-start.10 = (bf16[256,768]{1,0:T(8,128)(2,1)S(1)}, bf16[256,768]{1,0:T(8,128)(2,1)S(1)}, u32[]{:S(2)}, u32[]{:S(2)}) collective-permute-start(bf16[256,768]{1,0:T(8,128)(2,1)S(1)} %collective-permute-done.8), channel_id=1, source_target_pairs={{0,4},{4,8},{8,12},{12,0},{1,5},{5,9},{9,13},{13,1},{2,6},{6,10},{... | collective-permute-start | bytes 1179656 | tf_op jit(solution)/shard_map/ppermute | solution.py:210
  35.8 10.5 %collective-permute-start.9 = (bf16[256,768]{1,0:T(8,128)(2,1)S(1)}, bf16[256,768]{1,0:T(8,128)(2,1)}, u32[]{:S(2)}, u32[]{:S(2)}) collective-permute-start(bf16[256,768]{1,0:T(8,128)(2,1)S(1)} %collective-permute-done.8), channel_id=1, source_target_pairs={{0,2},{2,0},{1,3},{3,1},{4,6},{6,4},{5,7},{7,5},{8,10},{10,8},{9,1... | collective-permute-start | bytes 1179656 | tf_op jit(solution)/shard_map/ppermute | solution.py:210
  39.7 11.9 %copy-start.4 = (bf16[2048,768]{1,0:T(8,128)(2,1)S(1)}, bf16[2048,768]{1,0:T(8,128)(2,1)}, u32[]{:S(2)}) copy-start(bf16[2048,768]{1,0:T(8,128)(2,1)} %constant_dynamic-update-slice_fusion.3) | copy-start | bytes 9437188
  46.3 10.0 %copy-start.2 = (bf16[2,512,2048]{2,1,0:T(8,128)(2,1)S(1)}, bf16[2,512,2048]{2,1,0:T(8,128)(2,1)}, u32[]{:S(2)}) copy-start(bf16[2,512,2048]{2,1,0:T(8,128)(2,1)} %norm.1) | copy-start | bytes 12582916
  46.3 38.5 %copy-start.18 = (bf16[128,2048]{1,0:T(8,128)(2,1)}, bf16[128,2048]{1,0:T(8,128)(2,1)S(1)}, u32[]{:S(2)}) copy-start(bf16[128,2048]{1,0:T(8,128)(2,1)S(1)} %collective-permute-done.11.c01) | copy-start | bytes 1572868
  47.3 8.8 %collective-permute-start.12 = (bf16[256,768]{1,0:T(8,128)(2,1)S(1)}, bf16[256,768]{1,0:T(8,128)(2,1)S(1)}, u32[]{:S(2)}, u32[]{:S(2)}) collective-permute-start(bf16[256,768]{1,0:T(8,128)(2,1)S(1)} %collective-permute-done.10), channel_id=1, source_target_pairs={{0,2},{2,0},{1,3},{3,1},{4,6},{6,4},{5,7},{7,5},{8,10},{10,8},{9,1... | collective-permute-start | bytes 1179656 | tf_op jit(solution)/shard_map/ppermute | solution.py:210
  49.0 16.3 %collective-permute-start.21 = (bf16[256,1024]{1,0:T(8,128)(2,1)S(1)}, bf16[256,1024]{1,0:T(8,128)(2,1)S(1)}, u32[]{:S(2)}, u32[]{:S(2)}) collective-permute-start(bf16[256,1024]{1,0:T(8,128)(2,1)S(1)} %get-tuple-element.84), channel_id=1, source_target_pairs={{0,4},{13,9},{20,16},{25,29},{2,6},{15,11},{22,18},{27,31}} | collective-permute-start | bytes 1572872 | tf_op jit(solution)/shard_map/ppermute | solution.py:257
  50.3 15.0 %collective-permute-start.16 = (bf16[256,1024]{1,0:T(8,128)(2,1)S(1)}, bf16[256,1024]{1,0:T(8,128)(2,1)S(1)}, u32[]{:S(2)}, u32[]{:S(2)}) collective-permute-start(bf16[256,1024]{1,0:T(8,128)(2,1)S(1)} %get-tuple-element.85), channel_id=1, source_target_pairs={{0,4},{13,9},{20,16},{25,29},{2,6},{15,11},{22,18},{27,31}} | collective-permute-start | bytes 1572872 | tf_op jit(solution)/shard_map/ppermute | solution.py:257
  56.2 34.6 %copy-start.5 = (bf16[2048,768]{1,0:T(8,128)(2,1)}, bf16[2048,768]{1,0:T(8,128)(2,1)S(1)}, u32[]{:S(2)}) copy-start(bf16[2048,768]{1,0:T(8,128)(2,1)S(1)} %constant_dynamic-update-slice_fusion.w.wm) | copy-start | bytes 9437188
  58.5 6.4 %collective-permute-start.17 = (bf16[2,2,128,256]{3,2,1,0:T(8,128)(2,1)S(1)}, bf16[2,2,128,256]{3,2,1,0:T(8,128)(2,1)S(1)}, u32[]{:S(2)}, u32[]{:S(2)}) collective-permute-start(bf16[2,2,128,256]{3,2,1,0:T(8,128)(2,1)S(1)} %fusion.15), channel_id=1, source_target_pairs={{0,2},{2,0},{1,3},{3,1},{4,6},{6,4},{5,7},{7,5},{8,10},{10,8},{9,1... | collective-permute-start | bytes 786440 | tf_op jit(solution)/shard_map/ppermute | solution.py:297
  65.2 6.4 %collective-permute-start.22 = (bf16[2,2,128,256]{3,2,1,0:T(8,128)(2,1)S(1)}, bf16[2,2,128,256]{3,2,1,0:T(8,128)(2,1)S(1)}, u32[]{:S(2)}, u32[]{:S(2)}) collective-permute-start(bf16[2,2,128,256]{3,2,1,0:T(8,128)(2,1)S(1)} %broadcast_select_fusion.4), channel_id=1, source_target_pairs={{0,4},{4,0},{8,12},{12,8},{1,5},{5,1},{9,13},{13,9},{2,6},{6,2},{1... | collective-permute-start | bytes 786440 | tf_op jit(solution)/shard_map/ppermute | solution.py:297
  65.4 28.7 %copy-start.11 = (bf16[256,1024]{1,0:T(8,128)(2,1)}, bf16[256,1024]{1,0:T(8,128)(2,1)S(1)}, u32[]{:S(2)}) copy-start(bf16[256,1024]{1,0:T(8,128)(2,1)S(1)} %get-tuple-element.44.refs_2_) | copy-start | bytes 1572868
  65.4 28.7 %copy-start.12 = (bf16[256,1024]{1,0:T(8,128)(2,1)}, bf16[256,1024]{1,0:T(8,128)(2,1)S(1)}, u32[]{:S(2)}) copy-start(bf16[256,1024]{1,0:T(8,128)(2,1)S(1)} %get-tuple-element.42.refs_0_) | copy-start | bytes 1572868
  65.4 10.4 %collective-permute-start.18 = (bf16[256,1024]{1,0:T(8,128)(2,1)S(1)}, bf16[256,1024]{1,0:T(8,128)(2,1)S(1)}, u32[]{:S(2)}, u32[]{:S(2)}) collective-permute-start(bf16[256,1024]{1,0:T(8,128)(2,1)S(1)} %get-tuple-element.42.refs_0_), channel_id=1, source_target_pairs={{4,8},{9,5},{20,24},{25,21},{6,10},{11,7},{22,26},{27,23}} | collective-permute-start | bytes 1572872 | tf_op jit(solution)/shard_map/ppermute | solution.py:257
  66.1 11.1 %collective-permute-start.19 = (bf16[256,1024]{1,0:T(8,128)(2,1)S(1)}, bf16[256,1024]{1,0:T(8,128)(2,1)S(1)}, u32[]{:S(2)}, u32[]{:S(2)}) collective-permute-start(bf16[256,1024]{1,0:T(8,128)(2,1)S(1)} %get-tuple-element.42.refs_0_), channel_id=1, source_target_pairs={{0,2},{2,0},{4,6},{6,4},{13,15},{15,13},{9,11},{11,9},{20,22},{22,... | collective-permute-start | bytes 1572872 | tf_op jit(solution)/shard_map/ppermute | solution.py:265
  71.6 6.3 %collective-permute-start.23 = (bf16[256,1024]{1,0:T(8,128)(2,1)S(1)}, bf16[256,1024]{1,0:T(8,128)(2,1)S(1)}, u32[]{:S(2)}, u32[]{:S(2)}) collective-permute-start(bf16[256,1024]{1,0:T(8,128)(2,1)S(1)} %get-tuple-element.44.refs_2_), channel_id=1, source_target_pairs={{4,8},{9,5},{20,24},{25,21},{6,10},{11,7},{22,26},{27,23}} | collective-permute-start | bytes 1572872 | tf_op jit(solution)/shard_map/ppermute | solution.py:257
  72.3 11.1 %collective-permute-start.24 = (bf16[256,1024]{1,0:T(8,128)(2,1)S(1)}, bf16[256,1024]{1,0:T(8,128)(2,1)S(1)}, u32[]{:S(2)}, u32[]{:S(2)}) collective-permute-start(bf16[256,1024]{1,0:T(8,128)(2,1)S(1)} %get-tuple-element.44.refs_2_), channel_id=1, source_target_pairs={{0,2},{2,0},{4,6},{6,4},{13,15},{15,13},{9,11},{11,9},{20,22},{22,... | collective-permute-start | bytes 1572872 | tf_op jit(solution)/shard_map/ppermute | solution.py:265
  75.7 18.4 %collective-permute-start.13 = (bf16[128,2048]{1,0:T(8,128)(2,1)S(1)}, bf16[128,2048]{1,0:T(8,128)(2,1)S(1)}, u32[]{:S(2)}, u32[]{:S(2)}) collective-permute-start(bf16[128,2048]{1,0:T(8,128)(2,1)S(1)} %copy-done.15), channel_id=1, source_target_pairs={{0,1},{1,0},{2,3},{3,2},{4,5},{5,4},{6,7},{7,6},{8,9},{9,8},{10,11... | collective-permute-start | bytes 1572872 | tf_op jit(solution)/shard_map/ppermute | solution.py:197
  77.2 16.9 %copy-start.19 = (bf16[256,1024]{1,0:T(8,128)(2,1)}, bf16[256,1024]{1,0:T(8,128)(2,1)S(1)}, u32[]{:S(2)}) copy-start(bf16[256,1024]{1,0:T(8,128)(2,1)S(1)} %collective-permute-done.19.refs_4_) | copy-start | bytes 1572868
  77.2 11.0 %collective-permute-start.20 = (bf16[256,1024]{1,0:T(8,128)(2,1)S(1)}, bf16[256,1024]{1,0:T(8,128)(2,1)S(1)}, u32[]{:S(2)}, u32[]{:S(2)}) collective-permute-start(bf16[256,1024]{1,0:T(8,128)(2,1)S(1)} %collective-permute-done.18), channel_id=1, source_target_pairs={{8,12},{5,1},{24,28},{21,17},{10,14},{7,3},{26,30},{23,19}} | collective-permute-start | bytes 1572872 | tf_op jit(solution)/shard_map/ppermute | solution.py:257
  83.4 5.7 %copy-start.20 = (bf16[256,1024]{1,0:T(8,128)(2,1)}, bf16[256,1024]{1,0:T(8,128)(2,1)S(1)}, u32[]{:S(2)}) copy-start(bf16[256,1024]{1,0:T(8,128)(2,1)S(1)} %collective-permute-done.24.refs_6_) | copy-start | bytes 1572868
  83.4 5.7 %collective-permute-start.25 = (bf16[256,1024]{1,0:T(8,128)(2,1)S(1)}, bf16[256,1024]{1,0:T(8,128)(2,1)S(1)}, u32[]{:S(2)}, u32[]{:S(2)}) collective-permute-start(bf16[256,1024]{1,0:T(8,128)(2,1)S(1)} %collective-permute-done.23), channel_id=1, source_target_pairs={{8,12},{5,1},{24,28},{21,17},{10,14},{7,3},{26,30},{23,19}} | collective-permute-start | bytes 1572872 | tf_op jit(solution)/shard_map/ppermute | solution.py:257
  84.7 18.5 %collective-permute-start.14 = (bf16[128,2048]{1,0:T(8,128)(2,1)S(1)}, bf16[128,2048]{1,0:T(8,128)(2,1)S(1)}, u32[]{:S(2)}, u32[]{:S(2)}) collective-permute-start(bf16[128,2048]{1,0:T(8,128)(2,1)S(1)} %collective-permute-done.11.c01), channel_id=1, source_target_pairs={{0,1},{1,0},{2,3},{3,2},{4,5},{5,4},{6,7},{7,6},{8,9},{9,8},{10,11... | collective-permute-start | bytes 1572872 | tf_op jit(solution)/shard_map/ppermute | solution.py:197
  85.1 15.7 %collective-permute-start.30 = (bf16[2,2,128,256]{3,2,1,0:T(8,128)(2,1)S(1)}, bf16[2,2,128,256]{3,2,1,0:T(8,128)(2,1)S(1)}, u32[]{:S(2)}, u32[]{:S(2)}) collective-permute-start(bf16[2,2,128,256]{3,2,1,0:T(8,128)(2,1)S(1)} %get-tuple-element.76), channel_id=1, source_target_pairs={{0,8},{4,12},{8,0},{12,4},{1,9},{5,13},{9,1},{13,5},{2,10},{6,14},... | collective-permute-start | bytes 786440 | tf_op jit(solution)/shard_map/ppermute | solution.py:297
  88.4 5.7 %copy-start.8 = (bf16[256,1024]{1,0:T(8,128)(2,1)}, bf16[256,1024]{1,0:T(8,128)(2,1)S(1)}, u32[]{:S(2)}) copy-start(bf16[256,1024]{1,0:T(8,128)(2,1)S(1)} %add.303.refs_1_) | copy-start | bytes 1572868
  88.4 14.8 %collective-permute-start.26 = (bf16[256,1024]{1,0:T(8,128)(2,1)S(1)}, bf16[256,1024]{1,0:T(8,128)(2,1)S(1)}, u32[]{:S(2)}, u32[]{:S(2)}) collective-permute-start(bf16[256,1024]{1,0:T(8,128)(2,1)S(1)} %add.303.refs_1_), channel_id=1, source_target_pairs={{8,10},{10,8},{12,14},{14,12},{5,7},{7,5},{1,3},{3,1},{24,26},{26,... | collective-permute-start | bytes 1572872 | tf_op jit(solution)/shard_map/ppermute | solution.py:265
  89.3 4.8 %copy-start.9 = (bf16[256,1024]{1,0:T(8,128)(2,1)}, bf16[256,1024]{1,0:T(8,128)(2,1)S(1)}, u32[]{:S(2)}) copy-start(bf16[256,1024]{1,0:T(8,128)(2,1)S(1)} %add.309.refs_3_) | copy-start | bytes 1572868
  89.3 15.6 %collective-permute-start.27 = (bf16[256,1024]{1,0:T(8,128)(2,1)S(1)}, bf16[256,1024]{1,0:T(8,128)(2,1)}, u32[]{:S(2)}, u32[]{:S(2)}) collective-permute-start(bf16[256,1024]{1,0:T(8,128)(2,1)S(1)} %add.309.refs_3_), channel_id=1, source_target_pairs={{8,10},{10,8},{12,14},{14,12},{5,7},{7,5},{1,3},{3,1},{24,26},{26,... | collective-permute-start | bytes 1572872 | tf_op jit(solution)/shard_map/ppermute | solution.py:265
  94.1 9.1 %copy-start.21 = (bf16[128,2048]{1,0:T(8,128)(2,1)}, bf16[128,2048]{1,0:T(8,128)(2,1)S(1)}, u32[]{:S(2)}) copy-start(bf16[128,2048]{1,0:T(8,128)(2,1)S(1)} %collective-permute-done.13.c10) | copy-start | bytes 1572868
  94.2 15.9 %collective-permute-start.28 = (bf16[2,128,256]{2,1,0:T(8,128)(2,1)S(1)}, bf16[2,128,256]{2,1,0:T(8,128)(2,1)S(1)}, u32[]{:S(2)}, u32[]{:S(2)}) collective-permute-start(bf16[2,128,256]{2,1,0:T(8,128)(2,1)S(1)} %get-tuple-element.88), channel_id=1, source_target_pairs={{0,2},{2,4},{4,6},{6,8},{8,10},{10,12},{12,14},{1,3},{3,5},{5,7},{... | collective-permute-start | bytes 393224 | tf_op jit(solution)/shard_map/ppermute | solution.py:361
  100.8 9.2 %collective-permute-start.29 = (bf16[2,128,256]{2,1,0:T(8,128)(2,1)S(1)}, bf16[2,128,256]{2,1,0:T(8,128)(2,1)S(1)}, u32[]{:S(2)}, u32[]{:S(2)}) collective-permute-start(bf16[2,128,256]{2,1,0:T(8,128)(2,1)S(1)} %get-tuple-element.86), channel_id=1, source_target_pairs={{2,0},{4,2},{6,4},{8,6},{10,8},{12,10},{14,12},{3,1},{5,3},{7,5},{... | collective-permute-start | bytes 393224 | tf_op jit(solution)/shard_map/ppermute | solution.py:361
  124.4 12.7 %collective-permute-start.35 = (bf16[2,2,128,256]{3,2,1,0:T(8,128)(2,1)S(1)}, bf16[2,2,128,256]{3,2,1,0:T(8,128)(2,1)S(1)}, u32[]{:S(2)}, u32[]{:S(2)}) collective-permute-start(bf16[2,2,128,256]{3,2,1,0:T(8,128)(2,1)S(1)} %broadcast_select_fusion), channel_id=1, source_target_pairs={{0,2},{2,0},{1,3},{3,1},{4,6},{6,4},{5,7},{7,5},{8,10},{10,8},{9,1... | collective-permute-start | bytes 786440 | tf_op jit(solution)/shard_map/ppermute | solution.py:297
  127.1 10.0 %copy-start.6 = (bf16[2,2,128,256]{3,2,1,0:T(8,128)(2,1)S(1)}, bf16[2,2,128,256]{3,2,1,0:T(8,128)(2,1)}, u32[]{:S(2)}) copy-start(bf16[2,2,128,256]{3,2,1,0:T(8,128)(2,1)} %get-tuple-element.55) | copy-start | bytes 786436
  127.1 10.0 %copy-start.7 = (bf16[2,2,128,256]{3,2,1,0:T(8,128)(2,1)S(1)}, bf16[2,2,128,256]{3,2,1,0:T(8,128)(2,1)}, u32[]{:S(2)}) copy-start(bf16[2,2,128,256]{3,2,1,0:T(8,128)(2,1)} %get-tuple-element.54) | copy-start | bytes 786436
  127.1 10.2 %copy-start.28 = (bf16[2,128,256]{2,1,0:T(8,128)(2,1)S(1)}, bf16[2,128,256]{2,1,0:T(8,128)(2,1)}, u32[]{:S(2)}) copy-start(bf16[2,128,256]{2,1,0:T(8,128)(2,1)} %get-tuple-element.52) | copy-start | bytes 393220
  127.1 11.5 %copy-start.27 = (bf16[2,128,256]{2,1,0:T(8,128)(2,1)S(1)}, bf16[2,128,256]{2,1,0:T(8,128)(2,1)}, u32[]{:S(2)}) copy-start(bf16[2,128,256]{2,1,0:T(8,128)(2,1)} %get-tuple-element.53) | copy-start | bytes 393220
  132.7 15.0 %copy-start.10 = (f32[256,2048]{1,0:T(8,128)S(1)}, f32[256,2048]{1,0:T(8,128)}, u32[]{:S(2)}) copy-start(f32[256,2048]{1,0:T(8,128)} %get-tuple-element.49) | copy-start | bytes 6291460
  132.7 15.0 %collective-permute-start.31 = (bf16[256,2048]{1,0:T(8,128)(2,1)}, bf16[256,2048]{1,0:T(8,128)(2,1)S(1)}, u32[]{:S(2)}, u32[]{:S(2)}) collective-permute-start(bf16[256,2048]{1,0:T(8,128)(2,1)} %get-tuple-element.50), channel_id=1, source_target_pairs={{0,1},{1,0},{2,3},{3,2},{4,5},{5,4},{6,7},{7,6},{8,9},{9,8},{10,11... | collective-permute-start | bytes 3145736 | tf_op jit(solution)/shard_map/ppermute | solution.py:197
  137.2 9.2 %collective-permute-start.36 = (bf16[2,2,128,256]{3,2,1,0:T(8,128)(2,1)S(1)}, bf16[2,2,128,256]{3,2,1,0:T(8,128)(2,1)S(1)}, u32[]{:S(2)}, u32[]{:S(2)}) collective-permute-start(bf16[2,2,128,256]{3,2,1,0:T(8,128)(2,1)S(1)} %broadcast_select_fusion.1), channel_id=1, source_target_pairs={{0,4},{4,0},{8,12},{12,8},{1,5},{5,1},{9,13},{13,9},{2,6},{6,2},{1... | collective-permute-start | bytes 786440 | tf_op jit(solution)/shard_map/ppermute | solution.py:297
  137.3 24.3 %collective-permute-start.33 = (bf16[2,128,256]{2,1,0:T(8,128)(2,1)S(1)}, bf16[2,128,256]{2,1,0:T(8,128)(2,1)S(1)}, u32[]{:S(2)}, u32[]{:S(2)}) collective-permute-start(bf16[2,128,256]{2,1,0:T(8,128)(2,1)S(1)} %copy-done.28), channel_id=1, source_target_pairs={{2,0},{4,2},{6,4},{8,6},{10,8},{12,10},{14,12},{3,1},{5,3},{7,5},{... | collective-permute-start | bytes 393224 | tf_op jit(solution)/shard_map/ppermute | solution.py:414
  138.6 23.0 %collective-permute-start.34 = (bf16[2,128,256]{2,1,0:T(8,128)(2,1)S(1)}, bf16[2,128,256]{2,1,0:T(8,128)(2,1)S(1)}, u32[]{:S(2)}, u32[]{:S(2)}) collective-permute-start(bf16[2,128,256]{2,1,0:T(8,128)(2,1)S(1)} %copy-done.27), channel_id=1, source_target_pairs={{0,2},{2,4},{4,6},{6,8},{8,10},{10,12},{12,14},{1,3},{3,5},{5,7},{... | collective-permute-start | bytes 393224 | tf_op jit(solution)/shard_map/ppermute | solution.py:414
  146.7 13.0 %collective-permute-start.37 = (bf16[2,2,128,256]{3,2,1,0:T(8,128)(2,1)S(1)}, bf16[2,2,128,256]{3,2,1,0:T(8,128)(2,1)S(1)}, u32[]{:S(2)}, u32[]{:S(2)}) collective-permute-start(bf16[2,2,128,256]{3,2,1,0:T(8,128)(2,1)S(1)} %get-tuple-element.68), channel_id=1, source_target_pairs={{0,8},{4,12},{8,0},{12,4},{1,9},{5,13},{9,1},{13,5},{2,10},{6,14},... | collective-permute-start | bytes 786440 | tf_op jit(solution)/shard_map/ppermute | solution.py:297
  148.0 12.7 %collective-permute-start.32 = (bf16[128,2048]{1,0:T(8,128)(2,1)S(1)}, bf16[128,2048]{1,0:T(8,128)(2,1)S(1)}, u32[]{:S(2)}, u32[]{:S(2)}) collective-permute-start(bf16[128,2048]{1,0:T(8,128)(2,1)S(1)} %slice.97), channel_id=1, source_target_pairs={{0,16},{16,0},{1,17},{17,1},{2,18},{18,2},{3,19},{19,3},{4,20},{20... | collective-permute-start | bytes 1572872 | tf_op jit(solution)/shard_map/ppermute | solution.py:197
  166.3 2.1 %collective-permute-start.38 = (bf16[256,1024]{1,0:T(8,128)(2,1)}, bf16[256,1024]{1,0:T(8,128)(2,1)S(1)}, u32[]{:S(2)}, u32[]{:S(2)}) collective-permute-start(bf16[256,1024]{1,0:T(8,128)(2,1)} %get-tuple-element.64), channel_id=1, source_target_pairs={{0,1},{1,0},{2,3},{3,2},{4,5},{5,4},{6,7},{7,6},{8,9},{9,8},{10,11... | collective-permute-start | bytes 1572872 | tf_op jit(solution)/shard_map/ppermute | solution.py:197
  169.8 4.2 %copy-start.1 = (bf16[128,2048]{1,0:T(8,128)(2,1)S(1)}, bf16[128,2048]{1,0:T(8,128)(2,1)}, u32[]{:S(2)}) copy-start(bf16[128,2048]{1,0:T(8,128)(2,1)} %h00.1) | copy-start | bytes 1572868
  173.9 2.1 %collective-permute-start.40 = (bf16[256,1024]{1,0:T(8,128)(2,1)}, bf16[256,1024]{1,0:T(8,128)(2,1)S(1)}, u32[]{:S(2)}, u32[]{:S(2)}) collective-permute-start(bf16[256,1024]{1,0:T(8,128)(2,1)} %get-tuple-element.67), channel_id=1, source_target_pairs={{0,1},{1,0},{2,3},{3,2},{4,5},{5,4},{6,7},{7,6},{8,9},{9,8},{10,11... | collective-permute-start | bytes 1572872 | tf_op jit(solution)/shard_map/ppermute | solution.py:197
  174.2 9.2 %collective-permute-start.39 = (bf16[128,1024]{1,0:T(8,128)(2,1)S(1)}, bf16[128,1024]{1,0:T(8,128)(2,1)S(1)}, u32[]{:S(2)}, u32[]{:S(2)}) collective-permute-start(bf16[128,1024]{1,0:T(8,128)(2,1)S(1)} %slice.99), channel_id=1, source_target_pairs={{0,16},{16,0},{1,17},{17,1},{2,18},{18,2},{3,19},{19,3},{4,20},{20... | collective-permute-start | bytes 786440 | tf_op jit(solution)/shard_map/ppermute | solution.py:197
  177.4 11.1 %collective-permute-start.41 = (bf16[128,1024]{1,0:T(8,128)(2,1)S(1)}, bf16[128,1024]{1,0:T(8,128)(2,1)S(1)}, u32[]{:S(2)}, u32[]{:S(2)}) collective-permute-start(bf16[128,1024]{1,0:T(8,128)(2,1)S(1)} %slice.98), channel_id=1, source_target_pairs={{0,16},{16,0},{1,17},{17,1},{2,18},{18,2},{3,19},{19,3},{4,20},{20... | collective-permute-start | bytes 786440 | tf_op jit(solution)/shard_map/ppermute | solution.py:197
  (10 other events, 8.5 us)

commit v3 on v2

--- a/solution.py
+++ b/solution.py
@@ -83,7 +83,7 @@
     return 2 * lax.axis_size("a") * lax.axis_size("b") - 1
 
 
-def attention_kernel(chosen, q, ga, kv, near_p, near_m, far_p, far_m, att, gq, dkv, dnear_p, dnear_m, dfar_p, dfar_m):
+def attention_kernel(chosen, q, ga, kv, near_p, near_m, far_p, far_m, att, gq, dkv, dnear_p, dnear_m, dfar_p, dfar_m, pack):
     last = last_block()
     t = position()
     g_dyn = chosen[pl.program_id(0)]
@@ -142,6 +142,8 @@
         for target, (dk, dv) in zip(targets, sums):
             target[:, :HDIM] = dk.astype(target.dtype)
             target[:, HDIM:] = dv.astype(target.dtype)
+    for i, owner in enumerate((last // 2, g_dyn // 2)):
+        pack[i, 0] = jnp.where(t % 2 == owner % 2, dfar_m[i, 0], dfar_p[i, 0])
 
 
 def output_kernel(att, w, keep, send):
@@ -231,7 +233,7 @@
     return full, chunk
 
 
-def output_rows(w_out, x, a, b, c, held, arrived):
+def output_rows(w_out, x, a, b, c, held, arrived, kv):
     na, nb = lax.axis_size("a"), lax.axis_size("b")
     mine = head_group(x, c)
     half = w_out.shape[1] // 2
@@ -267,7 +269,7 @@
     start = after(current, held)
     parts = [start[:, :half], start[:, half:]]
     first = [send(v, {(0, 0): (0, 1), (0, 1): (3, 2), (1, 0): (1, 0), (1, 1): (2, 3)}) for v in parts]
-    parts = [after(v + w, z) for v, w, z in zip(parts, first, arrived)]
+    parts = [after(parts[0] + first[0], kv), after(parts[1] + first[1], arrived[0])]
     second = [send(v, {(0, 0): (1, 2), (0, 1): (2, 1), (1, 0): (1, 2), (1, 1): (2, 1)}) for v in parts]
     early = [across(v, {(0, 0): (0, 1), (0, 1): (3, 2), (1, 0): (1, 0), (1, 1): (2, 3)}) for v in parts]
     third = [
@@ -288,13 +290,15 @@
             bit *= 2
 
 
-def trade(first, second, t, owner, inward, states, held=()):
+def trade(first, second, t, owner, inward, states, held=(), packed=None):
     for number, (axis, weight, pairs) in enumerate(rounds()):
         if number == 2:
             first = after(first, *held)
         same = (t // weight) % 2 == (owner // weight) % 2
         give = same != inward
-        got = lax.ppermute(jnp.where(give, first, second), axis, pairs)
+        if number > 0 or packed is None:
+            packed = jnp.where(give, first, second)
+        got = lax.ppermute(packed, axis, pairs)
         states.append(got)
         first, second = jnp.where(give, first, first + got), jnp.where(give, second + got, second)
     return first, second
@@ -367,7 +371,7 @@
     first = after(first, c01)
     arrived = []
     first, second = trade(first, second, t, owner, False, arrived)
-    wo_parts = output_rows(w_out, x, a, b, c, far_chunk, arrived)
+    wo_parts = output_rows(w_out, x, a, b, c, far_chunk, arrived, kv)
 
     queries = dot(normed, q_weight, 1, 0).astype(BF16).reshape(2, 2, 2, BLK, REP * HDIM)
 
@@ -392,7 +396,7 @@
     near_shape = jax.ShapeDtypeStruct((2, BLK, 2 * HDIM), BF16)
     far_shape = jax.ShapeDtypeStruct((2, 2, BLK, 2 * HDIM), BF16)
     extras = [near_spec, near_spec, far_spec, far_spec]
-    att, gq, dkv, dnear_p, dnear_m, dfar_p, dfar_m = pl.pallas_call(
+    att, gq, dkv, dnear_p, dnear_m, dfar_p, dfar_m, pack = pl.pallas_call(
         attention_kernel,
         grid=(2,),
         out_shape=(
@@ -403,9 +407,10 @@
             near_shape,
             far_shape,
             far_shape,
+            far_shape,
         ),
         in_specs=[smem(), wide, pl.BlockSpec((2, 1, BLK, REP * HDIM), lambda g: (0, g, 0, 0)), pairs_spec] + extras,
-        out_specs=[wide, wide, pairs_spec] + extras,
+        out_specs=[wide, wide, pairs_spec] + extras + [far_spec],
         cost_estimate=cost(8 * 10**9, 10 * 2**20),
         compiler_params=params(),
         name="attention",
@@ -415,8 +420,7 @@
     rows = 2 * BLK
 
     def finish(keep, send):
-        got = swap(send, "c")
-        total = keep + got.astype(F32)
+        total = keep + swap(send, "c").astype(F32)
         return total[:BLK] + swap(total[BLK:].astype(BF16), "x").astype(F32), total
 
     chunk = width // 4
@@ -435,7 +439,7 @@
             name="output",
         )(att.reshape(2, 2, rows, REP * HDIM), o_weight)
     arrived = []
-    far_p, far_m = trade(dfar_p, dfar_m, t, owner, True, arrived, (out_parts[1],))
+    far_p, far_m = trade(dfar_p, dfar_m, t, owner, True, arrived, (out_parts[1],), pack)
     combined, _ = finish(*out_parts)
     combined = combined.astype(BF16)
 

time: 191 us -> 186 us (0.974)
  waiting for transfers between devices: 55.5 us -> 49.3 us
  starting transfers between devices: 54.4 us -> 56.7 us
    ppermute x6, waiting for transfers between devices: 15.6 us -> 8.22 us  [trade(): got = lax.ppermute(packed, axis, pairs)]
    ppermute x6, waiting for transfers between devices: 0.02 us -> 2.45 us  [send(): return lax.ppermute(value, ('x', 'a', 'c'), pairs)]
  transfers between devices with their start and end apart: 42 -> 42, of which waited for: 19 -> 17; matrix products, arithmetic and copies ran while one was open for 12% -> 12% of each run, Pallas kernels for 13% -> 14%
where the time goes in v3:
time: 186 us; the launch traced here: 185 us
  starting transfers between devices  56.7 us (30%)
  waiting for transfers between devices  49.3 us (27%)
  Pallas kernels  46.1 us (25%)
  other arithmetic  13.1 us (7%)
  local copies, waits for them, and re-layouts  12.7 us (7%)
  matrix products  4.59 us (2%)
  between operations  2.6 us (1%)
    ppermute x15, waiting for transfers between devices, swap(): return lax.ppermute(value, axis, [(0, 1), (1, 0)])  18.6 us
    ppermute x7, waiting for transfers between devices, ring(): lax.ppermute(value, axis, [(i, (i + 1) % count) for i in range(count)])  14.7 us
    ppermute x15, starting transfers between devices, swap(): return lax.ppermute(value, axis, [(0, 1), (1, 0)])  14.4 us
    pallas_call x1, Pallas kernels, body(): pl.pallas_call(attention_kernel, grid=(2,), out_shape=(jax.ShapeDtypeStru...  12.7 us
    ppermute x6, starting transfers between devices, trade(): got = lax.ppermute(packed, axis, pairs)  10 us
    pallas_call x1, Pallas kernels, body(): pl.pallas_call(query_part_kernel, grid=(steps,), out_shape=(jax.ShapeDtyp...  9.87 us
    ppermute x7, starting transfers between devices, ring(): lax.ppermute(value, axis, [(i, (i + 1) % count) for i in range(count)])  8.49 us
    ppermute x6, waiting for transfers between devices, trade(): got = lax.ppermute(packed, axis, pairs)  8.22 us
  transfers between devices with their start and end apart: 42, of which 17 were waited for; matrix products, arithmetic and copies ran while one was open for 12% of the time, Pallas kernels for 14%

profile of v3, /device:TPU:0, one launch (start us, length us, event | category | flops | bytes accessed | tf_op | source)
XLA Modules:
  0.0 185.1 jit_solution(7386809155518261560)
XLA Ops:
  0.7 3.0 %collective-permute-start = (bf16[128,2048]{1,0:T(8,128)(2,1)}, bf16[128,2048]{1,0:T(8,128)(2,1)S(1)}, u32[]{:S(2)}, u32[]{:S(2)}) collective-permute-start(bf16[128,2048]{1,0:T(8,128)(2,1)} %h00.1), channel_id=1, source_target_pairs={{0,16},{16,0},{1,17},{17,1},{2,18},{18,2},{3,19},{19,3},{4,20},{20... | collective-permute-start | bytes 1572872 | tf_op jit(solution)/shard_map/ppermute | solution.py:199
  3.7 1.0 constant_dynamic-slice_fusion
  4.7 0.8 constant_dynamic-slice_fusion.2
  6.1 1.1 collective-permute-done.4
  7.4 0.8 constant_dynamic-update-slice_fusion.7
  8.2 1.5 collective-permute-start.5
  9.9 1.6 collective-permute-start.6
  12.9 2.9 %collective-permute-done.h01 = bf16[128,2048]{1,0:T(8,128)(2,1)S(1)} collective-permute-done((bf16[128,2048]{1,0:T(8,128)(2,1)}, bf16[128,2048]{1,0:T(8,128)(2,1)S(1)}, u32[]{:S(2)}, u32[]{:S(2)}) %collective-permute-start) | collective-permute-done | bytes 524320 | tf_op jit(solution)/shard_map/ppermute | solution.py:199
  15.8 1.7 collective-permute-start.1
  17.6 1.6 fusion.14
  20.6 1.8 collective-permute-start.11
  22.5 0.8 collective-permute-done.6
  23.4 0.8 collective-permute-start.8
  24.2 1.5 collective-permute-start.7
  26.5 7.5 %collective-permute-done.7 = bf16[256,768]{1,0:T(8,128)(2,1)S(1)} collective-permute-done((bf16[256,768]{1,0:T(8,128)(2,1)S(1)}, bf16[256,768]{1,0:T(8,128)(2,1)S(1)}, u32[]{:S(2)}, u32[]{:S(2)}) %collective-permute-start.7) | collective-permute-done | bytes 393248 | tf_op jit(solution)/shard_map/ppermute | solution.py:212
  34.0 1.8 collective-permute-done.8
  35.8 1.5 collective-permute-start.9
  37.3 0.8 constant_dynamic-update-slice_fusion.5
  38.1 0.8 constant_dynamic-update-slice_fusion.4
  40.5 0.9 copy-done.22
  41.3 4.9 %norm.1 = bf16[2,512,2048]{2,1,0:T(8,128)(2,1)} custom-call(bf16[128,2048]{1,0:T(8,128)(2,1)} %h00.1, bf16[128,2048]{1,0:T(8,128)(2,1)} %copy-done.16, bf16[128,2048]{1,0:T(8,128)(2,1)} %copy-done.17, bf16[128,2048]{1,0:T(8,128)(2,1)} %copy-done.22), custom_call_target="tpu_custom_call" | custom-call | flops 1000000000 | bytes 6291456 | tf_op jit(solution)/shard_map/norm/pallas_call | solution.py:343
  46.3 1.1 collective-permute-done.10
  47.3 1.5 collective-permute-start.12
  49.0 1.3 collective-permute-start.20
  50.3 1.3 collective-permute-start.16
  51.6 1.0 constant_dynamic-update-slice_fusion.2
  52.7 3.5 %collective-permute-done.12 = bf16[256,768]{1,0:T(8,128)(2,1)S(1)} collective-permute-done((bf16[256,768]{1,0:T(8,128)(2,1)S(1)}, bf16[256,768]{1,0:T(8,128)(2,1)S(1)}, u32[]{:S(2)}, u32[]{:S(2)}) %collective-permute-start.12) | collective-permute-done | bytes 393248 | tf_op jit(solution)/shard_map/ppermute | solution.py:212
  56.2 1.3 convolution_convert_fusion
  58.5 1.6 collective-permute-start.21
  60.1 2.4 %collective-permute-done.16 = bf16[256,1024]{1,0:T(8,128)(2,1)S(1)} collective-permute-done((bf16[256,1024]{1,0:T(8,128)(2,1)S(1)}, bf16[256,1024]{1,0:T(8,128)(2,1)S(1)}, u32[]{:S(2)}, u32[]{:S(2)}) %collective-permute-start.16) | collective-permute-done | bytes 524320 | tf_op jit(solution)/shard_map/ppermute | solution.py:259
  63.4 3.1 %collective-permute-start.18 = (bf16[256,1024]{1,0:T(8,128)(2,1)S(1)}, bf16[256,1024]{1,0:T(8,128)(2,1)S(1)}, u32[]{:S(2)}, u32[]{:S(2)}) collective-permute-start(bf16[256,1024]{1,0:T(8,128)(2,1)S(1)} %get-tuple-element.42.refs_0_), channel_id=1, source_target_pairs={{0,2},{2,0},{4,6},{6,4},{13,15},{15,13},{9,11},{11,9},{20,22},{22,... | collective-permute-start | bytes 1572872 | tf_op jit(solution)/shard_map/ppermute | solution.py:267
  67.2 2.7 %collective-permute-start.23 = (bf16[256,1024]{1,0:T(8,128)(2,1)S(1)}, bf16[256,1024]{1,0:T(8,128)(2,1)S(1)}, u32[]{:S(2)}, u32[]{:S(2)}) collective-permute-start(bf16[256,1024]{1,0:T(8,128)(2,1)S(1)} %get-tuple-element.45.refs_2_), channel_id=1, source_target_pairs={{0,2},{2,0},{4,6},{6,4},{13,15},{15,13},{9,11},{11,9},{20,22},{22,... | collective-permute-start | bytes 1572872 | tf_op jit(solution)/shard_map/ppermute | solution.py:267
  70.2 3.8 %collective-permute-start.29 = (bf16[2,2,128,256]{3,2,1,0:T(8,128)(2,1)S(1)}, bf16[2,2,128,256]{3,2,1,0:T(8,128)(2,1)S(1)}, u32[]{:S(2)}, u32[]{:S(2)}) collective-permute-start(bf16[2,2,128,256]{3,2,1,0:T(8,128)(2,1)S(1)} %broadcast_select_fusion.2), channel_id=1, source_target_pairs={{0,4},{4,0},{8,12},{12,8},{1,5},{5,1},{9,13},{13,9},{2,6},{6,2},{1... | collective-permute-start | bytes 786440 | tf_op jit(solution)/shard_map/ppermute | solution.py:301
  75.2 4.9 %collective-permute-done.23.refs_6_ = bf16[256,1024]{1,0:T(8,128)(2,1)S(1)} collective-permute-done((bf16[256,1024]{1,0:T(8,128)(2,1)S(1)}, bf16[256,1024]{1,0:T(8,128)(2,1)S(1)}, u32[]{:S(2)}, u32[]{:S(2)}) %collective-permute-start.23) | collective-permute-done | bytes 524320 | tf_op jit(solution)/shard_map/ppermute | solution.py:267
  81.8 1.3 collective-permute-start.30
  84.2 1.5 collective-permute-start.26
  85.7 3.3 %fusion.2 = bf16[1024,512]{1,0:T(8,128)(2,1)} fusion(bf16[1024,2048]{1,0:T(8,128)(2,1)S(1)} %bitcast.20, bf16[2048,768]{1,0:T(8,128)(2,1)S(1)} %constant_dynamic-update-slice_fusion.w.wm), kind=kOutput, calls=%fused_computation.3 | convolution fusion | flops 2148007936 | bytes 7340032 | tf_op jit(solution)/shard_map/dot_general | solution.py:21
  89.1 3.1 %collective-permute-start.27 = (bf16[2,128,256]{2,1,0:T(8,128)(2,1)S(1)}, bf16[2,128,256]{2,1,0:T(8,128)(2,1)S(1)}, u32[]{:S(2)}, u32[]{:S(2)}) collective-permute-start(bf16[2,128,256]{2,1,0:T(8,128)(2,1)S(1)} %get-tuple-element.90), channel_id=1, source_target_pairs={{0,2},{2,4},{4,6},{6,8},{8,10},{10,12},{12,14},{1,3},{3,5},{5,7},{... | collective-permute-start | bytes 393224 | tf_op jit(solution)/shard_map/ppermute | solution.py:365
  92.2 4.9 %collective-permute-done.30 = bf16[2,2,128,256]{3,2,1,0:T(8,128)(2,1)S(1)} collective-permute-done((bf16[2,2,128,256]{3,2,1,0:T(8,128)(2,1)S(1)}, bf16[2,2,128,256]{3,2,1,0:T(8,128)(2,1)S(1)}, u32[]{:S(2)}, u32[]{:S(2)}) %collective-permute-start.30) | collective-permute-done | bytes 262176 | tf_op jit(solution)/shard_map/ppermute | solution.py:301
  97.1 1.5 collective-permute-start.28
  98.6 0.9 add_select_fusion.6
  99.5 0.8 copy-done.23
  100.3 0.8 copy-done.24
  101.2 5.1 %grad_att.1 = (bf16[512,512]{1,0:T(8,128)(2,1)}, bf16[512,2048]{1,0:T(8,128)(2,1)}) custom-call(bf16[128,2048]{1,0:T(8,128)(2,1)} %c00.1, bf16[128,2048]{1,0:T(8,128)(2,1)} %copy-done.18, bf16[128,2048]{1,0:T(8,128)(2,1)} %copy-done.21, bf16[128,2048]{1,0:T(8,128)(2,1)} %copy-done.23, bf16[256,1024]{1,0:T(8,128)(2,1)} %copy-done.10, ...), custom_call_target="tpu_custom_call" | custom-call | flops 1000000000 | bytes 9437184 | tf_op jit(solution)/shard_map/grad_att/pallas_call | solution.py:378
  107.0 12.7 %attention.1 = (bf16[2,2,2,128,512]{4,3,2,1,0:T(8,128)(2,1)}, bf16[2,2,2,128,512]{4,3,2,1,0:T(8,128)(2,1)}, f32[2,2,2,128,256]{4,3,2,1,0:T(8,128)}, bf16[2,128,2...) custom-call(s32[2]{0:T(128)} %pad_add_fusion.chosen, ...), custom_call_target="tpu_custom_call" | custom-call | flops 8000000000 | bytes 10485760 | tf_op jit(solution)/shard_map/attention/pallas_call | solution.py:399
  119.7 2.7 %collective-permute-start.35 = (bf16[2,2,128,256]{3,2,1,0:T(8,128)(2,1)}, bf16[2,2,128,256]{3,2,1,0:T(8,128)(2,1)S(1)}, u32[]{:S(2)}, u32[]{:S(2)}) collective-permute-start(bf16[2,2,128,256]{3,2,1,0:T(8,128)(2,1)} %get-tuple-element.56), channel_id=1, source_target_pairs={{0,2},{2,0},{1,3},{3,1},{4,6},{6,4},{5,7},{7,5},{8,10},{10,8},{9,1... | collective-permute-start | bytes 786440 | tf_op jit(solution)/shard_map/ppermute | solution.py:301
  122.4 5.5 %output.1 = (f32[256,2048]{1,0:T(8,128)}, bf16[256,2048]{1,0:T(8,128)(2,1)}) custom-call(bf16[2,2,256,512]{3,2,1,0:T(8,128)(2,1)} %bitcast.26, bf16[512,2048]{1,0:T(8,128)(2,1)} %get-tuple-element.49.w), custom_call_target="tpu_custom_call" | custom-call | flops 2000000000 | bytes 7340032 | tf_op jit(solution)/shard_map/output/pallas_call | solution.py:428
  128.0 4.2 %collective-permute-start.31 = (bf16[256,2048]{1,0:T(8,128)(2,1)}, bf16[256,2048]{1,0:T(8,128)(2,1)S(1)}, u32[]{:S(2)}, u32[]{:S(2)}) collective-permute-start(bf16[256,2048]{1,0:T(8,128)(2,1)} %get-tuple-element.51), channel_id=1, source_target_pairs={{0,1},{1,0},{2,3},{3,2},{4,5},{5,4},{6,7},{7,6},{8,9},{9,8},{10,11... | collective-permute-start | bytes 3145736 | tf_op jit(solution)/shard_map/ppermute | solution.py:199
  132.4 1.3 collective-permute-start.33
  133.7 4.6 %collective-permute-start.34 = (bf16[2,128,256]{2,1,0:T(8,128)(2,1)S(1)}, bf16[2,128,256]{2,1,0:T(8,128)(2,1)S(1)}, u32[]{:S(2)}, u32[]{:S(2)}) collective-permute-start(bf16[2,128,256]{2,1,0:T(8,128)(2,1)S(1)} %copy-done.27), channel_id=1, source_target_pairs={{0,2},{2,4},{4,6},{6,8},{8,10},{10,12},{12,14},{1,3},{3,5},{5,7},{... | collective-permute-start | bytes 393224 | tf_op jit(solution)/shard_map/ppermute | solution.py:419
  138.2 3.3 %collective-permute-done.36 = bf16[2,2,128,256]{3,2,1,0:T(8,128)(2,1)S(1)} collective-permute-done((bf16[2,2,128,256]{3,2,1,0:T(8,128)(2,1)S(1)}, bf16[2,2,128,256]{3,2,1,0:T(8,128)(2,1)S(1)}, u32[]{:S(2)}, u32[]{:S(2)}) %collective-permute-start.36) | collective-permute-done | bytes 262176 | tf_op jit(solution)/shard_map/ppermute | solution.py:301
  142.6 2.3 %collective-permute-start.32 = (bf16[128,2048]{1,0:T(8,128)(2,1)S(1)}, bf16[128,2048]{1,0:T(8,128)(2,1)S(1)}, u32[]{:S(2)}, u32[]{:S(2)}) collective-permute-start(bf16[128,2048]{1,0:T(8,128)(2,1)S(1)} %slice.97), channel_id=1, source_target_pairs={{0,16},{16,0},{1,17},{17,1},{2,18},{18,2},{3,19},{19,3},{4,20},{20... | collective-permute-start | bytes 1572872 | tf_op jit(solution)/shard_map/ppermute | solution.py:199
  145.0 9.9 %query_part.1 = (f32[2,256,2048]{2,1,0:T(8,128)}, bf16[2048,256]{1,0:T(8,128)(2,1)}, bf16[2048,256]{1,0:T(8,128)(2,1)}) custom-call(bf16[2,2,256,512]{3,2,1,0:T(8,128)(2,1)} %bitcast.24, bf16[2048,768]{1,0:T(8,128)(2,1)} %copy-done.5, bf16[2048,768]{1,0:T(8,128)(2,1)} %copy-done.5), custom_call_target="tpu_custom_call" | custom-call | flops 3000000000 | bytes 13631488 | tf_op jit(solution)/shard_map/query_part/pallas_call | solution.py:452
  154.8 0.9 add_select_fusion
  155.8 0.9 fusion.12
  157.4 4.0 %key_part.2 = (f32[256,1024]{1,0:T(8,128)}, bf16[256,1024]{1,0:T(8,128)(2,1)}) custom-call(s32[2]{0:T(128)} %pad_add_fusion.chosen, f32[2,2,2,128,256]{4,3,2,1,0:T(8,128)} %get-tuple-element.52.dkv, bf16[2,128,256]{2,1,0:T(8,128)(2,1)} %copy-done.13, bf16[2,128,256]{2,1,0:T(8,128)(2,1)} %copy-done.14, bf16[2,2,128,256]{3,2,1,0:T(8,128)(2,1)} %get-tuple-element.67.far_p, ...), custom_call_target="tpu_custom_call" | custom-call | flops 500000000 | bytes 8388608 | tf_op jit(solution)/shard_map/key_part/pallas_call | solution.py:480
  161.4 2.1 %collective-permute-done.38 = bf16[256,1024]{1,0:T(8,128)(2,1)S(1)} collective-permute-done((bf16[256,1024]{1,0:T(8,128)(2,1)}, bf16[256,1024]{1,0:T(8,128)(2,1)S(1)}, u32[]{:S(2)}, u32[]{:S(2)}) %collective-permute-start.38) | collective-permute-done | bytes 524320 | tf_op jit(solution)/shard_map/ppermute | solution.py:199
  163.5 1.4 convert_add_fusion.2
  164.9 4.0 %key_part.3 = (f32[256,1024]{1,0:T(8,128)}, bf16[256,1024]{1,0:T(8,128)(2,1)}) custom-call(s32[2]{0:T(128)} %pad_add_fusion.chosen, f32[2,2,2,128,256]{4,3,2,1,0:T(8,128)} %get-tuple-element.52.dkv, bf16[2,128,256]{2,1,0:T(8,128)(2,1)} %copy-done.13, bf16[2,128,256]{2,1,0:T(8,128)(2,1)} %copy-done.14, bf16[2,2,128,256]{3,2,1,0:T(8,128)(2,1)} %get-tuple-element.67.far_p, ...), custom_call_target="tpu_custom_call" | custom-call | flops 500000000 | bytes 8388608 | tf_op jit(solution)/shard_map/key_part/pallas_call | solution.py:480
  169.4 1.7 collective-permute-done.40
  171.1 1.4 convert_add_fusion.1
  172.9 5.6 %collective-permute-done.39 = bf16[128,1024]{1,0:T(8,128)(2,1)S(1)} collective-permute-done((bf16[128,1024]{1,0:T(8,128)(2,1)S(1)}, bf16[128,1024]{1,0:T(8,128)(2,1)S(1)}, u32[]{:S(2)}, u32[]{:S(2)}) %collective-permute-start.39) | collective-permute-done | bytes 262176 | tf_op jit(solution)/shard_map/ppermute | solution.py:199
  178.6 5.0 %collective-permute-done.41 = bf16[128,1024]{1,0:T(8,128)(2,1)S(1)} collective-permute-done((bf16[128,1024]{1,0:T(8,128)(2,1)S(1)}, bf16[128,1024]{1,0:T(8,128)(2,1)S(1)}, u32[]{:S(2)}, u32[]{:S(2)}) %collective-permute-start.41) | collective-permute-done | bytes 262176 | tf_op jit(solution)/shard_map/ppermute | solution.py:199
  183.9 1.1 fusion.10
  (143 shorter events, 15.8 us)
Async XLA Ops:
  0.6 10.9 %copy-start = (bf16[128,2048]{1,0:T(8,128)(2,1)S(1)}, bf16[128,2048]{1,0:T(8,128)(2,1)}, u32[]{:S(2)}) copy-start(bf16[128,2048]{1,0:T(8,128)(2,1)} %h00.1) | copy-start | bytes 1572868
  0.6 16.9 %copy-start.26 = (bf16[128,2048]{1,0:T(8,128)(2,1)S(1)}, bf16[128,2048]{1,0:T(8,128)(2,1)}, u32[]{:S(2)}) copy-start(bf16[128,2048]{1,0:T(8,128)(2,1)} %param.9) | copy-start | bytes 1572868
  0.7 10.9 %copy-start.31 = (s32[2]{0:T(128)S(1)}, s32[2]{0:T(128)}, u32[]{:S(2)}) copy-start(s32[2]{0:T(128)} %param.10) | copy-start | bytes 28
  0.7 15.1 %collective-permute-start = (bf16[128,2048]{1,0:T(8,128)(2,1)}, bf16[128,2048]{1,0:T(8,128)(2,1)S(1)}, u32[]{:S(2)}, u32[]{:S(2)}) collective-permute-start(bf16[128,2048]{1,0:T(8,128)(2,1)} %h00.1), channel_id=1, source_target_pairs={{0,16},{16,0},{1,17},{17,1},{2,18},{18,2},{3,19},{19,3},{4,20},{20... | collective-permute-start | bytes 1572872 | tf_op jit(solution)/shard_map/ppermute | solution.py:199
  3.7 13.9 %collective-permute-start.15 = (bf16[128,2048]{1,0:T(8,128)(2,1)}, bf16[128,2048]{1,0:T(8,128)(2,1)}, u32[]{:S(2)}, u32[]{:S(2)}) collective-permute-start(bf16[128,2048]{1,0:T(8,128)(2,1)} %param.9), channel_id=1, source_target_pairs={{0,1},{1,0},{2,3},{3,2},{4,5},{5,4},{6,7},{7,6},{8,9},{9,8},{10,11... | collective-permute-start | bytes 1572872 | tf_op jit(solution)/shard_map/ppermute | solution.py:199
  5.5 1.6 collective-permute-start.4
  7.2 13.4 %copy-start.15 = (bf16[128,2048]{1,0:T(8,128)(2,1)S(1)}, bf16[128,2048]{1,0:T(8,128)(2,1)}, u32[]{:S(2)}) copy-start(bf16[128,2048]{1,0:T(8,128)(2,1)} %c00.1) | copy-start | bytes 1572868
  8.2 14.3 %collective-permute-start.5 = (bf16[256,768]{1,0:T(8,128)(2,1)}, bf16[256,768]{1,0:T(8,128)(2,1)S(1)}, u32[]{:S(2)}, u32[]{:S(2)}) collective-permute-start(bf16[256,768]{1,0:T(8,128)(2,1)} %get-tuple-element.83), channel_id=1, source_target_pairs={{0,2},{2,0},{1,3},{3,1},{4,6},{6,4},{5,7},{7,5},{8,10},{10,8},{9,1... | collective-permute-start | bytes 1179656 | tf_op jit(solution)/shard_map/ppermute | solution.py:212
  9.9 13.5 %collective-permute-start.6 = (bf16[256,768]{1,0:T(8,128)(2,1)}, bf16[256,768]{1,0:T(8,128)(2,1)S(1)}, u32[]{:S(2)}, u32[]{:S(2)}) collective-permute-start(bf16[256,768]{1,0:T(8,128)(2,1)} %get-tuple-element.83), channel_id=1, source_target_pairs={{0,4},{4,8},{8,12},{12,0},{1,5},{5,9},{9,13},{13,1},{2,6},{6,10},{... | collective-permute-start | bytes 1179656 | tf_op jit(solution)/shard_map/ppermute | solution.py:212
  11.5 28.2 %collective-permute-start.2 = (bf16[128,2048]{1,0:T(8,128)(2,1)S(1)}, bf16[128,2048]{1,0:T(8,128)(2,1)S(1)}, u32[]{:S(2)}, u32[]{:S(2)}) collective-permute-start(bf16[128,2048]{1,0:T(8,128)(2,1)S(1)} %copy-done), channel_id=1, source_target_pairs={{0,1},{1,0},{2,3},{3,2},{4,5},{5,4},{6,7},{7,6},{8,9},{9,8},{10,11... | collective-permute-start | bytes 1572872 | tf_op jit(solution)/shard_map/ppermute | solution.py:199
  15.8 23.9 %copy-start.16 = (bf16[128,2048]{1,0:T(8,128)(2,1)}, bf16[128,2048]{1,0:T(8,128)(2,1)S(1)}, u32[]{:S(2)}) copy-start(bf16[128,2048]{1,0:T(8,128)(2,1)S(1)} %collective-permute-done.h01) | copy-start | bytes 1572868
  15.8 3.6 %collective-permute-start.1 = (f32[8,128]{1,0:T(8,128)S(1)}, f32[8,128]{1,0:T(8,128)S(1)}, u32[]{:S(2)}, u32[]{:S(2)}) collective-permute-start(f32[8,128]{1,0:T(8,128)S(1)} %broadcast_in_dim.125), channel_id=1, source_target_pairs={{0,16},{16,0},{1,17},{17,1},{2,18},{18,2},{3,19},{19,3},{4,20},{20... | collective-permute-start | bytes 12296 | tf_op jit(solution)/shard_map/ppermute | solution.py:199
  17.5 22.1 %collective-permute-start.3 = (bf16[128,2048]{1,0:T(8,128)(2,1)S(1)}, bf16[128,2048]{1,0:T(8,128)(2,1)S(1)}, u32[]{:S(2)}, u32[]{:S(2)}) collective-permute-start(bf16[128,2048]{1,0:T(8,128)(2,1)S(1)} %collective-permute-done.h01), channel_id=1, source_target_pairs={{0,1},{1,0},{2,3},{3,2},{4,5},{5,4},{6,7},{7,6},{8,9},{9,8},{10,11... | collective-permute-start | bytes 1572872 | tf_op jit(solution)/shard_map/ppermute | solution.py:199
  20.6 25.6 %collective-permute-start.11 = (bf16[128,2048]{1,0:T(8,128)(2,1)S(1)}, bf16[128,2048]{1,0:T(8,128)(2,1)S(1)}, u32[]{:S(2)}, u32[]{:S(2)}) collective-permute-start(bf16[128,2048]{1,0:T(8,128)(2,1)S(1)} %copy-done.15), channel_id=1, source_target_pairs={{0,16},{16,0},{1,17},{17,1},{2,18},{18,2},{3,19},{19,3},{4,20},{20... | collective-permute-start | bytes 1572872 | tf_op jit(solution)/shard_map/ppermute | solution.py:199
  23.4 12.4 %collective-permute-start.8 = (bf16[256,768]{1,0:T(8,128)(2,1)S(1)}, bf16[256,768]{1,0:T(8,128)(2,1)S(1)}, u32[]{:S(2)}, u32[]{:S(2)}) collective-permute-start(bf16[256,768]{1,0:T(8,128)(2,1)S(1)} %collective-permute-done.6), channel_id=1, source_target_pairs={{0,4},{4,8},{8,12},{12,0},{1,5},{5,9},{9,13},{13,1},{2,6},{6,10},{... | collective-permute-start | bytes 1179656 | tf_op jit(solution)/shard_map/ppermute | solution.py:212
  24.2 9.8 %collective-permute-start.7 = (bf16[256,768]{1,0:T(8,128)(2,1)S(1)}, bf16[256,768]{1,0:T(8,128)(2,1)S(1)}, u32[]{:S(2)}, u32[]{:S(2)}) collective-permute-start(bf16[256,768]{1,0:T(8,128)(2,1)S(1)} %collective-permute-done.6), channel_id=1, source_target_pairs={{0,2},{2,0},{1,3},{3,1},{4,6},{6,4},{5,7},{7,5},{8,10},{10,8},{9,1... | collective-permute-start | bytes 1179656 | tf_op jit(solution)/shard_map/ppermute | solution.py:212
  35.8 11.5 %collective-permute-start.10 = (bf16[256,768]{1,0:T(8,128)(2,1)S(1)}, bf16[256,768]{1,0:T(8,128)(2,1)S(1)}, u32[]{:S(2)}, u32[]{:S(2)}) collective-permute-start(bf16[256,768]{1,0:T(8,128)(2,1)S(1)} %collective-permute-done.8), channel_id=1, source_target_pairs={{0,4},{4,8},{8,12},{12,0},{1,5},{5,9},{9,13},{13,1},{2,6},{6,10},{... | collective-permute-start | bytes 1179656 | tf_op jit(solution)/shard_map/ppermute | solution.py:212
  35.8 10.5 %collective-permute-start.9 = (bf16[256,768]{1,0:T(8,128)(2,1)S(1)}, bf16[256,768]{1,0:T(8,128)(2,1)}, u32[]{:S(2)}, u32[]{:S(2)}) collective-permute-start(bf16[256,768]{1,0:T(8,128)(2,1)S(1)} %collective-permute-done.8), channel_id=1, source_target_pairs={{0,2},{2,0},{1,3},{3,1},{4,6},{6,4},{5,7},{7,5},{8,10},{10,8},{9,1... | collective-permute-start | bytes 1179656 | tf_op jit(solution)/shard_map/ppermute | solution.py:212
  39.7 11.9 %copy-start.4 = (bf16[2048,768]{1,0:T(8,128)(2,1)S(1)}, bf16[2048,768]{1,0:T(8,128)(2,1)}, u32[]{:S(2)}) copy-start(bf16[2048,768]{1,0:T(8,128)(2,1)} %constant_dynamic-update-slice_fusion.3) | copy-start | bytes 9437188
  46.3 10.0 %copy-start.2 = (bf16[2,512,2048]{2,1,0:T(8,128)(2,1)S(1)}, bf16[2,512,2048]{2,1,0:T(8,128)(2,1)}, u32[]{:S(2)}) copy-start(bf16[2,512,2048]{2,1,0:T(8,128)(2,1)} %norm.1) | copy-start | bytes 12582916
  46.3 35.2 %copy-start.18 = (bf16[128,2048]{1,0:T(8,128)(2,1)}, bf16[128,2048]{1,0:T(8,128)(2,1)S(1)}, u32[]{:S(2)}) copy-start(bf16[128,2048]{1,0:T(8,128)(2,1)S(1)} %collective-permute-done.11.c01) | copy-start | bytes 1572868
  47.3 8.8 %collective-permute-start.12 = (bf16[256,768]{1,0:T(8,128)(2,1)S(1)}, bf16[256,768]{1,0:T(8,128)(2,1)S(1)}, u32[]{:S(2)}, u32[]{:S(2)}) collective-permute-start(bf16[256,768]{1,0:T(8,128)(2,1)S(1)} %collective-permute-done.10), channel_id=1, source_target_pairs={{0,2},{2,0},{1,3},{3,1},{4,6},{6,4},{5,7},{7,5},{8,10},{10,8},{9,1... | collective-permute-start | bytes 1179656 | tf_op jit(solution)/shard_map/ppermute | solution.py:212
  49.0 11.2 %collective-permute-start.20 = (bf16[256,1024]{1,0:T(8,128)(2,1)S(1)}, bf16[256,1024]{1,0:T(8,128)(2,1)S(1)}, u32[]{:S(2)}, u32[]{:S(2)}) collective-permute-start(bf16[256,1024]{1,0:T(8,128)(2,1)S(1)} %get-tuple-element.86), channel_id=1, source_target_pairs={{0,4},{13,9},{20,16},{25,29},{2,6},{15,11},{22,18},{27,31}} | collective-permute-start | bytes 1572872 | tf_op jit(solution)/shard_map/ppermute | solution.py:259
  50.3 12.3 %collective-permute-start.16 = (bf16[256,1024]{1,0:T(8,128)(2,1)S(1)}, bf16[256,1024]{1,0:T(8,128)(2,1)S(1)}, u32[]{:S(2)}, u32[]{:S(2)}) collective-permute-start(bf16[256,1024]{1,0:T(8,128)(2,1)S(1)} %get-tuple-element.87), channel_id=1, source_target_pairs={{0,4},{13,9},{20,16},{25,29},{2,6},{15,11},{22,18},{27,31}} | collective-permute-start | bytes 1572872 | tf_op jit(solution)/shard_map/ppermute | solution.py:259
  56.2 29.5 %copy-start.5 = (bf16[2048,768]{1,0:T(8,128)(2,1)}, bf16[2048,768]{1,0:T(8,128)(2,1)S(1)}, u32[]{:S(2)}) copy-start(bf16[2048,768]{1,0:T(8,128)(2,1)S(1)} %constant_dynamic-update-slice_fusion.w.wm) | copy-start | bytes 9437188
  58.5 8.0 %collective-permute-start.21 = (bf16[2,2,128,256]{3,2,1,0:T(8,128)(2,1)S(1)}, bf16[2,2,128,256]{3,2,1,0:T(8,128)(2,1)S(1)}, u32[]{:S(2)}, u32[]{:S(2)}) collective-permute-start(bf16[2,2,128,256]{3,2,1,0:T(8,128)(2,1)S(1)} %fusion.15), channel_id=1, source_target_pairs={{0,2},{2,0},{1,3},{3,1},{4,6},{6,4},{5,7},{7,5},{8,10},{10,8},{9,1... | collective-permute-start | bytes 786440 | tf_op jit(solution)/shard_map/ppermute | solution.py:301
  62.7 21.5 %copy-start.9 = (bf16[256,1024]{1,0:T(8,128)(2,1)}, bf16[256,1024]{1,0:T(8,128)(2,1)S(1)}, u32[]{:S(2)}) copy-start(bf16[256,1024]{1,0:T(8,128)(2,1)S(1)} %get-tuple-element.45.refs_2_) | copy-start | bytes 1572868
  62.7 21.5 %copy-start.10 = (bf16[256,1024]{1,0:T(8,128)(2,1)}, bf16[256,1024]{1,0:T(8,128)(2,1)S(1)}, u32[]{:S(2)}) copy-start(bf16[256,1024]{1,0:T(8,128)(2,1)S(1)} %get-tuple-element.42.refs_0_) | copy-start | bytes 1572868
  62.7 11.3 %collective-permute-start.17 = (bf16[256,1024]{1,0:T(8,128)(2,1)S(1)}, bf16[256,1024]{1,0:T(8,128)(2,1)S(1)}, u32[]{:S(2)}, u32[]{:S(2)}) collective-permute-start(bf16[256,1024]{1,0:T(8,128)(2,1)S(1)} %get-tuple-element.42.refs_0_), channel_id=1, source_target_pairs={{4,8},{9,5},{20,24},{25,21},{6,10},{11,7},{22,26},{27,23}} | collective-permute-start | bytes 1572872 | tf_op jit(solution)/shard_map/ppermute | solution.py:259
  63.4 11.1 %collective-permute-start.18 = (bf16[256,1024]{1,0:T(8,128)(2,1)S(1)}, bf16[256,1024]{1,0:T(8,128)(2,1)S(1)}, u32[]{:S(2)}, u32[]{:S(2)}) collective-permute-start(bf16[256,1024]{1,0:T(8,128)(2,1)S(1)} %get-tuple-element.42.refs_0_), channel_id=1, source_target_pairs={{0,2},{2,0},{4,6},{6,4},{13,15},{15,13},{9,11},{11,9},{20,22},{22,... | collective-permute-start | bytes 1572872 | tf_op jit(solution)/shard_map/ppermute | solution.py:267
  66.5 8.7 %collective-permute-start.22 = (bf16[256,1024]{1,0:T(8,128)(2,1)S(1)}, bf16[256,1024]{1,0:T(8,128)(2,1)S(1)}, u32[]{:S(2)}, u32[]{:S(2)}) collective-permute-start(bf16[256,1024]{1,0:T(8,128)(2,1)S(1)} %get-tuple-element.45.refs_2_), channel_id=1, source_target_pairs={{4,8},{9,5},{20,24},{25,21},{6,10},{11,7},{22,26},{27,23}} | collective-permute-start | bytes 1572872 | tf_op jit(solution)/shard_map/ppermute | solution.py:259
  67.2 12.9 %collective-permute-start.23 = (bf16[256,1024]{1,0:T(8,128)(2,1)S(1)}, bf16[256,1024]{1,0:T(8,128)(2,1)S(1)}, u32[]{:S(2)}, u32[]{:S(2)}) collective-permute-start(bf16[256,1024]{1,0:T(8,128)(2,1)S(1)} %get-tuple-element.45.refs_2_), channel_id=1, source_target_pairs={{0,2},{2,0},{4,6},{6,4},{13,15},{15,13},{9,11},{11,9},{20,22},{22,... | collective-permute-start | bytes 1572872 | tf_op jit(solution)/shard_map/ppermute | solution.py:267
  70.2 11.3 %collective-permute-start.29 = (bf16[2,2,128,256]{3,2,1,0:T(8,128)(2,1)S(1)}, bf16[2,2,128,256]{3,2,1,0:T(8,128)(2,1)S(1)}, u32[]{:S(2)}, u32[]{:S(2)}) collective-permute-start(bf16[2,2,128,256]{3,2,1,0:T(8,128)(2,1)S(1)} %broadcast_select_fusion.2), channel_id=1, source_target_pairs={{0,4},{4,0},{8,12},{12,8},{1,5},{5,1},{9,13},{13,9},{2,6},{6,2},{1... | collective-permute-start | bytes 786440 | tf_op jit(solution)/shard_map/ppermute | solution.py:301
  74.0 15.1 %collective-permute-start.13 = (bf16[128,2048]{1,0:T(8,128)(2,1)S(1)}, bf16[128,2048]{1,0:T(8,128)(2,1)S(1)}, u32[]{:S(2)}, u32[]{:S(2)}) collective-permute-start(bf16[128,2048]{1,0:T(8,128)(2,1)S(1)} %copy-done.15), channel_id=1, source_target_pairs={{0,1},{1,0},{2,3},{3,2},{4,5},{5,4},{6,7},{7,6},{8,9},{9,8},{10,11... | collective-permute-start | bytes 1572872 | tf_op jit(solution)/shard_map/ppermute | solution.py:199
  74.5 14.6 %copy-start.19 = (bf16[256,1024]{1,0:T(8,128)(2,1)}, bf16[256,1024]{1,0:T(8,128)(2,1)S(1)}, u32[]{:S(2)}) copy-start(bf16[256,1024]{1,0:T(8,128)(2,1)S(1)} %collective-permute-done.18.refs_4_) | copy-start | bytes 1572868
  74.5 8.6 %collective-permute-start.19 = (bf16[256,1024]{1,0:T(8,128)(2,1)S(1)}, bf16[256,1024]{1,0:T(8,128)(2,1)S(1)}, u32[]{:S(2)}, u32[]{:S(2)}) collective-permute-start(bf16[256,1024]{1,0:T(8,128)(2,1)S(1)} %collective-permute-done.17), channel_id=1, source_target_pairs={{8,12},{5,1},{24,28},{21,17},{10,14},{7,3},{26,30},{23,19}} | collective-permute-start | bytes 1572872 | tf_op jit(solution)/shard_map/ppermute | solution.py:259
  80.1 3.9 %copy-start.20 = (bf16[256,1024]{1,0:T(8,128)(2,1)}, bf16[256,1024]{1,0:T(8,128)(2,1)S(1)}, u32[]{:S(2)}) copy-start(bf16[256,1024]{1,0:T(8,128)(2,1)S(1)} %collective-permute-done.23.refs_6_) | copy-start | bytes 1572868
  80.1 3.9 %collective-permute-start.24 = (bf16[256,1024]{1,0:T(8,128)(2,1)S(1)}, bf16[256,1024]{1,0:T(8,128)(2,1)S(1)}, u32[]{:S(2)}, u32[]{:S(2)}) collective-permute-start(bf16[256,1024]{1,0:T(8,128)(2,1)S(1)} %collective-permute-done.22), channel_id=1, source_target_pairs={{8,12},{5,1},{24,28},{21,17},{10,14},{7,3},{26,30},{23,19}} | collective-permute-start | bytes 1572872 | tf_op jit(solution)/shard_map/ppermute | solution.py:259
  81.4 18.1 %collective-permute-start.14 = (bf16[128,2048]{1,0:T(8,128)(2,1)S(1)}, bf16[128,2048]{1,0:T(8,128)(2,1)S(1)}, u32[]{:S(2)}, u32[]{:S(2)}) collective-permute-start(bf16[128,2048]{1,0:T(8,128)(2,1)S(1)} %collective-permute-done.11.c01), channel_id=1, source_target_pairs={{0,1},{1,0},{2,3},{3,2},{4,5},{5,4},{6,7},{7,6},{8,9},{9,8},{10,11... | collective-permute-start | bytes 1572872 | tf_op jit(solution)/shard_map/ppermute | solution.py:199
  81.8 15.3 %collective-permute-start.30 = (bf16[2,2,128,256]{3,2,1,0:T(8,128)(2,1)S(1)}, bf16[2,2,128,256]{3,2,1,0:T(8,128)(2,1)S(1)}, u32[]{:S(2)}, u32[]{:S(2)}) collective-permute-start(bf16[2,2,128,256]{3,2,1,0:T(8,128)(2,1)S(1)} %get-tuple-element.78), channel_id=1, source_target_pairs={{0,8},{4,12},{8,0},{12,4},{1,9},{5,13},{9,1},{13,5},{2,10},{6,14},... | collective-permute-start | bytes 786440 | tf_op jit(solution)/shard_map/ppermute | solution.py:301
  83.3 5.8 %copy-start.6 = (bf16[256,1024]{1,0:T(8,128)(2,1)}, bf16[256,1024]{1,0:T(8,128)(2,1)S(1)}, u32[]{:S(2)}) copy-start(bf16[256,1024]{1,0:T(8,128)(2,1)S(1)} %add.299.refs_1_) | copy-start | bytes 1572868
  83.3 16.2 %collective-permute-start.25 = (bf16[256,1024]{1,0:T(8,128)(2,1)S(1)}, bf16[256,1024]{1,0:T(8,128)(2,1)S(1)}, u32[]{:S(2)}, u32[]{:S(2)}) collective-permute-start(bf16[256,1024]{1,0:T(8,128)(2,1)S(1)} %add.299.refs_1_), channel_id=1, source_target_pairs={{8,10},{10,8},{12,14},{14,12},{5,7},{7,5},{1,3},{3,1},{24,26},{26,... | collective-permute-start | bytes 1572872 | tf_op jit(solution)/shard_map/ppermute | solution.py:267
  84.2 4.8 %copy-start.7 = (bf16[256,1024]{1,0:T(8,128)(2,1)}, bf16[256,1024]{1,0:T(8,128)(2,1)S(1)}, u32[]{:S(2)}) copy-start(bf16[256,1024]{1,0:T(8,128)(2,1)S(1)} %add.305.refs_3_) | copy-start | bytes 1572868
  84.2 16.9 %collective-permute-start.26 = (bf16[256,1024]{1,0:T(8,128)(2,1)S(1)}, bf16[256,1024]{1,0:T(8,128)(2,1)}, u32[]{:S(2)}, u32[]{:S(2)}) collective-permute-start(bf16[256,1024]{1,0:T(8,128)(2,1)S(1)} %add.305.refs_3_), channel_id=1, source_target_pairs={{8,10},{10,8},{12,14},{14,12},{5,7},{7,5},{1,3},{3,1},{24,26},{26,... | collective-permute-start | bytes 1572872 | tf_op jit(solution)/shard_map/ppermute | solution.py:267
  89.0 10.5 %copy-start.21 = (bf16[128,2048]{1,0:T(8,128)(2,1)}, bf16[128,2048]{1,0:T(8,128)(2,1)S(1)}, u32[]{:S(2)}) copy-start(bf16[128,2048]{1,0:T(8,128)(2,1)S(1)} %collective-permute-done.13.c10) | copy-start | bytes 1572868
  89.1 17.3 %collective-permute-start.27 = (bf16[2,128,256]{2,1,0:T(8,128)(2,1)S(1)}, bf16[2,128,256]{2,1,0:T(8,128)(2,1)S(1)}, u32[]{:S(2)}, u32[]{:S(2)}) collective-permute-start(bf16[2,128,256]{2,1,0:T(8,128)(2,1)S(1)} %get-tuple-element.90), channel_id=1, source_target_pairs={{0,2},{2,4},{4,6},{6,8},{8,10},{10,12},{12,14},{1,3},{3,5},{5,7},{... | collective-permute-start | bytes 393224 | tf_op jit(solution)/shard_map/ppermute | solution.py:365
  97.1 9.2 %collective-permute-start.28 = (bf16[2,128,256]{2,1,0:T(8,128)(2,1)S(1)}, bf16[2,128,256]{2,1,0:T(8,128)(2,1)S(1)}, u32[]{:S(2)}, u32[]{:S(2)}) collective-permute-start(bf16[2,128,256]{2,1,0:T(8,128)(2,1)S(1)} %get-tuple-element.88), channel_id=1, source_target_pairs={{2,0},{4,2},{6,4},{8,6},{10,8},{12,10},{14,12},{3,1},{5,3},{7,5},{... | collective-permute-start | bytes 393224 | tf_op jit(solution)/shard_map/ppermute | solution.py:365
  119.7 12.4 %collective-permute-start.35 = (bf16[2,2,128,256]{3,2,1,0:T(8,128)(2,1)}, bf16[2,2,128,256]{3,2,1,0:T(8,128)(2,1)S(1)}, u32[]{:S(2)}, u32[]{:S(2)}) collective-permute-start(bf16[2,2,128,256]{3,2,1,0:T(8,128)(2,1)} %get-tuple-element.56), channel_id=1, source_target_pairs={{0,2},{2,0},{1,3},{3,1},{4,6},{6,4},{5,7},{7,5},{8,10},{10,8},{9,1... | collective-permute-start | bytes 786440 | tf_op jit(solution)/shard_map/ppermute | solution.py:301
  122.4 9.7 %copy-start.11 = (bf16[2,2,128,256]{3,2,1,0:T(8,128)(2,1)S(1)}, bf16[2,2,128,256]{3,2,1,0:T(8,128)(2,1)}, u32[]{:S(2)}) copy-start(bf16[2,2,128,256]{3,2,1,0:T(8,128)(2,1)} %get-tuple-element.57) | copy-start | bytes 786436
  122.4 9.7 %copy-start.12 = (bf16[2,2,128,256]{3,2,1,0:T(8,128)(2,1)S(1)}, bf16[2,2,128,256]{3,2,1,0:T(8,128)(2,1)}, u32[]{:S(2)}) copy-start(bf16[2,2,128,256]{3,2,1,0:T(8,128)(2,1)} %get-tuple-element.55) | copy-start | bytes 786436
  122.4 10.0 %copy-start.28 = (bf16[2,128,256]{2,1,0:T(8,128)(2,1)S(1)}, bf16[2,128,256]{2,1,0:T(8,128)(2,1)}, u32[]{:S(2)}) copy-start(bf16[2,128,256]{2,1,0:T(8,128)(2,1)} %get-tuple-element.53) | copy-start | bytes 393220
  122.4 11.3 %copy-start.27 = (bf16[2,128,256]{2,1,0:T(8,128)(2,1)S(1)}, bf16[2,128,256]{2,1,0:T(8,128)(2,1)}, u32[]{:S(2)}) copy-start(bf16[2,128,256]{2,1,0:T(8,128)(2,1)} %get-tuple-element.54) | copy-start | bytes 393220
  127.9 14.3 %copy-start.8 = (f32[256,2048]{1,0:T(8,128)S(1)}, f32[256,2048]{1,0:T(8,128)}, u32[]{:S(2)}) copy-start(f32[256,2048]{1,0:T(8,128)} %get-tuple-element.50) | copy-start | bytes 6291460
  128.0 14.3 %collective-permute-start.31 = (bf16[256,2048]{1,0:T(8,128)(2,1)}, bf16[256,2048]{1,0:T(8,128)(2,1)S(1)}, u32[]{:S(2)}, u32[]{:S(2)}) collective-permute-start(bf16[256,2048]{1,0:T(8,128)(2,1)} %get-tuple-element.51), channel_id=1, source_target_pairs={{0,1},{1,0},{2,3},{3,2},{4,5},{5,4},{6,7},{7,6},{8,9},{9,8},{10,11... | collective-permute-start | bytes 3145736 | tf_op jit(solution)/shard_map/ppermute | solution.py:199
  132.3 9.2 %collective-permute-start.36 = (bf16[2,2,128,256]{3,2,1,0:T(8,128)(2,1)S(1)}, bf16[2,2,128,256]{3,2,1,0:T(8,128)(2,1)S(1)}, u32[]{:S(2)}, u32[]{:S(2)}) collective-permute-start(bf16[2,2,128,256]{3,2,1,0:T(8,128)(2,1)S(1)} %broadcast_select_fusion), channel_id=1, source_target_pairs={{0,4},{4,0},{8,12},{12,8},{1,5},{5,1},{9,13},{13,9},{2,6},{6,2},{1... | collective-permute-start | bytes 786440 | tf_op jit(solution)/shard_map/ppermute | solution.py:301
  132.4 24.3 %collective-permute-start.33 = (bf16[2,128,256]{2,1,0:T(8,128)(2,1)S(1)}, bf16[2,128,256]{2,1,0:T(8,128)(2,1)S(1)}, u32[]{:S(2)}, u32[]{:S(2)}) collective-permute-start(bf16[2,128,256]{2,1,0:T(8,128)(2,1)S(1)} %copy-done.28), channel_id=1, source_target_pairs={{2,0},{4,2},{6,4},{8,6},{10,8},{12,10},{14,12},{3,1},{5,3},{7,5},{... | collective-permute-start | bytes 393224 | tf_op jit(solution)/shard_map/ppermute | solution.py:419
  133.7 23.0 %collective-permute-start.34 = (bf16[2,128,256]{2,1,0:T(8,128)(2,1)S(1)}, bf16[2,128,256]{2,1,0:T(8,128)(2,1)S(1)}, u32[]{:S(2)}, u32[]{:S(2)}) collective-permute-start(bf16[2,128,256]{2,1,0:T(8,128)(2,1)S(1)} %copy-done.27), channel_id=1, source_target_pairs={{0,2},{2,4},{4,6},{6,8},{8,10},{10,12},{12,14},{1,3},{3,5},{5,7},{... | collective-permute-start | bytes 393224 | tf_op jit(solution)/shard_map/ppermute | solution.py:419
  141.8 13.1 %collective-permute-start.37 = (bf16[2,2,128,256]{3,2,1,0:T(8,128)(2,1)S(1)}, bf16[2,2,128,256]{3,2,1,0:T(8,128)(2,1)S(1)}, u32[]{:S(2)}, u32[]{:S(2)}) collective-permute-start(bf16[2,2,128,256]{3,2,1,0:T(8,128)(2,1)S(1)} %get-tuple-element.70), channel_id=1, source_target_pairs={{0,8},{4,12},{8,0},{12,4},{1,9},{5,13},{9,1},{13,5},{2,10},{6,14},... | collective-permute-start | bytes 786440 | tf_op jit(solution)/shard_map/ppermute | solution.py:301
  142.6 13.1 %collective-permute-start.32 = (bf16[128,2048]{1,0:T(8,128)(2,1)S(1)}, bf16[128,2048]{1,0:T(8,128)(2,1)S(1)}, u32[]{:S(2)}, u32[]{:S(2)}) collective-permute-start(bf16[128,2048]{1,0:T(8,128)(2,1)S(1)} %slice.97), channel_id=1, source_target_pairs={{0,16},{16,0},{1,17},{17,1},{2,18},{18,2},{3,19},{19,3},{4,20},{20... | collective-permute-start | bytes 1572872 | tf_op jit(solution)/shard_map/ppermute | solution.py:199
  161.4 2.1 %collective-permute-start.38 = (bf16[256,1024]{1,0:T(8,128)(2,1)}, bf16[256,1024]{1,0:T(8,128)(2,1)S(1)}, u32[]{:S(2)}, u32[]{:S(2)}) collective-permute-start(bf16[256,1024]{1,0:T(8,128)(2,1)} %get-tuple-element.66), channel_id=1, source_target_pairs={{0,1},{1,0},{2,3},{3,2},{4,5},{5,4},{6,7},{7,6},{8,9},{9,8},{10,11... | collective-permute-start | bytes 1572872 | tf_op jit(solution)/shard_map/ppermute | solution.py:199
  164.9 4.2 %copy-start.1 = (bf16[128,2048]{1,0:T(8,128)(2,1)S(1)}, bf16[128,2048]{1,0:T(8,128)(2,1)}, u32[]{:S(2)}) copy-start(bf16[128,2048]{1,0:T(8,128)(2,1)} %h00.1) | copy-start | bytes 1572868
  168.9 2.1 %collective-permute-start.40 = (bf16[256,1024]{1,0:T(8,128)(2,1)}, bf16[256,1024]{1,0:T(8,128)(2,1)S(1)}, u32[]{:S(2)}, u32[]{:S(2)}) collective-permute-start(bf16[256,1024]{1,0:T(8,128)(2,1)} %get-tuple-element.69), channel_id=1, source_target_pairs={{0,1},{1,0},{2,3},{3,2},{4,5},{5,4},{6,7},{7,6},{8,9},{9,8},{10,11... | collective-permute-start | bytes 1572872 | tf_op jit(solution)/shard_map/ppermute | solution.py:199
  169.3 9.2 %collective-permute-start.39 = (bf16[128,1024]{1,0:T(8,128)(2,1)S(1)}, bf16[128,1024]{1,0:T(8,128)(2,1)S(1)}, u32[]{:S(2)}, u32[]{:S(2)}) collective-permute-start(bf16[128,1024]{1,0:T(8,128)(2,1)S(1)} %slice.99), channel_id=1, source_target_pairs={{0,16},{16,0},{1,17},{17,1},{2,18},{18,2},{3,19},{19,3},{4,20},{20... | collective-permute-start | bytes 786440 | tf_op jit(solution)/shard_map/ppermute | solution.py:199
  172.5 11.1 %collective-permute-start.41 = (bf16[128,1024]{1,0:T(8,128)(2,1)S(1)}, bf16[128,1024]{1,0:T(8,128)(2,1)S(1)}, u32[]{:S(2)}, u32[]{:S(2)}) collective-permute-start(bf16[128,1024]{1,0:T(8,128)(2,1)S(1)} %slice.98), channel_id=1, source_target_pairs={{0,16},{16,0},{1,17},{17,1},{2,18},{18,2},{3,19},{19,3},{4,20},{20... | collective-permute-start | bytes 786440 | tf_op jit(solution)/shard_map/ppermute | solution.py:199
  (10 other events, 8.5 us)

commit v4 on v3

--- a/solution.py
+++ b/solution.py
@@ -12,6 +12,7 @@
 REP = HEADS // KVH
 EPS = 1e-05
 SCALE = HDIM ** (-0.5)
+LOG2E = 1.4426950408889634
 F32 = jnp.float32
 BF16 = jnp.bfloat16
 VMEM = 56 * 1024 * 1024
@@ -87,61 +88,76 @@
     last = last_block()
     t = position()
     g_dyn = chosen[pl.program_id(0)]
-    for strand in range(2):
-        near, far, dnear, dfar = ((near_p, far_p, dnear_p, dfar_p), (near_m, far_m, dnear_m, dfar_m))[strand]
-        sets = [kv[strand, 0, 0], kv[strand, 1, 0], near[0], far[0, 0], far[1, 0]]
+    sums = {}
+
+    def load(strand, side):
+        near, far = ((near_p, far_p), (near_m, far_m))[strand]
+        sets = [kv.at[strand, 0, 0], kv.at[strand, 1, 0], near.at[0], far.at[0, 0], far.at[1, 0]]
+        if strand == 0:
+            near_set = 2 if side == 0 else 0
+        else:
+            near_set = 1 if side == 0 else 2
+        order = (near_set, side, 3, 4)
+        keys = jnp.concatenate([sets[i][:, :HDIM] for i in order], axis=0)
+        values = jnp.concatenate([sets[i][:, HDIM:] for i in order], axis=0)
+        rows = jnp.concatenate([q[strand, side, 0, :, i * HDIM : (i + 1) * HDIM] for i in range(REP)], axis=0)
+        ups = jnp.concatenate([ga[side, 0, :, i * HDIM : (i + 1) * HDIM] for i in range(REP)], axis=0)
+        return order, keys, values, rows, ups, dot(rows, keys, 1, 1), dot(ups, values, 1, 1)
+
+    def weigh(strand, side, s, dp):
+        block = 2 * t + side
         stat_block = last if strand == 0 else 0
         dyn_block = g_dyn if strand == 0 else last - g_dyn
-        sums = [None] * 5
-        for side in range(2):
-            block = 2 * t + side
-            next_to = block - 1 if strand == 0 else block + 1
-            if strand == 0:
-                near_set = 2 if side == 0 else 0
-            else:
-                near_set = 1 if side == 0 else 2
-            order = (near_set, side, 3, 4)
-            flags = (
-                (next_to >= 0) & (next_to <= last),
-                None,
-                (stat_block != block) & (stat_block != next_to),
-                (dyn_block != block) & (dyn_block != next_to),
-            )
-            keys = jnp.concatenate([sets[i][:, :HDIM] for i in order], axis=0)
-            values = jnp.concatenate([sets[i][:, HDIM:] for i in order], axis=0)
-            qs = q[strand, side, 0]
-            gs = ga[side, 0]
-            rows = jnp.concatenate([qs[:, i * HDIM : (i + 1) * HDIM] for i in range(REP)], axis=0)
-            ups = jnp.concatenate([gs[:, i * HDIM : (i + 1) * HDIM] for i in range(REP)], axis=0)
-            s = dot(rows, keys, 1, 1) * SCALE
-            parts = []
-            for i in range(4):
-                part = s[:, i * BLK : (i + 1) * BLK]
-                if flags[i] is not None:
-                    part = jnp.where(flags[i], part, -jnp.inf)
-                parts.append(part)
-            s = jnp.concatenate(parts, axis=1)
-            e = jnp.exp(s - jnp.max(s, axis=1, keepdims=True))
-            p = e * (1.0 / jnp.sum(e, axis=1, keepdims=True))
-            ph = p.astype(BF16)
-            o = dot(ph, values, 1, 0)
-            dp = dot(ups, values, 1, 1)
-            center = jnp.sum(p * dp, axis=1, keepdims=True)
-            ds = (p * (dp - center) * SCALE).astype(BF16)
-            dq = dot(ds, keys, 1, 0)
-            dk = dot(ds, rows, 0, 0)
-            dv = dot(ph, ups, 0, 0)
-            for i in range(REP):
-                att[strand, side, 0, :, i * HDIM : (i + 1) * HDIM] = o[i * BLK : (i + 1) * BLK].astype(BF16)
-                gq[strand, side, 0, :, i * HDIM : (i + 1) * HDIM] = dq[i * BLK : (i + 1) * BLK].astype(BF16)
-            for i in range(4):
-                term = (dk[i * BLK : (i + 1) * BLK], dv[i * BLK : (i + 1) * BLK])
-                old = sums[order[i]]
-                sums[order[i]] = term if old is None else (old[0] + term[0], old[1] + term[1])
-        targets = (dkv.at[strand, 0, 0], dkv.at[strand, 1, 0], dnear.at[0], dfar.at[0, 0], dfar.at[1, 0])
-        for target, (dk, dv) in zip(targets, sums):
-            target[:, :HDIM] = dk.astype(target.dtype)
-            target[:, HDIM:] = dv.astype(target.dtype)
+        next_to = block - 1 if strand == 0 else block + 1
+        flags = (
+            (next_to >= 0) & (next_to <= last),
+            None,
+            (stat_block != block) & (stat_block != next_to),
+            (dyn_block != block) & (dyn_block != next_to),
+        )
+        parts = []
+        for i in range(4):
+            part = s[:, i * BLK : (i + 1) * BLK]
+            parts.append(part if flags[i] is None else jnp.where(flags[i], part, -jnp.inf))
+        s = jnp.concatenate(parts, axis=1)
+        e = jnp.exp2((s - jnp.max(s, axis=1, keepdims=True)) * (SCALE * LOG2E))
+        inverse = 1.0 / jnp.sum(e, axis=1, keepdims=True)
+        center = jnp.sum(e * dp, axis=1, keepdims=True) * inverse
+        p = e * inverse
+        return p.astype(BF16), (p * (dp - center)).astype(BF16)
+
+    def emit(strand, side, order, keys, values, rows, ups, ph, ds):
+        o = dot(ph, values, 1, 0).astype(BF16)
+        dq = (dot(ds, keys, 1, 0) * SCALE).astype(BF16)
+        dk = dot(ds, rows, 0, 0) * SCALE
+        dv = dot(ph, ups, 0, 0)
+        for i in range(REP):
+            att[strand, side, 0, :, i * HDIM : (i + 1) * HDIM] = o[i * BLK : (i + 1) * BLK]
+            gq[strand, side, 0, :, i * HDIM : (i + 1) * HDIM] = dq[i * BLK : (i + 1) * BLK]
+        for i in range(4):
+            term = (dk[i * BLK : (i + 1) * BLK], dv[i * BLK : (i + 1) * BLK])
+            old = sums.get((strand, order[i]))
+            sums[strand, order[i]] = term if old is None else (old[0] + term[0], old[1] + term[1])
+        if side == 1:
+            dnear, dfar = ((dnear_p, dfar_p), (dnear_m, dfar_m))[strand]
+            targets = (dkv.at[strand, 0, 0], dkv.at[strand, 1, 0], dnear.at[0], dfar.at[0, 0], dfar.at[1, 0])
+            for i, target in enumerate(targets):
+                target[:, :HDIM] = sums[strand, i][0].astype(target.dtype)
+                target[:, HDIM:] = sums[strand, i][1].astype(target.dtype)
+
+    units = [(strand, side) for strand in range(2) for side in range(2)]
+    following = load(*units[0])
+    ready = None
+    for number, unit in enumerate(units):
+        *held, s, dp = following
+        if number + 1 < len(units):
+            following = load(*units[number + 1])
+        weighed = weigh(*unit, s, dp)
+        if ready is not None:
+            emit(*ready)
+        ready = (*unit, *held, *weighed)
+    emit(*ready)
+
     for i, owner in enumerate((last // 2, g_dyn // 2)):
         pack[i, 0] = jnp.where(t % 2 == owner % 2, dfar_m[i, 0], dfar_p[i, 0])
 
@@ -162,8 +178,14 @@
         part[i] = dot(gq[0, place], w[:, 2 * HDIM :], 1, 1) + dot(gq[1, place], flipped[:, 2 * HDIM :], 1, 1)
 
 
-def key_part_kernel(chosen, dkv, near_p, near_m, far_p, far_m, part, wkv, wkvf, keep, send, kg):
+def project_keys(kg, part, wkv, wkvf, keep, send):
     core = lax.axis_index("c")
+    for i, (target, place) in enumerate(((keep, core), (send, 1 - core))):
+        total = part[i] + dot(kg[0, place], wkv[...], 1, 1) + dot(kg[1, place], wkvf[...], 1, 1)
+        target[...] = total.astype(target.dtype)
+
+
+def first_key_kernel(chosen, dkv, near_p, near_m, far_p, far_m, part, wkv, wkvf, keep, send, kg):
     t = position()
     last = last_block()
 
@@ -177,14 +199,14 @@
                     total = dkv[strand, side, grp]
                     if side != strand:
                         total = total + near[grp].astype(F32)
-                        total = total + jnp.where(2 * t + side == stat_block, far[0, grp].astype(F32), 0.0)
+                        term = far[0, grp].astype(F32)
+                        total = total + jnp.where(2 * t + side == stat_block, term, 0.0)
                     dyn_block = chosen[grp] if strand == 0 else last - chosen[grp]
-                    total = total + jnp.where(2 * t + side == dyn_block, far[1, grp].astype(F32), 0.0)
+                    term = far[1, grp].astype(F32)
+                    total = total + jnp.where(2 * t + side == dyn_block, term, 0.0)
                     kg[strand, side, grp * BLK : (grp + 1) * BLK, :] = total.astype(BF16)
 
-    for i, (target, place) in enumerate(((keep, core), (send, 1 - core))):
-        total = part[i] + dot(kg[0, place], wkv[...], 1, 1) + dot(kg[1, place], wkvf[...], 1, 1)
-        target[...] = total.astype(target.dtype)
+    project_keys(kg, part, wkv, wkvf, keep, send)
 
 
 def head_group(x, c):
@@ -233,7 +255,7 @@
     return full, chunk
 
 
-def output_rows(w_out, x, a, b, c, held, arrived, kv):
+def output_rows(w_out, x, a, b, c, held, arrived, kv, awaited):
     na, nb = lax.axis_size("a"), lax.axis_size("b")
     mine = head_group(x, c)
     half = w_out.shape[1] // 2
@@ -273,7 +295,7 @@
     second = [send(v, {(0, 0): (1, 2), (0, 1): (2, 1), (1, 0): (1, 2), (1, 1): (2, 1)}) for v in parts]
     early = [across(v, {(0, 0): (0, 1), (0, 1): (3, 2), (1, 0): (1, 0), (1, 1): (2, 3)}) for v in parts]
     third = [
-        send(after(v, w), {(0, 0): (2, 3), (0, 1): (1, 0), (1, 0): (2, 3), (1, 1): (1, 0)})
+        send(after(v, w, *awaited), {(0, 0): (2, 3), (0, 1): (1, 0), (1, 0): (2, 3), (1, 1): (1, 0)})
         for v, w in zip(second, early)
     ]
     late = [v + w for v, w in zip(second, third)]
@@ -371,7 +393,7 @@
     first = after(first, c01)
     arrived = []
     first, second = trade(first, second, t, owner, False, arrived)
-    wo_parts = output_rows(w_out, x, a, b, c, far_chunk, arrived, kv)
+    wo_parts = output_rows(w_out, x, a, b, c, far_chunk, arrived, kv, ())
 
     queries = dot(normed, q_weight, 1, 0).astype(BF16).reshape(2, 2, 2, BLK, REP * HDIM)
 
@@ -420,8 +442,10 @@
     rows = 2 * BLK
 
     def finish(keep, send):
-        total = keep + swap(send, "c").astype(F32)
-        return total[:BLK] + swap(total[BLK:].astype(BF16), "x").astype(F32), total
+        got = swap(send, "c")
+        other = (keep[BLK:] + got[BLK:].astype(F32)).astype(BF16)
+        back = swap(other, "x")
+        return keep[:BLK] + got[:BLK].astype(F32) + back.astype(F32), other, back
 
     chunk = width // 4
     partial = (jax.ShapeDtypeStruct((rows, width), F32), jax.ShapeDtypeStruct((rows, width), BF16))
@@ -440,7 +464,8 @@
         )(att.reshape(2, 2, rows, REP * HDIM), o_weight)
     arrived = []
     far_p, far_m = trade(dfar_p, dfar_m, t, owner, True, arrived, (out_parts[1],), pack)
-    combined, _ = finish(*out_parts)
+    total = out_parts[0] + swap(out_parts[1], "c").astype(F32)
+    combined = total[:BLK] + swap(total[BLK:].astype(BF16), "x").astype(F32)
     combined = combined.astype(BF16)
 
     chunk = 256
@@ -472,39 +497,44 @@
         name="query_part",
     )(after(gq, arrived[1]).reshape(2, 2, rows, REP * HDIM), weight, weight)
 
-    far_p = after(far_p, combined)
     chunk = width // 4
-    halves = []
-    for start in (0, 2):
-        half, total = finish(
-                *pl.pallas_call(
-                    key_part_kernel,
-                    grid=(2,),
-                    out_shape=(
-                        jax.ShapeDtypeStruct((rows, 2 * chunk), F32),
-                        jax.ShapeDtypeStruct((rows, 2 * chunk), BF16),
-                    ),
-                    in_specs=[
-                        smem(),
-                        fixed(dkv.shape),
-                        fixed(near_shape.shape),
-                        fixed(near_shape.shape),
-                        fixed(far_shape.shape),
-                        fixed(far_shape.shape),
-                        pl.BlockSpec((2, rows, chunk), lambda k, start=start: (0, 0, k + start)),
-                        pl.BlockSpec((chunk, 2 * HDIM), lambda k, start=start: (k + start, 0)),
-                        pl.BlockSpec((chunk, 2 * HDIM), lambda k, start=start: (k + start, 0)),
-                    ],
-                    out_specs=[pl.BlockSpec((rows, chunk), lambda k: (0, k))] * 2,
-                    scratch_shapes=[pltpu.VMEM((2, 2, rows, 2 * HDIM), BF16)],
-                    cost_estimate=cost(5 * 10**8, 8 * 2**20),
-                    compiler_params=params(),
-                    name="key_part",
-                )(chosen, dkv, near_p, near_m, far_p, far_m, part, kv_plain, kv_flipped)
-        )
-        halves.append(half)
-        far_p = after(far_p, total)
-    grad_norm = jnp.concatenate(halves, axis=1)
+    halves = (jax.ShapeDtypeStruct((rows, 2 * chunk), F32), jax.ShapeDtypeStruct((rows, 2 * chunk), BF16))
+    key_shape = (2, 2, rows, 2 * HDIM)
+
+    def sections(start):
+        return [
+            pl.BlockSpec((2, rows, chunk), lambda k: (0, 0, k + start)),
+            pl.BlockSpec((chunk, 2 * HDIM), lambda k: (k + start, 0)),
+            pl.BlockSpec((chunk, 2 * HDIM), lambda k: (k + start, 0)),
+        ]
+
+    *first_half, key_grads = pl.pallas_call(
+        first_key_kernel,
+        grid=(2,),
+        out_shape=halves + (jax.ShapeDtypeStruct(key_shape, BF16),),
+        in_specs=[smem()]
+        + [fixed(v) for v in (dkv.shape, near_shape.shape, near_shape.shape)]
+        + [fixed(far_shape.shape)] * 2
+        + sections(0),
+        out_specs=[pl.BlockSpec((rows, chunk), lambda k: (0, k))] * 2 + [fixed(key_shape)],
+        cost_estimate=cost(5 * 10**8, 8 * 2**20),
+        compiler_params=params(),
+        name="first_key",
+    )(chosen, dkv, near_p, near_m, after(far_p, combined), far_m, part, kv_plain, kv_flipped)
+    left, other, _ = finish(*first_half)
+    right, _, _ = finish(
+        *pl.pallas_call(
+            project_keys,
+            grid=(2,),
+            out_shape=halves,
+            in_specs=[fixed(key_shape)] + sections(2),
+            out_specs=[pl.BlockSpec((rows, chunk), lambda k: (0, k))] * 2,
+            cost_estimate=cost(5 * 10**8, 5 * 2**20),
+            compiler_params=params(),
+            name="second_key",
+        )(after(key_grads, other), part, kv_plain, kv_flipped)
+    )
+    grad_norm = jnp.concatenate([left, right], axis=1)
 
     u = hidden.astype(F32)
     inv_rms = lax.rsqrt(jnp.mean(u * u, axis=1, keepdims=True) + EPS)

time: 186 us -> 183 us (0.984)
  Pallas kernels: 46.1 us -> 43.5 us
    add x5 -> x3, other arithmetic: 3.13 us -> 0.44 us  [the longest x1 0.26 us: body(): total = out_parts[0] + swap(out_parts[1], 'c').astype(F32)]
    convert_element_type x0 -> x2, other arithmetic: none -> 2.2 us  [finish(): other = (keep[BLK:] + got[BLK:].astype(F32)).astype(BF16)]
    pallas_call x1, Pallas kernels: 12.7 us -> 10.7 us  [body(): pl.pallas_call(attention_kernel, grid=(2,), out_shape=(jax.ShapeDtypeStru...]
    unnamed x64 -> x68, local copies, waits for them, and re-layouts: 5.61 us -> 5.65 us
where the time goes in v4:
time: 183 us; the launch traced here: 182 us
  starting transfers between devices  56.3 us (31%)
  waiting for transfers between devices  50 us (27%)
  Pallas kernels  43.5 us (24%)
  local copies, waits for them, and re-layouts  12.6 us (7%)
  other arithmetic  12.6 us (7%)
  matrix products  4.57 us (2%)
  between operations  2.53 us (1%)
    ppermute x15, waiting for transfers between devices, swap(): return lax.ppermute(value, axis, [(0, 1), (1, 0)])  18.8 us
    ppermute x7, waiting for transfers between devices, ring(): lax.ppermute(value, axis, [(i, (i + 1) % count) for i in range(count)])  14.9 us
    ppermute x15, starting transfers between devices, swap(): return lax.ppermute(value, axis, [(0, 1), (1, 0)])  14.3 us
    pallas_call x1, Pallas kernels, body(): pl.pallas_call(attention_kernel, grid=(2,), out_shape=(jax.ShapeDtypeStru...  10.7 us
    ppermute x6, starting transfers between devices, trade(): got = lax.ppermute(packed, axis, pairs)  10.1 us
    pallas_call x1, Pallas kernels, body(): pl.pallas_call(query_part_kernel, grid=(steps,), out_shape=(jax.ShapeDtyp...  9.81 us
    ppermute x6, waiting for transfers between devices, trade(): got = lax.ppermute(packed, axis, pairs)  8.4 us
    ppermute x7, starting transfers between devices, ring(): lax.ppermute(value, axis, [(i, (i + 1) % count) for i in range(count)])  8.34 us
  transfers between devices with their start and end apart: 42, of which 17 were waited for; matrix products, arithmetic and copies ran while one was open for 12% of the time, Pallas kernels for 14%

profile of v4, /device:TPU:0, one launch (start us, length us, event | category | flops | bytes accessed | tf_op | source)
XLA Modules:
  0.0 182.2 jit_solution(14839614012130741485)
XLA Ops:
  0.7 3.0 %collective-permute-start = (bf16[128,2048]{1,0:T(8,128)(2,1)}, bf16[128,2048]{1,0:T(8,128)(2,1)S(1)}, u32[]{:S(2)}, u32[]{:S(2)}) collective-permute-start(bf16[128,2048]{1,0:T(8,128)(2,1)} %h00.1), channel_id=1, source_target_pairs={{0,16},{16,0},{1,17},{17,1},{2,18},{18,2},{3,19},{19,3},{4,20},{20... | collective-permute-start | bytes 1572872 | tf_op jit(solution)/shard_map/ppermute | solution.py:221
  3.7 1.0 constant_dynamic-slice_fusion
  4.7 0.8 constant_dynamic-slice_fusion.2
  6.1 1.1 collective-permute-done.4
  7.4 0.8 constant_dynamic-update-slice_fusion.7
  8.2 1.5 collective-permute-start.5
  9.9 1.6 collective-permute-start.6
  12.9 2.9 %collective-permute-done.h01 = bf16[128,2048]{1,0:T(8,128)(2,1)S(1)} collective-permute-done((bf16[128,2048]{1,0:T(8,128)(2,1)}, bf16[128,2048]{1,0:T(8,128)(2,1)S(1)}, u32[]{:S(2)}, u32[]{:S(2)}) %collective-permute-start) | collective-permute-done | bytes 524320 | tf_op jit(solution)/shard_map/ppermute | solution.py:221
  15.8 1.7 collective-permute-start.1
  17.6 1.6 fusion.14
  20.5 1.8 collective-permute-start.11
  22.4 1.0 collective-permute-done.6
  24.0 1.5 collective-permute-start.7
  25.6 0.8 constant_dynamic-update-slice_fusion.6
  26.4 7.6 %collective-permute-done.7 = bf16[256,768]{1,0:T(8,128)(2,1)S(1)} collective-permute-done((bf16[256,768]{1,0:T(8,128)(2,1)S(1)}, bf16[256,768]{1,0:T(8,128)(2,1)S(1)}, u32[]{:S(2)}, u32[]{:S(2)}) %collective-permute-start.7) | collective-permute-done | bytes 393248 | tf_op jit(solution)/shard_map/ppermute | solution.py:234
  34.0 1.8 collective-permute-done.8
  35.8 1.5 collective-permute-start.9
  37.3 0.8 constant_dynamic-update-slice_fusion.5
  38.1 0.8 constant_dynamic-update-slice_fusion.4
  40.5 0.9 copy-done.22
  41.4 4.9 %norm.1 = bf16[2,512,2048]{2,1,0:T(8,128)(2,1)} custom-call(bf16[128,2048]{1,0:T(8,128)(2,1)} %h00.1, bf16[128,2048]{1,0:T(8,128)(2,1)} %copy-done.16, bf16[128,2048]{1,0:T(8,128)(2,1)} %copy-done.17, bf16[128,2048]{1,0:T(8,128)(2,1)} %copy-done.22), custom_call_target="tpu_custom_call" | custom-call | flops 1000000000 | bytes 6291456 | tf_op jit(solution)/shard_map/norm/pallas_call | solution.py:365
  46.3 1.0 collective-permute-done.10
  47.4 1.5 collective-permute-start.12
  49.0 1.3 collective-permute-start.20
  50.3 1.3 collective-permute-start.16
  51.6 1.0 constant_dynamic-update-slice_fusion.2
  52.7 3.5 %collective-permute-done.12 = bf16[256,768]{1,0:T(8,128)(2,1)S(1)} collective-permute-done((bf16[256,768]{1,0:T(8,128)(2,1)S(1)}, bf16[256,768]{1,0:T(8,128)(2,1)S(1)}, u32[]{:S(2)}, u32[]{:S(2)}) %collective-permute-start.12) | collective-permute-done | bytes 393248 | tf_op jit(solution)/shard_map/ppermute | solution.py:234
  56.2 1.3 convolution_convert_fusion
  58.5 1.6 collective-permute-start.21
  60.1 2.4 %collective-permute-done.16 = bf16[256,1024]{1,0:T(8,128)(2,1)S(1)} collective-permute-done((bf16[256,1024]{1,0:T(8,128)(2,1)S(1)}, bf16[256,1024]{1,0:T(8,128)(2,1)S(1)}, u32[]{:S(2)}, u32[]{:S(2)}) %collective-permute-start.16) | collective-permute-done | bytes 524320 | tf_op jit(solution)/shard_map/ppermute | solution.py:281
  63.4 3.0 %collective-permute-start.18 = (bf16[256,1024]{1,0:T(8,128)(2,1)S(1)}, bf16[256,1024]{1,0:T(8,128)(2,1)S(1)}, u32[]{:S(2)}, u32[]{:S(2)}) collective-permute-start(bf16[256,1024]{1,0:T(8,128)(2,1)S(1)} %get-tuple-element.43.refs_0_), channel_id=1, source_target_pairs={{0,2},{2,0},{4,6},{6,4},{13,15},{15,13},{9,11},{11,9},{20,22},{22,... | collective-permute-start | bytes 1572872 | tf_op jit(solution)/shard_map/ppermute | solution.py:289
  67.1 2.9 %collective-permute-start.23 = (bf16[256,1024]{1,0:T(8,128)(2,1)S(1)}, bf16[256,1024]{1,0:T(8,128)(2,1)S(1)}, u32[]{:S(2)}, u32[]{:S(2)}) collective-permute-start(bf16[256,1024]{1,0:T(8,128)(2,1)S(1)} %get-tuple-element.46.refs_2_), channel_id=1, source_target_pairs={{0,2},{2,0},{4,6},{6,4},{13,15},{15,13},{9,11},{11,9},{20,22},{22,... | collective-permute-start | bytes 1572872 | tf_op jit(solution)/shard_map/ppermute | solution.py:289
  70.2 3.8 %collective-permute-start.29 = (bf16[2,2,128,256]{3,2,1,0:T(8,128)(2,1)S(1)}, bf16[2,2,128,256]{3,2,1,0:T(8,128)(2,1)S(1)}, u32[]{:S(2)}, u32[]{:S(2)}) collective-permute-start(bf16[2,2,128,256]{3,2,1,0:T(8,128)(2,1)S(1)} %broadcast_select_fusion.2), channel_id=1, source_target_pairs={{0,4},{4,0},{8,12},{12,8},{1,5},{5,1},{9,13},{13,9},{2,6},{6,2},{1... | collective-permute-start | bytes 786440 | tf_op jit(solution)/shard_map/ppermute | solution.py:323
  75.2 4.9 %collective-permute-done.23.refs_6_ = bf16[256,1024]{1,0:T(8,128)(2,1)S(1)} collective-permute-done((bf16[256,1024]{1,0:T(8,128)(2,1)S(1)}, bf16[256,1024]{1,0:T(8,128)(2,1)S(1)}, u32[]{:S(2)}, u32[]{:S(2)}) %collective-permute-start.23) | collective-permute-done | bytes 524320 | tf_op jit(solution)/shard_map/ppermute | solution.py:289
  81.8 1.3 collective-permute-start.30
  84.3 1.5 collective-permute-start.26
  85.7 3.3 %fusion.2 = bf16[1024,512]{1,0:T(8,128)(2,1)} fusion(bf16[1024,2048]{1,0:T(8,128)(2,1)S(1)} %bitcast.20, bf16[2048,768]{1,0:T(8,128)(2,1)S(1)} %constant_dynamic-update-slice_fusion.w.wm), kind=kOutput, calls=%fused_computation.3 | convolution fusion | flops 2148007936 | bytes 7340032 | tf_op jit(solution)/shard_map/dot_general | solution.py:22
  89.1 3.0 %collective-permute-start.27 = (bf16[2,128,256]{2,1,0:T(8,128)(2,1)S(1)}, bf16[2,128,256]{2,1,0:T(8,128)(2,1)S(1)}, u32[]{:S(2)}, u32[]{:S(2)}) collective-permute-start(bf16[2,128,256]{2,1,0:T(8,128)(2,1)S(1)} %get-tuple-element.92), channel_id=1, source_target_pairs={{0,2},{2,4},{4,6},{6,8},{8,10},{10,12},{12,14},{1,3},{3,5},{5,7},{... | collective-permute-start | bytes 393224 | tf_op jit(solution)/shard_map/ppermute | solution.py:387
  92.1 5.1 %collective-permute-done.30 = bf16[2,2,128,256]{3,2,1,0:T(8,128)(2,1)S(1)} collective-permute-done((bf16[2,2,128,256]{3,2,1,0:T(8,128)(2,1)S(1)}, bf16[2,2,128,256]{3,2,1,0:T(8,128)(2,1)S(1)}, u32[]{:S(2)}, u32[]{:S(2)}) %collective-permute-start.30) | collective-permute-done | bytes 262176 | tf_op jit(solution)/shard_map/ppermute | solution.py:323
  97.1 1.5 collective-permute-start.28
  98.6 0.9 add_select_fusion.6
  99.6 0.8 copy-done.23
  100.4 0.8 copy-done.24
  101.2 5.1 %grad_att.1 = (bf16[512,512]{1,0:T(8,128)(2,1)}, bf16[512,2048]{1,0:T(8,128)(2,1)}) custom-call(bf16[128,2048]{1,0:T(8,128)(2,1)} %c00.1, bf16[128,2048]{1,0:T(8,128)(2,1)} %copy-done.18, bf16[128,2048]{1,0:T(8,128)(2,1)} %copy-done.21, bf16[128,2048]{1,0:T(8,128)(2,1)} %copy-done.23, bf16[256,1024]{1,0:T(8,128)(2,1)} %copy-done.10, ...), custom_call_target="tpu_custom_call" | custom-call | flops 1000000000 | bytes 9437184 | tf_op jit(solution)/shard_map/grad_att/pallas_call | solution.py:400
  107.0 10.7 %attention.1 = (bf16[2,2,2,128,512]{4,3,2,1,0:T(8,128)(2,1)}, bf16[2,2,2,128,512]{4,3,2,1,0:T(8,128)(2,1)}, f32[2,2,2,128,256]{4,3,2,1,0:T(8,128)}, bf16[2,128,2...) custom-call(s32[2]{0:T(128)} %pad_add_fusion.chosen, ...), custom_call_target="tpu_custom_call" | custom-call | flops 8000000000 | bytes 10485760 | tf_op jit(solution)/shard_map/attention/pallas_call | solution.py:421
  117.7 2.7 %collective-permute-start.35 = (bf16[2,2,128,256]{3,2,1,0:T(8,128)(2,1)}, bf16[2,2,128,256]{3,2,1,0:T(8,128)(2,1)S(1)}, u32[]{:S(2)}, u32[]{:S(2)}) collective-permute-start(bf16[2,2,128,256]{3,2,1,0:T(8,128)(2,1)} %get-tuple-element.57), channel_id=1, source_target_pairs={{0,2},{2,0},{1,3},{3,1},{4,6},{6,4},{5,7},{7,5},{8,10},{10,8},{9,1... | collective-permute-start | bytes 786440 | tf_op jit(solution)/shard_map/ppermute | solution.py:323
  120.5 5.5 %output.1 = (f32[256,2048]{1,0:T(8,128)}, bf16[256,2048]{1,0:T(8,128)(2,1)}) custom-call(bf16[2,2,256,512]{3,2,1,0:T(8,128)(2,1)} %bitcast.26, bf16[512,2048]{1,0:T(8,128)(2,1)} %get-tuple-element.50.w), custom_call_target="tpu_custom_call" | custom-call | flops 2000000000 | bytes 7340032 | tf_op jit(solution)/shard_map/output/pallas_call | solution.py:452
  126.0 4.1 %collective-permute-start.31 = (bf16[256,2048]{1,0:T(8,128)(2,1)}, bf16[256,2048]{1,0:T(8,128)(2,1)S(1)}, u32[]{:S(2)}, u32[]{:S(2)}) collective-permute-start(bf16[256,2048]{1,0:T(8,128)(2,1)} %get-tuple-element.52), channel_id=1, source_target_pairs={{0,1},{1,0},{2,3},{3,2},{4,5},{5,4},{6,7},{7,6},{8,9},{9,8},{10,11... | collective-permute-start | bytes 3145736 | tf_op jit(solution)/shard_map/ppermute | solution.py:221
  130.4 1.3 collective-permute-start.33
  131.7 4.6 %collective-permute-start.34 = (bf16[2,128,256]{2,1,0:T(8,128)(2,1)S(1)}, bf16[2,128,256]{2,1,0:T(8,128)(2,1)S(1)}, u32[]{:S(2)}, u32[]{:S(2)}) collective-permute-start(bf16[2,128,256]{2,1,0:T(8,128)(2,1)S(1)} %copy-done.29), channel_id=1, source_target_pairs={{0,2},{2,4},{4,6},{6,8},{8,10},{10,12},{12,14},{1,3},{3,5},{5,7},{... | collective-permute-start | bytes 393224 | tf_op jit(solution)/shard_map/ppermute | solution.py:441
  136.3 3.3 %collective-permute-done.36 = bf16[2,2,128,256]{3,2,1,0:T(8,128)(2,1)S(1)} collective-permute-done((bf16[2,2,128,256]{3,2,1,0:T(8,128)(2,1)S(1)}, bf16[2,2,128,256]{3,2,1,0:T(8,128)(2,1)S(1)}, u32[]{:S(2)}, u32[]{:S(2)}) %collective-permute-start.36) | collective-permute-done | bytes 262176 | tf_op jit(solution)/shard_map/ppermute | solution.py:323
  140.7 2.3 %collective-permute-start.32 = (bf16[128,2048]{1,0:T(8,128)(2,1)S(1)}, bf16[128,2048]{1,0:T(8,128)(2,1)S(1)}, u32[]{:S(2)}, u32[]{:S(2)}) collective-permute-start(bf16[128,2048]{1,0:T(8,128)(2,1)S(1)} %slice.115), channel_id=1, source_target_pairs={{0,16},{16,0},{1,17},{17,1},{2,18},{18,2},{3,19},{19,3},{4,20},{20... | collective-permute-start | bytes 1572872 | tf_op jit(solution)/shard_map/ppermute | solution.py:221
  143.0 9.8 %query_part.1 = (f32[2,256,2048]{2,1,0:T(8,128)}, bf16[2048,256]{1,0:T(8,128)(2,1)}, bf16[2048,256]{1,0:T(8,128)(2,1)}) custom-call(bf16[2,2,256,512]{3,2,1,0:T(8,128)(2,1)} %bitcast.24, bf16[2048,768]{1,0:T(8,128)(2,1)} %copy-done.5, bf16[2048,768]{1,0:T(8,128)(2,1)} %copy-done.5), custom_call_target="tpu_custom_call" | custom-call | flops 3000000000 | bytes 13631488 | tf_op jit(solution)/shard_map/query_part/pallas_call | solution.py:477
  152.9 0.9 add_select_fusion
  153.8 0.9 fusion.12
  155.4 4.0 %first_key.1 = (f32[256,1024]{1,0:T(8,128)}, bf16[256,1024]{1,0:T(8,128)(2,1)}, bf16[2,2,256,256]{3,2,1,0:T(8,128)(2,1)}) custom-call(s32[2]{0:T(128)} %pad_add_fusion.chosen, f32[2,2,2,128,256]{4,3,2,1,0:T(8,128)} %get-tuple-element.53.dkv, bf16[2,128,256]{2,1,0:T(8,128)(2,1)} %copy-done.27, bf16[2,128,256]{2,1,0:T(8,128)(2,1)} %copy-done.28, ...), custom_call_target="tpu_custom_call" | custom-call | flops 500000000 | bytes 8388608 | tf_op jit(solution)/shard_map/first_key/pallas_call | solution.py:511
  159.4 2.1 %collective-permute-done.38 = bf16[256,1024]{1,0:T(8,128)(2,1)S(1)} collective-permute-done((bf16[256,1024]{1,0:T(8,128)(2,1)}, bf16[256,1024]{1,0:T(8,128)(2,1)S(1)}, u32[]{:S(2)}, u32[]{:S(2)}) %collective-permute-start.38) | collective-permute-done | bytes 524320 | tf_op jit(solution)/shard_map/ppermute | solution.py:221
  161.5 1.1 add_convert_fusion.1
  162.6 3.5 %second_key.1 = (f32[256,1024]{1,0:T(8,128)}, bf16[256,1024]{1,0:T(8,128)(2,1)}) custom-call(bf16[2,2,256,256]{3,2,1,0:T(8,128)(2,1)} %get-tuple-element.69.kg, f32[2,256,2048]{2,1,0:T(8,128)} %get-tuple-element.63.part, bf16[2048,256]{1,0:T(8,128)(2,1)} %get-tuple-element.64.wkv, bf16[2048,256]{1,0:T(8,128)(2,1)} %get-tuple-element.65.wkvf), custom_call_target="tpu_custom_call" | custom-call | flops 500000000 | bytes 5242880 | tf_op jit(solution)/shard_map/second_key/pallas_call | solution.py:526
  166.5 1.7 collective-permute-done.40
  168.2 1.1 add_convert_fusion
  169.7 5.9 %collective-permute-done.39 = bf16[128,1024]{1,0:T(8,128)(2,1)S(1)} collective-permute-done((bf16[128,1024]{1,0:T(8,128)(2,1)S(1)}, bf16[128,1024]{1,0:T(8,128)(2,1)S(1)}, u32[]{:S(2)}, u32[]{:S(2)}) %collective-permute-start.39) | collective-permute-done | bytes 262176 | tf_op jit(solution)/shard_map/ppermute | solution.py:221
  175.7 5.0 %collective-permute-done.41 = bf16[128,1024]{1,0:T(8,128)(2,1)S(1)} collective-permute-done((bf16[128,1024]{1,0:T(8,128)(2,1)S(1)}, bf16[128,1024]{1,0:T(8,128)(2,1)S(1)}, u32[]{:S(2)}, u32[]{:S(2)}) %collective-permute-start.41) | collective-permute-done | bytes 262176 | tf_op jit(solution)/shard_map/ppermute | solution.py:221
  181.0 1.1 fusion.10
  (145 shorter events, 15.7 us)
Async XLA Ops:
  0.6 10.9 %copy-start = (bf16[128,2048]{1,0:T(8,128)(2,1)S(1)}, bf16[128,2048]{1,0:T(8,128)(2,1)}, u32[]{:S(2)}) copy-start(bf16[128,2048]{1,0:T(8,128)(2,1)} %h00.1) | copy-start | bytes 1572868
  0.6 16.9 %copy-start.26 = (bf16[128,2048]{1,0:T(8,128)(2,1)S(1)}, bf16[128,2048]{1,0:T(8,128)(2,1)}, u32[]{:S(2)}) copy-start(bf16[128,2048]{1,0:T(8,128)(2,1)} %param.9) | copy-start | bytes 1572868
  0.7 10.9 %copy-start.33 = (s32[2]{0:T(128)S(1)}, s32[2]{0:T(128)}, u32[]{:S(2)}) copy-start(s32[2]{0:T(128)} %param.10) | copy-start | bytes 28
  0.7 15.1 %collective-permute-start = (bf16[128,2048]{1,0:T(8,128)(2,1)}, bf16[128,2048]{1,0:T(8,128)(2,1)S(1)}, u32[]{:S(2)}, u32[]{:S(2)}) collective-permute-start(bf16[128,2048]{1,0:T(8,128)(2,1)} %h00.1), channel_id=1, source_target_pairs={{0,16},{16,0},{1,17},{17,1},{2,18},{18,2},{3,19},{19,3},{4,20},{20... | collective-permute-start | bytes 1572872 | tf_op jit(solution)/shard_map/ppermute | solution.py:221
  3.7 13.9 %collective-permute-start.15 = (bf16[128,2048]{1,0:T(8,128)(2,1)}, bf16[128,2048]{1,0:T(8,128)(2,1)}, u32[]{:S(2)}, u32[]{:S(2)}) collective-permute-start(bf16[128,2048]{1,0:T(8,128)(2,1)} %param.9), channel_id=1, source_target_pairs={{0,1},{1,0},{2,3},{3,2},{4,5},{5,4},{6,7},{7,6},{8,9},{9,8},{10,11... | collective-permute-start | bytes 1572872 | tf_op jit(solution)/shard_map/ppermute | solution.py:221
  5.5 1.6 collective-permute-start.4
  7.2 13.3 %copy-start.15 = (bf16[128,2048]{1,0:T(8,128)(2,1)S(1)}, bf16[128,2048]{1,0:T(8,128)(2,1)}, u32[]{:S(2)}) copy-start(bf16[128,2048]{1,0:T(8,128)(2,1)} %c00.1) | copy-start | bytes 1572868
  8.2 14.2 %collective-permute-start.5 = (bf16[256,768]{1,0:T(8,128)(2,1)}, bf16[256,768]{1,0:T(8,128)(2,1)S(1)}, u32[]{:S(2)}, u32[]{:S(2)}) collective-permute-start(bf16[256,768]{1,0:T(8,128)(2,1)} %get-tuple-element.85), channel_id=1, source_target_pairs={{0,2},{2,0},{1,3},{3,1},{4,6},{6,4},{5,7},{7,5},{8,10},{10,8},{9,1... | collective-permute-start | bytes 1179656 | tf_op jit(solution)/shard_map/ppermute | solution.py:234
  9.9 13.5 %collective-permute-start.6 = (bf16[256,768]{1,0:T(8,128)(2,1)}, bf16[256,768]{1,0:T(8,128)(2,1)S(1)}, u32[]{:S(2)}, u32[]{:S(2)}) collective-permute-start(bf16[256,768]{1,0:T(8,128)(2,1)} %get-tuple-element.85), channel_id=1, source_target_pairs={{0,4},{4,8},{8,12},{12,0},{1,5},{5,9},{9,13},{13,1},{2,6},{6,10},{... | collective-permute-start | bytes 1179656 | tf_op jit(solution)/shard_map/ppermute | solution.py:234
  11.5 28.2 %collective-permute-start.2 = (bf16[128,2048]{1,0:T(8,128)(2,1)S(1)}, bf16[128,2048]{1,0:T(8,128)(2,1)S(1)}, u32[]{:S(2)}, u32[]{:S(2)}) collective-permute-start(bf16[128,2048]{1,0:T(8,128)(2,1)S(1)} %copy-done), channel_id=1, source_target_pairs={{0,1},{1,0},{2,3},{3,2},{4,5},{5,4},{6,7},{7,6},{8,9},{9,8},{10,11... | collective-permute-start | bytes 1572872 | tf_op jit(solution)/shard_map/ppermute | solution.py:221
  15.8 23.9 %copy-start.16 = (bf16[128,2048]{1,0:T(8,128)(2,1)}, bf16[128,2048]{1,0:T(8,128)(2,1)S(1)}, u32[]{:S(2)}) copy-start(bf16[128,2048]{1,0:T(8,128)(2,1)S(1)} %collective-permute-done.h01) | copy-start | bytes 1572868
  15.8 3.6 %collective-permute-start.1 = (f32[8,128]{1,0:T(8,128)S(1)}, f32[8,128]{1,0:T(8,128)S(1)}, u32[]{:S(2)}, u32[]{:S(2)}) collective-permute-start(f32[8,128]{1,0:T(8,128)S(1)} %broadcast_in_dim.125), channel_id=1, source_target_pairs={{0,16},{16,0},{1,17},{17,1},{2,18},{18,2},{3,19},{19,3},{4,20},{20... | collective-permute-start | bytes 12296 | tf_op jit(solution)/shard_map/ppermute | solution.py:221
  17.5 22.2 %collective-permute-start.3 = (bf16[128,2048]{1,0:T(8,128)(2,1)S(1)}, bf16[128,2048]{1,0:T(8,128)(2,1)S(1)}, u32[]{:S(2)}, u32[]{:S(2)}) collective-permute-start(bf16[128,2048]{1,0:T(8,128)(2,1)S(1)} %collective-permute-done.h01), channel_id=1, source_target_pairs={{0,1},{1,0},{2,3},{3,2},{4,5},{5,4},{6,7},{7,6},{8,9},{9,8},{10,11... | collective-permute-start | bytes 1572872 | tf_op jit(solution)/shard_map/ppermute | solution.py:221
  20.5 25.8 %collective-permute-start.11 = (bf16[128,2048]{1,0:T(8,128)(2,1)S(1)}, bf16[128,2048]{1,0:T(8,128)(2,1)S(1)}, u32[]{:S(2)}, u32[]{:S(2)}) collective-permute-start(bf16[128,2048]{1,0:T(8,128)(2,1)S(1)} %copy-done.15), channel_id=1, source_target_pairs={{0,16},{16,0},{1,17},{17,1},{2,18},{18,2},{3,19},{19,3},{4,20},{20... | collective-permute-start | bytes 1572872 | tf_op jit(solution)/shard_map/ppermute | solution.py:221
  23.4 12.4 %collective-permute-start.8 = (bf16[256,768]{1,0:T(8,128)(2,1)S(1)}, bf16[256,768]{1,0:T(8,128)(2,1)S(1)}, u32[]{:S(2)}, u32[]{:S(2)}) collective-permute-start(bf16[256,768]{1,0:T(8,128)(2,1)S(1)} %collective-permute-done.6), channel_id=1, source_target_pairs={{0,4},{4,8},{8,12},{12,0},{1,5},{5,9},{9,13},{13,1},{2,6},{6,10},{... | collective-permute-start | bytes 1179656 | tf_op jit(solution)/shard_map/ppermute | solution.py:234
  24.0 10.0 %collective-permute-start.7 = (bf16[256,768]{1,0:T(8,128)(2,1)S(1)}, bf16[256,768]{1,0:T(8,128)(2,1)S(1)}, u32[]{:S(2)}, u32[]{:S(2)}) collective-permute-start(bf16[256,768]{1,0:T(8,128)(2,1)S(1)} %collective-permute-done.6), channel_id=1, source_target_pairs={{0,2},{2,0},{1,3},{3,1},{4,6},{6,4},{5,7},{7,5},{8,10},{10,8},{9,1... | collective-permute-start | bytes 1179656 | tf_op jit(solution)/shard_map/ppermute | solution.py:234
  35.8 11.5 %collective-permute-start.10 = (bf16[256,768]{1,0:T(8,128)(2,1)S(1)}, bf16[256,768]{1,0:T(8,128)(2,1)S(1)}, u32[]{:S(2)}, u32[]{:S(2)}) collective-permute-start(bf16[256,768]{1,0:T(8,128)(2,1)S(1)} %collective-permute-done.8), channel_id=1, source_target_pairs={{0,4},{4,8},{8,12},{12,0},{1,5},{5,9},{9,13},{13,1},{2,6},{6,10},{... | collective-permute-start | bytes 1179656 | tf_op jit(solution)/shard_map/ppermute | solution.py:234
  35.8 10.5 %collective-permute-start.9 = (bf16[256,768]{1,0:T(8,128)(2,1)S(1)}, bf16[256,768]{1,0:T(8,128)(2,1)}, u32[]{:S(2)}, u32[]{:S(2)}) collective-permute-start(bf16[256,768]{1,0:T(8,128)(2,1)S(1)} %collective-permute-done.8), channel_id=1, source_target_pairs={{0,2},{2,0},{1,3},{3,1},{4,6},{6,4},{5,7},{7,5},{8,10},{10,8},{9,1... | collective-permute-start | bytes 1179656 | tf_op jit(solution)/shard_map/ppermute | solution.py:234
  39.7 11.9 %copy-start.4 = (bf16[2048,768]{1,0:T(8,128)(2,1)S(1)}, bf16[2048,768]{1,0:T(8,128)(2,1)}, u32[]{:S(2)}) copy-start(bf16[2048,768]{1,0:T(8,128)(2,1)} %constant_dynamic-update-slice_fusion.3) | copy-start | bytes 9437188
  46.3 9.9 %copy-start.2 = (bf16[2,512,2048]{2,1,0:T(8,128)(2,1)S(1)}, bf16[2,512,2048]{2,1,0:T(8,128)(2,1)}, u32[]{:S(2)}) copy-start(bf16[2,512,2048]{2,1,0:T(8,128)(2,1)} %norm.1) | copy-start | bytes 12582916
  46.3 35.1 %copy-start.18 = (bf16[128,2048]{1,0:T(8,128)(2,1)}, bf16[128,2048]{1,0:T(8,128)(2,1)S(1)}, u32[]{:S(2)}) copy-start(bf16[128,2048]{1,0:T(8,128)(2,1)S(1)} %collective-permute-done.11.c01) | copy-start | bytes 1572868
  47.4 8.8 %collective-permute-start.12 = (bf16[256,768]{1,0:T(8,128)(2,1)S(1)}, bf16[256,768]{1,0:T(8,128)(2,1)S(1)}, u32[]{:S(2)}, u32[]{:S(2)}) collective-permute-start(bf16[256,768]{1,0:T(8,128)(2,1)S(1)} %collective-permute-done.10), channel_id=1, source_target_pairs={{0,2},{2,0},{1,3},{3,1},{4,6},{6,4},{5,7},{7,5},{8,10},{10,8},{9,1... | collective-permute-start | bytes 1179656 | tf_op jit(solution)/shard_map/ppermute | solution.py:234
  49.0 11.2 %collective-permute-start.20 = (bf16[256,1024]{1,0:T(8,128)(2,1)S(1)}, bf16[256,1024]{1,0:T(8,128)(2,1)S(1)}, u32[]{:S(2)}, u32[]{:S(2)}) collective-permute-start(bf16[256,1024]{1,0:T(8,128)(2,1)S(1)} %get-tuple-element.88), channel_id=1, source_target_pairs={{0,4},{13,9},{20,16},{25,29},{2,6},{15,11},{22,18},{27,31}} | collective-permute-start | bytes 1572872 | tf_op jit(solution)/shard_map/ppermute | solution.py:281
  50.3 12.3 %collective-permute-start.16 = (bf16[256,1024]{1,0:T(8,128)(2,1)S(1)}, bf16[256,1024]{1,0:T(8,128)(2,1)S(1)}, u32[]{:S(2)}, u32[]{:S(2)}) collective-permute-start(bf16[256,1024]{1,0:T(8,128)(2,1)S(1)} %get-tuple-element.89), channel_id=1, source_target_pairs={{0,4},{13,9},{20,16},{25,29},{2,6},{15,11},{22,18},{27,31}} | collective-permute-start | bytes 1572872 | tf_op jit(solution)/shard_map/ppermute | solution.py:281
  56.2 29.5 %copy-start.5 = (bf16[2048,768]{1,0:T(8,128)(2,1)}, bf16[2048,768]{1,0:T(8,128)(2,1)S(1)}, u32[]{:S(2)}) copy-start(bf16[2048,768]{1,0:T(8,128)(2,1)S(1)} %constant_dynamic-update-slice_fusion.w.wm) | copy-start | bytes 9437188
  58.5 7.8 %collective-permute-start.21 = (bf16[2,2,128,256]{3,2,1,0:T(8,128)(2,1)S(1)}, bf16[2,2,128,256]{3,2,1,0:T(8,128)(2,1)S(1)}, u32[]{:S(2)}, u32[]{:S(2)}) collective-permute-start(bf16[2,2,128,256]{3,2,1,0:T(8,128)(2,1)S(1)} %fusion.15), channel_id=1, source_target_pairs={{0,2},{2,0},{1,3},{3,1},{4,6},{6,4},{5,7},{7,5},{8,10},{10,8},{9,1... | collective-permute-start | bytes 786440 | tf_op jit(solution)/shard_map/ppermute | solution.py:323
  62.7 21.6 %copy-start.9 = (bf16[256,1024]{1,0:T(8,128)(2,1)}, bf16[256,1024]{1,0:T(8,128)(2,1)S(1)}, u32[]{:S(2)}) copy-start(bf16[256,1024]{1,0:T(8,128)(2,1)S(1)} %get-tuple-element.46.refs_2_) | copy-start | bytes 1572868
  62.7 21.6 %copy-start.10 = (bf16[256,1024]{1,0:T(8,128)(2,1)}, bf16[256,1024]{1,0:T(8,128)(2,1)S(1)}, u32[]{:S(2)}) copy-start(bf16[256,1024]{1,0:T(8,128)(2,1)S(1)} %get-tuple-element.43.refs_0_) | copy-start | bytes 1572868
  62.7 11.3 %collective-permute-start.17 = (bf16[256,1024]{1,0:T(8,128)(2,1)S(1)}, bf16[256,1024]{1,0:T(8,128)(2,1)S(1)}, u32[]{:S(2)}, u32[]{:S(2)}) collective-permute-start(bf16[256,1024]{1,0:T(8,128)(2,1)S(1)} %get-tuple-element.43.refs_0_), channel_id=1, source_target_pairs={{4,8},{9,5},{20,24},{25,21},{6,10},{11,7},{22,26},{27,23}} | collective-permute-start | bytes 1572872 | tf_op jit(solution)/shard_map/ppermute | solution.py:281
  63.4 11.1 %collective-permute-start.18 = (bf16[256,1024]{1,0:T(8,128)(2,1)S(1)}, bf16[256,1024]{1,0:T(8,128)(2,1)S(1)}, u32[]{:S(2)}, u32[]{:S(2)}) collective-permute-start(bf16[256,1024]{1,0:T(8,128)(2,1)S(1)} %get-tuple-element.43.refs_0_), channel_id=1, source_target_pairs={{0,2},{2,0},{4,6},{6,4},{13,15},{15,13},{9,11},{11,9},{20,22},{22,... | collective-permute-start | bytes 1572872 | tf_op jit(solution)/shard_map/ppermute | solution.py:289
  66.4 8.8 %collective-permute-start.22 = (bf16[256,1024]{1,0:T(8,128)(2,1)S(1)}, bf16[256,1024]{1,0:T(8,128)(2,1)S(1)}, u32[]{:S(2)}, u32[]{:S(2)}) collective-permute-start(bf16[256,1024]{1,0:T(8,128)(2,1)S(1)} %get-tuple-element.46.refs_2_), channel_id=1, source_target_pairs={{4,8},{9,5},{20,24},{25,21},{6,10},{11,7},{22,26},{27,23}} | collective-permute-start | bytes 1572872 | tf_op jit(solution)/shard_map/ppermute | solution.py:281
  67.1 13.0 %collective-permute-start.23 = (bf16[256,1024]{1,0:T(8,128)(2,1)S(1)}, bf16[256,1024]{1,0:T(8,128)(2,1)S(1)}, u32[]{:S(2)}, u32[]{:S(2)}) collective-permute-start(bf16[256,1024]{1,0:T(8,128)(2,1)S(1)} %get-tuple-element.46.refs_2_), channel_id=1, source_target_pairs={{0,2},{2,0},{4,6},{6,4},{13,15},{15,13},{9,11},{11,9},{20,22},{22,... | collective-permute-start | bytes 1572872 | tf_op jit(solution)/shard_map/ppermute | solution.py:289
  70.2 11.3 %collective-permute-start.29 = (bf16[2,2,128,256]{3,2,1,0:T(8,128)(2,1)S(1)}, bf16[2,2,128,256]{3,2,1,0:T(8,128)(2,1)S(1)}, u32[]{:S(2)}, u32[]{:S(2)}) collective-permute-start(bf16[2,2,128,256]{3,2,1,0:T(8,128)(2,1)S(1)} %broadcast_select_fusion.2), channel_id=1, source_target_pairs={{0,4},{4,0},{8,12},{12,8},{1,5},{5,1},{9,13},{13,9},{2,6},{6,2},{1... | collective-permute-start | bytes 786440 | tf_op jit(solution)/shard_map/ppermute | solution.py:323
  74.0 15.1 %collective-permute-start.13 = (bf16[128,2048]{1,0:T(8,128)(2,1)S(1)}, bf16[128,2048]{1,0:T(8,128)(2,1)S(1)}, u32[]{:S(2)}, u32[]{:S(2)}) collective-permute-start(bf16[128,2048]{1,0:T(8,128)(2,1)S(1)} %copy-done.15), channel_id=1, source_target_pairs={{0,1},{1,0},{2,3},{3,2},{4,5},{5,4},{6,7},{7,6},{8,9},{9,8},{10,11... | collective-permute-start | bytes 1572872 | tf_op jit(solution)/shard_map/ppermute | solution.py:221
  74.5 14.6 %copy-start.19 = (bf16[256,1024]{1,0:T(8,128)(2,1)}, bf16[256,1024]{1,0:T(8,128)(2,1)S(1)}, u32[]{:S(2)}) copy-start(bf16[256,1024]{1,0:T(8,128)(2,1)S(1)} %collective-permute-done.18.refs_4_) | copy-start | bytes 1572868
  74.5 8.6 %collective-permute-start.19 = (bf16[256,1024]{1,0:T(8,128)(2,1)S(1)}, bf16[256,1024]{1,0:T(8,128)(2,1)S(1)}, u32[]{:S(2)}, u32[]{:S(2)}) collective-permute-start(bf16[256,1024]{1,0:T(8,128)(2,1)S(1)} %collective-permute-done.17), channel_id=1, source_target_pairs={{8,12},{5,1},{24,28},{21,17},{10,14},{7,3},{26,30},{23,19}} | collective-permute-start | bytes 1572872 | tf_op jit(solution)/shard_map/ppermute | solution.py:281
  80.1 3.9 %collective-permute-start.24 = (bf16[256,1024]{1,0:T(8,128)(2,1)S(1)}, bf16[256,1024]{1,0:T(8,128)(2,1)S(1)}, u32[]{:S(2)}, u32[]{:S(2)}) collective-permute-start(bf16[256,1024]{1,0:T(8,128)(2,1)S(1)} %collective-permute-done.22), channel_id=1, source_target_pairs={{8,12},{5,1},{24,28},{21,17},{10,14},{7,3},{26,30},{23,19}} | collective-permute-start | bytes 1572872 | tf_op jit(solution)/shard_map/ppermute | solution.py:281
  81.5 18.1 %collective-permute-start.14 = (bf16[128,2048]{1,0:T(8,128)(2,1)S(1)}, bf16[128,2048]{1,0:T(8,128)(2,1)S(1)}, u32[]{:S(2)}, u32[]{:S(2)}) collective-permute-start(bf16[128,2048]{1,0:T(8,128)(2,1)S(1)} %collective-permute-done.11.c01), channel_id=1, source_target_pairs={{0,1},{1,0},{2,3},{3,2},{4,5},{5,4},{6,7},{7,6},{8,9},{9,8},{10,11... | collective-permute-start | bytes 1572872 | tf_op jit(solution)/shard_map/ppermute | solution.py:221
  81.8 15.3 %collective-permute-start.30 = (bf16[2,2,128,256]{3,2,1,0:T(8,128)(2,1)S(1)}, bf16[2,2,128,256]{3,2,1,0:T(8,128)(2,1)S(1)}, u32[]{:S(2)}, u32[]{:S(2)}) collective-permute-start(bf16[2,2,128,256]{3,2,1,0:T(8,128)(2,1)S(1)} %get-tuple-element.80), channel_id=1, source_target_pairs={{0,8},{4,12},{8,0},{12,4},{1,9},{5,13},{9,1},{13,5},{2,10},{6,14},... | collective-permute-start | bytes 786440 | tf_op jit(solution)/shard_map/ppermute | solution.py:323
  83.3 5.8 %copy-start.6 = (bf16[256,1024]{1,0:T(8,128)(2,1)}, bf16[256,1024]{1,0:T(8,128)(2,1)S(1)}, u32[]{:S(2)}) copy-start(bf16[256,1024]{1,0:T(8,128)(2,1)S(1)} %add.305.refs_1_) | copy-start | bytes 1572868
  83.3 16.2 %collective-permute-start.25 = (bf16[256,1024]{1,0:T(8,128)(2,1)S(1)}, bf16[256,1024]{1,0:T(8,128)(2,1)S(1)}, u32[]{:S(2)}, u32[]{:S(2)}) collective-permute-start(bf16[256,1024]{1,0:T(8,128)(2,1)S(1)} %add.305.refs_1_), channel_id=1, source_target_pairs={{8,10},{10,8},{12,14},{14,12},{5,7},{7,5},{1,3},{3,1},{24,26},{26,... | collective-permute-start | bytes 1572872 | tf_op jit(solution)/shard_map/ppermute | solution.py:289
  84.3 4.8 %copy-start.7 = (bf16[256,1024]{1,0:T(8,128)(2,1)}, bf16[256,1024]{1,0:T(8,128)(2,1)S(1)}, u32[]{:S(2)}) copy-start(bf16[256,1024]{1,0:T(8,128)(2,1)S(1)} %add.311.refs_3_) | copy-start | bytes 1572868
  84.3 17.0 %collective-permute-start.26 = (bf16[256,1024]{1,0:T(8,128)(2,1)S(1)}, bf16[256,1024]{1,0:T(8,128)(2,1)}, u32[]{:S(2)}, u32[]{:S(2)}) collective-permute-start(bf16[256,1024]{1,0:T(8,128)(2,1)S(1)} %add.311.refs_3_), channel_id=1, source_target_pairs={{8,10},{10,8},{12,14},{14,12},{5,7},{7,5},{1,3},{3,1},{24,26},{26,... | collective-permute-start | bytes 1572872 | tf_op jit(solution)/shard_map/ppermute | solution.py:289
  89.1 10.5 %copy-start.21 = (bf16[128,2048]{1,0:T(8,128)(2,1)}, bf16[128,2048]{1,0:T(8,128)(2,1)S(1)}, u32[]{:S(2)}) copy-start(bf16[128,2048]{1,0:T(8,128)(2,1)S(1)} %collective-permute-done.13.c10) | copy-start | bytes 1572868
  89.1 17.3 %collective-permute-start.27 = (bf16[2,128,256]{2,1,0:T(8,128)(2,1)S(1)}, bf16[2,128,256]{2,1,0:T(8,128)(2,1)S(1)}, u32[]{:S(2)}, u32[]{:S(2)}) collective-permute-start(bf16[2,128,256]{2,1,0:T(8,128)(2,1)S(1)} %get-tuple-element.92), channel_id=1, source_target_pairs={{0,2},{2,4},{4,6},{6,8},{8,10},{10,12},{12,14},{1,3},{3,5},{5,7},{... | collective-permute-start | bytes 393224 | tf_op jit(solution)/shard_map/ppermute | solution.py:387
  97.1 9.2 %collective-permute-start.28 = (bf16[2,128,256]{2,1,0:T(8,128)(2,1)S(1)}, bf16[2,128,256]{2,1,0:T(8,128)(2,1)S(1)}, u32[]{:S(2)}, u32[]{:S(2)}) collective-permute-start(bf16[2,128,256]{2,1,0:T(8,128)(2,1)S(1)} %get-tuple-element.90), channel_id=1, source_target_pairs={{2,0},{4,2},{6,4},{8,6},{10,8},{12,10},{14,12},{3,1},{5,3},{7,5},{... | collective-permute-start | bytes 393224 | tf_op jit(solution)/shard_map/ppermute | solution.py:387
  117.7 12.4 %collective-permute-start.35 = (bf16[2,2,128,256]{3,2,1,0:T(8,128)(2,1)}, bf16[2,2,128,256]{3,2,1,0:T(8,128)(2,1)S(1)}, u32[]{:S(2)}, u32[]{:S(2)}) collective-permute-start(bf16[2,2,128,256]{3,2,1,0:T(8,128)(2,1)} %get-tuple-element.57), channel_id=1, source_target_pairs={{0,2},{2,0},{1,3},{3,1},{4,6},{6,4},{5,7},{7,5},{8,10},{10,8},{9,1... | collective-permute-start | bytes 786440 | tf_op jit(solution)/shard_map/ppermute | solution.py:323
  120.5 9.7 %copy-start.11 = (bf16[2,2,128,256]{3,2,1,0:T(8,128)(2,1)S(1)}, bf16[2,2,128,256]{3,2,1,0:T(8,128)(2,1)}, u32[]{:S(2)}) copy-start(bf16[2,2,128,256]{3,2,1,0:T(8,128)(2,1)} %get-tuple-element.58) | copy-start | bytes 786436
  120.5 9.7 %copy-start.12 = (bf16[2,2,128,256]{3,2,1,0:T(8,128)(2,1)S(1)}, bf16[2,2,128,256]{3,2,1,0:T(8,128)(2,1)}, u32[]{:S(2)}) copy-start(bf16[2,2,128,256]{3,2,1,0:T(8,128)(2,1)} %get-tuple-element.56) | copy-start | bytes 786436
  120.5 9.9 %copy-start.30 = (bf16[2,128,256]{2,1,0:T(8,128)(2,1)S(1)}, bf16[2,128,256]{2,1,0:T(8,128)(2,1)}, u32[]{:S(2)}) copy-start(bf16[2,128,256]{2,1,0:T(8,128)(2,1)} %get-tuple-element.54) | copy-start | bytes 393220
  120.5 11.2 %copy-start.29 = (bf16[2,128,256]{2,1,0:T(8,128)(2,1)S(1)}, bf16[2,128,256]{2,1,0:T(8,128)(2,1)}, u32[]{:S(2)}) copy-start(bf16[2,128,256]{2,1,0:T(8,128)(2,1)} %get-tuple-element.55) | copy-start | bytes 393220
  126.0 14.4 %copy-start.8 = (f32[256,2048]{1,0:T(8,128)S(1)}, f32[256,2048]{1,0:T(8,128)}, u32[]{:S(2)}) copy-start(f32[256,2048]{1,0:T(8,128)} %get-tuple-element.51) | copy-start | bytes 6291460
  126.0 14.4 %collective-permute-start.31 = (bf16[256,2048]{1,0:T(8,128)(2,1)}, bf16[256,2048]{1,0:T(8,128)(2,1)S(1)}, u32[]{:S(2)}, u32[]{:S(2)}) collective-permute-start(bf16[256,2048]{1,0:T(8,128)(2,1)} %get-tuple-element.52), channel_id=1, source_target_pairs={{0,1},{1,0},{2,3},{3,2},{4,5},{5,4},{6,7},{7,6},{8,9},{9,8},{10,11... | collective-permute-start | bytes 3145736 | tf_op jit(solution)/shard_map/ppermute | solution.py:221
  130.3 9.2 %collective-permute-start.36 = (bf16[2,2,128,256]{3,2,1,0:T(8,128)(2,1)S(1)}, bf16[2,2,128,256]{3,2,1,0:T(8,128)(2,1)S(1)}, u32[]{:S(2)}, u32[]{:S(2)}) collective-permute-start(bf16[2,2,128,256]{3,2,1,0:T(8,128)(2,1)S(1)} %broadcast_select_fusion), channel_id=1, source_target_pairs={{0,4},{4,0},{8,12},{12,8},{1,5},{5,1},{9,13},{13,9},{2,6},{6,2},{1... | collective-permute-start | bytes 786440 | tf_op jit(solution)/shard_map/ppermute | solution.py:323
  130.4 24.3 %collective-permute-start.33 = (bf16[2,128,256]{2,1,0:T(8,128)(2,1)S(1)}, bf16[2,128,256]{2,1,0:T(8,128)(2,1)S(1)}, u32[]{:S(2)}, u32[]{:S(2)}) collective-permute-start(bf16[2,128,256]{2,1,0:T(8,128)(2,1)S(1)} %copy-done.30), channel_id=1, source_target_pairs={{2,0},{4,2},{6,4},{8,6},{10,8},{12,10},{14,12},{3,1},{5,3},{7,5},{... | collective-permute-start | bytes 393224 | tf_op jit(solution)/shard_map/ppermute | solution.py:441
  131.7 23.0 %collective-permute-start.34 = (bf16[2,128,256]{2,1,0:T(8,128)(2,1)S(1)}, bf16[2,128,256]{2,1,0:T(8,128)(2,1)S(1)}, u32[]{:S(2)}, u32[]{:S(2)}) collective-permute-start(bf16[2,128,256]{2,1,0:T(8,128)(2,1)S(1)} %copy-done.29), channel_id=1, source_target_pairs={{0,2},{2,4},{4,6},{6,8},{8,10},{10,12},{12,14},{1,3},{3,5},{5,7},{... | collective-permute-start | bytes 393224 | tf_op jit(solution)/shard_map/ppermute | solution.py:441
  139.8 13.0 %collective-permute-start.37 = (bf16[2,2,128,256]{3,2,1,0:T(8,128)(2,1)S(1)}, bf16[2,2,128,256]{3,2,1,0:T(8,128)(2,1)S(1)}, u32[]{:S(2)}, u32[]{:S(2)}) collective-permute-start(bf16[2,2,128,256]{3,2,1,0:T(8,128)(2,1)S(1)} %get-tuple-element.72), channel_id=1, source_target_pairs={{0,8},{4,12},{8,0},{12,4},{1,9},{5,13},{9,1},{13,5},{2,10},{6,14},... | collective-permute-start | bytes 786440 | tf_op jit(solution)/shard_map/ppermute | solution.py:323
  140.7 13.0 %collective-permute-start.32 = (bf16[128,2048]{1,0:T(8,128)(2,1)S(1)}, bf16[128,2048]{1,0:T(8,128)(2,1)S(1)}, u32[]{:S(2)}, u32[]{:S(2)}) collective-permute-start(bf16[128,2048]{1,0:T(8,128)(2,1)S(1)} %slice.115), channel_id=1, source_target_pairs={{0,16},{16,0},{1,17},{17,1},{2,18},{18,2},{3,19},{19,3},{4,20},{20... | collective-permute-start | bytes 1572872 | tf_op jit(solution)/shard_map/ppermute | solution.py:221
  159.3 2.1 %collective-permute-start.38 = (bf16[256,1024]{1,0:T(8,128)(2,1)}, bf16[256,1024]{1,0:T(8,128)(2,1)S(1)}, u32[]{:S(2)}, u32[]{:S(2)}) collective-permute-start(bf16[256,1024]{1,0:T(8,128)(2,1)} %get-tuple-element.67), channel_id=1, source_target_pairs={{0,1},{1,0},{2,3},{3,2},{4,5},{5,4},{6,7},{7,6},{8,9},{9,8},{10,11... | collective-permute-start | bytes 1572872 | tf_op jit(solution)/shard_map/ppermute | solution.py:221
  162.6 13.0 %copy-start.13 = (f32[256,1024]{1,0:T(8,128)S(1)}, f32[256,1024]{1,0:T(8,128)}, u32[]{:S(2)}) copy-start(f32[256,1024]{1,0:T(8,128)} %get-tuple-element.66) | copy-start | bytes 3145732
  166.0 14.6 %copy-start.14 = (f32[256,1024]{1,0:T(8,128)S(1)}, f32[256,1024]{1,0:T(8,128)}, u32[]{:S(2)}) copy-start(f32[256,1024]{1,0:T(8,128)} %get-tuple-element.70) | copy-start | bytes 3145732
  166.0 2.1 %collective-permute-start.40 = (bf16[256,1024]{1,0:T(8,128)(2,1)}, bf16[256,1024]{1,0:T(8,128)(2,1)S(1)}, u32[]{:S(2)}, u32[]{:S(2)}) collective-permute-start(bf16[256,1024]{1,0:T(8,128)(2,1)} %get-tuple-element.71), channel_id=1, source_target_pairs={{0,1},{1,0},{2,3},{3,2},{4,5},{5,4},{6,7},{7,6},{8,9},{9,8},{10,11... | collective-permute-start | bytes 1572872 | tf_op jit(solution)/shard_map/ppermute | solution.py:221
  166.4 9.2 %collective-permute-start.39 = (bf16[128,1024]{1,0:T(8,128)(2,1)S(1)}, bf16[128,1024]{1,0:T(8,128)(2,1)S(1)}, u32[]{:S(2)}, u32[]{:S(2)}) collective-permute-start(bf16[128,1024]{1,0:T(8,128)(2,1)S(1)} %add_convert_fusion.1), channel_id=1, source_target_pairs={{0,16},{16,0},{1,17},{17,1},{2,18},{18,2},{3,19},{19,3},{4,20},{20... | collective-permute-start | bytes 786440 | tf_op jit(solution)/shard_map/ppermute | solution.py:221
  169.3 11.4 %collective-permute-start.41 = (bf16[128,1024]{1,0:T(8,128)(2,1)S(1)}, bf16[128,1024]{1,0:T(8,128)(2,1)S(1)}, u32[]{:S(2)}, u32[]{:S(2)}) collective-permute-start(bf16[128,1024]{1,0:T(8,128)(2,1)S(1)} %add_convert_fusion), channel_id=1, source_target_pairs={{0,16},{16,0},{1,17},{17,1},{2,18},{18,2},{3,19},{19,3},{4,20},{20... | collective-permute-start | bytes 786440 | tf_op jit(solution)/shard_map/ppermute | solution.py:221
  (12 other events, 16.1 us)

commit v5 on v4

--- a/solution.py
+++ b/solution.py
@@ -185,7 +185,7 @@
         target[...] = total.astype(target.dtype)
 
 
-def first_key_kernel(chosen, dkv, near_p, near_m, far_p, far_m, part, wkv, wkvf, keep, send, kg):
+def key_part_kernel(chosen, dkv, near_p, near_m, far_p, far_m, part, wkv, wkvf, keep, send, kg):
     t = position()
     last = last_block()
 
@@ -465,7 +465,8 @@
     arrived = []
     far_p, far_m = trade(dfar_p, dfar_m, t, owner, True, arrived, (out_parts[1],), pack)
     total = out_parts[0] + swap(out_parts[1], "c").astype(F32)
-    combined = total[:BLK] + swap(total[BLK:].astype(BF16), "x").astype(F32)
+    combined_back = swap(total[BLK:].astype(BF16), "x")
+    combined = total[:BLK] + combined_back.astype(F32)
     combined = combined.astype(BF16)
 
     chunk = 256
@@ -498,7 +499,6 @@
     )(after(gq, arrived[1]).reshape(2, 2, rows, REP * HDIM), weight, weight)
 
     chunk = width // 4
-    halves = (jax.ShapeDtypeStruct((rows, 2 * chunk), F32), jax.ShapeDtypeStruct((rows, 2 * chunk), BF16))
     key_shape = (2, 2, rows, 2 * HDIM)
 
     def sections(start):
@@ -508,33 +508,21 @@
             pl.BlockSpec((chunk, 2 * HDIM), lambda k: (k + start, 0)),
         ]
 
-    *first_half, key_grads = pl.pallas_call(
-        first_key_kernel,
-        grid=(2,),
-        out_shape=halves + (jax.ShapeDtypeStruct(key_shape, BF16),),
+    key_parts = pl.pallas_call(
+        key_part_kernel,
+        grid=(4,),
+        out_shape=partial,
         in_specs=[smem()]
         + [fixed(v) for v in (dkv.shape, near_shape.shape, near_shape.shape)]
         + [fixed(far_shape.shape)] * 2
         + sections(0),
-        out_specs=[pl.BlockSpec((rows, chunk), lambda k: (0, k))] * 2 + [fixed(key_shape)],
+        out_specs=[pl.BlockSpec((rows, chunk), lambda k: (0, k))] * 2,
+        scratch_shapes=[pltpu.VMEM(key_shape, BF16)],
         cost_estimate=cost(5 * 10**8, 8 * 2**20),
         compiler_params=params(),
-        name="first_key",
-    )(chosen, dkv, near_p, near_m, after(far_p, combined), far_m, part, kv_plain, kv_flipped)
-    left, other, _ = finish(*first_half)
-    right, _, _ = finish(
-        *pl.pallas_call(
-            project_keys,
-            grid=(2,),
-            out_shape=halves,
-            in_specs=[fixed(key_shape)] + sections(2),
-            out_specs=[pl.BlockSpec((rows, chunk), lambda k: (0, k))] * 2,
-            cost_estimate=cost(5 * 10**8, 5 * 2**20),
-            compiler_params=params(),
-            name="second_key",
-        )(after(key_grads, other), part, kv_plain, kv_flipped)
-    )
-    grad_norm = jnp.concatenate([left, right], axis=1)
+        name="key_part",
+    )(chosen, dkv, near_p, near_m, after(far_p, combined_back), far_m, part, kv_plain, kv_flipped)
+    grad_norm, _, _ = finish(*key_parts)
 
     u = hidden.astype(F32)
     inv_rms = lax.rsqrt(jnp.mean(u * u, axis=1, keepdims=True) + EPS)

time: 183 us -> 182 us (level)
    pallas_call x2 -> x1, Pallas kernels: 7.43 us -> 6.41 us  [body(): pl.pallas_call(key_part_kernel, grid=(4,), out_shape=partial, in_specs=[s...]
    ppermute x15 -> x13, waiting for transfers between devices: 18.8 us -> 19.8 us  [swap(): return lax.ppermute(value, axis, [(0, 1), (1, 0)])]
    ppermute x15 -> x13, starting transfers between devices: 14.3 us -> 13.9 us  [swap(): return lax.ppermute(value, axis, [(0, 1), (1, 0)])]
    unnamed x68 -> x66, local copies, waits for them, and re-layouts: 5.65 us -> 5.58 us
  transfers between devices with their start and end apart: 42 -> 40, of which waited for: 17 -> 15; matrix products, arithmetic and copies ran while one was open for 12% -> 11% of each run, Pallas kernels for 14% -> 14%
where the time goes in v5:
time: 182 us; the launch traced here: 181 us
  starting transfers between devices  55.9 us (31%)
  waiting for transfers between devices  51.1 us (28%)
  Pallas kernels  42.5 us (23%)
  local copies, waits for them, and re-layouts  12.5 us (7%)
  other arithmetic  11.7 us (6%)
  matrix products  4.6 us (3%)
  between operations  2.5 us (1%)
    ppermute x13, waiting for transfers between devices, swap(): return lax.ppermute(value, axis, [(0, 1), (1, 0)])  19.8 us
    ppermute x7, waiting for transfers between devices, ring(): lax.ppermute(value, axis, [(i, (i + 1) % count) for i in range(count)])  15 us
    ppermute x13, starting transfers between devices, swap(): return lax.ppermute(value, axis, [(0, 1), (1, 0)])  13.9 us
    pallas_call x1, Pallas kernels, body(): pl.pallas_call(attention_kernel, grid=(2,), out_shape=(jax.ShapeDtypeStru...  10.7 us
    ppermute x6, starting transfers between devices, trade(): got = lax.ppermute(packed, axis, pairs)  10.1 us
    pallas_call x1, Pallas kernels, body(): pl.pallas_call(query_part_kernel, grid=(steps,), out_shape=(jax.ShapeDtyp...  9.81 us
    ppermute x6, waiting for transfers between devices, trade(): got = lax.ppermute(packed, axis, pairs)  8.37 us
    ppermute x7, starting transfers between devices, ring(): lax.ppermute(value, axis, [(i, (i + 1) % count) for i in range(count)])  8.33 us
  transfers between devices with their start and end apart: 40, of which 15 were waited for; matrix products, arithmetic and copies ran while one was open for 11% of the time, Pallas kernels for 14%

profile of v5, /device:TPU:0, one launch (start us, length us, event | category | flops | bytes accessed | tf_op | source)
XLA Modules:
  0.0 180.8 jit_solution(18172996101714176347)
XLA Ops:
  0.7 3.0 %collective-permute-start = (bf16[128,2048]{1,0:T(8,128)(2,1)}, bf16[128,2048]{1,0:T(8,128)(2,1)S(1)}, u32[]{:S(2)}, u32[]{:S(2)}) collective-permute-start(bf16[128,2048]{1,0:T(8,128)(2,1)} %h00.1), channel_id=1, source_target_pairs={{0,16},{16,0},{1,17},{17,1},{2,18},{18,2},{3,19},{19,3},{4,20},{20... | collective-permute-start | bytes 1572872 | tf_op jit(solution)/shard_map/ppermute | solution.py:221
  3.7 1.0 constant_dynamic-slice_fusion
  4.7 0.8 constant_dynamic-slice_fusion.2
  6.1 1.1 collective-permute-done.4
  7.4 0.8 constant_dynamic-update-slice_fusion.7
  8.2 1.5 collective-permute-start.5
  9.9 1.6 collective-permute-start.6
  12.9 2.9 %collective-permute-done.h01 = bf16[128,2048]{1,0:T(8,128)(2,1)S(1)} collective-permute-done((bf16[128,2048]{1,0:T(8,128)(2,1)}, bf16[128,2048]{1,0:T(8,128)(2,1)S(1)}, u32[]{:S(2)}, u32[]{:S(2)}) %collective-permute-start) | collective-permute-done | bytes 524320 | tf_op jit(solution)/shard_map/ppermute | solution.py:221
  15.8 1.7 collective-permute-start.1
  17.6 1.6 fusion.14
  20.5 1.8 collective-permute-start.11
  22.4 1.0 collective-permute-done.6
  24.0 1.5 collective-permute-start.7
  25.6 0.8 constant_dynamic-update-slice_fusion.6
  26.3 7.7 %collective-permute-done.7 = bf16[256,768]{1,0:T(8,128)(2,1)S(1)} collective-permute-done((bf16[256,768]{1,0:T(8,128)(2,1)S(1)}, bf16[256,768]{1,0:T(8,128)(2,1)S(1)}, u32[]{:S(2)}, u32[]{:S(2)}) %collective-permute-start.7) | collective-permute-done | bytes 393248 | tf_op jit(solution)/shard_map/ppermute | solution.py:234
  34.0 1.8 collective-permute-done.8
  35.8 1.5 collective-permute-start.9
  37.3 0.8 constant_dynamic-update-slice_fusion.5
  38.1 0.8 constant_dynamic-update-slice_fusion.4
  38.9 0.8 constant_dynamic-update-slice_fusion.3
  39.7 0.8 copy-done.16
  40.5 0.8 copy-done.21
  41.3 4.9 %norm.1 = bf16[2,512,2048]{2,1,0:T(8,128)(2,1)} custom-call(bf16[128,2048]{1,0:T(8,128)(2,1)} %h00.1, bf16[128,2048]{1,0:T(8,128)(2,1)} %copy-done.15, bf16[128,2048]{1,0:T(8,128)(2,1)} %copy-done.16, bf16[128,2048]{1,0:T(8,128)(2,1)} %copy-done.21), custom_call_target="tpu_custom_call" | custom-call | flops 1000000000 | bytes 6291456 | tf_op jit(solution)/shard_map/norm/pallas_call | solution.py:365
  46.2 1.1 collective-permute-done.10
  47.3 1.5 collective-permute-start.12
  48.9 1.3 collective-permute-start.20
  50.3 1.3 collective-permute-start.16
  51.6 1.0 constant_dynamic-update-slice_fusion.2
  52.7 3.5 %collective-permute-done.12 = bf16[256,768]{1,0:T(8,128)(2,1)S(1)} collective-permute-done((bf16[256,768]{1,0:T(8,128)(2,1)S(1)}, bf16[256,768]{1,0:T(8,128)(2,1)S(1)}, u32[]{:S(2)}, u32[]{:S(2)}) %collective-permute-start.12) | collective-permute-done | bytes 393248 | tf_op jit(solution)/shard_map/ppermute | solution.py:234
  56.2 1.3 convolution_convert_fusion
  57.5 0.7 copy-done.24
  58.5 1.6 collective-permute-start.21
  60.1 2.4 %collective-permute-done.16 = bf16[256,1024]{1,0:T(8,128)(2,1)S(1)} collective-permute-done((bf16[256,1024]{1,0:T(8,128)(2,1)S(1)}, bf16[256,1024]{1,0:T(8,128)(2,1)S(1)}, u32[]{:S(2)}, u32[]{:S(2)}) %collective-permute-start.16) | collective-permute-done | bytes 524320 | tf_op jit(solution)/shard_map/ppermute | solution.py:281
  62.7 0.7 collective-permute-start.17
  63.4 2.9 %collective-permute-start.18 = (bf16[256,1024]{1,0:T(8,128)(2,1)S(1)}, bf16[256,1024]{1,0:T(8,128)(2,1)S(1)}, u32[]{:S(2)}, u32[]{:S(2)}) collective-permute-start(bf16[256,1024]{1,0:T(8,128)(2,1)S(1)} %get-tuple-element.39.refs_0_), channel_id=1, source_target_pairs={{0,2},{2,0},{4,6},{6,4},{13,15},{15,13},{9,11},{11,9},{20,22},{22,... | collective-permute-start | bytes 1572872 | tf_op jit(solution)/shard_map/ppermute | solution.py:289
  67.0 2.9 %collective-permute-start.23 = (bf16[256,1024]{1,0:T(8,128)(2,1)S(1)}, bf16[256,1024]{1,0:T(8,128)(2,1)S(1)}, u32[]{:S(2)}, u32[]{:S(2)}) collective-permute-start(bf16[256,1024]{1,0:T(8,128)(2,1)S(1)} %get-tuple-element.42.refs_2_), channel_id=1, source_target_pairs={{0,2},{2,0},{4,6},{6,4},{13,15},{15,13},{9,11},{11,9},{20,22},{22,... | collective-permute-start | bytes 1572872 | tf_op jit(solution)/shard_map/ppermute | solution.py:289
  70.2 3.8 %collective-permute-start.29 = (bf16[2,2,128,256]{3,2,1,0:T(8,128)(2,1)S(1)}, bf16[2,2,128,256]{3,2,1,0:T(8,128)(2,1)S(1)}, u32[]{:S(2)}, u32[]{:S(2)}) collective-permute-start(bf16[2,2,128,256]{3,2,1,0:T(8,128)(2,1)S(1)} %broadcast_select_fusion.2), channel_id=1, source_target_pairs={{0,4},{4,0},{8,12},{12,8},{1,5},{5,1},{9,13},{13,9},{2,6},{6,2},{1... | collective-permute-start | bytes 786440 | tf_op jit(solution)/shard_map/ppermute | solution.py:323
  75.2 4.9 %collective-permute-done.23.refs_6_ = bf16[256,1024]{1,0:T(8,128)(2,1)S(1)} collective-permute-done((bf16[256,1024]{1,0:T(8,128)(2,1)S(1)}, bf16[256,1024]{1,0:T(8,128)(2,1)S(1)}, u32[]{:S(2)}, u32[]{:S(2)}) %collective-permute-start.23) | collective-permute-done | bytes 524320 | tf_op jit(solution)/shard_map/ppermute | solution.py:289
  81.8 1.3 collective-permute-start.30
  84.2 1.5 collective-permute-start.26
  85.7 3.3 %fusion.2 = bf16[1024,512]{1,0:T(8,128)(2,1)} fusion(bf16[1024,2048]{1,0:T(8,128)(2,1)S(1)} %bitcast.20, bf16[2048,768]{1,0:T(8,128)(2,1)S(1)} %constant_dynamic-update-slice_fusion.w.wm), kind=kOutput, calls=%fused_computation.3 | convolution fusion | flops 2148007936 | bytes 7340032 | tf_op jit(solution)/shard_map/dot_general | solution.py:22
  89.1 2.9 %collective-permute-start.27 = (bf16[2,128,256]{2,1,0:T(8,128)(2,1)S(1)}, bf16[2,128,256]{2,1,0:T(8,128)(2,1)S(1)}, u32[]{:S(2)}, u32[]{:S(2)}) collective-permute-start(bf16[2,128,256]{2,1,0:T(8,128)(2,1)S(1)} %get-tuple-element.84), channel_id=1, source_target_pairs={{0,2},{2,4},{4,6},{6,8},{8,10},{10,12},{12,14},{1,3},{3,5},{5,7},{... | collective-permute-start | bytes 393224 | tf_op jit(solution)/shard_map/ppermute | solution.py:387
  92.0 5.1 %collective-permute-done.30 = bf16[2,2,128,256]{3,2,1,0:T(8,128)(2,1)S(1)} collective-permute-done((bf16[2,2,128,256]{3,2,1,0:T(8,128)(2,1)S(1)}, bf16[2,2,128,256]{3,2,1,0:T(8,128)(2,1)S(1)}, u32[]{:S(2)}, u32[]{:S(2)}) %collective-permute-start.30) | collective-permute-done | bytes 262176 | tf_op jit(solution)/shard_map/ppermute | solution.py:323
  97.1 1.5 collective-permute-start.28
  98.6 0.9 add_select_fusion.6
  99.5 0.8 copy-done.22
  100.3 0.8 copy-done.23
  101.2 5.1 %grad_att.1 = (bf16[512,512]{1,0:T(8,128)(2,1)}, bf16[512,2048]{1,0:T(8,128)(2,1)}) custom-call(bf16[128,2048]{1,0:T(8,128)(2,1)} %c00.1, bf16[128,2048]{1,0:T(8,128)(2,1)} %copy-done.17, bf16[128,2048]{1,0:T(8,128)(2,1)} %copy-done.20, bf16[128,2048]{1,0:T(8,128)(2,1)} %copy-done.22, bf16[256,1024]{1,0:T(8,128)(2,1)} %copy-done.11, ...), custom_call_target="tpu_custom_call" | custom-call | flops 1000000000 | bytes 9437184 | tf_op jit(solution)/shard_map/grad_att/pallas_call | solution.py:400
  107.0 10.7 %attention.1 = (bf16[2,2,2,128,512]{4,3,2,1,0:T(8,128)(2,1)}, bf16[2,2,2,128,512]{4,3,2,1,0:T(8,128)(2,1)}, f32[2,2,2,128,256]{4,3,2,1,0:T(8,128)}, bf16[2,128,2...) custom-call(s32[2]{0:T(128)} %pad_add_fusion.chosen, ...), custom_call_target="tpu_custom_call" | custom-call | flops 8000000000 | bytes 10485760 | tf_op jit(solution)/shard_map/attention/pallas_call | solution.py:421
  117.7 2.7 %collective-permute-start.35 = (bf16[2,2,128,256]{3,2,1,0:T(8,128)(2,1)}, bf16[2,2,128,256]{3,2,1,0:T(8,128)(2,1)S(1)}, u32[]{:S(2)}, u32[]{:S(2)}) collective-permute-start(bf16[2,2,128,256]{3,2,1,0:T(8,128)(2,1)} %get-tuple-element.53), channel_id=1, source_target_pairs={{0,2},{2,0},{1,3},{3,1},{4,6},{6,4},{5,7},{7,5},{8,10},{10,8},{9,1... | collective-permute-start | bytes 786440 | tf_op jit(solution)/shard_map/ppermute | solution.py:323
  120.4 5.5 %output.1 = (f32[256,2048]{1,0:T(8,128)}, bf16[256,2048]{1,0:T(8,128)(2,1)}) custom-call(bf16[2,2,256,512]{3,2,1,0:T(8,128)(2,1)} %bitcast.26, bf16[512,2048]{1,0:T(8,128)(2,1)} %get-tuple-element.46.w), custom_call_target="tpu_custom_call" | custom-call | flops 2000000000 | bytes 7340032 | tf_op jit(solution)/shard_map/output/pallas_call | solution.py:452
  126.0 4.2 %collective-permute-start.31 = (bf16[256,2048]{1,0:T(8,128)(2,1)}, bf16[256,2048]{1,0:T(8,128)(2,1)S(1)}, u32[]{:S(2)}, u32[]{:S(2)}) collective-permute-start(bf16[256,2048]{1,0:T(8,128)(2,1)} %get-tuple-element.48), channel_id=1, source_target_pairs={{0,1},{1,0},{2,3},{3,2},{4,5},{5,4},{6,7},{7,6},{8,9},{9,8},{10,11... | collective-permute-start | bytes 3145736 | tf_op jit(solution)/shard_map/ppermute | solution.py:221
  130.4 1.3 collective-permute-start.33
  131.7 4.6 %collective-permute-start.34 = (bf16[2,128,256]{2,1,0:T(8,128)(2,1)S(1)}, bf16[2,128,256]{2,1,0:T(8,128)(2,1)S(1)}, u32[]{:S(2)}, u32[]{:S(2)}) collective-permute-start(bf16[2,128,256]{2,1,0:T(8,128)(2,1)S(1)} %copy-done.28), channel_id=1, source_target_pairs={{0,2},{2,4},{4,6},{6,8},{8,10},{10,12},{12,14},{1,3},{3,5},{5,7},{... | collective-permute-start | bytes 393224 | tf_op jit(solution)/shard_map/ppermute | solution.py:441
  136.2 3.3 %collective-permute-done.36 = bf16[2,2,128,256]{3,2,1,0:T(8,128)(2,1)S(1)} collective-permute-done((bf16[2,2,128,256]{3,2,1,0:T(8,128)(2,1)S(1)}, bf16[2,2,128,256]{3,2,1,0:T(8,128)(2,1)S(1)}, u32[]{:S(2)}, u32[]{:S(2)}) %collective-permute-start.36) | collective-permute-done | bytes 262176 | tf_op jit(solution)/shard_map/ppermute | solution.py:323
  140.7 2.3 %collective-permute-start.32 = (bf16[128,2048]{1,0:T(8,128)(2,1)S(1)}, bf16[128,2048]{1,0:T(8,128)(2,1)S(1)}, u32[]{:S(2)}, u32[]{:S(2)}) collective-permute-start(bf16[128,2048]{1,0:T(8,128)(2,1)S(1)} %slice.101), channel_id=1, source_target_pairs={{0,16},{16,0},{1,17},{17,1},{2,18},{18,2},{3,19},{19,3},{4,20},{20... | collective-permute-start | bytes 1572872 | tf_op jit(solution)/shard_map/ppermute | solution.py:221
  143.0 9.8 %query_part.1 = (f32[2,256,2048]{2,1,0:T(8,128)}, bf16[2048,256]{1,0:T(8,128)(2,1)}, bf16[2048,256]{1,0:T(8,128)(2,1)}) custom-call(bf16[2,2,256,512]{3,2,1,0:T(8,128)(2,1)} %bitcast.24, bf16[2048,768]{1,0:T(8,128)(2,1)} %copy-done.6, bf16[2048,768]{1,0:T(8,128)(2,1)} %copy-done.6), custom_call_target="tpu_custom_call" | custom-call | flops 3000000000 | bytes 13631488 | tf_op jit(solution)/shard_map/query_part/pallas_call | solution.py:478
  152.8 0.9 add_select_fusion
  154.4 6.4 %key_part.1 = (f32[256,2048]{1,0:T(8,128)}, bf16[256,2048]{1,0:T(8,128)(2,1)}) custom-call(s32[2]{0:T(128)} %pad_add_fusion.chosen, f32[2,2,2,128,256]{4,3,2,1,0:T(8,128)} %get-tuple-element.49.dkv, bf16[2,128,256]{2,1,0:T(8,128)(2,1)} %copy-done.26, bf16[2,128,256]{2,1,0:T(8,128)(2,1)} %copy-done.27, bf16[2,2,128,256]{3,2,1,0:T(8,128)(2,1)} %get-tuple-element.56.far_p, ...), custom_call_target="tpu_custom_call" | custom-call | flops 500000000 | bytes 8388608 | tf_op jit(solution)/shard_map/key_part/pallas_call | solution.py:511
  161.1 2.7 %collective-permute-done.38 = bf16[256,2048]{1,0:T(8,128)(2,1)S(1)} collective-permute-done((bf16[256,2048]{1,0:T(8,128)(2,1)}, bf16[256,2048]{1,0:T(8,128)(2,1)S(1)}, u32[]{:S(2)}, u32[]{:S(2)}) %collective-permute-start.38) | collective-permute-done | bytes 1048608 | tf_op jit(solution)/shard_map/ppermute | solution.py:221
  163.8 1.4 add_convert_fusion
  165.3 0.9 fusion.12
  166.2 13.0 %collective-permute-done.39 = bf16[128,2048]{1,0:T(8,128)(2,1)S(1)} collective-permute-done((bf16[128,2048]{1,0:T(8,128)(2,1)S(1)}, bf16[128,2048]{1,0:T(8,128)(2,1)S(1)}, u32[]{:S(2)}, u32[]{:S(2)}) %collective-permute-start.39) | collective-permute-done | bytes 524320 | tf_op jit(solution)/shard_map/ppermute | solution.py:221
  179.6 1.2 fusion.10
  (135 shorter events, 12.2 us)
Async XLA Ops:
  0.6 10.9 %copy-start = (bf16[128,2048]{1,0:T(8,128)(2,1)S(1)}, bf16[128,2048]{1,0:T(8,128)(2,1)}, u32[]{:S(2)}) copy-start(bf16[128,2048]{1,0:T(8,128)(2,1)} %h00.1) | copy-start | bytes 1572868
  0.6 16.9 %copy-start.25 = (bf16[128,2048]{1,0:T(8,128)(2,1)S(1)}, bf16[128,2048]{1,0:T(8,128)(2,1)}, u32[]{:S(2)}) copy-start(bf16[128,2048]{1,0:T(8,128)(2,1)} %param.9) | copy-start | bytes 1572868
  0.7 10.9 %copy-start.32 = (s32[2]{0:T(128)S(1)}, s32[2]{0:T(128)}, u32[]{:S(2)}) copy-start(s32[2]{0:T(128)} %param.10) | copy-start | bytes 28
  0.7 15.1 %collective-permute-start = (bf16[128,2048]{1,0:T(8,128)(2,1)}, bf16[128,2048]{1,0:T(8,128)(2,1)S(1)}, u32[]{:S(2)}, u32[]{:S(2)}) collective-permute-start(bf16[128,2048]{1,0:T(8,128)(2,1)} %h00.1), channel_id=1, source_target_pairs={{0,16},{16,0},{1,17},{17,1},{2,18},{18,2},{3,19},{19,3},{4,20},{20... | collective-permute-start | bytes 1572872 | tf_op jit(solution)/shard_map/ppermute | solution.py:221
  3.7 13.9 %collective-permute-start.15 = (bf16[128,2048]{1,0:T(8,128)(2,1)}, bf16[128,2048]{1,0:T(8,128)(2,1)}, u32[]{:S(2)}, u32[]{:S(2)}) collective-permute-start(bf16[128,2048]{1,0:T(8,128)(2,1)} %param.9), channel_id=1, source_target_pairs={{0,1},{1,0},{2,3},{3,2},{4,5},{5,4},{6,7},{7,6},{8,9},{9,8},{10,11... | collective-permute-start | bytes 1572872 | tf_op jit(solution)/shard_map/ppermute | solution.py:221
  5.5 1.6 collective-permute-start.4
  7.2 13.3 %copy-start.14 = (bf16[128,2048]{1,0:T(8,128)(2,1)S(1)}, bf16[128,2048]{1,0:T(8,128)(2,1)}, u32[]{:S(2)}) copy-start(bf16[128,2048]{1,0:T(8,128)(2,1)} %c00.1) | copy-start | bytes 1572868
  8.2 1.7 copy-start.4
  8.2 14.1 %collective-permute-start.5 = (bf16[256,768]{1,0:T(8,128)(2,1)}, bf16[256,768]{1,0:T(8,128)(2,1)S(1)}, u32[]{:S(2)}, u32[]{:S(2)}) collective-permute-start(bf16[256,768]{1,0:T(8,128)(2,1)} %get-tuple-element.77), channel_id=1, source_target_pairs={{0,2},{2,0},{1,3},{3,1},{4,6},{6,4},{5,7},{7,5},{8,10},{10,8},{9,1... | collective-permute-start | bytes 1179656 | tf_op jit(solution)/shard_map/ppermute | solution.py:234
  9.9 13.5 %collective-permute-start.6 = (bf16[256,768]{1,0:T(8,128)(2,1)}, bf16[256,768]{1,0:T(8,128)(2,1)S(1)}, u32[]{:S(2)}, u32[]{:S(2)}) collective-permute-start(bf16[256,768]{1,0:T(8,128)(2,1)} %get-tuple-element.77), channel_id=1, source_target_pairs={{0,4},{4,8},{8,12},{12,0},{1,5},{5,9},{9,13},{13,1},{2,6},{6,10},{... | collective-permute-start | bytes 1179656 | tf_op jit(solution)/shard_map/ppermute | solution.py:234
  11.5 28.2 %collective-permute-start.2 = (bf16[128,2048]{1,0:T(8,128)(2,1)S(1)}, bf16[128,2048]{1,0:T(8,128)(2,1)S(1)}, u32[]{:S(2)}, u32[]{:S(2)}) collective-permute-start(bf16[128,2048]{1,0:T(8,128)(2,1)S(1)} %copy-done), channel_id=1, source_target_pairs={{0,1},{1,0},{2,3},{3,2},{4,5},{5,4},{6,7},{7,6},{8,9},{9,8},{10,11... | collective-permute-start | bytes 1572872 | tf_op jit(solution)/shard_map/ppermute | solution.py:221
  15.8 23.9 %copy-start.15 = (bf16[128,2048]{1,0:T(8,128)(2,1)}, bf16[128,2048]{1,0:T(8,128)(2,1)S(1)}, u32[]{:S(2)}) copy-start(bf16[128,2048]{1,0:T(8,128)(2,1)S(1)} %collective-permute-done.h01) | copy-start | bytes 1572868
  15.8 3.6 %collective-permute-start.1 = (f32[8,128]{1,0:T(8,128)S(1)}, f32[8,128]{1,0:T(8,128)S(1)}, u32[]{:S(2)}, u32[]{:S(2)}) collective-permute-start(f32[8,128]{1,0:T(8,128)S(1)} %broadcast_in_dim.125), channel_id=1, source_target_pairs={{0,16},{16,0},{1,17},{17,1},{2,18},{18,2},{3,19},{19,3},{4,20},{20... | collective-permute-start | bytes 12296 | tf_op jit(solution)/shard_map/ppermute | solution.py:221
  17.5 22.1 %collective-permute-start.3 = (bf16[128,2048]{1,0:T(8,128)(2,1)S(1)}, bf16[128,2048]{1,0:T(8,128)(2,1)S(1)}, u32[]{:S(2)}, u32[]{:S(2)}) collective-permute-start(bf16[128,2048]{1,0:T(8,128)(2,1)S(1)} %collective-permute-done.h01), channel_id=1, source_target_pairs={{0,1},{1,0},{2,3},{3,2},{4,5},{5,4},{6,7},{7,6},{8,9},{9,8},{10,11... | collective-permute-start | bytes 1572872 | tf_op jit(solution)/shard_map/ppermute | solution.py:221
  20.5 25.8 %collective-permute-start.11 = (bf16[128,2048]{1,0:T(8,128)(2,1)S(1)}, bf16[128,2048]{1,0:T(8,128)(2,1)S(1)}, u32[]{:S(2)}, u32[]{:S(2)}) collective-permute-start(bf16[128,2048]{1,0:T(8,128)(2,1)S(1)} %copy-done.14), channel_id=1, source_target_pairs={{0,16},{16,0},{1,17},{17,1},{2,18},{18,2},{3,19},{19,3},{4,20},{20... | collective-permute-start | bytes 1572872 | tf_op jit(solution)/shard_map/ppermute | solution.py:221
  23.4 12.4 %collective-permute-start.8 = (bf16[256,768]{1,0:T(8,128)(2,1)S(1)}, bf16[256,768]{1,0:T(8,128)(2,1)S(1)}, u32[]{:S(2)}, u32[]{:S(2)}) collective-permute-start(bf16[256,768]{1,0:T(8,128)(2,1)S(1)} %collective-permute-done.6), channel_id=1, source_target_pairs={{0,4},{4,8},{8,12},{12,0},{1,5},{5,9},{9,13},{13,1},{2,6},{6,10},{... | collective-permute-start | bytes 1179656 | tf_op jit(solution)/shard_map/ppermute | solution.py:234
  24.0 10.0 %collective-permute-start.7 = (bf16[256,768]{1,0:T(8,128)(2,1)S(1)}, bf16[256,768]{1,0:T(8,128)(2,1)S(1)}, u32[]{:S(2)}, u32[]{:S(2)}) collective-permute-start(bf16[256,768]{1,0:T(8,128)(2,1)S(1)} %collective-permute-done.6), channel_id=1, source_target_pairs={{0,2},{2,0},{1,3},{3,1},{4,6},{6,4},{5,7},{7,5},{8,10},{10,8},{9,1... | collective-permute-start | bytes 1179656 | tf_op jit(solution)/shard_map/ppermute | solution.py:234
  35.8 11.5 %collective-permute-start.10 = (bf16[256,768]{1,0:T(8,128)(2,1)S(1)}, bf16[256,768]{1,0:T(8,128)(2,1)S(1)}, u32[]{:S(2)}, u32[]{:S(2)}) collective-permute-start(bf16[256,768]{1,0:T(8,128)(2,1)S(1)} %collective-permute-done.8), channel_id=1, source_target_pairs={{0,4},{4,8},{8,12},{12,0},{1,5},{5,9},{9,13},{13,1},{2,6},{6,10},{... | collective-permute-start | bytes 1179656 | tf_op jit(solution)/shard_map/ppermute | solution.py:234
  35.8 10.4 %collective-permute-start.9 = (bf16[256,768]{1,0:T(8,128)(2,1)S(1)}, bf16[256,768]{1,0:T(8,128)(2,1)}, u32[]{:S(2)}, u32[]{:S(2)}) collective-permute-start(bf16[256,768]{1,0:T(8,128)(2,1)S(1)} %collective-permute-done.8), channel_id=1, source_target_pairs={{0,2},{2,0},{1,3},{3,1},{4,6},{6,4},{5,7},{7,5},{8,10},{10,8},{9,1... | collective-permute-start | bytes 1179656 | tf_op jit(solution)/shard_map/ppermute | solution.py:234
  39.7 11.9 %copy-start.5 = (bf16[2048,768]{1,0:T(8,128)(2,1)S(1)}, bf16[2048,768]{1,0:T(8,128)(2,1)}, u32[]{:S(2)}) copy-start(bf16[2048,768]{1,0:T(8,128)(2,1)} %constant_dynamic-update-slice_fusion.3) | copy-start | bytes 9437188
  46.2 10.0 %copy-start.3 = (bf16[2,512,2048]{2,1,0:T(8,128)(2,1)S(1)}, bf16[2,512,2048]{2,1,0:T(8,128)(2,1)}, u32[]{:S(2)}) copy-start(bf16[2,512,2048]{2,1,0:T(8,128)(2,1)} %norm.1) | copy-start | bytes 12582916
  46.2 35.2 %copy-start.17 = (bf16[128,2048]{1,0:T(8,128)(2,1)}, bf16[128,2048]{1,0:T(8,128)(2,1)S(1)}, u32[]{:S(2)}) copy-start(bf16[128,2048]{1,0:T(8,128)(2,1)S(1)} %collective-permute-done.11.c01) | copy-start | bytes 1572868
  47.3 8.8 %collective-permute-start.12 = (bf16[256,768]{1,0:T(8,128)(2,1)S(1)}, bf16[256,768]{1,0:T(8,128)(2,1)S(1)}, u32[]{:S(2)}, u32[]{:S(2)}) collective-permute-start(bf16[256,768]{1,0:T(8,128)(2,1)S(1)} %collective-permute-done.10), channel_id=1, source_target_pairs={{0,2},{2,0},{1,3},{3,1},{4,6},{6,4},{5,7},{7,5},{8,10},{10,8},{9,1... | collective-permute-start | bytes 1179656 | tf_op jit(solution)/shard_map/ppermute | solution.py:234
  48.9 11.2 %collective-permute-start.20 = (bf16[256,1024]{1,0:T(8,128)(2,1)S(1)}, bf16[256,1024]{1,0:T(8,128)(2,1)S(1)}, u32[]{:S(2)}, u32[]{:S(2)}) collective-permute-start(bf16[256,1024]{1,0:T(8,128)(2,1)S(1)} %get-tuple-element.80), channel_id=1, source_target_pairs={{0,4},{13,9},{20,16},{25,29},{2,6},{15,11},{22,18},{27,31}} | collective-permute-start | bytes 1572872 | tf_op jit(solution)/shard_map/ppermute | solution.py:281
  50.3 12.3 %collective-permute-start.16 = (bf16[256,1024]{1,0:T(8,128)(2,1)S(1)}, bf16[256,1024]{1,0:T(8,128)(2,1)S(1)}, u32[]{:S(2)}, u32[]{:S(2)}) collective-permute-start(bf16[256,1024]{1,0:T(8,128)(2,1)S(1)} %get-tuple-element.81), channel_id=1, source_target_pairs={{0,4},{13,9},{20,16},{25,29},{2,6},{15,11},{22,18},{27,31}} | collective-permute-start | bytes 1572872 | tf_op jit(solution)/shard_map/ppermute | solution.py:281
  56.2 29.5 %copy-start.6 = (bf16[2048,768]{1,0:T(8,128)(2,1)}, bf16[2048,768]{1,0:T(8,128)(2,1)S(1)}, u32[]{:S(2)}) copy-start(bf16[2048,768]{1,0:T(8,128)(2,1)S(1)} %constant_dynamic-update-slice_fusion.w.wm) | copy-start | bytes 9437188
  58.5 7.8 %collective-permute-start.21 = (bf16[2,2,128,256]{3,2,1,0:T(8,128)(2,1)S(1)}, bf16[2,2,128,256]{3,2,1,0:T(8,128)(2,1)S(1)}, u32[]{:S(2)}, u32[]{:S(2)}) collective-permute-start(bf16[2,2,128,256]{3,2,1,0:T(8,128)(2,1)S(1)} %fusion.15), channel_id=1, source_target_pairs={{0,2},{2,0},{1,3},{3,1},{4,6},{6,4},{5,7},{7,5},{8,10},{10,8},{9,1... | collective-permute-start | bytes 786440 | tf_op jit(solution)/shard_map/ppermute | solution.py:323
  62.7 21.6 %copy-start.10 = (bf16[256,1024]{1,0:T(8,128)(2,1)}, bf16[256,1024]{1,0:T(8,128)(2,1)S(1)}, u32[]{:S(2)}) copy-start(bf16[256,1024]{1,0:T(8,128)(2,1)S(1)} %get-tuple-element.42.refs_2_) | copy-start | bytes 1572868
  62.7 21.6 %copy-start.11 = (bf16[256,1024]{1,0:T(8,128)(2,1)}, bf16[256,1024]{1,0:T(8,128)(2,1)S(1)}, u32[]{:S(2)}) copy-start(bf16[256,1024]{1,0:T(8,128)(2,1)S(1)} %get-tuple-element.39.refs_0_) | copy-start | bytes 1572868
  62.7 11.3 %collective-permute-start.17 = (bf16[256,1024]{1,0:T(8,128)(2,1)S(1)}, bf16[256,1024]{1,0:T(8,128)(2,1)S(1)}, u32[]{:S(2)}, u32[]{:S(2)}) collective-permute-start(bf16[256,1024]{1,0:T(8,128)(2,1)S(1)} %get-tuple-element.39.refs_0_), channel_id=1, source_target_pairs={{4,8},{9,5},{20,24},{25,21},{6,10},{11,7},{22,26},{27,23}} | collective-permute-start | bytes 1572872 | tf_op jit(solution)/shard_map/ppermute | solution.py:281
  63.4 11.1 %collective-permute-start.18 = (bf16[256,1024]{1,0:T(8,128)(2,1)S(1)}, bf16[256,1024]{1,0:T(8,128)(2,1)S(1)}, u32[]{:S(2)}, u32[]{:S(2)}) collective-permute-start(bf16[256,1024]{1,0:T(8,128)(2,1)S(1)} %get-tuple-element.39.refs_0_), channel_id=1, source_target_pairs={{0,2},{2,0},{4,6},{6,4},{13,15},{15,13},{9,11},{11,9},{20,22},{22,... | collective-permute-start | bytes 1572872 | tf_op jit(solution)/shard_map/ppermute | solution.py:289
  66.3 8.8 %collective-permute-start.22 = (bf16[256,1024]{1,0:T(8,128)(2,1)S(1)}, bf16[256,1024]{1,0:T(8,128)(2,1)S(1)}, u32[]{:S(2)}, u32[]{:S(2)}) collective-permute-start(bf16[256,1024]{1,0:T(8,128)(2,1)S(1)} %get-tuple-element.42.refs_2_), channel_id=1, source_target_pairs={{4,8},{9,5},{20,24},{25,21},{6,10},{11,7},{22,26},{27,23}} | collective-permute-start | bytes 1572872 | tf_op jit(solution)/shard_map/ppermute | solution.py:281
  67.0 13.0 %collective-permute-start.23 = (bf16[256,1024]{1,0:T(8,128)(2,1)S(1)}, bf16[256,1024]{1,0:T(8,128)(2,1)S(1)}, u32[]{:S(2)}, u32[]{:S(2)}) collective-permute-start(bf16[256,1024]{1,0:T(8,128)(2,1)S(1)} %get-tuple-element.42.refs_2_), channel_id=1, source_target_pairs={{0,2},{2,0},{4,6},{6,4},{13,15},{15,13},{9,11},{11,9},{20,22},{22,... | collective-permute-start | bytes 1572872 | tf_op jit(solution)/shard_map/ppermute | solution.py:289
  70.2 11.3 %collective-permute-start.29 = (bf16[2,2,128,256]{3,2,1,0:T(8,128)(2,1)S(1)}, bf16[2,2,128,256]{3,2,1,0:T(8,128)(2,1)S(1)}, u32[]{:S(2)}, u32[]{:S(2)}) collective-permute-start(bf16[2,2,128,256]{3,2,1,0:T(8,128)(2,1)S(1)} %broadcast_select_fusion.2), channel_id=1, source_target_pairs={{0,4},{4,0},{8,12},{12,8},{1,5},{5,1},{9,13},{13,9},{2,6},{6,2},{1... | collective-permute-start | bytes 786440 | tf_op jit(solution)/shard_map/ppermute | solution.py:323
  74.0 15.1 %collective-permute-start.13 = (bf16[128,2048]{1,0:T(8,128)(2,1)S(1)}, bf16[128,2048]{1,0:T(8,128)(2,1)S(1)}, u32[]{:S(2)}, u32[]{:S(2)}) collective-permute-start(bf16[128,2048]{1,0:T(8,128)(2,1)S(1)} %copy-done.14), channel_id=1, source_target_pairs={{0,1},{1,0},{2,3},{3,2},{4,5},{5,4},{6,7},{7,6},{8,9},{9,8},{10,11... | collective-permute-start | bytes 1572872 | tf_op jit(solution)/shard_map/ppermute | solution.py:221
  74.5 14.6 %copy-start.18 = (bf16[256,1024]{1,0:T(8,128)(2,1)}, bf16[256,1024]{1,0:T(8,128)(2,1)S(1)}, u32[]{:S(2)}) copy-start(bf16[256,1024]{1,0:T(8,128)(2,1)S(1)} %collective-permute-done.18.refs_4_) | copy-start | bytes 1572868
  74.5 8.6 %collective-permute-start.19 = (bf16[256,1024]{1,0:T(8,128)(2,1)S(1)}, bf16[256,1024]{1,0:T(8,128)(2,1)S(1)}, u32[]{:S(2)}, u32[]{:S(2)}) collective-permute-start(bf16[256,1024]{1,0:T(8,128)(2,1)S(1)} %collective-permute-done.17), channel_id=1, source_target_pairs={{8,12},{5,1},{24,28},{21,17},{10,14},{7,3},{26,30},{23,19}} | collective-permute-start | bytes 1572872 | tf_op jit(solution)/shard_map/ppermute | solution.py:281
  80.1 3.9 %copy-start.19 = (bf16[256,1024]{1,0:T(8,128)(2,1)}, bf16[256,1024]{1,0:T(8,128)(2,1)S(1)}, u32[]{:S(2)}) copy-start(bf16[256,1024]{1,0:T(8,128)(2,1)S(1)} %collective-permute-done.23.refs_6_) | copy-start | bytes 1572868
  80.1 3.9 %collective-permute-start.24 = (bf16[256,1024]{1,0:T(8,128)(2,1)S(1)}, bf16[256,1024]{1,0:T(8,128)(2,1)S(1)}, u32[]{:S(2)}, u32[]{:S(2)}) collective-permute-start(bf16[256,1024]{1,0:T(8,128)(2,1)S(1)} %collective-permute-done.22), channel_id=1, source_target_pairs={{8,12},{5,1},{24,28},{21,17},{10,14},{7,3},{26,30},{23,19}} | collective-permute-start | bytes 1572872 | tf_op jit(solution)/shard_map/ppermute | solution.py:281
  81.4 18.1 %collective-permute-start.14 = (bf16[128,2048]{1,0:T(8,128)(2,1)S(1)}, bf16[128,2048]{1,0:T(8,128)(2,1)S(1)}, u32[]{:S(2)}, u32[]{:S(2)}) collective-permute-start(bf16[128,2048]{1,0:T(8,128)(2,1)S(1)} %collective-permute-done.11.c01), channel_id=1, source_target_pairs={{0,1},{1,0},{2,3},{3,2},{4,5},{5,4},{6,7},{7,6},{8,9},{9,8},{10,11... | collective-permute-start | bytes 1572872 | tf_op jit(solution)/shard_map/ppermute | solution.py:221
  81.8 15.3 %collective-permute-start.30 = (bf16[2,2,128,256]{3,2,1,0:T(8,128)(2,1)S(1)}, bf16[2,2,128,256]{3,2,1,0:T(8,128)(2,1)S(1)}, u32[]{:S(2)}, u32[]{:S(2)}) collective-permute-start(bf16[2,2,128,256]{3,2,1,0:T(8,128)(2,1)S(1)} %get-tuple-element.72), channel_id=1, source_target_pairs={{0,8},{4,12},{8,0},{12,4},{1,9},{5,13},{9,1},{13,5},{2,10},{6,14},... | collective-permute-start | bytes 786440 | tf_op jit(solution)/shard_map/ppermute | solution.py:323
  83.3 5.8 %copy-start.7 = (bf16[256,1024]{1,0:T(8,128)(2,1)}, bf16[256,1024]{1,0:T(8,128)(2,1)S(1)}, u32[]{:S(2)}) copy-start(bf16[256,1024]{1,0:T(8,128)(2,1)S(1)} %add.296.refs_1_) | copy-start | bytes 1572868
  83.3 16.2 %collective-permute-start.25 = (bf16[256,1024]{1,0:T(8,128)(2,1)S(1)}, bf16[256,1024]{1,0:T(8,128)(2,1)S(1)}, u32[]{:S(2)}, u32[]{:S(2)}) collective-permute-start(bf16[256,1024]{1,0:T(8,128)(2,1)S(1)} %add.296.refs_1_), channel_id=1, source_target_pairs={{8,10},{10,8},{12,14},{14,12},{5,7},{7,5},{1,3},{3,1},{24,26},{26,... | collective-permute-start | bytes 1572872 | tf_op jit(solution)/shard_map/ppermute | solution.py:289
  84.2 4.8 %copy-start.8 = (bf16[256,1024]{1,0:T(8,128)(2,1)}, bf16[256,1024]{1,0:T(8,128)(2,1)S(1)}, u32[]{:S(2)}) copy-start(bf16[256,1024]{1,0:T(8,128)(2,1)S(1)} %add.302.refs_3_) | copy-start | bytes 1572868
  84.2 16.9 %collective-permute-start.26 = (bf16[256,1024]{1,0:T(8,128)(2,1)S(1)}, bf16[256,1024]{1,0:T(8,128)(2,1)}, u32[]{:S(2)}, u32[]{:S(2)}) collective-permute-start(bf16[256,1024]{1,0:T(8,128)(2,1)S(1)} %add.302.refs_3_), channel_id=1, source_target_pairs={{8,10},{10,8},{12,14},{14,12},{5,7},{7,5},{1,3},{3,1},{24,26},{26,... | collective-permute-start | bytes 1572872 | tf_op jit(solution)/shard_map/ppermute | solution.py:289
  89.1 10.5 %copy-start.20 = (bf16[128,2048]{1,0:T(8,128)(2,1)}, bf16[128,2048]{1,0:T(8,128)(2,1)S(1)}, u32[]{:S(2)}) copy-start(bf16[128,2048]{1,0:T(8,128)(2,1)S(1)} %collective-permute-done.13.c10) | copy-start | bytes 1572868
  89.1 17.2 %collective-permute-start.27 = (bf16[2,128,256]{2,1,0:T(8,128)(2,1)S(1)}, bf16[2,128,256]{2,1,0:T(8,128)(2,1)S(1)}, u32[]{:S(2)}, u32[]{:S(2)}) collective-permute-start(bf16[2,128,256]{2,1,0:T(8,128)(2,1)S(1)} %get-tuple-element.84), channel_id=1, source_target_pairs={{0,2},{2,4},{4,6},{6,8},{8,10},{10,12},{12,14},{1,3},{3,5},{5,7},{... | collective-permute-start | bytes 393224 | tf_op jit(solution)/shard_map/ppermute | solution.py:387
  97.1 9.2 %collective-permute-start.28 = (bf16[2,128,256]{2,1,0:T(8,128)(2,1)S(1)}, bf16[2,128,256]{2,1,0:T(8,128)(2,1)S(1)}, u32[]{:S(2)}, u32[]{:S(2)}) collective-permute-start(bf16[2,128,256]{2,1,0:T(8,128)(2,1)S(1)} %get-tuple-element.82), channel_id=1, source_target_pairs={{2,0},{4,2},{6,4},{8,6},{10,8},{12,10},{14,12},{3,1},{5,3},{7,5},{... | collective-permute-start | bytes 393224 | tf_op jit(solution)/shard_map/ppermute | solution.py:387
  117.7 12.4 %collective-permute-start.35 = (bf16[2,2,128,256]{3,2,1,0:T(8,128)(2,1)}, bf16[2,2,128,256]{3,2,1,0:T(8,128)(2,1)S(1)}, u32[]{:S(2)}, u32[]{:S(2)}) collective-permute-start(bf16[2,2,128,256]{3,2,1,0:T(8,128)(2,1)} %get-tuple-element.53), channel_id=1, source_target_pairs={{0,2},{2,0},{1,3},{3,1},{4,6},{6,4},{5,7},{7,5},{8,10},{10,8},{9,1... | collective-permute-start | bytes 786440 | tf_op jit(solution)/shard_map/ppermute | solution.py:323
  120.4 9.7 %copy-start.12 = (bf16[2,2,128,256]{3,2,1,0:T(8,128)(2,1)S(1)}, bf16[2,2,128,256]{3,2,1,0:T(8,128)(2,1)}, u32[]{:S(2)}) copy-start(bf16[2,2,128,256]{3,2,1,0:T(8,128)(2,1)} %get-tuple-element.54) | copy-start | bytes 786436
  120.4 9.7 %copy-start.13 = (bf16[2,2,128,256]{3,2,1,0:T(8,128)(2,1)S(1)}, bf16[2,2,128,256]{3,2,1,0:T(8,128)(2,1)}, u32[]{:S(2)}) copy-start(bf16[2,2,128,256]{3,2,1,0:T(8,128)(2,1)} %get-tuple-element.52) | copy-start | bytes 786436
  120.4 9.9 %copy-start.29 = (bf16[2,128,256]{2,1,0:T(8,128)(2,1)S(1)}, bf16[2,128,256]{2,1,0:T(8,128)(2,1)}, u32[]{:S(2)}) copy-start(bf16[2,128,256]{2,1,0:T(8,128)(2,1)} %get-tuple-element.50) | copy-start | bytes 393220
  120.4 11.2 %copy-start.28 = (bf16[2,128,256]{2,1,0:T(8,128)(2,1)S(1)}, bf16[2,128,256]{2,1,0:T(8,128)(2,1)}, u32[]{:S(2)}) copy-start(bf16[2,128,256]{2,1,0:T(8,128)(2,1)} %get-tuple-element.51) | copy-start | bytes 393220
  126.0 14.4 %copy-start.9 = (f32[256,2048]{1,0:T(8,128)S(1)}, f32[256,2048]{1,0:T(8,128)}, u32[]{:S(2)}) copy-start(f32[256,2048]{1,0:T(8,128)} %get-tuple-element.47) | copy-start | bytes 6291460
  126.0 14.4 %collective-permute-start.31 = (bf16[256,2048]{1,0:T(8,128)(2,1)}, bf16[256,2048]{1,0:T(8,128)(2,1)S(1)}, u32[]{:S(2)}, u32[]{:S(2)}) collective-permute-start(bf16[256,2048]{1,0:T(8,128)(2,1)} %get-tuple-element.48), channel_id=1, source_target_pairs={{0,1},{1,0},{2,3},{3,2},{4,5},{5,4},{6,7},{7,6},{8,9},{9,8},{10,11... | collective-permute-start | bytes 3145736 | tf_op jit(solution)/shard_map/ppermute | solution.py:221
  130.2 9.2 %collective-permute-start.36 = (bf16[2,2,128,256]{3,2,1,0:T(8,128)(2,1)S(1)}, bf16[2,2,128,256]{3,2,1,0:T(8,128)(2,1)S(1)}, u32[]{:S(2)}, u32[]{:S(2)}) collective-permute-start(bf16[2,2,128,256]{3,2,1,0:T(8,128)(2,1)S(1)} %broadcast_select_fusion), channel_id=1, source_target_pairs={{0,4},{4,0},{8,12},{12,8},{1,5},{5,1},{9,13},{13,9},{2,6},{6,2},{1... | collective-permute-start | bytes 786440 | tf_op jit(solution)/shard_map/ppermute | solution.py:323
  130.4 23.4 %collective-permute-start.33 = (bf16[2,128,256]{2,1,0:T(8,128)(2,1)S(1)}, bf16[2,128,256]{2,1,0:T(8,128)(2,1)S(1)}, u32[]{:S(2)}, u32[]{:S(2)}) collective-permute-start(bf16[2,128,256]{2,1,0:T(8,128)(2,1)S(1)} %copy-done.29), channel_id=1, source_target_pairs={{2,0},{4,2},{6,4},{8,6},{10,8},{12,10},{14,12},{3,1},{5,3},{7,5},{... | collective-permute-start | bytes 393224 | tf_op jit(solution)/shard_map/ppermute | solution.py:441
  131.7 22.1 %collective-permute-start.34 = (bf16[2,128,256]{2,1,0:T(8,128)(2,1)S(1)}, bf16[2,128,256]{2,1,0:T(8,128)(2,1)S(1)}, u32[]{:S(2)}, u32[]{:S(2)}) collective-permute-start(bf16[2,128,256]{2,1,0:T(8,128)(2,1)S(1)} %copy-done.28), channel_id=1, source_target_pairs={{0,2},{2,4},{4,6},{6,8},{8,10},{10,12},{12,14},{1,3},{3,5},{5,7},{... | collective-permute-start | bytes 393224 | tf_op jit(solution)/shard_map/ppermute | solution.py:441
  139.8 13.1 %collective-permute-start.37 = (bf16[2,2,128,256]{3,2,1,0:T(8,128)(2,1)S(1)}, bf16[2,2,128,256]{3,2,1,0:T(8,128)(2,1)S(1)}, u32[]{:S(2)}, u32[]{:S(2)}) collective-permute-start(bf16[2,2,128,256]{3,2,1,0:T(8,128)(2,1)S(1)} %get-tuple-element.64), channel_id=1, source_target_pairs={{0,8},{4,12},{8,0},{12,4},{1,9},{5,13},{9,1},{13,5},{2,10},{6,14},... | collective-permute-start | bytes 786440 | tf_op jit(solution)/shard_map/ppermute | solution.py:323
  140.7 13.0 %collective-permute-start.32 = (bf16[128,2048]{1,0:T(8,128)(2,1)S(1)}, bf16[128,2048]{1,0:T(8,128)(2,1)S(1)}, u32[]{:S(2)}, u32[]{:S(2)}) collective-permute-start(bf16[128,2048]{1,0:T(8,128)(2,1)S(1)} %slice.101), channel_id=1, source_target_pairs={{0,16},{16,0},{1,17},{17,1},{2,18},{18,2},{3,19},{19,3},{4,20},{20... | collective-permute-start | bytes 1572872 | tf_op jit(solution)/shard_map/ppermute | solution.py:221
  154.4 6.5 %copy-start.1 = (bf16[128,2048]{1,0:T(8,128)(2,1)S(1)}, bf16[128,2048]{1,0:T(8,128)(2,1)}, u32[]{:S(2)}) copy-start(bf16[128,2048]{1,0:T(8,128)(2,1)} %h00.1) | copy-start | bytes 1572868
  160.8 18.3 %copy-start.2 = (f32[256,2048]{1,0:T(8,128)S(1)}, f32[256,2048]{1,0:T(8,128)}, u32[]{:S(2)}) copy-start(f32[256,2048]{1,0:T(8,128)} %get-tuple-element.62) | copy-start | bytes 6291460
  160.8 2.9 %collective-permute-start.38 = (bf16[256,2048]{1,0:T(8,128)(2,1)}, bf16[256,2048]{1,0:T(8,128)(2,1)S(1)}, u32[]{:S(2)}, u32[]{:S(2)}) collective-permute-start(bf16[256,2048]{1,0:T(8,128)(2,1)} %get-tuple-element.63), channel_id=1, source_target_pairs={{0,1},{1,0},{2,3},{3,2},{4,5},{5,4},{6,7},{7,6},{8,9},{9,8},{10,11... | collective-permute-start | bytes 3145736 | tf_op jit(solution)/shard_map/ppermute | solution.py:221
  165.1 14.0 %collective-permute-start.39 = (bf16[128,2048]{1,0:T(8,128)(2,1)S(1)}, bf16[128,2048]{1,0:T(8,128)(2,1)S(1)}, u32[]{:S(2)}, u32[]{:S(2)}) collective-permute-start(bf16[128,2048]{1,0:T(8,128)(2,1)S(1)} %add_convert_fusion), channel_id=1, source_target_pairs={{0,16},{16,0},{1,17},{17,1},{2,18},{18,2},{3,19},{19,3},{4,20},{20... | collective-permute-start | bytes 1572872 | tf_op jit(solution)/shard_map/ppermute | solution.py:221
  (9 other events, 6.8 us)

commit v6 on v5

--- a/solution.py
+++ b/solution.py
@@ -498,7 +498,7 @@
         name="query_part",
     )(after(gq, arrived[1]).reshape(2, 2, rows, REP * HDIM), weight, weight)
 
-    chunk = width // 4
+    chunk = width // 2
     key_shape = (2, 2, rows, 2 * HDIM)
 
     def sections(start):
@@ -510,7 +510,7 @@
 
     key_parts = pl.pallas_call(
         key_part_kernel,
-        grid=(4,),
+        grid=(2,),
         out_shape=partial,
         in_specs=[smem()]
         + [fixed(v) for v in (dkv.shape, near_shape.shape, near_shape.shape)]

time: 182 us -> 181 us (level)
  no operation moved by 1% of the time
where the time goes in v6:
time: 181 us; the launch traced here: 180 us
  starting transfers between devices  55.9 us (31%)
  waiting for transfers between devices  51.1 us (28%)
  Pallas kernels  41.4 us (23%)
  local copies, waits for them, and re-layouts  12.5 us (7%)
  other arithmetic  11.7 us (6%)
  matrix products  4.6 us (3%)
  between operations  2.5 us (1%)
    ppermute x13, waiting for transfers between devices, swap(): return lax.ppermute(value, axis, [(0, 1), (1, 0)])  19.8 us
    ppermute x7, waiting for transfers between devices, ring(): lax.ppermute(value, axis, [(i, (i + 1) % count) for i in range(count)])  15 us
    ppermute x13, starting transfers between devices, swap(): return lax.ppermute(value, axis, [(0, 1), (1, 0)])  13.9 us
    pallas_call x1, Pallas kernels, body(): pl.pallas_call(attention_kernel, grid=(2,), out_shape=(jax.ShapeDtypeStru...  10.7 us
    ppermute x6, starting transfers between devices, trade(): got = lax.ppermute(packed, axis, pairs)  10.1 us
    pallas_call x1, Pallas kernels, body(): pl.pallas_call(query_part_kernel, grid=(steps,), out_shape=(jax.ShapeDtyp...  9.81 us
    ppermute x6, waiting for transfers between devices, trade(): got = lax.ppermute(packed, axis, pairs)  8.37 us
    ppermute x7, starting transfers between devices, ring(): lax.ppermute(value, axis, [(i, (i + 1) % count) for i in range(count)])  8.33 us
  transfers between devices with their start and end apart: 40, of which 15 were waited for; matrix products, arithmetic and copies ran while one was open for 11% of the time, Pallas kernels for 14%

profile of v6, /device:TPU:0, one launch (start us, length us, event | category | flops | bytes accessed | tf_op | source)
XLA Modules:
  0.0 179.8 jit_solution(9439246181197192760)
XLA Ops:
  0.7 3.0 %collective-permute-start = (bf16[128,2048]{1,0:T(8,128)(2,1)}, bf16[128,2048]{1,0:T(8,128)(2,1)S(1)}, u32[]{:S(2)}, u32[]{:S(2)}) collective-permute-start(bf16[128,2048]{1,0:T(8,128)(2,1)} %h00.1), channel_id=1, source_target_pairs={{0,16},{16,0},{1,17},{17,1},{2,18},{18,2},{3,19},{19,3},{4,20},{20... | collective-permute-start | bytes 1572872 | tf_op jit(solution)/shard_map/ppermute | solution.py:221
  3.7 1.0 constant_dynamic-slice_fusion
  4.7 0.8 constant_dynamic-slice_fusion.2
  6.1 1.1 collective-permute-done.4
  7.4 0.8 constant_dynamic-update-slice_fusion.7
  8.2 1.5 collective-permute-start.5
  9.9 1.6 collective-permute-start.6
  12.9 2.9 %collective-permute-done.h01 = bf16[128,2048]{1,0:T(8,128)(2,1)S(1)} collective-permute-done((bf16[128,2048]{1,0:T(8,128)(2,1)}, bf16[128,2048]{1,0:T(8,128)(2,1)S(1)}, u32[]{:S(2)}, u32[]{:S(2)}) %collective-permute-start) | collective-permute-done | bytes 524320 | tf_op jit(solution)/shard_map/ppermute | solution.py:221
  15.8 1.7 collective-permute-start.1
  17.6 1.6 fusion.14
  20.5 1.8 %collective-permute-start.11 = (bf16[128,2048]{1,0:T(8,128)(2,1)S(1)}, bf16[128,2048]{1,0:T(8,128)(2,1)S(1)}, u32[]{:S(2)}, u32[]{:S(2)}) collective-permute-start(bf16[128,2048]{1,0:T(8,128)(2,1)S(1)} %copy-done.14), channel_id=1, source_target_pairs={{0,16},{16,0},{1,17},{17,1},{2,18},{18,2},{3,19},{19,3},{4,20},{20... | collective-permute-start | bytes 1572872 | tf_op jit(solution)/shard_map/ppermute | solution.py:221
  22.4 1.0 collective-permute-done.6
  24.0 1.5 collective-permute-start.7
  25.6 0.8 constant_dynamic-update-slice_fusion.6
  26.3 7.7 %collective-permute-done.7 = bf16[256,768]{1,0:T(8,128)(2,1)S(1)} collective-permute-done((bf16[256,768]{1,0:T(8,128)(2,1)S(1)}, bf16[256,768]{1,0:T(8,128)(2,1)S(1)}, u32[]{:S(2)}, u32[]{:S(2)}) %collective-permute-start.7) | collective-permute-done | bytes 393248 | tf_op jit(solution)/shard_map/ppermute | solution.py:234
  34.0 1.8 collective-permute-done.8
  35.8 1.5 collective-permute-start.9
  37.3 0.8 constant_dynamic-update-slice_fusion.5
  38.1 0.8 constant_dynamic-update-slice_fusion.4
  38.9 0.8 constant_dynamic-update-slice_fusion.3
  39.7 0.8 copy-done.16
  40.5 0.8 copy-done.21
  41.3 4.9 %norm.1 = bf16[2,512,2048]{2,1,0:T(8,128)(2,1)} custom-call(bf16[128,2048]{1,0:T(8,128)(2,1)} %h00.1, bf16[128,2048]{1,0:T(8,128)(2,1)} %copy-done.15, bf16[128,2048]{1,0:T(8,128)(2,1)} %copy-done.16, bf16[128,2048]{1,0:T(8,128)(2,1)} %copy-done.21), custom_call_target="tpu_custom_call" | custom-call | flops 1000000000 | bytes 6291456 | tf_op jit(solution)/shard_map/norm/pallas_call | solution.py:365
  46.2 1.1 collective-permute-done.10
  47.3 1.5 collective-permute-start.12
  48.9 1.3 collective-permute-start.20
  50.3 1.3 collective-permute-start.16
  51.6 1.0 constant_dynamic-update-slice_fusion.2
  52.7 3.5 %collective-permute-done.12 = bf16[256,768]{1,0:T(8,128)(2,1)S(1)} collective-permute-done((bf16[256,768]{1,0:T(8,128)(2,1)S(1)}, bf16[256,768]{1,0:T(8,128)(2,1)S(1)}, u32[]{:S(2)}, u32[]{:S(2)}) %collective-permute-start.12) | collective-permute-done | bytes 393248 | tf_op jit(solution)/shard_map/ppermute | solution.py:234
  56.2 1.3 convolution_convert_fusion
  57.5 0.7 copy-done.24
  58.5 1.6 collective-permute-start.21
  60.1 2.4 %collective-permute-done.16 = bf16[256,1024]{1,0:T(8,128)(2,1)S(1)} collective-permute-done((bf16[256,1024]{1,0:T(8,128)(2,1)S(1)}, bf16[256,1024]{1,0:T(8,128)(2,1)S(1)}, u32[]{:S(2)}, u32[]{:S(2)}) %collective-permute-start.16) | collective-permute-done | bytes 524320 | tf_op jit(solution)/shard_map/ppermute | solution.py:281
  62.7 0.7 collective-permute-start.17
  63.4 2.9 %collective-permute-start.18 = (bf16[256,1024]{1,0:T(8,128)(2,1)S(1)}, bf16[256,1024]{1,0:T(8,128)(2,1)S(1)}, u32[]{:S(2)}, u32[]{:S(2)}) collective-permute-start(bf16[256,1024]{1,0:T(8,128)(2,1)S(1)} %get-tuple-element.39.refs_0_), channel_id=1, source_target_pairs={{0,2},{2,0},{4,6},{6,4},{13,15},{15,13},{9,11},{11,9},{20,22},{22,... | collective-permute-start | bytes 1572872 | tf_op jit(solution)/shard_map/ppermute | solution.py:289
  67.0 2.9 %collective-permute-start.23 = (bf16[256,1024]{1,0:T(8,128)(2,1)S(1)}, bf16[256,1024]{1,0:T(8,128)(2,1)S(1)}, u32[]{:S(2)}, u32[]{:S(2)}) collective-permute-start(bf16[256,1024]{1,0:T(8,128)(2,1)S(1)} %get-tuple-element.42.refs_2_), channel_id=1, source_target_pairs={{0,2},{2,0},{4,6},{6,4},{13,15},{15,13},{9,11},{11,9},{20,22},{22,... | collective-permute-start | bytes 1572872 | tf_op jit(solution)/shard_map/ppermute | solution.py:289
  70.2 3.8 %collective-permute-start.29 = (bf16[2,2,128,256]{3,2,1,0:T(8,128)(2,1)S(1)}, bf16[2,2,128,256]{3,2,1,0:T(8,128)(2,1)S(1)}, u32[]{:S(2)}, u32[]{:S(2)}) collective-permute-start(bf16[2,2,128,256]{3,2,1,0:T(8,128)(2,1)S(1)} %broadcast_select_fusion.2), channel_id=1, source_target_pairs={{0,4},{4,0},{8,12},{12,8},{1,5},{5,1},{9,13},{13,9},{2,6},{6,2},{1... | collective-permute-start | bytes 786440 | tf_op jit(solution)/shard_map/ppermute | solution.py:323
  75.2 4.9 %collective-permute-done.23.refs_6_ = bf16[256,1024]{1,0:T(8,128)(2,1)S(1)} collective-permute-done((bf16[256,1024]{1,0:T(8,128)(2,1)S(1)}, bf16[256,1024]{1,0:T(8,128)(2,1)S(1)}, u32[]{:S(2)}, u32[]{:S(2)}) %collective-permute-start.23) | collective-permute-done | bytes 524320 | tf_op jit(solution)/shard_map/ppermute | solution.py:289
  81.8 1.3 collective-permute-start.30
  84.2 1.5 collective-permute-start.26
  85.7 3.3 %fusion.2 = bf16[1024,512]{1,0:T(8,128)(2,1)} fusion(bf16[1024,2048]{1,0:T(8,128)(2,1)S(1)} %bitcast.20, bf16[2048,768]{1,0:T(8,128)(2,1)S(1)} %constant_dynamic-update-slice_fusion.w.wm), kind=kOutput, calls=%fused_computation.3 | convolution fusion | flops 2148007936 | bytes 7340032 | tf_op jit(solution)/shard_map/dot_general | solution.py:22
  89.1 2.9 %collective-permute-start.27 = (bf16[2,128,256]{2,1,0:T(8,128)(2,1)S(1)}, bf16[2,128,256]{2,1,0:T(8,128)(2,1)S(1)}, u32[]{:S(2)}, u32[]{:S(2)}) collective-permute-start(bf16[2,128,256]{2,1,0:T(8,128)(2,1)S(1)} %get-tuple-element.84), channel_id=1, source_target_pairs={{0,2},{2,4},{4,6},{6,8},{8,10},{10,12},{12,14},{1,3},{3,5},{5,7},{... | collective-permute-start | bytes 393224 | tf_op jit(solution)/shard_map/ppermute | solution.py:387
  92.0 5.1 %collective-permute-done.30 = bf16[2,2,128,256]{3,2,1,0:T(8,128)(2,1)S(1)} collective-permute-done((bf16[2,2,128,256]{3,2,1,0:T(8,128)(2,1)S(1)}, bf16[2,2,128,256]{3,2,1,0:T(8,128)(2,1)S(1)}, u32[]{:S(2)}, u32[]{:S(2)}) %collective-permute-start.30) | collective-permute-done | bytes 262176 | tf_op jit(solution)/shard_map/ppermute | solution.py:323
  97.1 1.5 collective-permute-start.28
  98.6 0.9 add_select_fusion.6
  99.5 0.8 copy-done.22
  100.3 0.8 copy-done.23
  101.2 5.1 %grad_att.1 = (bf16[512,512]{1,0:T(8,128)(2,1)}, bf16[512,2048]{1,0:T(8,128)(2,1)}) custom-call(bf16[128,2048]{1,0:T(8,128)(2,1)} %c00.1, bf16[128,2048]{1,0:T(8,128)(2,1)} %copy-done.17, bf16[128,2048]{1,0:T(8,128)(2,1)} %copy-done.20, bf16[128,2048]{1,0:T(8,128)(2,1)} %copy-done.22, bf16[256,1024]{1,0:T(8,128)(2,1)} %copy-done.11, ...), custom_call_target="tpu_custom_call" | custom-call | flops 1000000000 | bytes 9437184 | tf_op jit(solution)/shard_map/grad_att/pallas_call | solution.py:400
  107.0 10.7 %attention.1 = (bf16[2,2,2,128,512]{4,3,2,1,0:T(8,128)(2,1)}, bf16[2,2,2,128,512]{4,3,2,1,0:T(8,128)(2,1)}, f32[2,2,2,128,256]{4,3,2,1,0:T(8,128)}, bf16[2,128,2...) custom-call(s32[2]{0:T(128)} %pad_add_fusion.chosen, ...), custom_call_target="tpu_custom_call" | custom-call | flops 8000000000 | bytes 10485760 | tf_op jit(solution)/shard_map/attention/pallas_call | solution.py:421
  117.7 2.7 %collective-permute-start.35 = (bf16[2,2,128,256]{3,2,1,0:T(8,128)(2,1)}, bf16[2,2,128,256]{3,2,1,0:T(8,128)(2,1)S(1)}, u32[]{:S(2)}, u32[]{:S(2)}) collective-permute-start(bf16[2,2,128,256]{3,2,1,0:T(8,128)(2,1)} %get-tuple-element.53), channel_id=1, source_target_pairs={{0,2},{2,0},{1,3},{3,1},{4,6},{6,4},{5,7},{7,5},{8,10},{10,8},{9,1... | collective-permute-start | bytes 786440 | tf_op jit(solution)/shard_map/ppermute | solution.py:323
  120.4 5.5 %output.1 = (f32[256,2048]{1,0:T(8,128)}, bf16[256,2048]{1,0:T(8,128)(2,1)}) custom-call(bf16[2,2,256,512]{3,2,1,0:T(8,128)(2,1)} %bitcast.26, bf16[512,2048]{1,0:T(8,128)(2,1)} %get-tuple-element.46.w), custom_call_target="tpu_custom_call" | custom-call | flops 2000000000 | bytes 7340032 | tf_op jit(solution)/shard_map/output/pallas_call | solution.py:452
  126.0 4.2 %collective-permute-start.31 = (bf16[256,2048]{1,0:T(8,128)(2,1)}, bf16[256,2048]{1,0:T(8,128)(2,1)S(1)}, u32[]{:S(2)}, u32[]{:S(2)}) collective-permute-start(bf16[256,2048]{1,0:T(8,128)(2,1)} %get-tuple-element.48), channel_id=1, source_target_pairs={{0,1},{1,0},{2,3},{3,2},{4,5},{5,4},{6,7},{7,6},{8,9},{9,8},{10,11... | collective-permute-start | bytes 3145736 | tf_op jit(solution)/shard_map/ppermute | solution.py:221
  130.4 1.3 collective-permute-start.33
  131.7 4.6 %collective-permute-start.34 = (bf16[2,128,256]{2,1,0:T(8,128)(2,1)S(1)}, bf16[2,128,256]{2,1,0:T(8,128)(2,1)S(1)}, u32[]{:S(2)}, u32[]{:S(2)}) collective-permute-start(bf16[2,128,256]{2,1,0:T(8,128)(2,1)S(1)} %copy-done.28), channel_id=1, source_target_pairs={{0,2},{2,4},{4,6},{6,8},{8,10},{10,12},{12,14},{1,3},{3,5},{5,7},{... | collective-permute-start | bytes 393224 | tf_op jit(solution)/shard_map/ppermute | solution.py:441
  136.2 3.3 %collective-permute-done.36 = bf16[2,2,128,256]{3,2,1,0:T(8,128)(2,1)S(1)} collective-permute-done((bf16[2,2,128,256]{3,2,1,0:T(8,128)(2,1)S(1)}, bf16[2,2,128,256]{3,2,1,0:T(8,128)(2,1)S(1)}, u32[]{:S(2)}, u32[]{:S(2)}) %collective-permute-start.36) | collective-permute-done | bytes 262176 | tf_op jit(solution)/shard_map/ppermute | solution.py:323
  140.7 2.3 %collective-permute-start.32 = (bf16[128,2048]{1,0:T(8,128)(2,1)S(1)}, bf16[128,2048]{1,0:T(8,128)(2,1)S(1)}, u32[]{:S(2)}, u32[]{:S(2)}) collective-permute-start(bf16[128,2048]{1,0:T(8,128)(2,1)S(1)} %slice.101), channel_id=1, source_target_pairs={{0,16},{16,0},{1,17},{17,1},{2,18},{18,2},{3,19},{19,3},{4,20},{20... | collective-permute-start | bytes 1572872 | tf_op jit(solution)/shard_map/ppermute | solution.py:221
  143.0 9.8 %query_part.1 = (f32[2,256,2048]{2,1,0:T(8,128)}, bf16[2048,256]{1,0:T(8,128)(2,1)}, bf16[2048,256]{1,0:T(8,128)(2,1)}) custom-call(bf16[2,2,256,512]{3,2,1,0:T(8,128)(2,1)} %bitcast.24, bf16[2048,768]{1,0:T(8,128)(2,1)} %copy-done.6, bf16[2048,768]{1,0:T(8,128)(2,1)} %copy-done.6), custom_call_target="tpu_custom_call" | custom-call | flops 3000000000 | bytes 13631488 | tf_op jit(solution)/shard_map/query_part/pallas_call | solution.py:478
  152.8 0.9 add_select_fusion
  154.4 5.4 %key_part.1 = (f32[256,2048]{1,0:T(8,128)}, bf16[256,2048]{1,0:T(8,128)(2,1)}) custom-call(s32[2]{0:T(128)} %pad_add_fusion.chosen, f32[2,2,2,128,256]{4,3,2,1,0:T(8,128)} %get-tuple-element.49.dkv, bf16[2,128,256]{2,1,0:T(8,128)(2,1)} %copy-done.26, bf16[2,128,256]{2,1,0:T(8,128)(2,1)} %copy-done.27, bf16[2,2,128,256]{3,2,1,0:T(8,128)(2,1)} %get-tuple-element.56.far_p, ...), custom_call_target="tpu_custom_call" | custom-call | flops 500000000 | bytes 8388608 | tf_op jit(solution)/shard_map/key_part/pallas_call | solution.py:511
  160.1 2.7 %collective-permute-done.38 = bf16[256,2048]{1,0:T(8,128)(2,1)S(1)} collective-permute-done((bf16[256,2048]{1,0:T(8,128)(2,1)}, bf16[256,2048]{1,0:T(8,128)(2,1)S(1)}, u32[]{:S(2)}, u32[]{:S(2)}) %collective-permute-start.38) | collective-permute-done | bytes 1048608 | tf_op jit(solution)/shard_map/ppermute | solution.py:221
  162.8 1.4 add_convert_fusion
  164.3 0.9 fusion.12
  165.2 13.0 %collective-permute-done.39 = bf16[128,2048]{1,0:T(8,128)(2,1)S(1)} collective-permute-done((bf16[128,2048]{1,0:T(8,128)(2,1)S(1)}, bf16[128,2048]{1,0:T(8,128)(2,1)S(1)}, u32[]{:S(2)}, u32[]{:S(2)}) %collective-permute-start.39) | collective-permute-done | bytes 524320 | tf_op jit(solution)/shard_map/ppermute | solution.py:221
  178.5 1.2 fusion.10
  (135 shorter events, 12.2 us)
Async XLA Ops:
  0.6 10.9 %copy-start = (bf16[128,2048]{1,0:T(8,128)(2,1)S(1)}, bf16[128,2048]{1,0:T(8,128)(2,1)}, u32[]{:S(2)}) copy-start(bf16[128,2048]{1,0:T(8,128)(2,1)} %h00.1) | copy-start | bytes 1572868
  0.6 16.9 %copy-start.25 = (bf16[128,2048]{1,0:T(8,128)(2,1)S(1)}, bf16[128,2048]{1,0:T(8,128)(2,1)}, u32[]{:S(2)}) copy-start(bf16[128,2048]{1,0:T(8,128)(2,1)} %param.9) | copy-start | bytes 1572868
  0.7 10.9 %copy-start.32 = (s32[2]{0:T(128)S(1)}, s32[2]{0:T(128)}, u32[]{:S(2)}) copy-start(s32[2]{0:T(128)} %param.10) | copy-start | bytes 28
  0.7 15.1 %collective-permute-start = (bf16[128,2048]{1,0:T(8,128)(2,1)}, bf16[128,2048]{1,0:T(8,128)(2,1)S(1)}, u32[]{:S(2)}, u32[]{:S(2)}) collective-permute-start(bf16[128,2048]{1,0:T(8,128)(2,1)} %h00.1), channel_id=1, source_target_pairs={{0,16},{16,0},{1,17},{17,1},{2,18},{18,2},{3,19},{19,3},{4,20},{20... | collective-permute-start | bytes 1572872 | tf_op jit(solution)/shard_map/ppermute | solution.py:221
  3.7 13.9 %collective-permute-start.15 = (bf16[128,2048]{1,0:T(8,128)(2,1)}, bf16[128,2048]{1,0:T(8,128)(2,1)}, u32[]{:S(2)}, u32[]{:S(2)}) collective-permute-start(bf16[128,2048]{1,0:T(8,128)(2,1)} %param.9), channel_id=1, source_target_pairs={{0,1},{1,0},{2,3},{3,2},{4,5},{5,4},{6,7},{7,6},{8,9},{9,8},{10,11... | collective-permute-start | bytes 1572872 | tf_op jit(solution)/shard_map/ppermute | solution.py:221
  5.5 1.6 collective-permute-start.4
  7.2 13.3 %copy-start.14 = (bf16[128,2048]{1,0:T(8,128)(2,1)S(1)}, bf16[128,2048]{1,0:T(8,128)(2,1)}, u32[]{:S(2)}) copy-start(bf16[128,2048]{1,0:T(8,128)(2,1)} %c00.1) | copy-start | bytes 1572868
  8.2 1.7 copy-start.4
  8.2 14.1 %collective-permute-start.5 = (bf16[256,768]{1,0:T(8,128)(2,1)}, bf16[256,768]{1,0:T(8,128)(2,1)S(1)}, u32[]{:S(2)}, u32[]{:S(2)}) collective-permute-start(bf16[256,768]{1,0:T(8,128)(2,1)} %get-tuple-element.77), channel_id=1, source_target_pairs={{0,2},{2,0},{1,3},{3,1},{4,6},{6,4},{5,7},{7,5},{8,10},{10,8},{9,1... | collective-permute-start | bytes 1179656 | tf_op jit(solution)/shard_map/ppermute | solution.py:234
  9.9 13.5 %collective-permute-start.6 = (bf16[256,768]{1,0:T(8,128)(2,1)}, bf16[256,768]{1,0:T(8,128)(2,1)S(1)}, u32[]{:S(2)}, u32[]{:S(2)}) collective-permute-start(bf16[256,768]{1,0:T(8,128)(2,1)} %get-tuple-element.77), channel_id=1, source_target_pairs={{0,4},{4,8},{8,12},{12,0},{1,5},{5,9},{9,13},{13,1},{2,6},{6,10},{... | collective-permute-start | bytes 1179656 | tf_op jit(solution)/shard_map/ppermute | solution.py:234
  11.5 28.2 %collective-permute-start.2 = (bf16[128,2048]{1,0:T(8,128)(2,1)S(1)}, bf16[128,2048]{1,0:T(8,128)(2,1)S(1)}, u32[]{:S(2)}, u32[]{:S(2)}) collective-permute-start(bf16[128,2048]{1,0:T(8,128)(2,1)S(1)} %copy-done), channel_id=1, source_target_pairs={{0,1},{1,0},{2,3},{3,2},{4,5},{5,4},{6,7},{7,6},{8,9},{9,8},{10,11... | collective-permute-start | bytes 1572872 | tf_op jit(solution)/shard_map/ppermute | solution.py:221
  15.8 23.9 %copy-start.15 = (bf16[128,2048]{1,0:T(8,128)(2,1)}, bf16[128,2048]{1,0:T(8,128)(2,1)S(1)}, u32[]{:S(2)}) copy-start(bf16[128,2048]{1,0:T(8,128)(2,1)S(1)} %collective-permute-done.h01) | copy-start | bytes 1572868
  15.8 3.6 %collective-permute-start.1 = (f32[8,128]{1,0:T(8,128)S(1)}, f32[8,128]{1,0:T(8,128)S(1)}, u32[]{:S(2)}, u32[]{:S(2)}) collective-permute-start(f32[8,128]{1,0:T(8,128)S(1)} %broadcast_in_dim.125), channel_id=1, source_target_pairs={{0,16},{16,0},{1,17},{17,1},{2,18},{18,2},{3,19},{19,3},{4,20},{20... | collective-permute-start | bytes 12296 | tf_op jit(solution)/shard_map/ppermute | solution.py:221
  17.5 22.1 %collective-permute-start.3 = (bf16[128,2048]{1,0:T(8,128)(2,1)S(1)}, bf16[128,2048]{1,0:T(8,128)(2,1)S(1)}, u32[]{:S(2)}, u32[]{:S(2)}) collective-permute-start(bf16[128,2048]{1,0:T(8,128)(2,1)S(1)} %collective-permute-done.h01), channel_id=1, source_target_pairs={{0,1},{1,0},{2,3},{3,2},{4,5},{5,4},{6,7},{7,6},{8,9},{9,8},{10,11... | collective-permute-start | bytes 1572872 | tf_op jit(solution)/shard_map/ppermute | solution.py:221
  20.5 25.8 %collective-permute-start.11 = (bf16[128,2048]{1,0:T(8,128)(2,1)S(1)}, bf16[128,2048]{1,0:T(8,128)(2,1)S(1)}, u32[]{:S(2)}, u32[]{:S(2)}) collective-permute-start(bf16[128,2048]{1,0:T(8,128)(2,1)S(1)} %copy-done.14), channel_id=1, source_target_pairs={{0,16},{16,0},{1,17},{17,1},{2,18},{18,2},{3,19},{19,3},{4,20},{20... | collective-permute-start | bytes 1572872 | tf_op jit(solution)/shard_map/ppermute | solution.py:221
  23.4 12.4 %collective-permute-start.8 = (bf16[256,768]{1,0:T(8,128)(2,1)S(1)}, bf16[256,768]{1,0:T(8,128)(2,1)S(1)}, u32[]{:S(2)}, u32[]{:S(2)}) collective-permute-start(bf16[256,768]{1,0:T(8,128)(2,1)S(1)} %collective-permute-done.6), channel_id=1, source_target_pairs={{0,4},{4,8},{8,12},{12,0},{1,5},{5,9},{9,13},{13,1},{2,6},{6,10},{... | collective-permute-start | bytes 1179656 | tf_op jit(solution)/shard_map/ppermute | solution.py:234
  24.0 10.0 %collective-permute-start.7 = (bf16[256,768]{1,0:T(8,128)(2,1)S(1)}, bf16[256,768]{1,0:T(8,128)(2,1)S(1)}, u32[]{:S(2)}, u32[]{:S(2)}) collective-permute-start(bf16[256,768]{1,0:T(8,128)(2,1)S(1)} %collective-permute-done.6), channel_id=1, source_target_pairs={{0,2},{2,0},{1,3},{3,1},{4,6},{6,4},{5,7},{7,5},{8,10},{10,8},{9,1... | collective-permute-start | bytes 1179656 | tf_op jit(solution)/shard_map/ppermute | solution.py:234
  35.8 11.5 %collective-permute-start.10 = (bf16[256,768]{1,0:T(8,128)(2,1)S(1)}, bf16[256,768]{1,0:T(8,128)(2,1)S(1)}, u32[]{:S(2)}, u32[]{:S(2)}) collective-permute-start(bf16[256,768]{1,0:T(8,128)(2,1)S(1)} %collective-permute-done.8), channel_id=1, source_target_pairs={{0,4},{4,8},{8,12},{12,0},{1,5},{5,9},{9,13},{13,1},{2,6},{6,10},{... | collective-permute-start | bytes 1179656 | tf_op jit(solution)/shard_map/ppermute | solution.py:234
  35.8 10.4 %collective-permute-start.9 = (bf16[256,768]{1,0:T(8,128)(2,1)S(1)}, bf16[256,768]{1,0:T(8,128)(2,1)}, u32[]{:S(2)}, u32[]{:S(2)}) collective-permute-start(bf16[256,768]{1,0:T(8,128)(2,1)S(1)} %collective-permute-done.8), channel_id=1, source_target_pairs={{0,2},{2,0},{1,3},{3,1},{4,6},{6,4},{5,7},{7,5},{8,10},{10,8},{9,1... | collective-permute-start | bytes 1179656 | tf_op jit(solution)/shard_map/ppermute | solution.py:234
  39.7 11.9 %copy-start.5 = (bf16[2048,768]{1,0:T(8,128)(2,1)S(1)}, bf16[2048,768]{1,0:T(8,128)(2,1)}, u32[]{:S(2)}) copy-start(bf16[2048,768]{1,0:T(8,128)(2,1)} %constant_dynamic-update-slice_fusion.3) | copy-start | bytes 9437188
  46.2 10.0 %copy-start.3 = (bf16[2,512,2048]{2,1,0:T(8,128)(2,1)S(1)}, bf16[2,512,2048]{2,1,0:T(8,128)(2,1)}, u32[]{:S(2)}) copy-start(bf16[2,512,2048]{2,1,0:T(8,128)(2,1)} %norm.1) | copy-start | bytes 12582916
  46.2 35.2 %copy-start.17 = (bf16[128,2048]{1,0:T(8,128)(2,1)}, bf16[128,2048]{1,0:T(8,128)(2,1)S(1)}, u32[]{:S(2)}) copy-start(bf16[128,2048]{1,0:T(8,128)(2,1)S(1)} %collective-permute-done.11.c01) | copy-start | bytes 1572868
  47.3 8.8 %collective-permute-start.12 = (bf16[256,768]{1,0:T(8,128)(2,1)S(1)}, bf16[256,768]{1,0:T(8,128)(2,1)S(1)}, u32[]{:S(2)}, u32[]{:S(2)}) collective-permute-start(bf16[256,768]{1,0:T(8,128)(2,1)S(1)} %collective-permute-done.10), channel_id=1, source_target_pairs={{0,2},{2,0},{1,3},{3,1},{4,6},{6,4},{5,7},{7,5},{8,10},{10,8},{9,1... | collective-permute-start | bytes 1179656 | tf_op jit(solution)/shard_map/ppermute | solution.py:234
  48.9 11.2 %collective-permute-start.20 = (bf16[256,1024]{1,0:T(8,128)(2,1)S(1)}, bf16[256,1024]{1,0:T(8,128)(2,1)S(1)}, u32[]{:S(2)}, u32[]{:S(2)}) collective-permute-start(bf16[256,1024]{1,0:T(8,128)(2,1)S(1)} %get-tuple-element.80), channel_id=1, source_target_pairs={{0,4},{13,9},{20,16},{25,29},{2,6},{15,11},{22,18},{27,31}} | collective-permute-start | bytes 1572872 | tf_op jit(solution)/shard_map/ppermute | solution.py:281
  50.3 12.3 %collective-permute-start.16 = (bf16[256,1024]{1,0:T(8,128)(2,1)S(1)}, bf16[256,1024]{1,0:T(8,128)(2,1)S(1)}, u32[]{:S(2)}, u32[]{:S(2)}) collective-permute-start(bf16[256,1024]{1,0:T(8,128)(2,1)S(1)} %get-tuple-element.81), channel_id=1, source_target_pairs={{0,4},{13,9},{20,16},{25,29},{2,6},{15,11},{22,18},{27,31}} | collective-permute-start | bytes 1572872 | tf_op jit(solution)/shard_map/ppermute | solution.py:281
  56.2 29.5 %copy-start.6 = (bf16[2048,768]{1,0:T(8,128)(2,1)}, bf16[2048,768]{1,0:T(8,128)(2,1)S(1)}, u32[]{:S(2)}) copy-start(bf16[2048,768]{1,0:T(8,128)(2,1)S(1)} %constant_dynamic-update-slice_fusion.w.wm) | copy-start | bytes 9437188
  58.5 7.8 %collective-permute-start.21 = (bf16[2,2,128,256]{3,2,1,0:T(8,128)(2,1)S(1)}, bf16[2,2,128,256]{3,2,1,0:T(8,128)(2,1)S(1)}, u32[]{:S(2)}, u32[]{:S(2)}) collective-permute-start(bf16[2,2,128,256]{3,2,1,0:T(8,128)(2,1)S(1)} %fusion.15), channel_id=1, source_target_pairs={{0,2},{2,0},{1,3},{3,1},{4,6},{6,4},{5,7},{7,5},{8,10},{10,8},{9,1... | collective-permute-start | bytes 786440 | tf_op jit(solution)/shard_map/ppermute | solution.py:323
  62.7 21.6 %copy-start.10 = (bf16[256,1024]{1,0:T(8,128)(2,1)}, bf16[256,1024]{1,0:T(8,128)(2,1)S(1)}, u32[]{:S(2)}) copy-start(bf16[256,1024]{1,0:T(8,128)(2,1)S(1)} %get-tuple-element.42.refs_2_) | copy-start | bytes 1572868
  62.7 21.6 %copy-start.11 = (bf16[256,1024]{1,0:T(8,128)(2,1)}, bf16[256,1024]{1,0:T(8,128)(2,1)S(1)}, u32[]{:S(2)}) copy-start(bf16[256,1024]{1,0:T(8,128)(2,1)S(1)} %get-tuple-element.39.refs_0_) | copy-start | bytes 1572868
  62.7 11.3 %collective-permute-start.17 = (bf16[256,1024]{1,0:T(8,128)(2,1)S(1)}, bf16[256,1024]{1,0:T(8,128)(2,1)S(1)}, u32[]{:S(2)}, u32[]{:S(2)}) collective-permute-start(bf16[256,1024]{1,0:T(8,128)(2,1)S(1)} %get-tuple-element.39.refs_0_), channel_id=1, source_target_pairs={{4,8},{9,5},{20,24},{25,21},{6,10},{11,7},{22,26},{27,23}} | collective-permute-start | bytes 1572872 | tf_op jit(solution)/shard_map/ppermute | solution.py:281
  63.4 11.1 %collective-permute-start.18 = (bf16[256,1024]{1,0:T(8,128)(2,1)S(1)}, bf16[256,1024]{1,0:T(8,128)(2,1)S(1)}, u32[]{:S(2)}, u32[]{:S(2)}) collective-permute-start(bf16[256,1024]{1,0:T(8,128)(2,1)S(1)} %get-tuple-element.39.refs_0_), channel_id=1, source_target_pairs={{0,2},{2,0},{4,6},{6,4},{13,15},{15,13},{9,11},{11,9},{20,22},{22,... | collective-permute-start | bytes 1572872 | tf_op jit(solution)/shard_map/ppermute | solution.py:289
  66.3 8.8 %collective-permute-start.22 = (bf16[256,1024]{1,0:T(8,128)(2,1)S(1)}, bf16[256,1024]{1,0:T(8,128)(2,1)S(1)}, u32[]{:S(2)}, u32[]{:S(2)}) collective-permute-start(bf16[256,1024]{1,0:T(8,128)(2,1)S(1)} %get-tuple-element.42.refs_2_), channel_id=1, source_target_pairs={{4,8},{9,5},{20,24},{25,21},{6,10},{11,7},{22,26},{27,23}} | collective-permute-start | bytes 1572872 | tf_op jit(solution)/shard_map/ppermute | solution.py:281
  67.0 13.0 %collective-permute-start.23 = (bf16[256,1024]{1,0:T(8,128)(2,1)S(1)}, bf16[256,1024]{1,0:T(8,128)(2,1)S(1)}, u32[]{:S(2)}, u32[]{:S(2)}) collective-permute-start(bf16[256,1024]{1,0:T(8,128)(2,1)S(1)} %get-tuple-element.42.refs_2_), channel_id=1, source_target_pairs={{0,2},{2,0},{4,6},{6,4},{13,15},{15,13},{9,11},{11,9},{20,22},{22,... | collective-permute-start | bytes 1572872 | tf_op jit(solution)/shard_map/ppermute | solution.py:289
  70.2 11.3 %collective-permute-start.29 = (bf16[2,2,128,256]{3,2,1,0:T(8,128)(2,1)S(1)}, bf16[2,2,128,256]{3,2,1,0:T(8,128)(2,1)S(1)}, u32[]{:S(2)}, u32[]{:S(2)}) collective-permute-start(bf16[2,2,128,256]{3,2,1,0:T(8,128)(2,1)S(1)} %broadcast_select_fusion.2), channel_id=1, source_target_pairs={{0,4},{4,0},{8,12},{12,8},{1,5},{5,1},{9,13},{13,9},{2,6},{6,2},{1... | collective-permute-start | bytes 786440 | tf_op jit(solution)/shard_map/ppermute | solution.py:323
  74.0 15.1 %collective-permute-start.13 = (bf16[128,2048]{1,0:T(8,128)(2,1)S(1)}, bf16[128,2048]{1,0:T(8,128)(2,1)S(1)}, u32[]{:S(2)}, u32[]{:S(2)}) collective-permute-start(bf16[128,2048]{1,0:T(8,128)(2,1)S(1)} %copy-done.14), channel_id=1, source_target_pairs={{0,1},{1,0},{2,3},{3,2},{4,5},{5,4},{6,7},{7,6},{8,9},{9,8},{10,11... | collective-permute-start | bytes 1572872 | tf_op jit(solution)/shard_map/ppermute | solution.py:221
  74.5 14.6 %copy-start.18 = (bf16[256,1024]{1,0:T(8,128)(2,1)}, bf16[256,1024]{1,0:T(8,128)(2,1)S(1)}, u32[]{:S(2)}) copy-start(bf16[256,1024]{1,0:T(8,128)(2,1)S(1)} %collective-permute-done.18.refs_4_) | copy-start | bytes 1572868
  74.5 8.6 %collective-permute-start.19 = (bf16[256,1024]{1,0:T(8,128)(2,1)S(1)}, bf16[256,1024]{1,0:T(8,128)(2,1)S(1)}, u32[]{:S(2)}, u32[]{:S(2)}) collective-permute-start(bf16[256,1024]{1,0:T(8,128)(2,1)S(1)} %collective-permute-done.17), channel_id=1, source_target_pairs={{8,12},{5,1},{24,28},{21,17},{10,14},{7,3},{26,30},{23,19}} | collective-permute-start | bytes 1572872 | tf_op jit(solution)/shard_map/ppermute | solution.py:281
  80.1 3.9 %copy-start.19 = (bf16[256,1024]{1,0:T(8,128)(2,1)}, bf16[256,1024]{1,0:T(8,128)(2,1)S(1)}, u32[]{:S(2)}) copy-start(bf16[256,1024]{1,0:T(8,128)(2,1)S(1)} %collective-permute-done.23.refs_6_) | copy-start | bytes 1572868
  80.1 3.9 %collective-permute-start.24 = (bf16[256,1024]{1,0:T(8,128)(2,1)S(1)}, bf16[256,1024]{1,0:T(8,128)(2,1)S(1)}, u32[]{:S(2)}, u32[]{:S(2)}) collective-permute-start(bf16[256,1024]{1,0:T(8,128)(2,1)S(1)} %collective-permute-done.22), channel_id=1, source_target_pairs={{8,12},{5,1},{24,28},{21,17},{10,14},{7,3},{26,30},{23,19}} | collective-permute-start | bytes 1572872 | tf_op jit(solution)/shard_map/ppermute | solution.py:281
  81.4 18.1 %collective-permute-start.14 = (bf16[128,2048]{1,0:T(8,128)(2,1)S(1)}, bf16[128,2048]{1,0:T(8,128)(2,1)S(1)}, u32[]{:S(2)}, u32[]{:S(2)}) collective-permute-start(bf16[128,2048]{1,0:T(8,128)(2,1)S(1)} %collective-permute-done.11.c01), channel_id=1, source_target_pairs={{0,1},{1,0},{2,3},{3,2},{4,5},{5,4},{6,7},{7,6},{8,9},{9,8},{10,11... | collective-permute-start | bytes 1572872 | tf_op jit(solution)/shard_map/ppermute | solution.py:221
  81.8 15.3 %collective-permute-start.30 = (bf16[2,2,128,256]{3,2,1,0:T(8,128)(2,1)S(1)}, bf16[2,2,128,256]{3,2,1,0:T(8,128)(2,1)S(1)}, u32[]{:S(2)}, u32[]{:S(2)}) collective-permute-start(bf16[2,2,128,256]{3,2,1,0:T(8,128)(2,1)S(1)} %get-tuple-element.72), channel_id=1, source_target_pairs={{0,8},{4,12},{8,0},{12,4},{1,9},{5,13},{9,1},{13,5},{2,10},{6,14},... | collective-permute-start | bytes 786440 | tf_op jit(solution)/shard_map/ppermute | solution.py:323
  83.3 5.8 %copy-start.7 = (bf16[256,1024]{1,0:T(8,128)(2,1)}, bf16[256,1024]{1,0:T(8,128)(2,1)S(1)}, u32[]{:S(2)}) copy-start(bf16[256,1024]{1,0:T(8,128)(2,1)S(1)} %add.296.refs_1_) | copy-start | bytes 1572868
  83.3 16.2 %collective-permute-start.25 = (bf16[256,1024]{1,0:T(8,128)(2,1)S(1)}, bf16[256,1024]{1,0:T(8,128)(2,1)S(1)}, u32[]{:S(2)}, u32[]{:S(2)}) collective-permute-start(bf16[256,1024]{1,0:T(8,128)(2,1)S(1)} %add.296.refs_1_), channel_id=1, source_target_pairs={{8,10},{10,8},{12,14},{14,12},{5,7},{7,5},{1,3},{3,1},{24,26},{26,... | collective-permute-start | bytes 1572872 | tf_op jit(solution)/shard_map/ppermute | solution.py:289
  84.2 4.8 %copy-start.8 = (bf16[256,1024]{1,0:T(8,128)(2,1)}, bf16[256,1024]{1,0:T(8,128)(2,1)S(1)}, u32[]{:S(2)}) copy-start(bf16[256,1024]{1,0:T(8,128)(2,1)S(1)} %add.302.refs_3_) | copy-start | bytes 1572868
  84.2 16.9 %collective-permute-start.26 = (bf16[256,1024]{1,0:T(8,128)(2,1)S(1)}, bf16[256,1024]{1,0:T(8,128)(2,1)}, u32[]{:S(2)}, u32[]{:S(2)}) collective-permute-start(bf16[256,1024]{1,0:T(8,128)(2,1)S(1)} %add.302.refs_3_), channel_id=1, source_target_pairs={{8,10},{10,8},{12,14},{14,12},{5,7},{7,5},{1,3},{3,1},{24,26},{26,... | collective-permute-start | bytes 1572872 | tf_op jit(solution)/shard_map/ppermute | solution.py:289
  89.1 10.5 %copy-start.20 = (bf16[128,2048]{1,0:T(8,128)(2,1)}, bf16[128,2048]{1,0:T(8,128)(2,1)S(1)}, u32[]{:S(2)}) copy-start(bf16[128,2048]{1,0:T(8,128)(2,1)S(1)} %collective-permute-done.13.c10) | copy-start | bytes 1572868
  89.1 17.2 %collective-permute-start.27 = (bf16[2,128,256]{2,1,0:T(8,128)(2,1)S(1)}, bf16[2,128,256]{2,1,0:T(8,128)(2,1)S(1)}, u32[]{:S(2)}, u32[]{:S(2)}) collective-permute-start(bf16[2,128,256]{2,1,0:T(8,128)(2,1)S(1)} %get-tuple-element.84), channel_id=1, source_target_pairs={{0,2},{2,4},{4,6},{6,8},{8,10},{10,12},{12,14},{1,3},{3,5},{5,7},{... | collective-permute-start | bytes 393224 | tf_op jit(solution)/shard_map/ppermute | solution.py:387
  97.1 9.2 %collective-permute-start.28 = (bf16[2,128,256]{2,1,0:T(8,128)(2,1)S(1)}, bf16[2,128,256]{2,1,0:T(8,128)(2,1)S(1)}, u32[]{:S(2)}, u32[]{:S(2)}) collective-permute-start(bf16[2,128,256]{2,1,0:T(8,128)(2,1)S(1)} %get-tuple-element.82), channel_id=1, source_target_pairs={{2,0},{4,2},{6,4},{8,6},{10,8},{12,10},{14,12},{3,1},{5,3},{7,5},{... | collective-permute-start | bytes 393224 | tf_op jit(solution)/shard_map/ppermute | solution.py:387
  117.7 12.4 %collective-permute-start.35 = (bf16[2,2,128,256]{3,2,1,0:T(8,128)(2,1)}, bf16[2,2,128,256]{3,2,1,0:T(8,128)(2,1)S(1)}, u32[]{:S(2)}, u32[]{:S(2)}) collective-permute-start(bf16[2,2,128,256]{3,2,1,0:T(8,128)(2,1)} %get-tuple-element.53), channel_id=1, source_target_pairs={{0,2},{2,0},{1,3},{3,1},{4,6},{6,4},{5,7},{7,5},{8,10},{10,8},{9,1... | collective-permute-start | bytes 786440 | tf_op jit(solution)/shard_map/ppermute | solution.py:323
  120.4 9.7 %copy-start.12 = (bf16[2,2,128,256]{3,2,1,0:T(8,128)(2,1)S(1)}, bf16[2,2,128,256]{3,2,1,0:T(8,128)(2,1)}, u32[]{:S(2)}) copy-start(bf16[2,2,128,256]{3,2,1,0:T(8,128)(2,1)} %get-tuple-element.54) | copy-start | bytes 786436
  120.4 9.7 %copy-start.13 = (bf16[2,2,128,256]{3,2,1,0:T(8,128)(2,1)S(1)}, bf16[2,2,128,256]{3,2,1,0:T(8,128)(2,1)}, u32[]{:S(2)}) copy-start(bf16[2,2,128,256]{3,2,1,0:T(8,128)(2,1)} %get-tuple-element.52) | copy-start | bytes 786436
  120.4 9.9 %copy-start.29 = (bf16[2,128,256]{2,1,0:T(8,128)(2,1)S(1)}, bf16[2,128,256]{2,1,0:T(8,128)(2,1)}, u32[]{:S(2)}) copy-start(bf16[2,128,256]{2,1,0:T(8,128)(2,1)} %get-tuple-element.50) | copy-start | bytes 393220
  120.4 11.2 %copy-start.28 = (bf16[2,128,256]{2,1,0:T(8,128)(2,1)S(1)}, bf16[2,128,256]{2,1,0:T(8,128)(2,1)}, u32[]{:S(2)}) copy-start(bf16[2,128,256]{2,1,0:T(8,128)(2,1)} %get-tuple-element.51) | copy-start | bytes 393220
  126.0 14.4 %copy-start.9 = (f32[256,2048]{1,0:T(8,128)S(1)}, f32[256,2048]{1,0:T(8,128)}, u32[]{:S(2)}) copy-start(f32[256,2048]{1,0:T(8,128)} %get-tuple-element.47) | copy-start | bytes 6291460
  126.0 14.4 %collective-permute-start.31 = (bf16[256,2048]{1,0:T(8,128)(2,1)}, bf16[256,2048]{1,0:T(8,128)(2,1)S(1)}, u32[]{:S(2)}, u32[]{:S(2)}) collective-permute-start(bf16[256,2048]{1,0:T(8,128)(2,1)} %get-tuple-element.48), channel_id=1, source_target_pairs={{0,1},{1,0},{2,3},{3,2},{4,5},{5,4},{6,7},{7,6},{8,9},{9,8},{10,11... | collective-permute-start | bytes 3145736 | tf_op jit(solution)/shard_map/ppermute | solution.py:221
  130.2 9.2 %collective-permute-start.36 = (bf16[2,2,128,256]{3,2,1,0:T(8,128)(2,1)S(1)}, bf16[2,2,128,256]{3,2,1,0:T(8,128)(2,1)S(1)}, u32[]{:S(2)}, u32[]{:S(2)}) collective-permute-start(bf16[2,2,128,256]{3,2,1,0:T(8,128)(2,1)S(1)} %broadcast_select_fusion), channel_id=1, source_target_pairs={{0,4},{4,0},{8,12},{12,8},{1,5},{5,1},{9,13},{13,9},{2,6},{6,2},{1... | collective-permute-start | bytes 786440 | tf_op jit(solution)/shard_map/ppermute | solution.py:323
  130.4 23.4 %collective-permute-start.33 = (bf16[2,128,256]{2,1,0:T(8,128)(2,1)S(1)}, bf16[2,128,256]{2,1,0:T(8,128)(2,1)S(1)}, u32[]{:S(2)}, u32[]{:S(2)}) collective-permute-start(bf16[2,128,256]{2,1,0:T(8,128)(2,1)S(1)} %copy-done.29), channel_id=1, source_target_pairs={{2,0},{4,2},{6,4},{8,6},{10,8},{12,10},{14,12},{3,1},{5,3},{7,5},{... | collective-permute-start | bytes 393224 | tf_op jit(solution)/shard_map/ppermute | solution.py:441
  131.7 22.1 %collective-permute-start.34 = (bf16[2,128,256]{2,1,0:T(8,128)(2,1)S(1)}, bf16[2,128,256]{2,1,0:T(8,128)(2,1)S(1)}, u32[]{:S(2)}, u32[]{:S(2)}) collective-permute-start(bf16[2,128,256]{2,1,0:T(8,128)(2,1)S(1)} %copy-done.28), channel_id=1, source_target_pairs={{0,2},{2,4},{4,6},{6,8},{8,10},{10,12},{12,14},{1,3},{3,5},{5,7},{... | collective-permute-start | bytes 393224 | tf_op jit(solution)/shard_map/ppermute | solution.py:441
  139.8 13.1 %collective-permute-start.37 = (bf16[2,2,128,256]{3,2,1,0:T(8,128)(2,1)S(1)}, bf16[2,2,128,256]{3,2,1,0:T(8,128)(2,1)S(1)}, u32[]{:S(2)}, u32[]{:S(2)}) collective-permute-start(bf16[2,2,128,256]{3,2,1,0:T(8,128)(2,1)S(1)} %get-tuple-element.64), channel_id=1, source_target_pairs={{0,8},{4,12},{8,0},{12,4},{1,9},{5,13},{9,1},{13,5},{2,10},{6,14},... | collective-permute-start | bytes 786440 | tf_op jit(solution)/shard_map/ppermute | solution.py:323
  140.7 13.0 %collective-permute-start.32 = (bf16[128,2048]{1,0:T(8,128)(2,1)S(1)}, bf16[128,2048]{1,0:T(8,128)(2,1)S(1)}, u32[]{:S(2)}, u32[]{:S(2)}) collective-permute-start(bf16[128,2048]{1,0:T(8,128)(2,1)S(1)} %slice.101), channel_id=1, source_target_pairs={{0,16},{16,0},{1,17},{17,1},{2,18},{18,2},{3,19},{19,3},{4,20},{20... | collective-permute-start | bytes 1572872 | tf_op jit(solution)/shard_map/ppermute | solution.py:221
  154.4 5.5 %copy-start.1 = (bf16[128,2048]{1,0:T(8,128)(2,1)S(1)}, bf16[128,2048]{1,0:T(8,128)(2,1)}, u32[]{:S(2)}) copy-start(bf16[128,2048]{1,0:T(8,128)(2,1)} %h00.1) | copy-start | bytes 1572868
  159.8 18.3 %copy-start.2 = (f32[256,2048]{1,0:T(8,128)S(1)}, f32[256,2048]{1,0:T(8,128)}, u32[]{:S(2)}) copy-start(f32[256,2048]{1,0:T(8,128)} %get-tuple-element.62) | copy-start | bytes 6291460
  159.8 2.9 %collective-permute-start.38 = (bf16[256,2048]{1,0:T(8,128)(2,1)}, bf16[256,2048]{1,0:T(8,128)(2,1)S(1)}, u32[]{:S(2)}, u32[]{:S(2)}) collective-permute-start(bf16[256,2048]{1,0:T(8,128)(2,1)} %get-tuple-element.63), channel_id=1, source_target_pairs={{0,1},{1,0},{2,3},{3,2},{4,5},{5,4},{6,7},{7,6},{8,9},{9,8},{10,11... | collective-permute-start | bytes 3145736 | tf_op jit(solution)/shard_map/ppermute | solution.py:221
  164.1 14.0 %collective-permute-start.39 = (bf16[128,2048]{1,0:T(8,128)(2,1)S(1)}, bf16[128,2048]{1,0:T(8,128)(2,1)S(1)}, u32[]{:S(2)}, u32[]{:S(2)}) collective-permute-start(bf16[128,2048]{1,0:T(8,128)(2,1)S(1)} %add_convert_fusion), channel_id=1, source_target_pairs={{0,16},{16,0},{1,17},{17,1},{2,18},{18,2},{3,19},{19,3},{4,20},{20... | collective-permute-start | bytes 1572872 | tf_op jit(solution)/shard_map/ppermute | solution.py:221
  (9 other events, 6.8 us)

commit v7 on v6

--- a/solution.py
+++ b/solution.py
@@ -447,7 +447,7 @@
         back = swap(other, "x")
         return keep[:BLK] + got[:BLK].astype(F32) + back.astype(F32), other, back
 
-    chunk = width // 4
+    chunk = width // 2
     partial = (jax.ShapeDtypeStruct((rows, width), F32), jax.ShapeDtypeStruct((rows, width), BF16))
     out_parts = pl.pallas_call(
             output_kernel,

time: 181 us -> 180 us (level)
  transfers between devices with their start and end apart: 40 -> 40, of which waited for: 15 -> 16; matrix products, arithmetic and copies ran while one was open for 11% -> 11% of each run, Pallas kernels for 14% -> 14%
where the time goes in v7:
time: 180 us
  starting transfers between devices  56.3 us (31%)
  waiting for transfers between devices  51 us (28%)
  Pallas kernels  40.9 us (23%)
  local copies, waits for them, and re-layouts  12.5 us (7%)
  other arithmetic  11.7 us (6%)
  matrix products  4.6 us (3%)
  between operations  2.49 us (1%)
    ppermute x13, waiting for transfers between devices, swap(): return lax.ppermute(value, axis, [(0, 1), (1, 0)])  19.8 us
    ppermute x7, waiting for transfers between devices, ring(): lax.ppermute(value, axis, [(i, (i + 1) % count) for i in range(count)])  15 us
    ppermute x13, starting transfers between devices, swap(): return lax.ppermute(value, axis, [(0, 1), (1, 0)])  13.7 us
    pallas_call x1, Pallas kernels, body(): pl.pallas_call(attention_kernel, grid=(2,), out_shape=(jax.ShapeDtypeStru...  10.7 us
    ppermute x6, starting transfers between devices, trade(): got = lax.ppermute(packed, axis, pairs)  10.7 us
    pallas_call x1, Pallas kernels, body(): pl.pallas_call(query_part_kernel, grid=(steps,), out_shape=(jax.ShapeDtyp...  9.81 us
    ppermute x6, waiting for transfers between devices, trade(): got = lax.ppermute(packed, axis, pairs)  8.37 us
    ppermute x7, starting transfers between devices, ring(): lax.ppermute(value, axis, [(i, (i + 1) % count) for i in range(count)])  8.33 us
  transfers between devices with their start and end apart: 40, of which 16 were waited for; matrix products, arithmetic and copies ran while one was open for 11% of the time, Pallas kernels for 14%

profile of v7, /device:TPU:0, one launch (start us, length us, event | category | flops | bytes accessed | tf_op | source)
XLA Modules:
  0.0 179.5 jit_solution(10624816893248356511)
XLA Ops:
  0.7 3.0 %collective-permute-start = (bf16[128,2048]{1,0:T(8,128)(2,1)}, bf16[128,2048]{1,0:T(8,128)(2,1)S(1)}, u32[]{:S(2)}, u32[]{:S(2)}) collective-permute-start(bf16[128,2048]{1,0:T(8,128)(2,1)} %h00.1), channel_id=1, source_target_pairs={{0,16},{16,0},{1,17},{17,1},{2,18},{18,2},{3,19},{19,3},{4,20},{20... | collective-permute-start | bytes 1572872 | tf_op jit(solution)/shard_map/ppermute | solution.py:221
  3.7 1.0 constant_dynamic-slice_fusion
  4.7 0.8 constant_dynamic-slice_fusion.2
  6.1 1.1 collective-permute-done.4
  7.4 0.8 constant_dynamic-update-slice_fusion.7
  8.2 1.5 collective-permute-start.5
  9.9 1.6 collective-permute-start.6
  12.9 2.9 %collective-permute-done.h01 = bf16[128,2048]{1,0:T(8,128)(2,1)S(1)} collective-permute-done((bf16[128,2048]{1,0:T(8,128)(2,1)}, bf16[128,2048]{1,0:T(8,128)(2,1)S(1)}, u32[]{:S(2)}, u32[]{:S(2)}) %collective-permute-start) | collective-permute-done | bytes 524320 | tf_op jit(solution)/shard_map/ppermute | solution.py:221
  15.8 1.7 collective-permute-start.1
  17.6 1.6 fusion.14
  20.5 1.8 %collective-permute-start.11 = (bf16[128,2048]{1,0:T(8,128)(2,1)S(1)}, bf16[128,2048]{1,0:T(8,128)(2,1)S(1)}, u32[]{:S(2)}, u32[]{:S(2)}) collective-permute-start(bf16[128,2048]{1,0:T(8,128)(2,1)S(1)} %copy-done.14), channel_id=1, source_target_pairs={{0,16},{16,0},{1,17},{17,1},{2,18},{18,2},{3,19},{19,3},{4,20},{20... | collective-permute-start | bytes 1572872 | tf_op jit(solution)/shard_map/ppermute | solution.py:221
  22.4 1.0 collective-permute-done.6
  24.0 1.5 collective-permute-start.7
  25.6 0.8 constant_dynamic-update-slice_fusion.6
  26.3 7.7 %collective-permute-done.7 = bf16[256,768]{1,0:T(8,128)(2,1)S(1)} collective-permute-done((bf16[256,768]{1,0:T(8,128)(2,1)S(1)}, bf16[256,768]{1,0:T(8,128)(2,1)S(1)}, u32[]{:S(2)}, u32[]{:S(2)}) %collective-permute-start.7) | collective-permute-done | bytes 393248 | tf_op jit(solution)/shard_map/ppermute | solution.py:234
  34.0 1.8 collective-permute-done.8
  35.8 1.5 collective-permute-start.9
  37.3 0.8 constant_dynamic-update-slice_fusion.5
  38.1 0.8 constant_dynamic-update-slice_fusion.4
  38.9 0.8 constant_dynamic-update-slice_fusion.3
  39.7 0.8 copy-done.16
  40.5 0.8 copy-done.21
  41.3 4.9 %norm.1 = bf16[2,512,2048]{2,1,0:T(8,128)(2,1)} custom-call(bf16[128,2048]{1,0:T(8,128)(2,1)} %h00.1, bf16[128,2048]{1,0:T(8,128)(2,1)} %copy-done.15, bf16[128,2048]{1,0:T(8,128)(2,1)} %copy-done.16, bf16[128,2048]{1,0:T(8,128)(2,1)} %copy-done.21), custom_call_target="tpu_custom_call" | custom-call | flops 1000000000 | bytes 6291456 | tf_op jit(solution)/shard_map/norm/pallas_call | solution.py:365
  46.2 1.1 collective-permute-done.10
  47.3 1.5 collective-permute-start.12
  48.9 1.3 collective-permute-start.20
  50.3 1.3 collective-permute-start.16
  51.6 1.0 constant_dynamic-update-slice_fusion.2
  52.7 3.5 %collective-permute-done.12 = bf16[256,768]{1,0:T(8,128)(2,1)S(1)} collective-permute-done((bf16[256,768]{1,0:T(8,128)(2,1)S(1)}, bf16[256,768]{1,0:T(8,128)(2,1)S(1)}, u32[]{:S(2)}, u32[]{:S(2)}) %collective-permute-start.12) | collective-permute-done | bytes 393248 | tf_op jit(solution)/shard_map/ppermute | solution.py:234
  56.2 1.3 convolution_convert_fusion
  57.5 0.7 copy-done.24
  58.5 1.6 collective-permute-start.21
  60.1 2.4 %collective-permute-done.16 = bf16[256,1024]{1,0:T(8,128)(2,1)S(1)} collective-permute-done((bf16[256,1024]{1,0:T(8,128)(2,1)S(1)}, bf16[256,1024]{1,0:T(8,128)(2,1)S(1)}, u32[]{:S(2)}, u32[]{:S(2)}) %collective-permute-start.16) | collective-permute-done | bytes 524320 | tf_op jit(solution)/shard_map/ppermute | solution.py:281
  63.4 2.9 %collective-permute-start.18 = (bf16[256,1024]{1,0:T(8,128)(2,1)S(1)}, bf16[256,1024]{1,0:T(8,128)(2,1)S(1)}, u32[]{:S(2)}, u32[]{:S(2)}) collective-permute-start(bf16[256,1024]{1,0:T(8,128)(2,1)S(1)} %get-tuple-element.39.refs_0_), channel_id=1, source_target_pairs={{0,2},{2,0},{4,6},{6,4},{13,15},{15,13},{9,11},{11,9},{20,22},{22,... | collective-permute-start | bytes 1572872 | tf_op jit(solution)/shard_map/ppermute | solution.py:289
  67.0 2.9 %collective-permute-start.23 = (bf16[256,1024]{1,0:T(8,128)(2,1)S(1)}, bf16[256,1024]{1,0:T(8,128)(2,1)S(1)}, u32[]{:S(2)}, u32[]{:S(2)}) collective-permute-start(bf16[256,1024]{1,0:T(8,128)(2,1)S(1)} %get-tuple-element.42.refs_2_), channel_id=1, source_target_pairs={{0,2},{2,0},{4,6},{6,4},{13,15},{15,13},{9,11},{11,9},{20,22},{22,... | collective-permute-start | bytes 1572872 | tf_op jit(solution)/shard_map/ppermute | solution.py:289
  70.2 3.8 %collective-permute-start.29 = (bf16[2,2,128,256]{3,2,1,0:T(8,128)(2,1)S(1)}, bf16[2,2,128,256]{3,2,1,0:T(8,128)(2,1)S(1)}, u32[]{:S(2)}, u32[]{:S(2)}) collective-permute-start(bf16[2,2,128,256]{3,2,1,0:T(8,128)(2,1)S(1)} %broadcast_select_fusion.2), channel_id=1, source_target_pairs={{0,4},{4,0},{8,12},{12,8},{1,5},{5,1},{9,13},{13,9},{2,6},{6,2},{1... | collective-permute-start | bytes 786440 | tf_op jit(solution)/shard_map/ppermute | solution.py:323
  75.2 4.9 %collective-permute-done.23.refs_6_ = bf16[256,1024]{1,0:T(8,128)(2,1)S(1)} collective-permute-done((bf16[256,1024]{1,0:T(8,128)(2,1)S(1)}, bf16[256,1024]{1,0:T(8,128)(2,1)S(1)}, u32[]{:S(2)}, u32[]{:S(2)}) %collective-permute-start.23) | collective-permute-done | bytes 524320 | tf_op jit(solution)/shard_map/ppermute | solution.py:289
  81.8 1.3 collective-permute-start.30
  84.2 1.5 collective-permute-start.26
  85.7 3.3 %fusion.2 = bf16[1024,512]{1,0:T(8,128)(2,1)} fusion(bf16[1024,2048]{1,0:T(8,128)(2,1)S(1)} %bitcast.20, bf16[2048,768]{1,0:T(8,128)(2,1)S(1)} %constant_dynamic-update-slice_fusion.w.wm), kind=kOutput, calls=%fused_computation.3 | convolution fusion | flops 2148007936 | bytes 7340032 | tf_op jit(solution)/shard_map/dot_general | solution.py:22
  89.1 2.9 %collective-permute-start.27 = (bf16[2,128,256]{2,1,0:T(8,128)(2,1)S(1)}, bf16[2,128,256]{2,1,0:T(8,128)(2,1)S(1)}, u32[]{:S(2)}, u32[]{:S(2)}) collective-permute-start(bf16[2,128,256]{2,1,0:T(8,128)(2,1)S(1)} %get-tuple-element.84), channel_id=1, source_target_pairs={{0,2},{2,4},{4,6},{6,8},{8,10},{10,12},{12,14},{1,3},{3,5},{5,7},{... | collective-permute-start | bytes 393224 | tf_op jit(solution)/shard_map/ppermute | solution.py:387
  92.0 5.1 %collective-permute-done.30 = bf16[2,2,128,256]{3,2,1,0:T(8,128)(2,1)S(1)} collective-permute-done((bf16[2,2,128,256]{3,2,1,0:T(8,128)(2,1)S(1)}, bf16[2,2,128,256]{3,2,1,0:T(8,128)(2,1)S(1)}, u32[]{:S(2)}, u32[]{:S(2)}) %collective-permute-start.30) | collective-permute-done | bytes 262176 | tf_op jit(solution)/shard_map/ppermute | solution.py:323
  97.1 1.5 collective-permute-start.28
  98.6 0.9 add_select_fusion.6
  99.5 0.8 copy-done.22
  100.3 0.8 copy-done.23
  101.2 5.1 %grad_att.1 = (bf16[512,512]{1,0:T(8,128)(2,1)}, bf16[512,2048]{1,0:T(8,128)(2,1)}) custom-call(bf16[128,2048]{1,0:T(8,128)(2,1)} %c00.1, bf16[128,2048]{1,0:T(8,128)(2,1)} %copy-done.17, bf16[128,2048]{1,0:T(8,128)(2,1)} %copy-done.20, bf16[128,2048]{1,0:T(8,128)(2,1)} %copy-done.22, bf16[256,1024]{1,0:T(8,128)(2,1)} %copy-done.11, ...), custom_call_target="tpu_custom_call" | custom-call | flops 1000000000 | bytes 9437184 | tf_op jit(solution)/shard_map/grad_att/pallas_call | solution.py:400
  107.0 10.7 %attention.1 = (bf16[2,2,2,128,512]{4,3,2,1,0:T(8,128)(2,1)}, bf16[2,2,2,128,512]{4,3,2,1,0:T(8,128)(2,1)}, f32[2,2,2,128,256]{4,3,2,1,0:T(8,128)}, bf16[2,128,2...) custom-call(s32[2]{0:T(128)} %pad_add_fusion.chosen, ...), custom_call_target="tpu_custom_call" | custom-call | flops 8000000000 | bytes 10485760 | tf_op jit(solution)/shard_map/attention/pallas_call | solution.py:421
  117.7 2.7 %collective-permute-start.35 = (bf16[2,2,128,256]{3,2,1,0:T(8,128)(2,1)}, bf16[2,2,128,256]{3,2,1,0:T(8,128)(2,1)S(1)}, u32[]{:S(2)}, u32[]{:S(2)}) collective-permute-start(bf16[2,2,128,256]{3,2,1,0:T(8,128)(2,1)} %get-tuple-element.53), channel_id=1, source_target_pairs={{0,2},{2,0},{1,3},{3,1},{4,6},{6,4},{5,7},{7,5},{8,10},{10,8},{9,1... | collective-permute-start | bytes 786440 | tf_op jit(solution)/shard_map/ppermute | solution.py:323
  120.4 5.0 %output.1 = (f32[256,2048]{1,0:T(8,128)}, bf16[256,2048]{1,0:T(8,128)(2,1)}) custom-call(bf16[2,2,256,512]{3,2,1,0:T(8,128)(2,1)} %bitcast.26, bf16[512,2048]{1,0:T(8,128)(2,1)} %get-tuple-element.46.w), custom_call_target="tpu_custom_call" | custom-call | flops 2000000000 | bytes 7340032 | tf_op jit(solution)/shard_map/output/pallas_call | solution.py:452
  125.4 4.2 %collective-permute-start.31 = (bf16[256,2048]{1,0:T(8,128)(2,1)}, bf16[256,2048]{1,0:T(8,128)(2,1)S(1)}, u32[]{:S(2)}, u32[]{:S(2)}) collective-permute-start(bf16[256,2048]{1,0:T(8,128)(2,1)} %get-tuple-element.48), channel_id=1, source_target_pairs={{0,1},{1,0},{2,3},{3,2},{4,5},{5,4},{6,7},{7,6},{8,9},{9,8},{10,11... | collective-permute-start | bytes 3145736 | tf_op jit(solution)/shard_map/ppermute | solution.py:221
  129.8 1.3 collective-permute-start.33
  131.1 4.6 %collective-permute-start.34 = (bf16[2,128,256]{2,1,0:T(8,128)(2,1)S(1)}, bf16[2,128,256]{2,1,0:T(8,128)(2,1)S(1)}, u32[]{:S(2)}, u32[]{:S(2)}) collective-permute-start(bf16[2,128,256]{2,1,0:T(8,128)(2,1)S(1)} %copy-done.28), channel_id=1, source_target_pairs={{0,2},{2,4},{4,6},{6,8},{8,10},{10,12},{12,14},{1,3},{3,5},{5,7},{... | collective-permute-start | bytes 393224 | tf_op jit(solution)/shard_map/ppermute | solution.py:441
  135.7 3.3 %collective-permute-done.36 = bf16[2,2,128,256]{3,2,1,0:T(8,128)(2,1)S(1)} collective-permute-done((bf16[2,2,128,256]{3,2,1,0:T(8,128)(2,1)S(1)}, bf16[2,2,128,256]{3,2,1,0:T(8,128)(2,1)S(1)}, u32[]{:S(2)}, u32[]{:S(2)}) %collective-permute-start.36) | collective-permute-done | bytes 262176 | tf_op jit(solution)/shard_map/ppermute | solution.py:323
  139.2 1.2 collective-permute-start.37
  140.7 1.9 %collective-permute-start.32 = (bf16[128,2048]{1,0:T(8,128)(2,1)S(1)}, bf16[128,2048]{1,0:T(8,128)(2,1)S(1)}, u32[]{:S(2)}, u32[]{:S(2)}) collective-permute-start(bf16[128,2048]{1,0:T(8,128)(2,1)S(1)} %slice.101), channel_id=1, source_target_pairs={{0,16},{16,0},{1,17},{17,1},{2,18},{18,2},{3,19},{19,3},{4,20},{20... | collective-permute-start | bytes 1572872 | tf_op jit(solution)/shard_map/ppermute | solution.py:221
  142.6 9.8 %query_part.1 = (f32[2,256,2048]{2,1,0:T(8,128)}, bf16[2048,256]{1,0:T(8,128)(2,1)}, bf16[2048,256]{1,0:T(8,128)(2,1)}) custom-call(bf16[2,2,256,512]{3,2,1,0:T(8,128)(2,1)} %bitcast.24, bf16[2048,768]{1,0:T(8,128)(2,1)} %copy-done.6, bf16[2048,768]{1,0:T(8,128)(2,1)} %copy-done.6), custom_call_target="tpu_custom_call" | custom-call | flops 3000000000 | bytes 13631488 | tf_op jit(solution)/shard_map/query_part/pallas_call | solution.py:478
  152.4 0.9 add_select_fusion
  154.2 5.4 %key_part.1 = (f32[256,2048]{1,0:T(8,128)}, bf16[256,2048]{1,0:T(8,128)(2,1)}) custom-call(s32[2]{0:T(128)} %pad_add_fusion.chosen, f32[2,2,2,128,256]{4,3,2,1,0:T(8,128)} %get-tuple-element.49.dkv, bf16[2,128,256]{2,1,0:T(8,128)(2,1)} %copy-done.26, bf16[2,128,256]{2,1,0:T(8,128)(2,1)} %copy-done.27, bf16[2,2,128,256]{3,2,1,0:T(8,128)(2,1)} %get-tuple-element.56.far_p, ...), custom_call_target="tpu_custom_call" | custom-call | flops 500000000 | bytes 8388608 | tf_op jit(solution)/shard_map/key_part/pallas_call | solution.py:511
  159.9 2.7 %collective-permute-done.38 = bf16[256,2048]{1,0:T(8,128)(2,1)S(1)} collective-permute-done((bf16[256,2048]{1,0:T(8,128)(2,1)}, bf16[256,2048]{1,0:T(8,128)(2,1)S(1)}, u32[]{:S(2)}, u32[]{:S(2)}) %collective-permute-start.38) | collective-permute-done | bytes 1048608 | tf_op jit(solution)/shard_map/ppermute | solution.py:221
  162.5 1.4 add_convert_fusion
  164.3 0.9 fusion.12
  165.2 12.8 %collective-permute-done.39 = bf16[128,2048]{1,0:T(8,128)(2,1)S(1)} collective-permute-done((bf16[128,2048]{1,0:T(8,128)(2,1)S(1)}, bf16[128,2048]{1,0:T(8,128)(2,1)S(1)}, u32[]{:S(2)}, u32[]{:S(2)}) %collective-permute-start.39) | collective-permute-done | bytes 524320 | tf_op jit(solution)/shard_map/ppermute | solution.py:221
  178.3 1.2 fusion.10
  (135 shorter events, 12.7 us)
Async XLA Ops:
  0.6 10.9 %copy-start = (bf16[128,2048]{1,0:T(8,128)(2,1)S(1)}, bf16[128,2048]{1,0:T(8,128)(2,1)}, u32[]{:S(2)}) copy-start(bf16[128,2048]{1,0:T(8,128)(2,1)} %h00.1) | copy-start | bytes 1572868
  0.6 16.9 %copy-start.25 = (bf16[128,2048]{1,0:T(8,128)(2,1)S(1)}, bf16[128,2048]{1,0:T(8,128)(2,1)}, u32[]{:S(2)}) copy-start(bf16[128,2048]{1,0:T(8,128)(2,1)} %param.9) | copy-start | bytes 1572868
  0.7 10.9 %copy-start.32 = (s32[2]{0:T(128)S(1)}, s32[2]{0:T(128)}, u32[]{:S(2)}) copy-start(s32[2]{0:T(128)} %param.10) | copy-start | bytes 28
  0.7 15.1 %collective-permute-start = (bf16[128,2048]{1,0:T(8,128)(2,1)}, bf16[128,2048]{1,0:T(8,128)(2,1)S(1)}, u32[]{:S(2)}, u32[]{:S(2)}) collective-permute-start(bf16[128,2048]{1,0:T(8,128)(2,1)} %h00.1), channel_id=1, source_target_pairs={{0,16},{16,0},{1,17},{17,1},{2,18},{18,2},{3,19},{19,3},{4,20},{20... | collective-permute-start | bytes 1572872 | tf_op jit(solution)/shard_map/ppermute | solution.py:221
  3.7 13.9 %collective-permute-start.15 = (bf16[128,2048]{1,0:T(8,128)(2,1)}, bf16[128,2048]{1,0:T(8,128)(2,1)}, u32[]{:S(2)}, u32[]{:S(2)}) collective-permute-start(bf16[128,2048]{1,0:T(8,128)(2,1)} %param.9), channel_id=1, source_target_pairs={{0,1},{1,0},{2,3},{3,2},{4,5},{5,4},{6,7},{7,6},{8,9},{9,8},{10,11... | collective-permute-start | bytes 1572872 | tf_op jit(solution)/shard_map/ppermute | solution.py:221
  5.5 1.6 collective-permute-start.4
  7.2 13.3 %copy-start.14 = (bf16[128,2048]{1,0:T(8,128)(2,1)S(1)}, bf16[128,2048]{1,0:T(8,128)(2,1)}, u32[]{:S(2)}) copy-start(bf16[128,2048]{1,0:T(8,128)(2,1)} %c00.1) | copy-start | bytes 1572868
  8.2 1.7 copy-start.4
  8.2 14.1 %collective-permute-start.5 = (bf16[256,768]{1,0:T(8,128)(2,1)}, bf16[256,768]{1,0:T(8,128)(2,1)S(1)}, u32[]{:S(2)}, u32[]{:S(2)}) collective-permute-start(bf16[256,768]{1,0:T(8,128)(2,1)} %get-tuple-element.77), channel_id=1, source_target_pairs={{0,2},{2,0},{1,3},{3,1},{4,6},{6,4},{5,7},{7,5},{8,10},{10,8},{9,1... | collective-permute-start | bytes 1179656 | tf_op jit(solution)/shard_map/ppermute | solution.py:234
  9.9 13.5 %collective-permute-start.6 = (bf16[256,768]{1,0:T(8,128)(2,1)}, bf16[256,768]{1,0:T(8,128)(2,1)S(1)}, u32[]{:S(2)}, u32[]{:S(2)}) collective-permute-start(bf16[256,768]{1,0:T(8,128)(2,1)} %get-tuple-element.77), channel_id=1, source_target_pairs={{0,4},{4,8},{8,12},{12,0},{1,5},{5,9},{9,13},{13,1},{2,6},{6,10},{... | collective-permute-start | bytes 1179656 | tf_op jit(solution)/shard_map/ppermute | solution.py:234
  11.5 28.2 %collective-permute-start.2 = (bf16[128,2048]{1,0:T(8,128)(2,1)S(1)}, bf16[128,2048]{1,0:T(8,128)(2,1)S(1)}, u32[]{:S(2)}, u32[]{:S(2)}) collective-permute-start(bf16[128,2048]{1,0:T(8,128)(2,1)S(1)} %copy-done), channel_id=1, source_target_pairs={{0,1},{1,0},{2,3},{3,2},{4,5},{5,4},{6,7},{7,6},{8,9},{9,8},{10,11... | collective-permute-start | bytes 1572872 | tf_op jit(solution)/shard_map/ppermute | solution.py:221
  15.8 23.9 %copy-start.15 = (bf16[128,2048]{1,0:T(8,128)(2,1)}, bf16[128,2048]{1,0:T(8,128)(2,1)S(1)}, u32[]{:S(2)}) copy-start(bf16[128,2048]{1,0:T(8,128)(2,1)S(1)} %collective-permute-done.h01) | copy-start | bytes 1572868
  15.8 3.6 %collective-permute-start.1 = (f32[8,128]{1,0:T(8,128)S(1)}, f32[8,128]{1,0:T(8,128)S(1)}, u32[]{:S(2)}, u32[]{:S(2)}) collective-permute-start(f32[8,128]{1,0:T(8,128)S(1)} %broadcast_in_dim.125), channel_id=1, source_target_pairs={{0,16},{16,0},{1,17},{17,1},{2,18},{18,2},{3,19},{19,3},{4,20},{20... | collective-permute-start | bytes 12296 | tf_op jit(solution)/shard_map/ppermute | solution.py:221
  17.5 22.1 %collective-permute-start.3 = (bf16[128,2048]{1,0:T(8,128)(2,1)S(1)}, bf16[128,2048]{1,0:T(8,128)(2,1)S(1)}, u32[]{:S(2)}, u32[]{:S(2)}) collective-permute-start(bf16[128,2048]{1,0:T(8,128)(2,1)S(1)} %collective-permute-done.h01), channel_id=1, source_target_pairs={{0,1},{1,0},{2,3},{3,2},{4,5},{5,4},{6,7},{7,6},{8,9},{9,8},{10,11... | collective-permute-start | bytes 1572872 | tf_op jit(solution)/shard_map/ppermute | solution.py:221
  20.5 25.8 %collective-permute-start.11 = (bf16[128,2048]{1,0:T(8,128)(2,1)S(1)}, bf16[128,2048]{1,0:T(8,128)(2,1)S(1)}, u32[]{:S(2)}, u32[]{:S(2)}) collective-permute-start(bf16[128,2048]{1,0:T(8,128)(2,1)S(1)} %copy-done.14), channel_id=1, source_target_pairs={{0,16},{16,0},{1,17},{17,1},{2,18},{18,2},{3,19},{19,3},{4,20},{20... | collective-permute-start | bytes 1572872 | tf_op jit(solution)/shard_map/ppermute | solution.py:221
  23.4 12.4 %collective-permute-start.8 = (bf16[256,768]{1,0:T(8,128)(2,1)S(1)}, bf16[256,768]{1,0:T(8,128)(2,1)S(1)}, u32[]{:S(2)}, u32[]{:S(2)}) collective-permute-start(bf16[256,768]{1,0:T(8,128)(2,1)S(1)} %collective-permute-done.6), channel_id=1, source_target_pairs={{0,4},{4,8},{8,12},{12,0},{1,5},{5,9},{9,13},{13,1},{2,6},{6,10},{... | collective-permute-start | bytes 1179656 | tf_op jit(solution)/shard_map/ppermute | solution.py:234
  24.0 10.0 %collective-permute-start.7 = (bf16[256,768]{1,0:T(8,128)(2,1)S(1)}, bf16[256,768]{1,0:T(8,128)(2,1)S(1)}, u32[]{:S(2)}, u32[]{:S(2)}) collective-permute-start(bf16[256,768]{1,0:T(8,128)(2,1)S(1)} %collective-permute-done.6), channel_id=1, source_target_pairs={{0,2},{2,0},{1,3},{3,1},{4,6},{6,4},{5,7},{7,5},{8,10},{10,8},{9,1... | collective-permute-start | bytes 1179656 | tf_op jit(solution)/shard_map/ppermute | solution.py:234
  35.8 11.5 %collective-permute-start.10 = (bf16[256,768]{1,0:T(8,128)(2,1)S(1)}, bf16[256,768]{1,0:T(8,128)(2,1)S(1)}, u32[]{:S(2)}, u32[]{:S(2)}) collective-permute-start(bf16[256,768]{1,0:T(8,128)(2,1)S(1)} %collective-permute-done.8), channel_id=1, source_target_pairs={{0,4},{4,8},{8,12},{12,0},{1,5},{5,9},{9,13},{13,1},{2,6},{6,10},{... | collective-permute-start | bytes 1179656 | tf_op jit(solution)/shard_map/ppermute | solution.py:234
  35.8 10.4 %collective-permute-start.9 = (bf16[256,768]{1,0:T(8,128)(2,1)S(1)}, bf16[256,768]{1,0:T(8,128)(2,1)}, u32[]{:S(2)}, u32[]{:S(2)}) collective-permute-start(bf16[256,768]{1,0:T(8,128)(2,1)S(1)} %collective-permute-done.8), channel_id=1, source_target_pairs={{0,2},{2,0},{1,3},{3,1},{4,6},{6,4},{5,7},{7,5},{8,10},{10,8},{9,1... | collective-permute-start | bytes 1179656 | tf_op jit(solution)/shard_map/ppermute | solution.py:234
  39.7 11.9 %copy-start.5 = (bf16[2048,768]{1,0:T(8,128)(2,1)S(1)}, bf16[2048,768]{1,0:T(8,128)(2,1)}, u32[]{:S(2)}) copy-start(bf16[2048,768]{1,0:T(8,128)(2,1)} %constant_dynamic-update-slice_fusion.3) | copy-start | bytes 9437188
  46.2 10.0 %copy-start.3 = (bf16[2,512,2048]{2,1,0:T(8,128)(2,1)S(1)}, bf16[2,512,2048]{2,1,0:T(8,128)(2,1)}, u32[]{:S(2)}) copy-start(bf16[2,512,2048]{2,1,0:T(8,128)(2,1)} %norm.1) | copy-start | bytes 12582916
  46.2 35.2 %copy-start.17 = (bf16[128,2048]{1,0:T(8,128)(2,1)}, bf16[128,2048]{1,0:T(8,128)(2,1)S(1)}, u32[]{:S(2)}) copy-start(bf16[128,2048]{1,0:T(8,128)(2,1)S(1)} %collective-permute-done.11.c01) | copy-start | bytes 1572868
  47.3 8.8 %collective-permute-start.12 = (bf16[256,768]{1,0:T(8,128)(2,1)S(1)}, bf16[256,768]{1,0:T(8,128)(2,1)S(1)}, u32[]{:S(2)}, u32[]{:S(2)}) collective-permute-start(bf16[256,768]{1,0:T(8,128)(2,1)S(1)} %collective-permute-done.10), channel_id=1, source_target_pairs={{0,2},{2,0},{1,3},{3,1},{4,6},{6,4},{5,7},{7,5},{8,10},{10,8},{9,1... | collective-permute-start | bytes 1179656 | tf_op jit(solution)/shard_map/ppermute | solution.py:234
  48.9 11.2 %collective-permute-start.20 = (bf16[256,1024]{1,0:T(8,128)(2,1)S(1)}, bf16[256,1024]{1,0:T(8,128)(2,1)S(1)}, u32[]{:S(2)}, u32[]{:S(2)}) collective-permute-start(bf16[256,1024]{1,0:T(8,128)(2,1)S(1)} %get-tuple-element.80), channel_id=1, source_target_pairs={{0,4},{13,9},{20,16},{25,29},{2,6},{15,11},{22,18},{27,31}} | collective-permute-start | bytes 1572872 | tf_op jit(solution)/shard_map/ppermute | solution.py:281
  50.3 12.3 %collective-permute-start.16 = (bf16[256,1024]{1,0:T(8,128)(2,1)S(1)}, bf16[256,1024]{1,0:T(8,128)(2,1)S(1)}, u32[]{:S(2)}, u32[]{:S(2)}) collective-permute-start(bf16[256,1024]{1,0:T(8,128)(2,1)S(1)} %get-tuple-element.81), channel_id=1, source_target_pairs={{0,4},{13,9},{20,16},{25,29},{2,6},{15,11},{22,18},{27,31}} | collective-permute-start | bytes 1572872 | tf_op jit(solution)/shard_map/ppermute | solution.py:281
  56.2 29.5 %copy-start.6 = (bf16[2048,768]{1,0:T(8,128)(2,1)}, bf16[2048,768]{1,0:T(8,128)(2,1)S(1)}, u32[]{:S(2)}) copy-start(bf16[2048,768]{1,0:T(8,128)(2,1)S(1)} %constant_dynamic-update-slice_fusion.w.wm) | copy-start | bytes 9437188
  58.5 7.8 %collective-permute-start.21 = (bf16[2,2,128,256]{3,2,1,0:T(8,128)(2,1)S(1)}, bf16[2,2,128,256]{3,2,1,0:T(8,128)(2,1)S(1)}, u32[]{:S(2)}, u32[]{:S(2)}) collective-permute-start(bf16[2,2,128,256]{3,2,1,0:T(8,128)(2,1)S(1)} %fusion.15), channel_id=1, source_target_pairs={{0,2},{2,0},{1,3},{3,1},{4,6},{6,4},{5,7},{7,5},{8,10},{10,8},{9,1... | collective-permute-start | bytes 786440 | tf_op jit(solution)/shard_map/ppermute | solution.py:323
  62.7 21.6 %copy-start.10 = (bf16[256,1024]{1,0:T(8,128)(2,1)}, bf16[256,1024]{1,0:T(8,128)(2,1)S(1)}, u32[]{:S(2)}) copy-start(bf16[256,1024]{1,0:T(8,128)(2,1)S(1)} %get-tuple-element.42.refs_2_) | copy-start | bytes 1572868
  62.7 21.6 %copy-start.11 = (bf16[256,1024]{1,0:T(8,128)(2,1)}, bf16[256,1024]{1,0:T(8,128)(2,1)S(1)}, u32[]{:S(2)}) copy-start(bf16[256,1024]{1,0:T(8,128)(2,1)S(1)} %get-tuple-element.39.refs_0_) | copy-start | bytes 1572868
  62.7 11.3 %collective-permute-start.17 = (bf16[256,1024]{1,0:T(8,128)(2,1)S(1)}, bf16[256,1024]{1,0:T(8,128)(2,1)S(1)}, u32[]{:S(2)}, u32[]{:S(2)}) collective-permute-start(bf16[256,1024]{1,0:T(8,128)(2,1)S(1)} %get-tuple-element.39.refs_0_), channel_id=1, source_target_pairs={{4,8},{9,5},{20,24},{25,21},{6,10},{11,7},{22,26},{27,23}} | collective-permute-start | bytes 1572872 | tf_op jit(solution)/shard_map/ppermute | solution.py:281
  63.4 11.1 %collective-permute-start.18 = (bf16[256,1024]{1,0:T(8,128)(2,1)S(1)}, bf16[256,1024]{1,0:T(8,128)(2,1)S(1)}, u32[]{:S(2)}, u32[]{:S(2)}) collective-permute-start(bf16[256,1024]{1,0:T(8,128)(2,1)S(1)} %get-tuple-element.39.refs_0_), channel_id=1, source_target_pairs={{0,2},{2,0},{4,6},{6,4},{13,15},{15,13},{9,11},{11,9},{20,22},{22,... | collective-permute-start | bytes 1572872 | tf_op jit(solution)/shard_map/ppermute | solution.py:289
  66.3 8.8 %collective-permute-start.22 = (bf16[256,1024]{1,0:T(8,128)(2,1)S(1)}, bf16[256,1024]{1,0:T(8,128)(2,1)S(1)}, u32[]{:S(2)}, u32[]{:S(2)}) collective-permute-start(bf16[256,1024]{1,0:T(8,128)(2,1)S(1)} %get-tuple-element.42.refs_2_), channel_id=1, source_target_pairs={{4,8},{9,5},{20,24},{25,21},{6,10},{11,7},{22,26},{27,23}} | collective-permute-start | bytes 1572872 | tf_op jit(solution)/shard_map/ppermute | solution.py:281
  67.0 13.0 %collective-permute-start.23 = (bf16[256,1024]{1,0:T(8,128)(2,1)S(1)}, bf16[256,1024]{1,0:T(8,128)(2,1)S(1)}, u32[]{:S(2)}, u32[]{:S(2)}) collective-permute-start(bf16[256,1024]{1,0:T(8,128)(2,1)S(1)} %get-tuple-element.42.refs_2_), channel_id=1, source_target_pairs={{0,2},{2,0},{4,6},{6,4},{13,15},{15,13},{9,11},{11,9},{20,22},{22,... | collective-permute-start | bytes 1572872 | tf_op jit(solution)/shard_map/ppermute | solution.py:289
  70.2 11.3 %collective-permute-start.29 = (bf16[2,2,128,256]{3,2,1,0:T(8,128)(2,1)S(1)}, bf16[2,2,128,256]{3,2,1,0:T(8,128)(2,1)S(1)}, u32[]{:S(2)}, u32[]{:S(2)}) collective-permute-start(bf16[2,2,128,256]{3,2,1,0:T(8,128)(2,1)S(1)} %broadcast_select_fusion.2), channel_id=1, source_target_pairs={{0,4},{4,0},{8,12},{12,8},{1,5},{5,1},{9,13},{13,9},{2,6},{6,2},{1... | collective-permute-start | bytes 786440 | tf_op jit(solution)/shard_map/ppermute | solution.py:323
  74.0 15.1 %collective-permute-start.13 = (bf16[128,2048]{1,0:T(8,128)(2,1)S(1)}, bf16[128,2048]{1,0:T(8,128)(2,1)S(1)}, u32[]{:S(2)}, u32[]{:S(2)}) collective-permute-start(bf16[128,2048]{1,0:T(8,128)(2,1)S(1)} %copy-done.14), channel_id=1, source_target_pairs={{0,1},{1,0},{2,3},{3,2},{4,5},{5,4},{6,7},{7,6},{8,9},{9,8},{10,11... | collective-permute-start | bytes 1572872 | tf_op jit(solution)/shard_map/ppermute | solution.py:221
  74.5 14.6 %copy-start.18 = (bf16[256,1024]{1,0:T(8,128)(2,1)}, bf16[256,1024]{1,0:T(8,128)(2,1)S(1)}, u32[]{:S(2)}) copy-start(bf16[256,1024]{1,0:T(8,128)(2,1)S(1)} %collective-permute-done.18.refs_4_) | copy-start | bytes 1572868
  74.5 8.6 %collective-permute-start.19 = (bf16[256,1024]{1,0:T(8,128)(2,1)S(1)}, bf16[256,1024]{1,0:T(8,128)(2,1)S(1)}, u32[]{:S(2)}, u32[]{:S(2)}) collective-permute-start(bf16[256,1024]{1,0:T(8,128)(2,1)S(1)} %collective-permute-done.17), channel_id=1, source_target_pairs={{8,12},{5,1},{24,28},{21,17},{10,14},{7,3},{26,30},{23,19}} | collective-permute-start | bytes 1572872 | tf_op jit(solution)/shard_map/ppermute | solution.py:281
  80.1 3.9 %copy-start.19 = (bf16[256,1024]{1,0:T(8,128)(2,1)}, bf16[256,1024]{1,0:T(8,128)(2,1)S(1)}, u32[]{:S(2)}) copy-start(bf16[256,1024]{1,0:T(8,128)(2,1)S(1)} %collective-permute-done.23.refs_6_) | copy-start | bytes 1572868
  80.1 3.9 %collective-permute-start.24 = (bf16[256,1024]{1,0:T(8,128)(2,1)S(1)}, bf16[256,1024]{1,0:T(8,128)(2,1)S(1)}, u32[]{:S(2)}, u32[]{:S(2)}) collective-permute-start(bf16[256,1024]{1,0:T(8,128)(2,1)S(1)} %collective-permute-done.22), channel_id=1, source_target_pairs={{8,12},{5,1},{24,28},{21,17},{10,14},{7,3},{26,30},{23,19}} | collective-permute-start | bytes 1572872 | tf_op jit(solution)/shard_map/ppermute | solution.py:281
  81.4 18.1 %collective-permute-start.14 = (bf16[128,2048]{1,0:T(8,128)(2,1)S(1)}, bf16[128,2048]{1,0:T(8,128)(2,1)S(1)}, u32[]{:S(2)}, u32[]{:S(2)}) collective-permute-start(bf16[128,2048]{1,0:T(8,128)(2,1)S(1)} %collective-permute-done.11.c01), channel_id=1, source_target_pairs={{0,1},{1,0},{2,3},{3,2},{4,5},{5,4},{6,7},{7,6},{8,9},{9,8},{10,11... | collective-permute-start | bytes 1572872 | tf_op jit(solution)/shard_map/ppermute | solution.py:221
  81.8 15.3 %collective-permute-start.30 = (bf16[2,2,128,256]{3,2,1,0:T(8,128)(2,1)S(1)}, bf16[2,2,128,256]{3,2,1,0:T(8,128)(2,1)S(1)}, u32[]{:S(2)}, u32[]{:S(2)}) collective-permute-start(bf16[2,2,128,256]{3,2,1,0:T(8,128)(2,1)S(1)} %get-tuple-element.72), channel_id=1, source_target_pairs={{0,8},{4,12},{8,0},{12,4},{1,9},{5,13},{9,1},{13,5},{2,10},{6,14},... | collective-permute-start | bytes 786440 | tf_op jit(solution)/shard_map/ppermute | solution.py:323
  83.3 5.8 %copy-start.7 = (bf16[256,1024]{1,0:T(8,128)(2,1)}, bf16[256,1024]{1,0:T(8,128)(2,1)S(1)}, u32[]{:S(2)}) copy-start(bf16[256,1024]{1,0:T(8,128)(2,1)S(1)} %add.296.refs_1_) | copy-start | bytes 1572868
  83.3 16.2 %collective-permute-start.25 = (bf16[256,1024]{1,0:T(8,128)(2,1)S(1)}, bf16[256,1024]{1,0:T(8,128)(2,1)S(1)}, u32[]{:S(2)}, u32[]{:S(2)}) collective-permute-start(bf16[256,1024]{1,0:T(8,128)(2,1)S(1)} %add.296.refs_1_), channel_id=1, source_target_pairs={{8,10},{10,8},{12,14},{14,12},{5,7},{7,5},{1,3},{3,1},{24,26},{26,... | collective-permute-start | bytes 1572872 | tf_op jit(solution)/shard_map/ppermute | solution.py:289
  84.2 4.8 %copy-start.8 = (bf16[256,1024]{1,0:T(8,128)(2,1)}, bf16[256,1024]{1,0:T(8,128)(2,1)S(1)}, u32[]{:S(2)}) copy-start(bf16[256,1024]{1,0:T(8,128)(2,1)S(1)} %add.302.refs_3_) | copy-start | bytes 1572868
  84.2 16.9 %collective-permute-start.26 = (bf16[256,1024]{1,0:T(8,128)(2,1)S(1)}, bf16[256,1024]{1,0:T(8,128)(2,1)}, u32[]{:S(2)}, u32[]{:S(2)}) collective-permute-start(bf16[256,1024]{1,0:T(8,128)(2,1)S(1)} %add.302.refs_3_), channel_id=1, source_target_pairs={{8,10},{10,8},{12,14},{14,12},{5,7},{7,5},{1,3},{3,1},{24,26},{26,... | collective-permute-start | bytes 1572872 | tf_op jit(solution)/shard_map/ppermute | solution.py:289
  89.1 10.5 %copy-start.20 = (bf16[128,2048]{1,0:T(8,128)(2,1)}, bf16[128,2048]{1,0:T(8,128)(2,1)S(1)}, u32[]{:S(2)}) copy-start(bf16[128,2048]{1,0:T(8,128)(2,1)S(1)} %collective-permute-done.13.c10) | copy-start | bytes 1572868
  89.1 17.2 %collective-permute-start.27 = (bf16[2,128,256]{2,1,0:T(8,128)(2,1)S(1)}, bf16[2,128,256]{2,1,0:T(8,128)(2,1)S(1)}, u32[]{:S(2)}, u32[]{:S(2)}) collective-permute-start(bf16[2,128,256]{2,1,0:T(8,128)(2,1)S(1)} %get-tuple-element.84), channel_id=1, source_target_pairs={{0,2},{2,4},{4,6},{6,8},{8,10},{10,12},{12,14},{1,3},{3,5},{5,7},{... | collective-permute-start | bytes 393224 | tf_op jit(solution)/shard_map/ppermute | solution.py:387
  97.1 9.2 %collective-permute-start.28 = (bf16[2,128,256]{2,1,0:T(8,128)(2,1)S(1)}, bf16[2,128,256]{2,1,0:T(8,128)(2,1)S(1)}, u32[]{:S(2)}, u32[]{:S(2)}) collective-permute-start(bf16[2,128,256]{2,1,0:T(8,128)(2,1)S(1)} %get-tuple-element.82), channel_id=1, source_target_pairs={{2,0},{4,2},{6,4},{8,6},{10,8},{12,10},{14,12},{3,1},{5,3},{7,5},{... | collective-permute-start | bytes 393224 | tf_op jit(solution)/shard_map/ppermute | solution.py:387
  117.7 11.9 %collective-permute-start.35 = (bf16[2,2,128,256]{3,2,1,0:T(8,128)(2,1)}, bf16[2,2,128,256]{3,2,1,0:T(8,128)(2,1)S(1)}, u32[]{:S(2)}, u32[]{:S(2)}) collective-permute-start(bf16[2,2,128,256]{3,2,1,0:T(8,128)(2,1)} %get-tuple-element.53), channel_id=1, source_target_pairs={{0,2},{2,0},{1,3},{3,1},{4,6},{6,4},{5,7},{7,5},{8,10},{10,8},{9,1... | collective-permute-start | bytes 786440 | tf_op jit(solution)/shard_map/ppermute | solution.py:323
  120.4 9.2 %copy-start.12 = (bf16[2,2,128,256]{3,2,1,0:T(8,128)(2,1)S(1)}, bf16[2,2,128,256]{3,2,1,0:T(8,128)(2,1)}, u32[]{:S(2)}) copy-start(bf16[2,2,128,256]{3,2,1,0:T(8,128)(2,1)} %get-tuple-element.54) | copy-start | bytes 786436
  120.4 9.2 %copy-start.13 = (bf16[2,2,128,256]{3,2,1,0:T(8,128)(2,1)S(1)}, bf16[2,2,128,256]{3,2,1,0:T(8,128)(2,1)}, u32[]{:S(2)}) copy-start(bf16[2,2,128,256]{3,2,1,0:T(8,128)(2,1)} %get-tuple-element.52) | copy-start | bytes 786436
  120.4 9.4 %copy-start.29 = (bf16[2,128,256]{2,1,0:T(8,128)(2,1)S(1)}, bf16[2,128,256]{2,1,0:T(8,128)(2,1)}, u32[]{:S(2)}) copy-start(bf16[2,128,256]{2,1,0:T(8,128)(2,1)} %get-tuple-element.50) | copy-start | bytes 393220
  120.4 10.7 %copy-start.28 = (bf16[2,128,256]{2,1,0:T(8,128)(2,1)S(1)}, bf16[2,128,256]{2,1,0:T(8,128)(2,1)}, u32[]{:S(2)}) copy-start(bf16[2,128,256]{2,1,0:T(8,128)(2,1)} %get-tuple-element.51) | copy-start | bytes 393220
  125.4 15.0 %copy-start.9 = (f32[256,2048]{1,0:T(8,128)S(1)}, f32[256,2048]{1,0:T(8,128)}, u32[]{:S(2)}) copy-start(f32[256,2048]{1,0:T(8,128)} %get-tuple-element.47) | copy-start | bytes 6291460
  125.4 15.0 %collective-permute-start.31 = (bf16[256,2048]{1,0:T(8,128)(2,1)}, bf16[256,2048]{1,0:T(8,128)(2,1)S(1)}, u32[]{:S(2)}, u32[]{:S(2)}) collective-permute-start(bf16[256,2048]{1,0:T(8,128)(2,1)} %get-tuple-element.48), channel_id=1, source_target_pairs={{0,1},{1,0},{2,3},{3,2},{4,5},{5,4},{6,7},{7,6},{8,9},{9,8},{10,11... | collective-permute-start | bytes 3145736 | tf_op jit(solution)/shard_map/ppermute | solution.py:221
  129.7 9.2 %collective-permute-start.36 = (bf16[2,2,128,256]{3,2,1,0:T(8,128)(2,1)S(1)}, bf16[2,2,128,256]{3,2,1,0:T(8,128)(2,1)S(1)}, u32[]{:S(2)}, u32[]{:S(2)}) collective-permute-start(bf16[2,2,128,256]{3,2,1,0:T(8,128)(2,1)S(1)} %broadcast_select_fusion), channel_id=1, source_target_pairs={{0,4},{4,0},{8,12},{12,8},{1,5},{5,1},{9,13},{13,9},{2,6},{6,2},{1... | collective-permute-start | bytes 786440 | tf_op jit(solution)/shard_map/ppermute | solution.py:323
  129.8 23.7 %collective-permute-start.33 = (bf16[2,128,256]{2,1,0:T(8,128)(2,1)S(1)}, bf16[2,128,256]{2,1,0:T(8,128)(2,1)S(1)}, u32[]{:S(2)}, u32[]{:S(2)}) collective-permute-start(bf16[2,128,256]{2,1,0:T(8,128)(2,1)S(1)} %copy-done.29), channel_id=1, source_target_pairs={{2,0},{4,2},{6,4},{8,6},{10,8},{12,10},{14,12},{3,1},{5,3},{7,5},{... | collective-permute-start | bytes 393224 | tf_op jit(solution)/shard_map/ppermute | solution.py:441
  131.1 22.4 %collective-permute-start.34 = (bf16[2,128,256]{2,1,0:T(8,128)(2,1)S(1)}, bf16[2,128,256]{2,1,0:T(8,128)(2,1)S(1)}, u32[]{:S(2)}, u32[]{:S(2)}) collective-permute-start(bf16[2,128,256]{2,1,0:T(8,128)(2,1)S(1)} %copy-done.28), channel_id=1, source_target_pairs={{0,2},{2,4},{4,6},{6,8},{8,10},{10,12},{12,14},{1,3},{3,5},{5,7},{... | collective-permute-start | bytes 393224 | tf_op jit(solution)/shard_map/ppermute | solution.py:441
  139.2 13.2 %collective-permute-start.37 = (bf16[2,2,128,256]{3,2,1,0:T(8,128)(2,1)S(1)}, bf16[2,2,128,256]{3,2,1,0:T(8,128)(2,1)S(1)}, u32[]{:S(2)}, u32[]{:S(2)}) collective-permute-start(bf16[2,2,128,256]{3,2,1,0:T(8,128)(2,1)S(1)} %get-tuple-element.64), channel_id=1, source_target_pairs={{0,8},{4,12},{8,0},{12,4},{1,9},{5,13},{9,1},{13,5},{2,10},{6,14},... | collective-permute-start | bytes 786440 | tf_op jit(solution)/shard_map/ppermute | solution.py:323
  140.7 12.8 %collective-permute-start.32 = (bf16[128,2048]{1,0:T(8,128)(2,1)S(1)}, bf16[128,2048]{1,0:T(8,128)(2,1)S(1)}, u32[]{:S(2)}, u32[]{:S(2)}) collective-permute-start(bf16[128,2048]{1,0:T(8,128)(2,1)S(1)} %slice.101), channel_id=1, source_target_pairs={{0,16},{16,0},{1,17},{17,1},{2,18},{18,2},{3,19},{19,3},{4,20},{20... | collective-permute-start | bytes 1572872 | tf_op jit(solution)/shard_map/ppermute | solution.py:221
  154.2 5.5 %copy-start.1 = (bf16[128,2048]{1,0:T(8,128)(2,1)S(1)}, bf16[128,2048]{1,0:T(8,128)(2,1)}, u32[]{:S(2)}) copy-start(bf16[128,2048]{1,0:T(8,128)(2,1)} %h00.1) | copy-start | bytes 1572868
  159.6 18.3 %copy-start.2 = (f32[256,2048]{1,0:T(8,128)S(1)}, f32[256,2048]{1,0:T(8,128)}, u32[]{:S(2)}) copy-start(f32[256,2048]{1,0:T(8,128)} %get-tuple-element.62) | copy-start | bytes 6291460
  159.6 2.9 %collective-permute-start.38 = (bf16[256,2048]{1,0:T(8,128)(2,1)}, bf16[256,2048]{1,0:T(8,128)(2,1)S(1)}, u32[]{:S(2)}, u32[]{:S(2)}) collective-permute-start(bf16[256,2048]{1,0:T(8,128)(2,1)} %get-tuple-element.63), channel_id=1, source_target_pairs={{0,1},{1,0},{2,3},{3,2},{4,5},{5,4},{6,7},{7,6},{8,9},{9,8},{10,11... | collective-permute-start | bytes 3145736 | tf_op jit(solution)/shard_map/ppermute | solution.py:221
  163.9 14.0 %collective-permute-start.39 = (bf16[128,2048]{1,0:T(8,128)(2,1)S(1)}, bf16[128,2048]{1,0:T(8,128)(2,1)S(1)}, u32[]{:S(2)}, u32[]{:S(2)}) collective-permute-start(bf16[128,2048]{1,0:T(8,128)(2,1)S(1)} %add_convert_fusion), channel_id=1, source_target_pairs={{0,16},{16,0},{1,17},{17,1},{2,18},{18,2},{3,19},{19,3},{4,20},{20... | collective-permute-start | bytes 1572872 | tf_op jit(solution)/shard_map/ppermute | solution.py:221
  (9 other events, 6.8 us)
